TPU v7x, 32 devices: a whole 2x2x4 slice. The times are simulated.
32 devices in a mesh: batch: 16 (over z, y, core), seq: 2 (over x).
Axes of the slice: x: 2, y: 2, z: 4, core: 2. Of those that a mesh axis runs over, the one named last changes fastest.
Arguments:
- frames: bfloat16 [4096, 1024], P(('batch', 'seq')), may hold values from -6 to 6
- lengths: int32 [16, 4], P('batch'), may hold values from 1 to 128, as said below
- cotangent: bfloat16 [4096, 1024], P(('batch', 'seq')), may hold values from -6 to 6
- ffn1_in: bfloat16 [1024, 4096], P(('batch', 'seq')), may hold values from -0.1875 to 0.1875
- ffn1_out: bfloat16 [4096, 1024], P(('batch', 'seq')), may hold values from -0.1875 to 0.1875
- query_w: bfloat16 [1024, 1024], P(('batch', 'seq')), may hold values from -0.1875 to 0.1875
- key_w: bfloat16 [1024, 1024], P(('batch', 'seq')), may hold values from -0.1875 to 0.1875
- value_w: bfloat16 [1024, 1024], P(('batch', 'seq')), may hold values from -0.1875 to 0.1875
- out_w: bfloat16 [1024, 1024], P(('batch', 'seq')), may hold values from -0.75 to 0.75
- point_in: bfloat16 [1024, 2048], P(('batch', 'seq')), may hold values from -0.1875 to 0.1875
- point_out: bfloat16 [1024, 1024], P(('batch', 'seq')), may hold values from -0.375 to 0.375
- ffn2_in: bfloat16 [1024, 4096], P(('batch', 'seq')), may hold values from -0.1875 to 0.1875
- ffn2_out: bfloat16 [4096, 1024], P(('batch', 'seq')), may hold values from -0.1875 to 0.1875
- depth_w: bfloat16 [5, 1024], replicated, may hold values from -2.5 to 2.5
- rel_table: bfloat16 [73, 128], replicated, may hold values from -4 to 4
- norm_gains: float32 [5, 1024], replicated, may hold values from 0.25 to 1.75
- norm_biases: float32 [5, 1024], replicated, may hold values from -2 to 2
- bn_gain: float32 [1024], replicated, may hold values from 0.25 to 1.75
- bn_shift: float32 [1024], replicated, may hold values from -2 to 2
Outputs:
- out_frames: bfloat16 [4096, 1024], P(('batch', 'seq'))
- grad_frames: bfloat16 [4096, 1024], P(('batch', 'seq'))
- grad_ffn1_in: float32 [1024, 4096], P(('batch', 'seq'))
- grad_ffn1_out: float32 [4096, 1024], P(('batch', 'seq'))
- grad_query_w: float32 [1024, 1024], P(('batch', 'seq'))
- grad_key_w: float32 [1024, 1024], P(('batch', 'seq'))
- grad_value_w: float32 [1024, 1024], P(('batch', 'seq'))
- grad_out_w: float32 [1024, 1024], P(('batch', 'seq'))
- grad_point_in: float32 [1024, 2048], P(('batch', 'seq'))
- grad_point_out: float32 [1024, 1024], P(('batch', 'seq'))
- grad_ffn2_in: float32 [1024, 4096], P(('batch', 'seq'))
- grad_ffn2_out: float32 [4096, 1024], P(('batch', 'seq'))
- grad_depth: float32 [5, 1024], replicated
- grad_rel: float32 [73, 128], replicated
- grad_gains: float32 [5, 1024], replicated
- grad_biases: float32 [5, 1024], replicated
- grad_bn_gain: float32 [1024], replicated
- grad_bn_shift: float32 [1024], replicated
- sample_variance: float32 [1024], replicated
Inputs may be any that keep to these rules, and one draw needn't show every extreme that they name: In each row the first 3 entries are the lengths of the utterances packed in order into the group, the last entry the frames of the padded tail; each row sums to 256. Some group holds an utterance of 128 frames.
All inputs are finite; a program needn't handle non-finite values.
Results may differ from a plain program's by a relative error of at most 0.023.
Values may be sent and summed in bfloat16 or wider, within the bound.
A program may use at most 256 MiB of HBM per device.

v0:
```python
import math

import jax
import jax.numpy as jnp
from jax import lax
from jax.sharding import PartitionSpec as P

HEADS = 8
REL_LEFT = 64
REL_RIGHT = 8


epsilon = 1e-05
masked_score = -1000000000.0


def padded_2(shard, sides, width):
    for axis, dim in sides:
        peers, length = (lax.axis_size(axis), shard.shape[dim])
        up = [(i, (i + 1) % peers) for i in range(peers - 1)]
        down = [(j, i) for i, j in up]
        last = lax.slice_in_dim(shard, length - width, length, axis=dim)
        first = lax.slice_in_dim(shard, 0, width, axis=dim)
        before = lax.ppermute(last, axis, up)
        after = lax.ppermute(first, axis, down)
        shard = jnp.concatenate([before, shard, after], axis=dim)
    return shard


def matmul(left, right):
    return jnp.dot(left, right, preferred_element_type=jnp.float32)


def transposed_left(left, right):
    return lax.dot_general(
        left, right, (((0,), (0,)), ((), ())), preferred_element_type=jnp.float32
    )


def transposed_right(left, right):
    return lax.dot_general(
        left, right, (((1,), (1,)), ((), ())), preferred_element_type=jnp.float32
    )


def flat_rows(matrices):
    return tuple((matrix.reshape(-1, 128) for matrix in matrices))


def block_rows_back(shards, matrices):
    return tuple((shard.reshape(-1, matrix.shape[1]) for shard, matrix in zip(shards, matrices)))


def swish_slope(values):
    sigma = jax.nn.sigmoid(values)
    return sigma * (1.0 + values * (1.0 - sigma))


def norm_forward(values, gain, shift):
    mean = jnp.mean(values, axis=-1, keepdims=True)
    centred = values - mean
    inverse = lax.rsqrt(jnp.mean(centred * centred, axis=-1, keepdims=True) + epsilon)
    unit = centred * inverse
    return (unit * gain + shift, unit, inverse)


def norm_backward(d_out, unit, inverse, gain):
    d_unit = d_out * gain
    d_values = inverse * (
        d_unit
        - jnp.mean(d_unit, axis=-1, keepdims=True)
        - unit * jnp.mean(d_unit * unit, axis=-1, keepdims=True)
    )
    return (d_values, jnp.sum(d_out * unit, axis=0), jnp.sum(d_out, axis=0))


def ffn_forward(values, gain, shift, weight_in, weight_out):
    normed, unit, inverse = norm_forward(values, gain, shift)
    hidden = normed.astype(jnp.bfloat16)
    act = matmul(hidden, weight_in)
    swish = jax.nn.silu(act).astype(jnp.bfloat16)
    return (values + 0.5 * matmul(swish, weight_out), (hidden, act, swish, unit, inverse))


def ffn_backward(d_out, kept, gain, weight_in, weight_out):
    hidden, act, swish, unit, inverse = kept
    d_branch = (0.5 * d_out).astype(jnp.bfloat16)
    grad_out = transposed_left(swish, d_branch)
    d_act = (transposed_right(d_branch, weight_out) * swish_slope(act)).astype(jnp.bfloat16)
    grad_in = transposed_left(hidden, d_act)
    d_norm, d_gain, d_shift = norm_backward(transposed_right(d_act, weight_in), unit, inverse, gain)
    return (d_out + d_norm, grad_in, grad_out, d_gain, d_shift)


def segment_ids(place, ends, group):
    inside = jnp.sum((place[:, None] >= ends[None, :]).astype(jnp.int32), axis=1)
    return jnp.where((place >= 0) & (place < group), inside, -1)


def to_heads(hidden, weight, heads):
    return matmul(hidden, weight).astype(jnp.bfloat16).reshape(hidden.shape[0], heads, -1)


def spread_band(project, start, group, left, right):
    heads, rows, width = project.shape
    band = rows + width - 1
    blank = jnp.zeros_like(project[:, :, :1])
    middle = jnp.concatenate([blank, project[:, :, 1 : width - 1], blank], axis=2)
    padded = jnp.pad(middle, ((0, 0), (0, 0), (0, band + 1 - width)))
    skewed = padded.reshape(heads, rows * (band + 1))[:, : rows * band].reshape(heads, rows, band)
    canvas = jnp.zeros((heads, rows, group + left + right), jnp.float32)
    anchor = jnp.zeros((), jnp.int32)
    canvas = lax.dynamic_update_slice(canvas, skewed, (anchor, anchor, start))
    return canvas[:, :, left : left + group]


def relative_bins(grad, difference, start, width, left, right):
    heads, rows, group = grad.shape
    band = rows + width - 1
    canvas = jnp.pad(grad, ((0, 0), (0, 0), (left, right)))
    anchor = jnp.zeros((), jnp.int32)
    strip = lax.dynamic_slice(canvas, (anchor, anchor, start), (heads, rows, band))
    flat = jnp.pad(strip.reshape(heads, rows * band), ((0, 0), (0, rows)))
    inner = flat.reshape(heads, rows, band + 1)[:, :, 1 : width - 1]
    below = jnp.sum(jnp.where(difference[None] <= -left, grad, 0.0), axis=2, keepdims=True)
    above = jnp.sum(jnp.where(difference[None] >= right, grad, 0.0), axis=2, keepdims=True)
    return jnp.concatenate([below, inner, above], axis=2)


def block_scores(rows_query, keys, table, segment, start, left, right):
    rows, heads, depth = rows_query.shape
    group = keys.shape[0]
    width = table.shape[0]
    scale = 1.0 / math.sqrt(depth)
    project = jnp.einsum("qhd,rd->hqr", rows_query, table, preferred_element_type=jnp.float32)
    content = jnp.einsum("qhd,khd->hqk", rows_query, keys, preferred_element_type=jnp.float32)
    key_place = jnp.arange(group, dtype=jnp.int32)
    row_place = start + jnp.arange(rows, dtype=jnp.int32)
    difference = key_place[None, :] - row_place[:, None]
    relative = spread_band(project, start, group, left, right)
    relative = relative + jnp.where(difference[None] <= -left, project[:, :, :1], 0.0)
    relative = relative + jnp.where(difference[None] >= right, project[:, :, width - 1 :], 0.0)
    row_segment = lax.dynamic_slice_in_dim(segment, start, rows)
    same = row_segment[:, None] == segment[None, :]
    return (jnp.where(same[None], scale * (content + relative), masked_score), difference)


def attention_forward(query, keys, values, table, segment, block_rows, left, right):
    group = query.shape[0]
    starts = jnp.arange(group // block_rows, dtype=jnp.int32) * block_rows

    def one_block(carry, start):
        rows_query = lax.dynamic_slice_in_dim(query, start, block_rows, 0)
        scores, difference = block_scores(rows_query, keys, table, segment, start, left, right)
        top = jnp.max(scores, axis=2, keepdims=True)
        weights = jnp.exp(scores - top)
        total = jnp.sum(weights, axis=2, keepdims=True)
        probs = (weights / total).astype(jnp.bfloat16)
        rows_out = jnp.einsum("hqk,khd->qhd", probs, values, preferred_element_type=jnp.float32)
        return (carry, (rows_out.astype(jnp.bfloat16), (top + jnp.log(total))[:, :, 0]))

    unused, (pieces, log_total) = lax.scan(one_block, 0, starts)
    return (pieces.reshape(query.shape), log_total)


def attention_backward(
    query, keys, values, table, segment, log_total, d_context, block_rows, left, right
):
    group, heads, depth = query.shape
    width = table.shape[0]
    scale = 1.0 / math.sqrt(depth)
    starts = jnp.arange(group // block_rows, dtype=jnp.int32) * block_rows

    def one_block(carry, operands):
        d_keys, d_values, d_table = carry
        start, block_total = operands
        rows_query = lax.dynamic_slice_in_dim(query, start, block_rows, 0)
        rows_grad = lax.dynamic_slice_in_dim(d_context, start, block_rows, 0)
        scores, difference = block_scores(rows_query, keys, table, segment, start, left, right)
        probs = jnp.exp(scores - block_total[:, :, None])
        d_values = d_values + jnp.einsum(
            "hqk,qhd->khd",
            probs.astype(jnp.bfloat16),
            rows_grad,
            preferred_element_type=jnp.float32,
        )
        d_probs = jnp.einsum("qhd,khd->hqk", rows_grad, values, preferred_element_type=jnp.float32)
        weighted = jnp.sum(probs * d_probs, axis=2, keepdims=True)
        d_scores = (probs * (d_probs - weighted)).astype(jnp.bfloat16)
        bins = relative_bins(
            scale * d_scores.astype(jnp.float32), difference, start, width, left, right
        )
        bins = bins.astype(jnp.bfloat16)
        d_rows = scale * jnp.einsum(
            "hqk,khd->qhd", d_scores, keys, preferred_element_type=jnp.float32
        )
        d_rows = d_rows + jnp.einsum("hqr,rd->qhd", bins, table, preferred_element_type=jnp.float32)
        d_keys = d_keys + scale * jnp.einsum(
            "hqk,qhd->khd", d_scores, rows_query, preferred_element_type=jnp.float32
        )
        d_table = d_table + jnp.einsum(
            "hqr,qhd->rd", bins, rows_query, preferred_element_type=jnp.float32
        )
        return ((d_keys, d_values, d_table), d_rows.astype(jnp.bfloat16))

    zeros_heads = jnp.zeros(query.shape, jnp.float32)
    zeros_table = jnp.zeros(table.shape, jnp.float32)
    (d_keys, d_values, d_table), d_rows = lax.scan(
        one_block, (zeros_heads, zeros_heads, zeros_table), (starts, log_total)
    )
    return (
        d_rows.reshape(query.shape),
        d_keys.astype(jnp.bfloat16),
        d_values.astype(jnp.bfloat16),
        d_table,
    )


def on_device(
    frames,
    lengths,
    cotangent,
    ffn1_in,
    ffn1_out,
    query_w,
    key_w,
    value_w,
    out_w,
    point_in,
    point_out,
    ffn2_in,
    ffn2_out,
    depth_w,
    rel_table,
    norm_gains,
    norm_biases,
    bn_gain,
    bn_shift,
):
    seq_count = lax.axis_size("seq")
    seq_rank = lax.axis_index("seq")
    frames_here, width = frames.shape
    group = frames_here * seq_count
    block_rows = min(512, group)
    kernel_size = depth_w.shape[0]
    reach = kernel_size // 2
    ends = jnp.cumsum(lengths[0])
    last_entry = lengths.shape[1] - 1
    first = seq_rank * frames_here
    wide_place = first - reach + jnp.arange(frames_here + 2 * reach, dtype=jnp.int32)
    wide_segment = segment_ids(wide_place, ends, group)
    own_segment = wide_segment[reach : reach + frames_here]
    mask = (own_segment < last_entry).astype(jnp.float32)[:, None]
    group_segment = segment_ids(jnp.arange(group, dtype=jnp.int32), ends, group)
    gathered = (
        lax.all_gather(ffn1_in, ("batch", "seq"), axis=0, tiled=True),
        lax.all_gather(ffn1_out, ("batch", "seq"), axis=0, tiled=True),
        lax.all_gather(query_w, ("batch", "seq"), axis=0, tiled=True),
        lax.all_gather(key_w, ("batch", "seq"), axis=0, tiled=True),
        lax.all_gather(value_w, ("batch", "seq"), axis=0, tiled=True),
        lax.all_gather(out_w, ("batch", "seq"), axis=0, tiled=True),
        lax.all_gather(point_in, ("batch", "seq"), axis=0, tiled=True),
        lax.all_gather(point_out, ("batch", "seq"), axis=0, tiled=True),
        lax.all_gather(ffn2_in, ("batch", "seq"), axis=0, tiled=True),
        lax.all_gather(ffn2_out, ("batch", "seq"), axis=0, tiled=True),
    )
    start_values = frames.astype(jnp.float32)
    after_first, kept_first = ffn_forward(
        start_values, norm_gains[0], norm_biases[0], gathered[0], gathered[1]
    )
    attn_norm, attn_unit, attn_inverse = norm_forward(after_first, norm_gains[1], norm_biases[1])
    attn_hidden = attn_norm.astype(jnp.bfloat16)
    query_heads, key_heads, value_heads = (
        lax.all_to_all(
            to_heads(attn_hidden, gathered[2], HEADS),
            "seq",
            split_axis=1,
            concat_axis=0,
            tiled=True,
        ),
        lax.all_to_all(
            to_heads(attn_hidden, gathered[3], HEADS),
            "seq",
            split_axis=1,
            concat_axis=0,
            tiled=True,
        ),
        lax.all_to_all(
            to_heads(attn_hidden, gathered[4], HEADS),
            "seq",
            split_axis=1,
            concat_axis=0,
            tiled=True,
        ),
    )
    context_heads, log_total = attention_forward(
        query_heads,
        key_heads,
        value_heads,
        rel_table,
        group_segment,
        block_rows,
        REL_LEFT,
        REL_RIGHT,
    )
    context = lax.all_to_all(context_heads, "seq", split_axis=0, concat_axis=1, tiled=True).reshape(
        frames_here, width
    )
    after_attn = after_first + matmul(context, gathered[5])
    conv_norm, conv_unit, conv_inverse = norm_forward(after_attn, norm_gains[2], norm_biases[2])
    conv_hidden = conv_norm.astype(jnp.bfloat16)
    pointwise = matmul(conv_hidden, gathered[6])
    gate_half = pointwise[:, :width]
    sigma_half = jax.nn.sigmoid(pointwise[:, width:])
    gated = (gate_half * sigma_half).astype(jnp.bfloat16)
    gated_wide = padded_2(gated, (("seq", 0),), reach)
    kernel = depth_w.astype(jnp.float32)
    mixed = jnp.zeros((frames_here, width), jnp.float32)
    for offset in range(kernel_size):
        same = (wide_segment[offset : offset + frames_here] == own_segment).astype(jnp.float32)[
            :, None
        ]
        mixed = (
            mixed
            + kernel[offset] * gated_wide[offset : offset + frames_here].astype(jnp.float32) * same
        )
    total, squares, count = lax.psum(
        (jnp.sum(mixed * mask, axis=0), jnp.sum(mixed * mixed * mask, axis=0), jnp.sum(mask)),
        ("batch", "seq"),
    )
    mean = total / count
    var = squares / count - mean * mean
    bn_inverse = lax.rsqrt(var + epsilon)
    centred = (mixed - mean) * bn_inverse
    bn_out = centred * bn_gain + bn_shift
    conv_swish = jax.nn.silu(bn_out).astype(jnp.bfloat16)
    after_conv = after_attn + matmul(conv_swish, gathered[7])
    after_second, kept_second = ffn_forward(
        after_conv, norm_gains[3], norm_biases[3], gathered[8], gathered[9]
    )
    final_norm, final_unit, final_inverse = norm_forward(
        after_second, norm_gains[4], norm_biases[4]
    )
    sample_variance = var * count / (count - 1.0)
    regathered = (
        lax.all_gather(ffn1_in, ("batch", "seq"), axis=0, tiled=True),
        lax.all_gather(ffn1_out, ("batch", "seq"), axis=0, tiled=True),
        lax.all_gather(query_w, ("batch", "seq"), axis=0, tiled=True),
        lax.all_gather(key_w, ("batch", "seq"), axis=0, tiled=True),
        lax.all_gather(value_w, ("batch", "seq"), axis=0, tiled=True),
        lax.all_gather(out_w, ("batch", "seq"), axis=0, tiled=True),
        lax.all_gather(point_in, ("batch", "seq"), axis=0, tiled=True),
        lax.all_gather(point_out, ("batch", "seq"), axis=0, tiled=True),
        lax.all_gather(ffn2_in, ("batch", "seq"), axis=0, tiled=True),
        lax.all_gather(ffn2_out, ("batch", "seq"), axis=0, tiled=True),
    )
    d_final = cotangent.astype(jnp.float32) * mask
    d_second, gain_four, shift_four = norm_backward(
        d_final, final_unit, final_inverse, norm_gains[4]
    )
    d_conv_res, grad_two_in, grad_two_out, gain_three, shift_three = ffn_backward(
        d_second, kept_second, norm_gains[3], regathered[8], regathered[9]
    )
    conv_branch = d_conv_res.astype(jnp.bfloat16)
    grad_point_out = transposed_left(conv_swish, conv_branch)
    d_bn_out = transposed_right(conv_branch, regathered[7]) * swish_slope(bn_out)
    grad_bn_gain, grad_bn_shift = lax.psum(
        (jnp.sum(d_bn_out * centred * mask, axis=0), jnp.sum(d_bn_out * mask, axis=0)),
        ("batch", "seq"),
    )
    d_mixed = (
        bn_gain * bn_inverse * (d_bn_out - mask * (grad_bn_shift + centred * grad_bn_gain) / count)
    )
    d_mixed = d_mixed.astype(jnp.bfloat16)
    d_mixed_wide = padded_2(d_mixed, (("seq", 0),), reach)
    d_mixed_value = d_mixed.astype(jnp.float32)
    d_gated = jnp.zeros((frames_here, width), jnp.float32)
    kernel_rows = []
    for offset in range(kernel_size):
        same = (wide_segment[offset : offset + frames_here] == own_segment).astype(jnp.float32)[
            :, None
        ]
        shifted_in = gated_wide[offset : offset + frames_here].astype(jnp.float32)
        kernel_rows.append(jnp.sum(d_mixed_value * shifted_in * same, axis=0))
        back = 2 * reach - offset
        same_back = (wide_segment[back : back + frames_here] == own_segment).astype(jnp.float32)[
            :, None
        ]
        d_gated = (
            d_gated
            + kernel[offset]
            * d_mixed_wide[back : back + frames_here].astype(jnp.float32)
            * same_back
        )
    d_pointwise = jnp.concatenate(
        [d_gated * sigma_half, d_gated * gate_half * sigma_half * (1.0 - sigma_half)], axis=1
    ).astype(jnp.bfloat16)
    grad_point_in = transposed_left(conv_hidden, d_pointwise)
    d_conv_norm, gain_two, shift_two = norm_backward(
        transposed_right(d_pointwise, regathered[6]), conv_unit, conv_inverse, norm_gains[2]
    )
    d_attn_res = d_conv_res + d_conv_norm
    attn_branch = d_attn_res.astype(jnp.bfloat16)
    grad_out_w = transposed_left(context, attn_branch)
    d_context = (
        transposed_right(attn_branch, regathered[5])
        .astype(jnp.bfloat16)
        .reshape(frames_here, HEADS, -1)
    )
    d_context_heads = lax.all_to_all(d_context, "seq", split_axis=1, concat_axis=0, tiled=True)
    d_query_heads, d_key_heads, d_value_heads, d_table = attention_backward(
        query_heads,
        key_heads,
        value_heads,
        rel_table,
        group_segment,
        log_total,
        d_context_heads,
        block_rows,
        REL_LEFT,
        REL_RIGHT,
    )
    d_query, d_keys, d_values = (
        lax.all_to_all(d_query_heads, "seq", split_axis=0, concat_axis=1, tiled=True),
        lax.all_to_all(d_key_heads, "seq", split_axis=0, concat_axis=1, tiled=True),
        lax.all_to_all(d_value_heads, "seq", split_axis=0, concat_axis=1, tiled=True),
    )
    d_query = d_query.reshape(frames_here, width)
    d_keys = d_keys.reshape(frames_here, width)
    d_values = d_values.reshape(frames_here, width)
    grad_query_w = transposed_left(attn_hidden, d_query)
    grad_key_w = transposed_left(attn_hidden, d_keys)
    grad_value_w = transposed_left(attn_hidden, d_values)
    d_attn_hidden = (
        transposed_right(d_query, regathered[2])
        + transposed_right(d_keys, regathered[3])
        + transposed_right(d_values, regathered[4])
    )
    d_attn_norm, gain_one, shift_one = norm_backward(
        d_attn_hidden, attn_unit, attn_inverse, norm_gains[1]
    )
    d_first_res = d_attn_res + d_attn_norm
    d_input, grad_one_in, grad_one_out, gain_zero, shift_zero = ffn_backward(
        d_first_res, kept_first, norm_gains[0], regathered[0], regathered[1]
    )
    all_local = (
        grad_one_in,
        grad_one_out,
        grad_query_w,
        grad_key_w,
        grad_value_w,
        grad_out_w,
        grad_point_in,
        grad_point_out,
        grad_two_in,
        grad_two_out,
    )
    all_flat = flat_rows(all_local)
    shards = (
        lax.psum_scatter(all_flat[0], ("batch", "seq"), scatter_dimension=0, tiled=True),
        lax.psum_scatter(all_flat[1], ("batch", "seq"), scatter_dimension=0, tiled=True),
        lax.psum_scatter(all_flat[2], ("batch", "seq"), scatter_dimension=0, tiled=True),
        lax.psum_scatter(all_flat[3], ("batch", "seq"), scatter_dimension=0, tiled=True),
        lax.psum_scatter(all_flat[4], ("batch", "seq"), scatter_dimension=0, tiled=True),
        lax.psum_scatter(all_flat[5], ("batch", "seq"), scatter_dimension=0, tiled=True),
        lax.psum_scatter(all_flat[6], ("batch", "seq"), scatter_dimension=0, tiled=True),
        lax.psum_scatter(all_flat[7], ("batch", "seq"), scatter_dimension=0, tiled=True),
        lax.psum_scatter(all_flat[8], ("batch", "seq"), scatter_dimension=0, tiled=True),
        lax.psum_scatter(all_flat[9], ("batch", "seq"), scatter_dimension=0, tiled=True),
    )
    shards = block_rows_back(shards, all_local)
    gains_local = jnp.stack([gain_zero, gain_one, gain_two, gain_three, gain_four])
    shifts_local = jnp.stack([shift_zero, shift_one, shift_two, shift_three, shift_four])
    kernel_local = jnp.stack(kernel_rows)
    grad_gains, grad_biases, grad_depth, grad_rel = lax.psum(
        (gains_local, shifts_local, kernel_local, d_table), ("batch", "seq")
    )
    return (
        final_norm.astype(jnp.bfloat16),
        d_input.astype(jnp.bfloat16),
        shards[0],
        shards[1],
        shards[2],
        shards[3],
        shards[4],
        shards[5],
        shards[6],
        shards[7],
        shards[8],
        shards[9],
        grad_depth,
        grad_rel,
        grad_gains,
        grad_biases,
        grad_bn_gain,
        grad_bn_shift,
        sample_variance,
    )


def solution(mesh):
    placed = (
        P(("batch", "seq"), None),
        P("batch", None),
        P(("batch", "seq"), None),
        P(("batch", "seq"), None),
        P(("batch", "seq"), None),
        P(("batch", "seq"), None),
        P(("batch", "seq"), None),
        P(("batch", "seq"), None),
        P(("batch", "seq"), None),
        P(("batch", "seq"), None),
        P(("batch", "seq"), None),
        P(("batch", "seq"), None),
        P(("batch", "seq"), None),
        P(),
        P(),
        P(),
        P(),
        P(),
        P(),
    )
    return jax.shard_map(
        on_device,
        mesh=mesh,
        in_specs=placed,
        out_specs=(
            P(("batch", "seq"), None),
            P(("batch", "seq"), None),
            P(("batch", "seq"), None),
            P(("batch", "seq"), None),
            P(("batch", "seq"), None),
            P(("batch", "seq"), None),
            P(("batch", "seq"), None),
            P(("batch", "seq"), None),
            P(("batch", "seq"), None),
            P(("batch", "seq"), None),
            P(("batch", "seq"), None),
            P(("batch", "seq"), None),
            P(),
            P(),
            P(),
            P(),
            P(),
            P(),
            P(),
        ),
        check_vma=False,
    )
```

profile of v0, /device:TPU:0, one launch (start us, length us, event | category | flops | bytes accessed | tf_op | source)
XLA Modules:
  0.0 3185.3 jit_solution(1468941535966042250)
XLA Ops:
  19.6 71.4 %all-gather.11.cloned.1.call-done = bf16[1024,4096]{1,0:T(8,128)(2,1)} async-done(((bf16[32,4096]{1,0:T(8,128)(2,1)}), bf16[1024,4096]{1,0:T(8,128)(2,1)}) %all-gather.11.cloned.1.call-update) | async-done | bytes 8388624 | tf_op jit(solution)/shard_map/all_gather | solution.py:256
  91.1 6.0 fusion.93
  97.1 72.8 %all-gather.13.cloned.1.call-done = bf16[4096,1024]{1,0:T(8,128)(2,1)} async-done(((bf16[128,1024]{1,0:T(8,128)(2,1)}), bf16[4096,1024]{1,0:T(8,128)(2,1)}) %all-gather.13.cloned.1.call-update) | async-done | bytes 8388624 | tf_op jit(solution)/shard_map/all_gather | solution.py:257
  170.0 5.4 fusion.106
  175.8 52.3 %all-gather.19.cloned.1.call-done = bf16[1024,1024]{1,0:T(8,128)(2,1)} async-done(((bf16[32,1024]{1,0:T(8,128)(2,1)}), bf16[1024,1024]{1,0:T(8,128)(2,1)}) %all-gather.19.cloned.1.call-update) | async-done | bytes 2097168 | tf_op jit(solution)/shard_map/all_gather | solution.py:259
  230.9 3.4 all-to-all-start.2
  234.3 51.9 %all-gather.17.cloned.1.call-done = bf16[1024,1024]{1,0:T(8,128)(2,1)} async-done(((bf16[32,1024]{1,0:T(8,128)(2,1)}), bf16[1024,1024]{1,0:T(8,128)(2,1)}) %all-gather.17.cloned.1.call-update) | async-done | bytes 2097168 | tf_op jit(solution)/shard_map/all_gather | solution.py:258
  289.1 3.4 all-to-all-start.1
  292.5 51.9 %all-gather.15.cloned.1.call-done = bf16[1024,1024]{1,0:T(8,128)(2,1)} async-done(((bf16[32,1024]{1,0:T(8,128)(2,1)}), bf16[1024,1024]{1,0:T(8,128)(2,1)}) %all-gather.15.cloned.1.call-update) | async-done | bytes 2097168 | tf_op jit(solution)/shard_map/all_gather | solution.py:260
  347.3 3.4 all-to-all-start
  351.5 5.1 all-to-all-done
  363.0 3.1 reshape.389
  373.4 3.4 all-to-all-start.3
  377.7 4.3 all-to-all-done.3
  382.2 20.5 all-gather.21.cloned.1.call-done
  405.1 61.6 %all-gather.23.cloned.1.call-done = bf16[1024,2048]{1,0:T(8,128)(2,1)} async-done(((bf16[32,2048]{1,0:T(8,128)(2,1)}), bf16[1024,2048]{1,0:T(8,128)(2,1)}) %all-gather.23.cloned.1.call-update) | async-done | bytes 4194320 | tf_op jit(solution)/shard_map/all_gather | solution.py:262
  470.8 3.2 collective-permute-start
  476.0 3.5 collective-permute-done.1
  480.1 39.6 %all-reduce.5 = (f32[1024]{0:T(1024)S(1)}, f32[]{:T(128)}, f32[1024]{0:T(1024)S(1)}) all-reduce(f32[1024]{0:T(1024)S(1)} %get-tuple-element.100, f32[]{:T(128)} %fusion.90, f32[1024]{0:T(1024)S(1)} %get-tuple-element.99), channel_id=1, replica_groups=mesh['batch'=16,'seq'=2] {'batch','seq'}, use_global_device_ids=true, to_apply=%region_16.17 | all-reduce | flops 2049 | bytes 16392 | tf_op jit(solution)/shard_map/psum | solution.py:327
  527.4 76.8 %all-gather.27.cloned.1.call-done = bf16[1024,4096]{1,0:T(8,128)(2,1)} async-done(((bf16[32,4096]{1,0:T(8,128)(2,1)}), bf16[1024,4096]{1,0:T(8,128)(2,1)}) %all-gather.27.cloned.1.call-update) | async-done | bytes 8388624 | tf_op jit(solution)/shard_map/all_gather | solution.py:264
  604.2 6.1 fusion.97
  610.3 72.6 %all-gather.29.cloned.1.call-done = bf16[4096,1024]{1,0:T(8,128)(2,1)} async-done(((bf16[128,1024]{1,0:T(8,128)(2,1)}), bf16[4096,1024]{1,0:T(8,128)(2,1)}) %all-gather.29.cloned.1.call-update) | async-done | bytes 8388624 | tf_op jit(solution)/shard_map/all_gather | solution.py:265
  682.9 5.6 fusion.110
  689.7 6.8 fusion
  696.6 3.5 multiply_reduce_fusion.2
  704.9 4.9 reshape.411
  709.8 4.0 multiply_reduce_fusion.8
  713.8 40.7 %all-reduce.4 = (f32[1024]{0:T(1024)}, f32[1024]{0:T(1024)}) all-reduce(f32[1024]{0:T(1024)} %get-tuple-element.98, f32[1024]{0:T(1024)} %get-tuple-element.97), channel_id=1, replica_groups=mesh['batch'=16,'seq'=2] {'batch','seq'}, use_global_device_ids=true, to_apply=%region_28.29 | all-reduce | flops 2048 | bytes 16384 | tf_op jit(solution)/shard_map/psum | solution.py:367
  754.5 4.0 fusion.55
  759.9 4.5 collective-permute-start.3
  767.6 4.6 multiply_reduce_fusion.3
  775.9 4.9 reshape.407
  784.1 4.1 all-to-all-start.4
  788.3 6.7 all-to-all-done.4
  799.5 11.6 all_to_all.132
  813.6 3.7 fusion.114
  817.4 4.9 reshape.405
  826.1 9.2 all_to_all.133
  838.3 4.9 reshape.403
  847.1 3.4 reshape.392
  852.6 3.6 reshape.393
  860.8 8.9 all_to_all.134
  872.7 4.9 reshape.401
  878.6 4.7 fusion.63
  883.3 9.3 reshape.409
  893.8 9.9 fusion.77
  903.7 18.0 reshape.415
  922.9 8.2 fusion.96
  931.1 18.0 reshape.413
  956.1 8.1 fusion.78
  964.3 18.0 reshape.399
  984.0 6.5 fusion.1
  991.5 8.3 fusion.91
  999.8 18.0 reshape.397
  1020.0 6.5 fusion.33
  1032.0 102.3 %reduce-scatter.19.cloned.1.call-done = f32[256,128]{1,0:T(8,128)} async-done(((f32[8192,128]{1,0:T(8,128)}), f32[256,128]{1,0:T(8,128)}) %reduce-scatter.19.cloned.1.call-update) | async-done | bytes 131088 | tf_op jit(solution)/shard_map/reduce_scatter | solution.py:464
  1135.9 140.7 %reduce-scatter.17.cloned.1.call-done = f32[256,128]{1,0:T(8,128)} async-done(((f32[8192,128]{1,0:T(8,128)}), f32[256,128]{1,0:T(8,128)}) %reduce-scatter.17.cloned.1.call-update) | async-done | bytes 131088 | tf_op jit(solution)/shard_map/reduce_scatter | solution.py:463
  1278.2 139.1 %reduce-scatter.15.cloned.1.call-done = f32[256,128]{1,0:T(8,128)} async-done(((f32[8192,128]{1,0:T(8,128)}), f32[256,128]{1,0:T(8,128)}) %reduce-scatter.15.cloned.1.call-update) | async-done | bytes 131088 | tf_op jit(solution)/shard_map/reduce_scatter | solution.py:462
  1418.9 181.0 %reduce-scatter.23.cloned.1.call-done = f32[512,128]{1,0:T(8,128)} async-done(((f32[16384,128]{1,0:T(8,128)}), f32[512,128]{1,0:T(8,128)}) %reduce-scatter.23.cloned.1.call-update) | async-done | bytes 262160 | tf_op jit(solution)/shard_map/reduce_scatter | solution.py:466
  1601.6 358.7 %reduce-scatter.29.cloned.1.call-done = f32[1024,128]{1,0:T(8,128)} async-done(((f32[32768,128]{1,0:T(8,128)}), f32[1024,128]{1,0:T(8,128)}) %reduce-scatter.29.cloned.1.call-update) | async-done | bytes 524304 | tf_op jit(solution)/shard_map/reduce_scatter | solution.py:469
  1962.2 358.9 %reduce-scatter.27.cloned.1.call-done = f32[1024,128]{1,0:T(8,128)} async-done(((f32[32768,128]{1,0:T(8,128)}), f32[1024,128]{1,0:T(8,128)}) %reduce-scatter.27.cloned.1.call-update) | async-done | bytes 524304 | tf_op jit(solution)/shard_map/reduce_scatter | solution.py:468
  2323.0 359.0 %reduce-scatter.13.cloned.1.call-done = f32[1024,128]{1,0:T(8,128)} async-done(((f32[32768,128]{1,0:T(8,128)}), f32[1024,128]{1,0:T(8,128)}) %reduce-scatter.13.cloned.1.call-update) | async-done | bytes 524304 | tf_op jit(solution)/shard_map/reduce_scatter | solution.py:461
  2683.9 358.9 %reduce-scatter.11.cloned.1.call-done = f32[1024,128]{1,0:T(8,128)} async-done(((f32[32768,128]{1,0:T(8,128)}), f32[1024,128]{1,0:T(8,128)}) %reduce-scatter.11.cloned.1.call-update) | async-done | bytes 524304 | tf_op jit(solution)/shard_map/reduce_scatter | solution.py:460
  3044.7 127.8 %all-reduce.8.cloned.1.call-done = (f32[5,1024]{1,0:T(8,128)}, f32[73,128]{1,0:T(8,128)}, f32[5,1024]{1,0:T(8,128)}, f32[5,1024]{1,0:T(8,128)}) async-done(((f32[5,1024]{1,0:T(8,128)}, f32[73,128]{1,0:T(8,128)}, f32[5,1024]{1,0:T(8,128)}, f32[5,1024]{1,0:T(8,128)}), (f32[5,1024]{1,0:T(8,128)}, f32[73,128]{1,0:T(8,128)}, f32[5,1024]{1,0:T(8,128)}, f32[5,1024]{1,0:T(8,128)})) %all-reduce.8.cloned.1.call-update) | async-done | bytes 98832 | tf_op jit(solution)/shard_map/psum | solution.py:475
  (398 shorter events, 137.1 us)
Async XLA Ops:
  7.2 350.5 %copy-start = (bf16[73,128]{1,0:T(8,128)(2,1)S(1)}, bf16[73,128]{1,0:T(8,128)(2,1)}, u32[]{:S(2)}) copy-start(bf16[73,128]{1,0:T(8,128)(2,1)} %param.33) | copy-start | bytes 56068
  7.2 83.9 %copy-start.4 = (bf16[128,1024]{1,0:T(8,128)(2,1)S(1)}, bf16[128,1024]{1,0:T(8,128)(2,1)}, u32[]{:S(2)}) copy-start(bf16[128,1024]{1,0:T(8,128)(2,1)} %param.19) | copy-start | bytes 786436
  7.2 11.0 copy-start.77
  7.2 11.0 copy-start.78
  7.2 83.8 %all-gather.11.cloned.1.call-start = ((), (), s32[]{:S(2)}) async-start(), calls=%async_computation.18 | async-start | bytes 8650752 | tf_op jit(solution)/shard_map/all_gather | solution.py:256
  8.0 162.0 %all-gather.13.cloned.1.call-start = ((), (), s32[]{:S(2)}) async-start(), calls=%async_computation.19 | async-start | bytes 8650752 | tf_op jit(solution)/shard_map/all_gather | solution.py:257
  8.7 219.3 %all-gather.19.cloned.1.call-start = ((), (), s32[]{:S(2)}) async-start(), calls=%async_computation.22 | async-start | bytes 2162688 | tf_op jit(solution)/shard_map/all_gather | solution.py:259
  9.5 276.8 %all-gather.17.cloned.1.call-start = ((), (), s32[]{:S(2)}) async-start(), calls=%async_computation.21 | async-start | bytes 2162688 | tf_op jit(solution)/shard_map/all_gather | solution.py:258
  10.0 334.4 %all-gather.15.cloned.1.call-start = ((), (), s32[]{:S(2)}) async-start(), calls=%async_computation.20 | async-start | bytes 2162688 | tf_op jit(solution)/shard_map/all_gather | solution.py:260
  10.6 392.1 %all-gather.21.cloned.1.call-start = ((), (), s32[]{:S(2)}) async-start(), calls=%async_computation.23 | async-start | bytes 2162688 | tf_op jit(solution)/shard_map/all_gather | solution.py:261
  11.2 455.5 %all-gather.23.cloned.1.call-start = ((), (), s32[]{:S(2)}) async-start(), calls=%async_computation.24 | async-start | bytes 4325376 | tf_op jit(solution)/shard_map/all_gather | solution.py:262
  11.9 512.9 %all-gather.25.cloned.1.call-start = ((), (), s32[]{:S(2)}) async-start(), calls=%async_computation.25 | async-start | bytes 2162688 | tf_op jit(solution)/shard_map/all_gather | solution.py:263
  12.7 591.5 %all-gather.27.cloned.1.call-start = ((), (), s32[]{:S(2)}) async-start(), calls=%async_computation.26 | async-start | bytes 8650752 | tf_op jit(solution)/shard_map/all_gather | solution.py:264
  13.4 669.5 %all-gather.29.cloned.1.call-start = ((), (), s32[]{:S(2)}) async-start(), calls=%async_computation.27 | async-start | bytes 8650752 | tf_op jit(solution)/shard_map/all_gather | solution.py:265
  16.1 81.0 %copy-start.52 = (f32[128]{0:T(128)}, f32[128]{0:T(128)S(1)}, u32[]{:S(2)}) copy-start(f32[128]{0:T(128)S(1)} %broadcast_multiply_fusion.14) | copy-start | bytes 1540
  17.3 79.8 %copy-start.54 = (f32[128]{0:T(128)}, f32[128]{0:T(128)S(1)}, u32[]{:S(2)}) copy-start(f32[128]{0:T(128)S(1)} %add_rsqrt_fusion.5) | copy-start | bytes 1540
  18.3 78.9 %copy-start.46 = (f32[1,1024]{1,0:T(1,128)}, f32[1,1024]{1,0:T(1,128)S(1)}, u32[]{:S(2)}) copy-start(f32[1,1024]{1,0:T(1,128)S(1)} %get-tuple-element.140) | copy-start | bytes 12292
  18.9 78.2 %copy-start.48 = (f32[1,1024]{1,0:T(1,128)}, f32[1,1024]{1,0:T(1,128)S(1)}, u32[]{:S(2)}) copy-start(f32[1,1024]{1,0:T(1,128)S(1)} %get-tuple-element.145) | copy-start | bytes 12292
  175.4 55.5 %copy-start.83 = (f32[128]{0:T(128)}, f32[128]{0:T(128)S(1)}, u32[]{:S(2)}) copy-start(f32[128]{0:T(128)S(1)} %broadcast_multiply_fusion.13) | copy-start | bytes 1540
  175.6 55.3 %copy-start.91 = (f32[128]{0:T(128)}, f32[128]{0:T(128)S(1)}, u32[]{:S(2)}) copy-start(f32[128]{0:T(128)S(1)} %add_rsqrt_fusion.4) | copy-start | bytes 1540
  230.9 58.2 %all-to-all-start.2 = ((bf16[128,8,128]{2,0,1:T(8,128)(2,1)}), bf16[128,8,128]{2,0,1:T(8,128)(2,1)S(1)}, u32[]{:S(2)}, u32[]{:S(2)}) async-start(bf16[128,8,128]{2,0,1:T(8,128)(2,1)} %bitcast.164), calls=%async_computation.2 | async-start | bytes 524288 | tf_op jit(solution)/shard_map/all_to_all | solution.py:281
  289.1 58.2 %all-to-all-start.1 = ((bf16[128,8,128]{2,0,1:T(8,128)(2,1)}), bf16[128,8,128]{2,0,1:T(8,128)(2,1)S(1)}, u32[]{:S(2)}, u32[]{:S(2)}) async-start(bf16[128,8,128]{2,0,1:T(8,128)(2,1)} %bitcast.165), calls=%async_computation.1 | async-start | bytes 524288 | tf_op jit(solution)/shard_map/all_to_all | solution.py:274
  347.3 9.3 all-to-all-start
  351.4 18.4 copy-start.43
  351.5 18.4 copy-start.31
  373.4 8.6 all-to-all-start.3
  376.8 652.0 %reduce-scatter.25.cloned.1.call-start = ((), (), s32[]{:S(2)}) async-start(), calls=%async_computation.35 | async-start | bytes 4325376 | tf_op jit(solution)/shard_map/reduce_scatter | solution.py:467
  377.7 101.8 %copy-start.56 = (f32[128]{0:T(128)}, f32[128]{0:T(128)S(1)}, u32[]{:S(2)}) copy-start(f32[128]{0:T(128)S(1)} %get-tuple-element.159) | copy-start | bytes 1540
  377.7 101.8 %copy-start.85 = (f32[128]{0:T(128)}, f32[128]{0:T(128)S(1)}, u32[]{:S(2)}) copy-start(f32[128]{0:T(128)S(1)} %get-tuple-element.155) | copy-start | bytes 1540
  382.2 84.4 %copy-start.27 = (bf16[128,2,4,128]{0,3,2,1:T(8,128)(2,1)}, bf16[128,2,4,128]{0,3,2,1:T(8,128)(2,1)S(1)}, u32[]{:S(2)}) copy-start(bf16[128,2,4,128]{0,3,2,1:T(8,128)(2,1)S(1)} %copy.147) | copy-start | bytes 786436
  404.9 64.8 %copy-start.79 = (f32[128]{0:T(128)}, f32[128]{0:T(128)S(1)}, u32[]{:S(2)}) copy-start(f32[128]{0:T(128)S(1)} %broadcast_multiply_fusion.12) | copy-start | bytes 1540
  405.1 64.6 %copy-start.81 = (f32[128]{0:T(128)}, f32[128]{0:T(128)S(1)}, u32[]{:S(2)}) copy-start(f32[128]{0:T(128)S(1)} %add_rsqrt_fusion.3) | copy-start | bytes 1540
  466.7 12.9 copy-start.86
  466.7 12.9 copy-start.87
  466.7 12.9 copy-start.88
  470.7 50.9 %copy-start.66 = (f32[1024]{0:T(1024)S(1)}, f32[1024]{0:T(1024)}, u32[]{:S(2)}) copy-start(f32[1024]{0:T(1024)} %param.36) | copy-start | bytes 12292
  470.8 54.1 %copy-start.24 = (bf16[128,1024]{1,0:T(8,128)(2,1)}, bf16[128,1024]{1,0:T(8,128)(2,1)S(1)}, u32[]{:S(2)}) copy-start(bf16[128,1024]{1,0:T(8,128)(2,1)S(1)} %multiply_convert_fusion.9) | copy-start | bytes 786436
  470.8 5.1 collective-permute-start
  474.0 5.5 collective-permute-start.1
  476.0 48.9 %copy-start.59 = (bf16[2,1024]{1,0:T(2,128)(2,1)}, bf16[2,1024]{1,0:T(2,128)(2,1)S(1)}, u32[]{:S(2)}) copy-start(bf16[2,1024]{1,0:T(2,128)(2,1)S(1)} %collective-permute-done) | copy-start | bytes 12292
  479.5 45.4 %copy-start.60 = (bf16[2,1024]{1,0:T(2,128)(2,1)}, bf16[2,1024]{1,0:T(2,128)(2,1)S(1)}, u32[]{:S(2)}) copy-start(bf16[2,1024]{1,0:T(2,128)(2,1)S(1)} %collective-permute-done.1) | copy-start | bytes 12292
  688.5 11.6 copy-start.12
  688.5 11.6 copy-start.89
  688.7 11.4 copy-start.93
  689.6 10.5 copy-start.98
  689.7 10.5 copy-start.100
  709.8 320.7 %reduce-scatter.21.cloned.1.call-start = ((), (), s32[]{:S(2)}) async-start(), calls=%async_computation.33 | async-start | bytes 4325376 | tf_op jit(solution)/shard_map/reduce_scatter | solution.py:465
  754.5 12.8 copy-start.3
  758.6 5.9 collective-permute-start.2
  759.9 5.9 collective-permute-start.3
  784.1 10.9 all-to-all-start.4
  788.2 346.2 %reduce-scatter.19.cloned.1.call-start = ((), (), s32[]{:S(2)}) async-start(), calls=%async_computation.32 | async-start | bytes 4325376 | tf_op jit(solution)/shard_map/reduce_scatter | solution.py:464
  822.3 454.3 %reduce-scatter.17.cloned.1.call-start = ((), (), s32[]{:S(2)}) async-start(), calls=%async_computation.31 | async-start | bytes 4325376 | tf_op jit(solution)/shard_map/reduce_scatter | solution.py:463
  843.3 574.0 %reduce-scatter.15.cloned.1.call-start = ((), (), s32[]{:S(2)}) async-start(), calls=%async_computation.30 | async-start | bytes 4325376 | tf_op jit(solution)/shard_map/reduce_scatter | solution.py:462
  877.6 722.2 %reduce-scatter.23.cloned.1.call-start = ((), (), s32[]{:S(2)}) async-start(), calls=%async_computation.34 | async-start | bytes 8650752 | tf_op jit(solution)/shard_map/reduce_scatter | solution.py:466
  892.7 1067.5 %reduce-scatter.29.cloned.1.call-start = ((), (), s32[]{:S(2)}) async-start(), calls=%async_computation.37 | async-start | bytes 17301504 | tf_op jit(solution)/shard_map/reduce_scatter | solution.py:469
  921.7 1399.3 %reduce-scatter.27.cloned.1.call-start = ((), (), s32[]{:S(2)}) async-start(), calls=%async_computation.36 | async-start | bytes 17301504 | tf_op jit(solution)/shard_map/reduce_scatter | solution.py:468
  949.2 1732.8 %reduce-scatter.13.cloned.1.call-start = ((), (), s32[]{:S(2)}) async-start(), calls=%async_computation.29 | async-start | bytes 17301504 | tf_op jit(solution)/shard_map/reduce_scatter | solution.py:461
  982.3 9.2 copy-start.5
  982.3 9.1 copy-start.47
  982.3 9.1 copy-start.49
  982.4 2060.4 %reduce-scatter.11.cloned.1.call-start = ((), (), s32[]{:S(2)}) async-start(), calls=%async_computation.28 | async-start | bytes 17301504 | tf_op jit(solution)/shard_map/reduce_scatter | solution.py:460
  1017.9 2154.6 %all-reduce.8.cloned.1.call-start = ((), (), s32[]{:S(2)}) async-start(), calls=%async_computation.38 | async-start | bytes 278528 | tf_op jit(solution)/shard_map/psum | solution.py:475
  1599.8 1578.2 %copy-start.1 = (bf16[73,128]{1,0:T(8,128)(2,1)S(1)}, bf16[73,128]{1,0:T(8,128)(2,1)}, u32[]{:S(2)}) copy-start(bf16[73,128]{1,0:T(8,128)(2,1)} %param.33) | copy-start | bytes 56068
  (71 other events, 215.9 us)
Sparse Core Ops, SparseCore 0:
  11.1 79.9 all-gather.10
  94.1 75.8 all-gather.12
  172.9 55.0 all-gather.18
  230.9 55.3 all-gather.16
  289.1 55.3 all-gather.14
  347.3 55.3 all-gather.20
  405.7 60.9 all-gather.22
  469.6 55.2 all-gather.24
  527.9 76.2 all-gather.26
  607.0 75.8 all-gather.28
  709.9 140.9 reduce-scatter.24
  853.0 139.4 reduce-scatter.20
  994.7 139.5 reduce-scatter.18
  1136.5 140.0 reduce-scatter.16
  1278.7 138.4 reduce-scatter.14
  1419.4 180.3 reduce-scatter.22
  1602.0 358.2 reduce-scatter.28
  1962.4 358.6 reduce-scatter.26
  2323.3 358.6 reduce-scatter.12
  2684.1 358.6 reduce-scatter.10
  3049.5 122.9 all-reduce.7
where the time goes:
time: 3200 us; the launch traced here: 3190 us
  waiting for transfers between devices  2690 us (84%)
  local copies, waits for them, and re-layouts  183 us (6%)
  matrix products  136 us (4%)
  blocking collectives  110 us (3%)
    reduce_scatter x1, waiting for transfers between devices, on_device(): lax.psum_scatter(all_flat[1], ('batch', 'seq'), scatter_dimension=0, tile...  359 us
    reduce_scatter x1, waiting for transfers between devices, on_device(): lax.psum_scatter(all_flat[8], ('batch', 'seq'), scatter_dimension=0, tile...  359 us
    reduce_scatter x1, waiting for transfers between devices, on_device(): lax.psum_scatter(all_flat[0], ('batch', 'seq'), scatter_dimension=0, tile...  359 us
    reduce_scatter x1, waiting for transfers between devices, on_device(): lax.psum_scatter(all_flat[9], ('batch', 'seq'), scatter_dimension=0, tile...  359 us
    reduce_scatter x1, waiting for transfers between devices, on_device(): lax.psum_scatter(all_flat[6], ('batch', 'seq'), scatter_dimension=0, tile...  181 us
    reduce_scatter x1, waiting for transfers between devices, on_device(): lax.psum_scatter(all_flat[3], ('batch', 'seq'), scatter_dimension=0, tile...  141 us
    reduce_scatter x1, waiting for transfers between devices, on_device(): lax.psum_scatter(all_flat[2], ('batch', 'seq'), scatter_dimension=0, tile...  139 us
    psum x1, waiting for transfers between devices, on_device(): lax.psum((gains_local, shifts_local, kernel_local, d_table), ('batch', 's...  128 us
  transfers between devices with their start and end apart: 30, of which 24 were waited for; matrix products, arithmetic and copies ran while one was open for 9% of the time, Pallas kernels for 0%

commit v1 on v0

--- a/solution.py
+++ b/solution.py
@@ -1,9 +1,15 @@
+import functools
 import math
 
 import jax
 import jax.numpy as jnp
 from jax import lax
+from jax.experimental import pallas as pl
+from jax.experimental.pallas import tpu as pltpu
 from jax.sharding import PartitionSpec as P
+
+MESH = pl.DeviceIdType.MESH
+AXES = ("batch", "seq")
 
 HEADS = 8
 REL_LEFT = 64
@@ -43,12 +49,341 @@
     )
 
 
-def flat_rows(matrices):
-    return tuple((matrix.reshape(-1, 128) for matrix in matrices))
-
-
-def block_rows_back(shards, matrices):
-    return tuple((shard.reshape(-1, matrix.shape[1]) for shard, matrix in zip(shards, matrices)))
+class Cube:
+    def __init__(self, batch, seq):
+        self.seq_bits, self.batch_bits = (seq.bit_length() - 1, batch.bit_length() - 1)
+        self.count = self.seq_bits + self.batch_bits
+        self.core = self.seq_bits
+        wide = (self.batch_bits - 1) // 2
+        self.x = list(range(self.seq_bits))[::-1]
+        self.y = list(range(self.core + 1, self.core + 1 + wide))[::-1]
+        self.z = list(range(self.core + 1 + wide, self.count))[::-1]
+
+    def bit(self, k):
+        if k < self.seq_bits:
+            return lax.rem(lax.axis_index("seq") // (1 << k), 2)
+        return lax.rem(lax.axis_index("batch") // (1 << (k - self.seq_bits)), 2)
+
+    def partner(self, k):
+        batch, seq = (lax.axis_index("batch"), lax.axis_index("seq"))
+        step = 1 - 2 * self.bit(k)
+        if k < self.seq_bits:
+            return (batch, seq + step * (1 << k))
+        return (batch + step * (1 << (k - self.seq_bits)), seq)
+
+    def swap(self, values, k):
+        if k < self.seq_bits:
+            axis, step = ("seq", 1 << k)
+        else:
+            axis, step = ("batch", 1 << (k - self.seq_bits))
+        pairs = [(i, i ^ step) for i in range(lax.axis_size(axis))]
+        return lax.ppermute(values, axis, pairs)
+
+
+def greet(cube, bits):
+    barrier = pltpu.get_barrier_semaphore()
+    for k in bits:
+        pl.semaphore_signal(barrier, inc=1, device_id=cube.partner(k), device_id_type=MESH)
+    pl.semaphore_wait(barrier, len(bits))
+
+
+def gather_kernel(cube, orders, count, which, cuts, *refs):
+    shards, outs = (refs[:count], refs[count : 2 * count])
+    send, recv, local = refs[2 * count :]
+    bits = range(cube.count)
+    own = [cube.bit(k) for k in bits]
+    kept = []
+    for m in range(count):
+        kept.append(
+            pltpu.make_async_copy(shards[m], outs[m].at[tuple(own[::-1])], local.at[m])
+        )
+        kept[m].start()
+    greet(cube, bits)
+    lanes = len(orders)
+
+    def copy(chunk, lane, stage):
+        m, order = (which[chunk], orders[lane])
+        row, rows, column, columns = cuts[chunk][lane]
+        block = (pl.ds(row, rows), pl.ds(column, columns))
+        lead = tuple(slice(None) if k in order[:stage] else own[k] for k in reversed(bits))
+        place = outs[m].at[lead + block]
+        return pltpu.make_async_remote_copy(
+            src_ref=shards[m].at[block] if stage == 0 else place,
+            dst_ref=place,
+            send_sem=send.at[chunk * lanes + lane, stage],
+            recv_sem=recv.at[chunk * lanes + lane, stage],
+            device_id=cube.partner(order[stage]),
+            device_id_type=MESH,
+        )
+
+    for chunk in range(len(cuts)):
+        for lane in range(lanes):
+            copy(chunk, lane, 0).start()
+    for one in kept:
+        one.wait()
+    stages = cube.count
+    for turn in range(len(cuts) + stages):
+        for stage in range(stages):
+            chunk = turn - stage - (stage == stages - 1)
+            if 0 <= chunk < len(cuts):
+                for lane in range(lanes):
+                    copy(chunk, lane, stage).wait_recv()
+                    if stage + 1 < stages:
+                        copy(chunk, lane, stage + 1).start()
+    for chunk in range(len(cuts)):
+        for lane in range(lanes):
+            for stage in range(stages):
+                copy(chunk, lane, stage).wait_send()
+
+
+def column_parts(width, shares):
+    units, total, at, parts = (width // 128, sum(shares), 0, [])
+    for share in shares:
+        size = units * share // total
+        parts.append((at * 128, size * 128))
+        at += size
+    return parts
+
+
+def gather_fast(shards, cube):
+    core = [cube.core]
+    orders = [
+        cube.z + cube.y + cube.x + core,
+        cube.z + cube.x + cube.y + core,
+        cube.x + cube.y + cube.z + core,
+    ]
+    which, cuts = ([], [])
+    for m, shard in enumerate(shards):
+        rows, columns = (min(64, shard.shape[0]), min(2048, shard.shape[1]))
+        for row in range(0, shard.shape[0], rows):
+            for column in range(0, shard.shape[1], columns):
+                which.append(m)
+                cuts.append(
+                    [(row, rows, column + a, w) for a, w in column_parts(columns, (3, 3, 2))]
+                )
+    count, items = (len(shards), len(cuts) * len(orders))
+    outs = pl.pallas_call(
+        functools.partial(gather_kernel, cube, orders, count, which, cuts),
+        out_shape=[
+            jax.ShapeDtypeStruct((2,) * cube.count + shard.shape, shard.dtype) for shard in shards
+        ],
+        in_specs=[pl.BlockSpec(memory_space=pl.ANY)] * count,
+        out_specs=[pl.BlockSpec(memory_space=pl.ANY)] * count,
+        scratch_shapes=[
+            pltpu.SemaphoreType.DMA((items, cube.count)),
+            pltpu.SemaphoreType.DMA((items, cube.count)),
+            pltpu.SemaphoreType.DMA((count,)),
+        ],
+        compiler_params=pltpu.CompilerParams(collective_id=0, has_side_effects=True),
+        name="gather_weights",
+    )(*shards)
+    return tuple(out.reshape(-1, shard.shape[1]) for out, shard in zip(outs, shards))
+
+
+def sum_kernel(cube, value, out, held, sent, send, recv):
+    bits = range(cube.count)
+    greet(cube, bits)
+    sent[0] = value[...]
+    for k in bits:
+        copy = pltpu.make_async_remote_copy(
+            src_ref=sent.at[k],
+            dst_ref=held.at[k],
+            send_sem=send.at[k],
+            recv_sem=recv.at[k],
+            device_id=cube.partner(k),
+            device_id_type=MESH,
+        )
+        copy.start()
+        copy.wait()
+        if k + 1 < cube.count:
+            sent[k + 1] = sent[k] + held[k]
+        else:
+            out[...] = sent[k] + held[k]
+
+
+def sum_fast(value, cube, number):
+    return pl.pallas_call(
+        functools.partial(sum_kernel, cube),
+        out_shape=jax.ShapeDtypeStruct(value.shape, value.dtype),
+        in_specs=[pl.BlockSpec(memory_space=pltpu.VMEM)],
+        out_specs=pl.BlockSpec(memory_space=pltpu.VMEM),
+        scratch_shapes=[
+            pltpu.VMEM((cube.count,) + value.shape, value.dtype),
+            pltpu.VMEM((cube.count,) + value.shape, value.dtype),
+            pltpu.SemaphoreType.DMA((cube.count,)),
+            pltpu.SemaphoreType.DMA((cube.count,)),
+        ],
+        compiler_params=pltpu.CompilerParams(collective_id=number, has_side_effects=True),
+        name="sum_over_devices",
+    )(value)
+
+
+def sum_everywhere(values, cube, number):
+    if cube is None:
+        return lax.psum(values, AXES)
+    flat = jnp.concatenate([value.reshape(-1) for value in values])
+    size = -(-flat.shape[0] // 8192) * 8192
+    flat = jnp.pad(flat, (0, size - flat.shape[0])).reshape(-1, 1024)
+    flat = sum_fast(flat, cube, number).reshape(-1)
+    out, at = ([], 0)
+    for value in values:
+        out.append(flat[at : at + value.size].reshape(value.shape))
+        at += value.size
+    return tuple(out)
+
+
+def reduce_kernel(cube, order, rows, columns, count, places, *refs):
+    parts, out, refs = (refs[:count], refs[count], refs[count + 1 :])
+    stages, number = (len(order), len(places))
+    own, refs = (refs[0], refs[1:])
+    recv_at, refs = (refs[:stages], refs[stages:])
+    send_at, refs = ((None,) + refs[: stages - 1], refs[stages - 1 :])
+    keep_at, refs = ((None,) + refs[: stages - 1], refs[stages - 1 :])
+    send, recv, local = refs
+    bits = [cube.bit(k) for k in order]
+    dims = sorted(order, reverse=True)
+
+    def spot(stage, flip):
+        left = [k for k in dims if k not in order[:stage]]
+        side = bits[stage]
+        side = 1 - side if flip else side
+        return tuple(side if k == order[stage] else slice(None) for k in left)
+
+    def remote(stage, chunk, source):
+        return pltpu.make_async_remote_copy(
+            src_ref=source,
+            dst_ref=recv_at[stage].at[chunk],
+            send_sem=send.at[stage, chunk],
+            recv_sem=recv.at[stage, chunk],
+            device_id=cube.partner(order[stage]),
+            device_id_type=MESH,
+        )
+
+    greet(cube, order)
+    for chunk, (m, row, column) in enumerate(places):
+        block = (pl.ds(row, rows), pl.ds(column, columns))
+        remote(0, chunk, parts[m].at[spot(0, True) + block]).start()
+        pltpu.make_async_copy(
+            parts[m].at[spot(0, False) + block], own.at[chunk], local.at[chunk]
+        ).start()
+
+    def turn(step, carry):
+        for stage in range(stages):
+            chunk = step - stage
+
+            @pl.when((chunk >= 0) & (chunk < number))
+            def _():
+                source = own if stage == 0 else keep_at[stage]
+                if stage == 0:
+                    pltpu.make_async_copy(own.at[chunk], own.at[chunk], local.at[chunk]).wait()
+                remote(stage, chunk, recv_at[stage].at[chunk]).wait_recv()
+                arrived = recv_at[stage]
+                if stage + 1 == stages:
+                    out[chunk] = source[chunk] + arrived[chunk].astype(jnp.float32)
+                else:
+                    away, home = (spot(stage + 1, True), spot(stage + 1, False))
+                    send_at[stage + 1][chunk] = (
+                        source[(chunk,) + away].astype(jnp.float32)
+                        + arrived[(chunk,) + away].astype(jnp.float32)
+                    ).astype(jnp.bfloat16)
+                    remote(stage + 1, chunk, send_at[stage + 1].at[chunk]).start()
+                    keep_at[stage + 1][chunk] = source[(chunk,) + home].astype(
+                        jnp.float32
+                    ) + arrived[(chunk,) + home].astype(jnp.float32)
+
+        return carry
+
+    lax.fori_loop(0, number + stages, turn, 0)
+
+    def finish(chunk, carry):
+        for stage in range(stages):
+            remote(stage, chunk, recv_at[stage].at[chunk]).wait_send()
+        return carry
+
+    lax.fori_loop(0, number, finish, 0)
+
+
+def reduce_fast(parts, cube, rows, columns):
+    order = cube.y + cube.z[::-1]
+    stages, count = (len(order), len(parts))
+    places = []
+    for m, part in enumerate(parts):
+        for row in range(0, part.shape[-2], rows):
+            for column in range(0, part.shape[-1], columns):
+                places.append((m, row, column))
+    number, tile = (len(places), (rows, columns))
+
+    def held(stage, dtype):
+        return pltpu.VMEM((number,) + (2,) * (stages - 1 - stage) + tile, dtype)
+
+    out = pl.pallas_call(
+        functools.partial(reduce_kernel, cube, order, rows, columns, count, places),
+        out_shape=jax.ShapeDtypeStruct((number,) + tile, jnp.float32),
+        in_specs=[pl.BlockSpec(memory_space=pl.ANY)] * count,
+        out_specs=pl.BlockSpec(memory_space=pltpu.VMEM),
+        scratch_shapes=[held(0, jnp.bfloat16)]
+        + [held(stage, jnp.bfloat16) for stage in range(stages)]
+        + [held(stage, jnp.bfloat16) for stage in range(1, stages)]
+        + [held(stage, jnp.float32) for stage in range(1, stages)]
+        + [
+            pltpu.SemaphoreType.DMA((stages, number)),
+            pltpu.SemaphoreType.DMA((stages, number)),
+            pltpu.SemaphoreType.DMA((number,)),
+        ],
+        compiler_params=pltpu.CompilerParams(
+            collective_id=4, has_side_effects=True, vmem_limit_bytes=56 * 1024 * 1024
+        ),
+        name="reduce_gradients",
+    )(*parts)
+    results, at = ([], 0)
+    for part in parts:
+        down, across = (part.shape[-2] // rows, part.shape[-1] // columns)
+        piece = out[at : at + down * across].reshape(down, across, rows, columns)
+        results.append(piece.transpose(0, 2, 1, 3).reshape(part.shape[-2], part.shape[-1]))
+        at += down * across
+    return results
+
+
+def near_sum(left, right, cube):
+    near = cube.seq_bits + 1
+    flipped = left.T
+    rows = flipped.shape[0] >> cube.count
+    flipped = flipped.reshape((-1,) + (2,) * near + (rows, left.shape[0]))
+    for k in range(near):
+        axis = flipped.ndim - 3
+        away = lax.dynamic_index_in_dim(flipped, 1 - cube.bit(k), axis, keepdims=False)
+        home = lax.dynamic_index_in_dim(flipped, cube.bit(k), axis, keepdims=False)
+        flipped = jnp.concatenate([home, cube.swap(away, k)], axis=-1)
+        right = jnp.concatenate([right, cube.swap(right, k)], axis=0)
+    sums = matmul(flipped.reshape(-1, flipped.shape[-1]), right).astype(jnp.bfloat16)
+    return sums.reshape((2,) * (cube.count - near) + (rows, right.shape[1]))
+
+
+def gradient_shards(pairs, cube):
+    if cube is None:
+        results = []
+        for left, right in pairs:
+            whole = transposed_left(left, right)
+            flat = whole.reshape(-1, 128)
+            shard = lax.psum_scatter(flat, AXES, scatter_dimension=0, tiled=True)
+            results.append(shard.reshape(-1, whole.shape[1]))
+        return results
+    return reduce_fast([near_sum(left, right, cube) for left, right in pairs], cube, 32, 1024)
+
+
+def gather_all(shards, cube):
+    if cube is None:
+        return tuple(lax.all_gather(shard, AXES, axis=0, tiled=True) for shard in shards)
+    return gather_fast(shards, cube)
+
+
+def cube_of(shards):
+    batch, seq = (lax.axis_size("batch"), lax.axis_size("seq"))
+    if seq != 2 or batch < 8 or batch & (batch - 1):
+        return None
+    if any(shard.shape[0] % 32 or shard.shape[1] % 1024 for shard in shards):
+        return None
+    return Cube(batch, seq)
 
 
 def swish_slope(values):
@@ -85,11 +420,9 @@
 def ffn_backward(d_out, kept, gain, weight_in, weight_out):
     hidden, act, swish, unit, inverse = kept
     d_branch = (0.5 * d_out).astype(jnp.bfloat16)
-    grad_out = transposed_left(swish, d_branch)
     d_act = (transposed_right(d_branch, weight_out) * swish_slope(act)).astype(jnp.bfloat16)
-    grad_in = transposed_left(hidden, d_act)
     d_norm, d_gain, d_shift = norm_backward(transposed_right(d_act, weight_in), unit, inverse, gain)
-    return (d_out + d_norm, grad_in, grad_out, d_gain, d_shift)
+    return (d_out + d_norm, (hidden, d_act), (swish, d_branch), d_gain, d_shift)
 
 
 def segment_ids(place, ends, group):
@@ -252,18 +585,20 @@
     own_segment = wide_segment[reach : reach + frames_here]
     mask = (own_segment < last_entry).astype(jnp.float32)[:, None]
     group_segment = segment_ids(jnp.arange(group, dtype=jnp.int32), ends, group)
-    gathered = (
-        lax.all_gather(ffn1_in, ("batch", "seq"), axis=0, tiled=True),
-        lax.all_gather(ffn1_out, ("batch", "seq"), axis=0, tiled=True),
-        lax.all_gather(query_w, ("batch", "seq"), axis=0, tiled=True),
-        lax.all_gather(key_w, ("batch", "seq"), axis=0, tiled=True),
-        lax.all_gather(value_w, ("batch", "seq"), axis=0, tiled=True),
-        lax.all_gather(out_w, ("batch", "seq"), axis=0, tiled=True),
-        lax.all_gather(point_in, ("batch", "seq"), axis=0, tiled=True),
-        lax.all_gather(point_out, ("batch", "seq"), axis=0, tiled=True),
-        lax.all_gather(ffn2_in, ("batch", "seq"), axis=0, tiled=True),
-        lax.all_gather(ffn2_out, ("batch", "seq"), axis=0, tiled=True),
-    )
+    shards = (
+        ffn1_in,
+        ffn1_out,
+        query_w,
+        key_w,
+        value_w,
+        out_w,
+        point_in,
+        point_out,
+        ffn2_in,
+        ffn2_out,
+    )
+    cube = cube_of(shards)
+    gathered = gather_all(shards, cube)
     start_values = frames.astype(jnp.float32)
     after_first, kept_first = ffn_forward(
         start_values, norm_gains[0], norm_biases[0], gathered[0], gathered[1]
@@ -324,9 +659,10 @@
             mixed
             + kernel[offset] * gated_wide[offset : offset + frames_here].astype(jnp.float32) * same
         )
-    total, squares, count = lax.psum(
+    total, squares, count = sum_everywhere(
         (jnp.sum(mixed * mask, axis=0), jnp.sum(mixed * mixed * mask, axis=0), jnp.sum(mask)),
-        ("batch", "seq"),
+        cube,
+        1,
     )
     mean = total / count
     var = squares / count - mean * mean
@@ -342,31 +678,17 @@
         after_second, norm_gains[4], norm_biases[4]
     )
     sample_variance = var * count / (count - 1.0)
-    regathered = (
-        lax.all_gather(ffn1_in, ("batch", "seq"), axis=0, tiled=True),
-        lax.all_gather(ffn1_out, ("batch", "seq"), axis=0, tiled=True),
-        lax.all_gather(query_w, ("batch", "seq"), axis=0, tiled=True),
-        lax.all_gather(key_w, ("batch", "seq"), axis=0, tiled=True),
-        lax.all_gather(value_w, ("batch", "seq"), axis=0, tiled=True),
-        lax.all_gather(out_w, ("batch", "seq"), axis=0, tiled=True),
-        lax.all_gather(point_in, ("batch", "seq"), axis=0, tiled=True),
-        lax.all_gather(point_out, ("batch", "seq"), axis=0, tiled=True),
-        lax.all_gather(ffn2_in, ("batch", "seq"), axis=0, tiled=True),
-        lax.all_gather(ffn2_out, ("batch", "seq"), axis=0, tiled=True),
-    )
     d_final = cotangent.astype(jnp.float32) * mask
     d_second, gain_four, shift_four = norm_backward(
         d_final, final_unit, final_inverse, norm_gains[4]
     )
     d_conv_res, grad_two_in, grad_two_out, gain_three, shift_three = ffn_backward(
-        d_second, kept_second, norm_gains[3], regathered[8], regathered[9]
+        d_second, kept_second, norm_gains[3], gathered[8], gathered[9]
     )
     conv_branch = d_conv_res.astype(jnp.bfloat16)
-    grad_point_out = transposed_left(conv_swish, conv_branch)
-    d_bn_out = transposed_right(conv_branch, regathered[7]) * swish_slope(bn_out)
-    grad_bn_gain, grad_bn_shift = lax.psum(
-        (jnp.sum(d_bn_out * centred * mask, axis=0), jnp.sum(d_bn_out * mask, axis=0)),
-        ("batch", "seq"),
+    d_bn_out = transposed_right(conv_branch, gathered[7]) * swish_slope(bn_out)
+    grad_bn_gain, grad_bn_shift = sum_everywhere(
+        (jnp.sum(d_bn_out * centred * mask, axis=0), jnp.sum(d_bn_out * mask, axis=0)), cube, 2
     )
     d_mixed = (
         bn_gain * bn_inverse * (d_bn_out - mask * (grad_bn_shift + centred * grad_bn_gain) / count)
@@ -395,15 +717,13 @@
     d_pointwise = jnp.concatenate(
         [d_gated * sigma_half, d_gated * gate_half * sigma_half * (1.0 - sigma_half)], axis=1
     ).astype(jnp.bfloat16)
-    grad_point_in = transposed_left(conv_hidden, d_pointwise)
     d_conv_norm, gain_two, shift_two = norm_backward(
-        transposed_right(d_pointwise, regathered[6]), conv_unit, conv_inverse, norm_gains[2]
+        transposed_right(d_pointwise, gathered[6]), conv_unit, conv_inverse, norm_gains[2]
     )
     d_attn_res = d_conv_res + d_conv_norm
     attn_branch = d_attn_res.astype(jnp.bfloat16)
-    grad_out_w = transposed_left(context, attn_branch)
     d_context = (
-        transposed_right(attn_branch, regathered[5])
+        transposed_right(attn_branch, gathered[5])
         .astype(jnp.bfloat16)
         .reshape(frames_here, HEADS, -1)
     )
@@ -428,66 +748,51 @@
     d_query = d_query.reshape(frames_here, width)
     d_keys = d_keys.reshape(frames_here, width)
     d_values = d_values.reshape(frames_here, width)
-    grad_query_w = transposed_left(attn_hidden, d_query)
-    grad_key_w = transposed_left(attn_hidden, d_keys)
-    grad_value_w = transposed_left(attn_hidden, d_values)
     d_attn_hidden = (
-        transposed_right(d_query, regathered[2])
-        + transposed_right(d_keys, regathered[3])
-        + transposed_right(d_values, regathered[4])
+        transposed_right(d_query, gathered[2])
+        + transposed_right(d_keys, gathered[3])
+        + transposed_right(d_values, gathered[4])
     )
     d_attn_norm, gain_one, shift_one = norm_backward(
         d_attn_hidden, attn_unit, attn_inverse, norm_gains[1]
     )
     d_first_res = d_attn_res + d_attn_norm
     d_input, grad_one_in, grad_one_out, gain_zero, shift_zero = ffn_backward(
-        d_first_res, kept_first, norm_gains[0], regathered[0], regathered[1]
-    )
-    all_local = (
-        grad_one_in,
-        grad_one_out,
-        grad_query_w,
-        grad_key_w,
-        grad_value_w,
-        grad_out_w,
-        grad_point_in,
-        grad_point_out,
-        grad_two_in,
-        grad_two_out,
-    )
-    all_flat = flat_rows(all_local)
-    shards = (
-        lax.psum_scatter(all_flat[0], ("batch", "seq"), scatter_dimension=0, tiled=True),
-        lax.psum_scatter(all_flat[1], ("batch", "seq"), scatter_dimension=0, tiled=True),
-        lax.psum_scatter(all_flat[2], ("batch", "seq"), scatter_dimension=0, tiled=True),
-        lax.psum_scatter(all_flat[3], ("batch", "seq"), scatter_dimension=0, tiled=True),
-        lax.psum_scatter(all_flat[4], ("batch", "seq"), scatter_dimension=0, tiled=True),
-        lax.psum_scatter(all_flat[5], ("batch", "seq"), scatter_dimension=0, tiled=True),
-        lax.psum_scatter(all_flat[6], ("batch", "seq"), scatter_dimension=0, tiled=True),
-        lax.psum_scatter(all_flat[7], ("batch", "seq"), scatter_dimension=0, tiled=True),
-        lax.psum_scatter(all_flat[8], ("batch", "seq"), scatter_dimension=0, tiled=True),
-        lax.psum_scatter(all_flat[9], ("batch", "seq"), scatter_dimension=0, tiled=True),
-    )
-    shards = block_rows_back(shards, all_local)
+        d_first_res, kept_first, norm_gains[0], gathered[0], gathered[1]
+    )
+    heads_in = jnp.concatenate([d_query, d_keys, d_values], axis=1)
+    two_out, two_in, conv_out, conv_in, attn_out, attn_in, one_out, one_in = gradient_shards(
+        (
+            grad_two_out,
+            grad_two_in,
+            (conv_swish, conv_branch),
+            (conv_hidden, d_pointwise),
+            (context, attn_branch),
+            (attn_hidden, heads_in),
+            grad_one_out,
+            grad_one_in,
+        ),
+        cube,
+    )
     gains_local = jnp.stack([gain_zero, gain_one, gain_two, gain_three, gain_four])
     shifts_local = jnp.stack([shift_zero, shift_one, shift_two, shift_three, shift_four])
     kernel_local = jnp.stack(kernel_rows)
-    grad_gains, grad_biases, grad_depth, grad_rel = lax.psum(
-        (gains_local, shifts_local, kernel_local, d_table), ("batch", "seq")
+    grad_gains, grad_biases, grad_depth, grad_rel = sum_everywhere(
+        (gains_local, shifts_local, kernel_local, d_table), cube, 3
     )
     return (
         final_norm.astype(jnp.bfloat16),
         d_input.astype(jnp.bfloat16),
-        shards[0],
-        shards[1],
-        shards[2],
-        shards[3],
-        shards[4],
-        shards[5],
-        shards[6],
-        shards[7],
-        shards[8],
-        shards[9],
+        one_in,
+        one_out,
+        attn_in[:, :width],
+        attn_in[:, width : 2 * width],
+        attn_in[:, 2 * width :],
+        attn_out,
+        conv_in,
+        conv_out,
+        two_in,
+        two_out,
         grad_depth,
         grad_rel,
         grad_gains,

time: 3200 us -> 804 us (0.25)
  waiting for transfers between devices: 2690 us -> 75.2 us
  Pallas kernels: 0 us -> 431 us
  blocking collectives: 110 us -> 0 us
  local copies, waits for them, and re-layouts: 183 us -> 83.3 us
  matrix products: 136 us -> 84.7 us
  starting transfers between devices: 29.8 us -> 62.3 us
    reduce_scatter x10 -> x0, waiting for transfers between devices: 2000 us -> none  [the longest x1 359 us: on_device(): lax.psum_scatter(all_flat[1], ('batch', 'seq'), scatter_dimension=0, tile...]
    all_gather x10 -> x0, waiting for transfers between devices: 535 us -> none  [the longest x1 76.8 us: on_device(): lax.all_gather(ffn2_in, ('batch', 'seq'), axis=0, tiled=True)]
    pallas_call x0 -> x5, Pallas kernels: none -> 431 us  [the longest x1 230 us: gather_fast(): pl.pallas_call(functools.partial(gather_kernel, cube, orders, count, whic...]
    psum x1 -> x0, waiting for transfers between devices: 128 us -> none  [on_device(): lax.psum((gains_local, shifts_local, kernel_local, d_table), ('batch', 's...]
    reshape x21 -> x9, local copies, waits for them, and re-layouts: 124 us -> 7 us  [the longest x2 3.34 us: near_sum(): flipped = flipped.reshape((-1,) + (2,) * near + (rows, left.shape[0]))]
    psum x2 -> x0, blocking collectives: 80.3 us -> none  [the longest x1 40.7 us: on_device(): lax.psum((jnp.sum(d_bn_out * centred * mask, axis=0), jnp.sum(d_bn_out *...]
    ppermute x0 -> x32, waiting for transfers between devices: none -> 57.7 us  [swap(): return lax.ppermute(values, axis, pairs)]
    dot_general x10 -> x0, matrix products: 54 us -> none  [transposed_left(): lax.dot_general(left, right, (((0,), (0,)), ((), ())), preferred_element_...]
  transfers between devices with their start and end apart: 30 -> 44, of which waited for: 24 -> 12; matrix products, arithmetic and copies ran while one was open for 9% -> 24% of each run, Pallas kernels for 0% -> 7%
where the time goes in v1:
time: 804 us; the launch traced here: 793 us
  Pallas kernels  431 us (54%)
  matrix products  84.7 us (11%)
  local copies, waits for them, and re-layouts  83.3 us (10%)
  waiting for transfers between devices  75.2 us (9%)
  starting transfers between devices  62.3 us (8%)
  other arithmetic  53.2 us (7%)
    pallas_call x1, Pallas kernels, gather_fast(): pl.pallas_call(functools.partial(gather_kernel, cube, orders, count, whic...  230 us
    pallas_call x1, Pallas kernels, reduce_fast(): pl.pallas_call(functools.partial(reduce_kernel, cube, order, rows, column...  144 us
    ppermute x32, waiting for transfers between devices, swap(): return lax.ppermute(values, axis, pairs)  57.7 us
    pallas_call x3, Pallas kernels, sum_fast(): pl.pallas_call(functools.partial(sum_kernel, cube), out_shape=jax.ShapeDt...  56.9 us
    dot_general x18, matrix products, matmul(): return jnp.dot(left, right, preferred_element_type=jnp.float32)  50.9 us
    dot_general x10, matrix products, transposed_right(): lax.dot_general(left, right, (((1,), (1,)), ((), ())), preferred_element_...  29.3 us
    unnamed x242, local copies, waits for them, and re-layouts  22.1 us
    ppermute x32, starting transfers between devices, swap(): return lax.ppermute(values, axis, pairs)  21.9 us
  transfers between devices with their start and end apart: 44, of which 12 were waited for; matrix products, arithmetic and copies ran while one was open for 24% of the time, Pallas kernels for 7%

profile of v1, /device:TPU:0, one launch (start us, length us, event | category | flops | bytes accessed | tf_op | source)
XLA Modules:
  0.0 793.0 jit_solution(6743482209201025432)
XLA Ops:
  6.1 229.5 %gather_weights.1 = (bf16[2,2,2,2,2,32,4096]{6,5,4,3,2,1,0:T(8,128)(2,1)}, bf16[2,2,2,2,2,128,1024]{6,5,4,3,2,1,0:T(8,128)(2,1)}, bf16[2,2,2,2,2,32,1024]{6,5,4,...) custom-call(bf16[32,4096]{1,0:T(8,128)(2,1)} %refs_0_.1, ...), custom_call_target="tpu_custom_call" | custom-call | tf_op jit(solution)/shard_map/gather_weights/pallas_call | solution.py:165
  235.6 5.1 fusion.35
  244.4 3.4 all-to-all-start.1
  248.6 3.1 constant_dynamic-slice_fusion
  253.6 2.0 collective-permute-start.28
  256.7 2.1 fusion.46
  263.9 3.5 copy.238
  268.1 4.3 all-to-all-start.2
  278.8 3.5 all-to-all-start
  284.1 3.9 all-to-all-done
  291.2 3.4 all-to-all-start.3
  296.4 3.5 all-to-all-done.3
  300.1 2.2 fusion.212
  302.7 3.0 fusion.193
  305.9 2.0 collective-permute-start
  310.1 2.6 collective-permute-start.20
  316.1 15.5 %sum_over_devices.3 = f32[8,1024]{1,0:T(8,128)} custom-call(f32[8,1024]{1,0:T(8,128)} %reshape.529.value), custom_call_target="tpu_custom_call" | custom-call | tf_op jit(solution)/shard_map/sum_over_devices/pallas_call | solution.py:205
  333.5 2.0 multiply_divide_fusion
  336.8 1.9 fusion.265
  338.7 2.5 fusion.213
  341.5 6.0 fusion.34
  351.1 4.2 fusion
  355.4 2.9 fusion.215
  361.3 2.7 multiply_reduce_fusion.8
  366.3 16.4 %sum_over_devices.4 = f32[8,1024]{1,0:T(8,128)} custom-call(f32[8,1024]{1,0:T(8,128)} %reshape.535.value), custom_call_target="tpu_custom_call" | custom-call | tf_op jit(solution)/shard_map/sum_over_devices/pallas_call | solution.py:205
  383.6 3.7 fusion.117
  389.8 5.7 collective-permute-start.3
  398.5 2.6 reshape.542
  401.1 5.1 constant_dynamic-slice_fusion.2
  407.6 3.5 copy.237
  411.1 3.5 copy.236
  414.6 2.0 collective-permute-start.12
  416.7 2.3 multiply_convert_fusion.7
  419.2 3.8 fusion.191
  428.6 3.4 all-to-all-start.4
  433.0 2.0 collective-permute-start.8
  436.6 7.2 collective-permute-done.12
  445.5 3.9 collective-permute-done.8
  454.0 4.1 all-to-all-start.7
  460.4 2.6 reshape.538
  465.9 2.0 collective-permute-start.4
  467.9 3.4 all-to-all-start.6
  473.9 2.0 collective-permute-start.22
  475.9 2.2 fusion.120
  478.2 5.6 all-to-all-done.6
  483.8 4.3 all-to-all-start.5
  493.2 3.9 all-to-all-done.5
  500.6 2.5 fusion.216
  508.1 6.6 fusion.1
  514.8 2.9 fusion.217
  521.1 2.0 fusion.94
  524.8 25.0 %sum_over_devices.5 = f32[32,1024]{1,0:T(8,128)} custom-call(f32[32,1024]{1,0:T(8,128)} %reshape.570.value), custom_call_target="tpu_custom_call" | custom-call | tf_op jit(solution)/shard_map/sum_over_devices/pallas_call | solution.py:205
  557.4 38.4 %collective-permute-done.32 = bf16[8,2,32,128]{3,2,1,0:T(8,128)(2,1)S(1)} collective-permute-done((bf16[8,2,32,128]{3,2,1,0:T(8,128)(2,1)S(1)}, bf16[8,2,32,128]{3,2,1,0:T(8,128)(2,1)S(1)}, u32[]{:S(2)}, u32[]{:S(2)}) %collective-permute-start.32) | collective-permute-done | bytes 131104 | tf_op jit(solution)/shard_map/ppermute | solution.py:80
  598.7 5.8 collective-permute-done.30
  608.5 2.4 convolution_convert_fusion.7
  610.9 2.3 convolution_convert_fusion.6
  613.2 3.9 convolution_convert_fusion.5
  618.6 2.6 convolution_convert_fusion.4
  621.7 2.8 convolution_convert_fusion.3
  624.9 5.6 convolution_convert_fusion.2
  630.5 3.9 convolution_convert_fusion.1
  634.4 2.5 convolution_convert_fusion
  636.9 144.4 %reduce_gradients.1 = f32[23,32,1024]{2,1,0:T(8,128)} custom-call(bf16[2,2,2,128,1024]{4,3,2,1,0:T(8,128)(2,1)} %bitcast.375, bf16[2,2,2,32,4096]{4,3,2,1,0:T(8,128)(2,1)} %bitcast.377, bf16[2,2,2,32,1024]{4,3,2,1,0:T(8,128)(2,1)} %bitcast.404, bf16[2,2,2,32,2048]{4,3,2,1,0:T(8,128)(2,1)} %bitcast.386, bf16[2,2,2,32,1024]{4,3,2,1,0:T(8,128)(2,1)} %bitcast.405, ...), custom_call_target="tpu_custom_call" | custom-call | tf_op jit(solution)/shard_map/reduce_gradients/pallas_call | solution.py:319
  781.3 2.7 fusion.200
  (471 shorter events, 123.0 us)
Async XLA Ops:
  0.7 272.5 %copy-start = (bf16[73,128]{1,0:T(8,128)(2,1)S(1)}, bf16[73,128]{1,0:T(8,128)(2,1)}, u32[]{:S(2)}) copy-start(bf16[73,128]{1,0:T(8,128)(2,1)} %param.33) | copy-start | bytes 56068
  0.7 234.9 %copy-start.9 = (bf16[128,1024]{1,0:T(8,128)(2,1)S(1)}, bf16[128,1024]{1,0:T(8,128)(2,1)}, u32[]{:S(2)}) copy-start(bf16[128,1024]{1,0:T(8,128)(2,1)} %param.19) | copy-start | bytes 786436
  3.8 236.9 %copy-start.79 = (f32[1,1024]{1,0:T(1,128)}, f32[1,1024]{1,0:T(1,128)S(1)}, u32[]{:S(2)}) copy-start(f32[1,1024]{1,0:T(1,128)S(1)} %get-tuple-element.211) | copy-start | bytes 12292
  4.9 235.8 %copy-start.96 = (f32[128]{0:T(128)}, f32[128]{0:T(128)S(1)}, u32[]{:S(2)}) copy-start(f32[128]{0:T(128)S(1)} %broadcast_multiply_fusion.14) | copy-start | bytes 1540
  6.1 234.7 %copy-start.101 = (f32[128]{0:T(128)}, f32[128]{0:T(128)S(1)}, u32[]{:S(2)}) copy-start(f32[128]{0:T(128)S(1)} %add_rsqrt_fusion.5) | copy-start | bytes 1540
  244.4 23.7 %all-to-all-start.1 = ((bf16[128,8,128]{2,0,1:T(8,128)(2,1)}), bf16[128,8,128]{2,0,1:T(8,128)(2,1)S(1)}, u32[]{:S(2)}, u32[]{:S(2)}) async-start(bf16[128,8,128]{2,0,1:T(8,128)(2,1)} %bitcast.334), calls=%async_computation.1 | async-start | bytes 524288 | tf_op jit(solution)/shard_map/all_to_all | solution.py:609
  253.6 220.3 %collective-permute-start.28 = (bf16[8,2,128,128]{3,2,1,0:T(8,128)(2,1)}, bf16[8,2,128,128]{3,2,1,0:T(8,128)(2,1)}, u32[]{:S(2)}, u32[]{:S(2)}) collective-permute-start(bf16[8,2,128,128]{3,2,1,0:T(8,128)(2,1)} %bitcast.119), channel_id=1, source_target_pairs={{0,1},{1,0},{2,3},{3,2},{4,5},{5,4},{6,7},{7,6},{8,9},{9,8},{10,11... | collective-permute-start | bytes 1572872 | tf_op jit(solution)/shard_map/ppermute | solution.py:80
  256.7 38.0 %collective-permute-start.24 = (bf16[8,2,32,128]{3,2,1,0:T(8,128)(2,1)}, bf16[8,2,32,128]{3,2,1,0:T(8,128)(2,1)}, u32[]{:S(2)}, u32[]{:S(2)}) collective-permute-start(bf16[8,2,32,128]{3,2,1,0:T(8,128)(2,1)} %get-tuple-element.176), channel_id=1, source_target_pairs={{0,1},{1,0},{2,3},{3,2},{4,5},{5,4},{6,7},{7,6},{8,9},{9,8},{10,11... | collective-permute-start | bytes 393224 | tf_op jit(solution)/shard_map/ppermute | solution.py:80
  261.8 51.6 %copy-start.57 = (f32[1,1024]{1,0:T(1,128)}, f32[1,1024]{1,0:T(1,128)S(1)}, u32[]{:S(2)}) copy-start(f32[1,1024]{1,0:T(1,128)S(1)} %get-tuple-element.213) | copy-start | bytes 12292
  268.1 10.6 %all-to-all-start.2 = ((bf16[128,8,128]{2,0,1:T(8,128)(2,1)}), bf16[128,8,128]{2,0,1:T(8,128)(2,1)}, u32[]{:S(2)}, u32[]{:S(2)}) async-start(bf16[128,8,128]{2,0,1:T(8,128)(2,1)} %bitcast.333), calls=%async_computation.2 | async-start | bytes 524288 | tf_op jit(solution)/shard_map/all_to_all | solution.py:616
  278.8 9.2 %all-to-all-start = ((bf16[128,8,128]{2,0,1:T(8,128)(2,1)}), bf16[128,8,128]{2,0,1:T(8,128)(2,1)S(1)}, u32[]{:S(2)}, u32[]{:S(2)}) async-start(bf16[128,8,128]{2,0,1:T(8,128)(2,1)} %bitcast.335), calls=%async_computation | async-start | bytes 524288 | tf_op jit(solution)/shard_map/all_to_all | solution.py:623
  291.2 8.6 %all-to-all-start.3 = ((bf16[256,4,128]{2,1,0:T(4,128)(2,1)}), bf16[256,4,128]{2,1,0:T(4,128)(2,1)S(1)}, u32[]{:S(2)}, u32[]{:S(2)}) async-start(bf16[256,4,128]{2,1,0:T(4,128)(2,1)} %copy.184), calls=%async_computation.3 | async-start | bytes 524288 | tf_op jit(solution)/shard_map/all_to_all | solution.py:641
  305.9 6.9 collective-permute-start
  307.9 5.5 collective-permute-start.1
  310.1 122.8 %collective-permute-start.20 = (bf16[8,2,32,128]{3,2,1,0:T(8,128)(2,1)}, bf16[8,2,32,128]{3,2,1,0:T(8,128)(2,1)}, u32[]{:S(2)}, u32[]{:S(2)}) collective-permute-start(bf16[8,2,32,128]{3,2,1,0:T(8,128)(2,1)} %get-tuple-element.180), channel_id=1, source_target_pairs={{0,1},{1,0},{2,3},{3,2},{4,5},{5,4},{6,7},{7,6},{8,9},{9,8},{10,11... | collective-permute-start | bytes 393224 | tf_op jit(solution)/shard_map/ppermute | solution.py:80
  335.5 25.8 %copy-start.67 = (f32[1,1024]{1,0:T(1,128)}, f32[1,1024]{1,0:T(1,128)S(1)}, u32[]{:S(2)}) copy-start(f32[1,1024]{1,0:T(1,128)S(1)} %get-tuple-element.134) | copy-start | bytes 12292
  361.3 22.3 %copy-start.73 = (f32[128]{0:T(128)S(1)}, f32[128]{0:T(128)}, u32[]{:S(2)}) copy-start(f32[128]{0:T(128)} %get-tuple-element.222) | copy-start | bytes 1540
  364.0 114.1 %collective-permute-start.14 = (bf16[128,1024]{1,0:T(8,128)(2,1)}, bf16[128,1024]{1,0:T(8,128)(2,1)}, u32[]{:S(2)}, u32[]{:S(2)}) collective-permute-start(bf16[128,1024]{1,0:T(8,128)(2,1)} %get-tuple-element.144), channel_id=1, source_target_pairs={{0,1},{1,0},{2,3},{3,2},{4,5},{5,4},{6,7},{7,6},{8,9},{9,8},{10,11... | collective-permute-start | bytes 786440 | tf_op jit(solution)/shard_map/ppermute | solution.py:80
  388.5 26.1 %collective-permute-start.2 = (bf16[2,1024]{1,0:T(2,128)(2,1)}, bf16[2,1024]{1,0:T(2,128)(2,1)}, u32[]{:S(2)}, u32[]{:S(2)}) collective-permute-start(bf16[2,1024]{1,0:T(2,128)(2,1)} %get-tuple-element.194), channel_id=1, source_target_pairs={{1,0},{3,2},{5,4},{7,6},{9,8},{11,10},{13,12},{15,14},{17,16},{19,... | collective-permute-start | bytes 12296 | tf_op jit(solution)/shard_map/ppermute | solution.py:31
  389.8 24.8 %collective-permute-start.3 = (bf16[2,1024]{1,0:T(2,128)(2,1)}, bf16[2,1024]{1,0:T(2,128)(2,1)}, u32[]{:S(2)}, u32[]{:S(2)}) collective-permute-start(bf16[2,1024]{1,0:T(2,128)(2,1)} %get-tuple-element.195), channel_id=1, source_target_pairs={{0,1},{2,3},{4,5},{6,7},{8,9},{10,11},{12,13},{14,15},{16,17},{18,... | collective-permute-start | bytes 12296 | tf_op jit(solution)/shard_map/ppermute | solution.py:30
  414.6 181.2 %collective-permute-start.10 = (bf16[128,4096]{1,0:T(8,128)(2,1)}, bf16[128,4096]{1,0:T(8,128)(2,1)}, u32[]{:S(2)}, u32[]{:S(2)}) collective-permute-start(bf16[128,4096]{1,0:T(8,128)(2,1)} %copy-done.7), channel_id=1, source_target_pairs={{0,1},{1,0},{2,3},{3,2},{4,5},{5,4},{6,7},{7,6},{8,9},{9,8},{10,11... | collective-permute-start | bytes 3145736 | tf_op jit(solution)/shard_map/ppermute | solution.py:80
  414.6 29.2 %collective-permute-start.12 = (bf16[8,2,32,128]{3,2,1,0:T(8,128)(2,1)}, bf16[8,2,32,128]{3,2,1,0:T(8,128)(2,1)}, u32[]{:S(2)}, u32[]{:S(2)}) collective-permute-start(bf16[8,2,32,128]{3,2,1,0:T(8,128)(2,1)} %get-tuple-element.188), channel_id=1, source_target_pairs={{0,1},{1,0},{2,3},{3,2},{4,5},{5,4},{6,7},{7,6},{8,9},{9,8},{10,11... | collective-permute-start | bytes 393224 | tf_op jit(solution)/shard_map/ppermute | solution.py:80
  426.0 17.9 %copy-start.45 = (bf16[8,2,32,128]{3,2,1,0:T(8,128)(2,1)S(1)}, bf16[8,2,32,128]{3,2,1,0:T(8,128)(2,1)}, u32[]{:S(2)}) copy-start(bf16[8,2,32,128]{3,2,1,0:T(8,128)(2,1)} %get-tuple-element.189) | copy-start | bytes 393220
  427.8 21.5 %copy-start.44 = (bf16[8,2,32,128]{3,2,1,0:T(8,128)(2,1)S(1)}, bf16[8,2,32,128]{3,2,1,0:T(8,128)(2,1)}, u32[]{:S(2)}) copy-start(bf16[8,2,32,128]{3,2,1,0:T(8,128)(2,1)} %get-tuple-element.193) | copy-start | bytes 393220
  428.6 21.5 %all-to-all-start.4 = ((bf16[128,8,128]{2,0,1:T(8,128)(2,1)}), bf16[128,8,128]{2,0,1:T(8,128)(2,1)S(1)}, u32[]{:S(2)}, u32[]{:S(2)}) async-start(bf16[128,8,128]{2,0,1:T(8,128)(2,1)} %bitcast.332), calls=%async_computation.4 | async-start | bytes 524288 | tf_op jit(solution)/shard_map/all_to_all | solution.py:730
  432.2 18.2 %copy-start.33 = (bf16[256,4,128]{0,2,1:T(8,128)(2,1)S(1)}, bf16[256,4,128]{0,2,1:T(8,128)(2,1)}, u32[]{:S(2)}) copy-start(bf16[256,4,128]{0,2,1:T(8,128)(2,1)} %copy-done.32) | copy-start | bytes 786436
  433.0 16.4 %collective-permute-start.8 = (bf16[8,2,32,128]{3,2,1,0:T(8,128)(2,1)S(1)}, bf16[8,2,32,128]{3,2,1,0:T(8,128)(2,1)S(1)}, u32[]{:S(2)}, u32[]{:S(2)}) collective-permute-start(bf16[8,2,32,128]{3,2,1,0:T(8,128)(2,1)S(1)} %copy-done.55), channel_id=1, source_target_pairs={{0,1},{1,0},{2,3},{3,2},{4,5},{5,4},{6,7},{7,6},{8,9},{9,8},{10,11... | collective-permute-start | bytes 393224 | tf_op jit(solution)/shard_map/ppermute | solution.py:80
  443.9 46.1 %collective-permute-start.6 = (bf16[128,1024]{1,0:T(8,128)(2,1)}, bf16[128,1024]{1,0:T(8,128)(2,1)}, u32[]{:S(2)}, u32[]{:S(2)}) collective-permute-start(bf16[128,1024]{1,0:T(8,128)(2,1)} %multiply_convert_fusion.9), channel_id=1, source_target_pairs={{0,1},{1,0},{2,3},{3,2},{4,5},{5,4},{6,7},{7,6},{8,9},{9,8},{10,11... | collective-permute-start | bytes 786440 | tf_op jit(solution)/shard_map/ppermute | solution.py:80
  449.4 16.5 %collective-permute-start.16 = (bf16[8,2,32,128]{3,2,1,0:T(8,128)(2,1)}, bf16[8,2,32,128]{3,2,1,0:T(8,128)(2,1)}, u32[]{:S(2)}, u32[]{:S(2)}) collective-permute-start(bf16[8,2,32,128]{3,2,1,0:T(8,128)(2,1)} %get-tuple-element.184), channel_id=1, source_target_pairs={{0,1},{1,0},{2,3},{3,2},{4,5},{5,4},{6,7},{7,6},{8,9},{9,8},{10,11... | collective-permute-start | bytes 393224 | tf_op jit(solution)/shard_map/ppermute | solution.py:80
  454.0 13.9 %all-to-all-start.7 = ((bf16[256,4,128]{2,1,0:T(4,128)(2,1)}), bf16[256,4,128]{2,1,0:T(4,128)(2,1)}, u32[]{:S(2)}, u32[]{:S(2)}) async-start(bf16[256,4,128]{2,1,0:T(4,128)(2,1)} %copy.207), calls=%async_computation.7 | async-start | bytes 524288 | tf_op jit(solution)/shard_map/all_to_all | solution.py:746
  465.9 85.5 %collective-permute-start.4 = (bf16[8,2,128,128]{3,2,1,0:T(8,128)(2,1)}, bf16[8,2,128,128]{3,2,1,0:T(8,128)(2,1)}, u32[]{:S(2)}, u32[]{:S(2)}) collective-permute-start(bf16[8,2,128,128]{3,2,1,0:T(8,128)(2,1)} %bitcast.403), channel_id=1, source_target_pairs={{0,1},{1,0},{2,3},{3,2},{4,5},{5,4},{6,7},{7,6},{8,9},{9,8},{10,11... | collective-permute-start | bytes 1572872 | tf_op jit(solution)/shard_map/ppermute | solution.py:80
  467.9 15.9 %all-to-all-start.6 = ((bf16[256,4,128]{2,1,0:T(4,128)(2,1)}), bf16[256,4,128]{2,1,0:T(4,128)(2,1)S(1)}, u32[]{:S(2)}, u32[]{:S(2)}) async-start(bf16[256,4,128]{2,1,0:T(4,128)(2,1)} %copy.202), calls=%async_computation.6 | async-start | bytes 524288 | tf_op jit(solution)/shard_map/all_to_all | solution.py:745
  473.9 45.0 %collective-permute-start.22 = (bf16[128,1024]{1,0:T(8,128)(2,1)}, bf16[128,1024]{1,0:T(8,128)(2,1)}, u32[]{:S(2)}, u32[]{:S(2)}) collective-permute-start(bf16[128,1024]{1,0:T(8,128)(2,1)} %get-tuple-element.140), channel_id=1, source_target_pairs={{0,1},{1,0},{2,3},{3,2},{4,5},{5,4},{6,7},{7,6},{8,9},{9,8},{10,11... | collective-permute-start | bytes 786440 | tf_op jit(solution)/shard_map/ppermute | solution.py:80
  478.1 76.8 %collective-permute-start.18 = (bf16[128,2048]{1,0:T(8,128)(2,1)}, bf16[128,2048]{1,0:T(8,128)(2,1)}, u32[]{:S(2)}, u32[]{:S(2)}) collective-permute-start(bf16[128,2048]{1,0:T(8,128)(2,1)} %pad_maximum_fusion.5), channel_id=1, source_target_pairs={{0,1},{1,0},{2,3},{3,2},{4,5},{5,4},{6,7},{7,6},{8,9},{9,8},{10,11... | collective-permute-start | bytes 1572872 | tf_op jit(solution)/shard_map/ppermute | solution.py:80
  483.8 13.3 %all-to-all-start.5 = ((bf16[256,4,128]{2,1,0:T(4,128)(2,1)}), bf16[256,4,128]{2,1,0:T(4,128)(2,1)}, u32[]{:S(2)}, u32[]{:S(2)}) async-start(bf16[256,4,128]{2,1,0:T(4,128)(2,1)} %copy.197), calls=%async_computation.5 | async-start | bytes 524288 | tf_op jit(solution)/shard_map/all_to_all | solution.py:744
  489.9 64.0 %collective-permute-start.21 = (bf16[8,32,256]{2,1,0:T(8,128)(2,1)}, bf16[8,32,256]{2,1,0:T(8,128)(2,1)}, u32[]{:S(2)}, u32[]{:S(2)}) collective-permute-start(bf16[8,32,256]{2,1,0:T(8,128)(2,1)} %get-tuple-element.179), channel_id=1, source_target_pairs={{0,2},{2,0},{4,6},{6,4},{8,10},{10,8},{12,14},{14,12},{16,18},{18,... | collective-permute-start | bytes 393224 | tf_op jit(solution)/shard_map/ppermute | solution.py:80
  518.9 33.6 %copy-start.24 = (bf16[8,2,1,128,128]{4,3,1,0,2:T(8,128)(2,1)S(1)}, bf16[8,2,1,128,128]{4,3,1,0,2:T(8,128)(2,1)}, u32[]{:S(2)}) copy-start(bf16[8,2,1,128,128]{4,3,1,0,2:T(8,128)(2,1)} %copy.236) | copy-start | bytes 1572868
  518.9 38.3 %collective-permute-start.13 = (bf16[8,32,256]{2,1,0:T(8,128)(2,1)}, bf16[8,32,256]{2,1,0:T(8,128)(2,1)}, u32[]{:S(2)}, u32[]{:S(2)}) collective-permute-start(bf16[8,32,256]{2,1,0:T(8,128)(2,1)} %get-tuple-element.187), channel_id=1, source_target_pairs={{0,2},{2,0},{4,6},{6,4},{8,10},{10,8},{12,14},{14,12},{16,18},{18,... | collective-permute-start | bytes 393224 | tf_op jit(solution)/shard_map/ppermute | solution.py:80
  523.1 32.9 %copy-start.12 = (bf16[128,1024]{1,0:T(8,128)(2,1)S(1)}, bf16[128,1024]{1,0:T(8,128)(2,1)}, u32[]{:S(2)}) copy-start(bf16[128,1024]{1,0:T(8,128)(2,1)} %copy-done.11) | copy-start | bytes 786436
  551.4 53.2 %collective-permute-start.26 = (bf16[128,3072]{0,1:T(8,128)(2,1)}, bf16[128,3072]{0,1:T(8,128)(2,1)S(1)}, u32[]{:S(2)}, u32[]{:S(2)}) collective-permute-start(bf16[128,3072]{0,1:T(8,128)(2,1)} %pad_maximum_fusion.4), channel_id=1, source_target_pairs={{0,1},{1,0},{2,3},{3,2},{4,5},{5,4},{6,7},{7,6},{8,9},{9,8},{10,11... | collective-permute-start | bytes 2359304 | tf_op jit(solution)/shard_map/ppermute | solution.py:80
  552.5 43.3 %copy-start.38 = (bf16[256,1024]{1,0:T(8,128)(2,1)S(1)}, bf16[256,1024]{1,0:T(8,128)(2,1)}, u32[]{:S(2)}) copy-start(bf16[256,1024]{1,0:T(8,128)(2,1)} %pad_maximum_fusion.7) | copy-start | bytes 1572868
  552.5 43.3 %copy-start.35 = (bf16[128,1024]{1,0:T(8,128)(2,1)S(1)}, bf16[128,1024]{1,0:T(8,128)(2,1)}, u32[]{:S(2)}) copy-start(bf16[128,1024]{1,0:T(8,128)(2,1)} %copy-done.34) | copy-start | bytes 786436
  552.5 44.5 %copy-start.8 = (bf16[128,4096]{1,0:T(8,128)(2,1)S(1)}, bf16[128,4096]{1,0:T(8,128)(2,1)}, u32[]{:S(2)}) copy-start(bf16[128,4096]{1,0:T(8,128)(2,1)} %copy-done.7) | copy-start | bytes 3145732
  554.0 51.9 %collective-permute-start.34 = (bf16[128,4096]{1,0:T(8,128)(2,1)S(1)}, bf16[128,4096]{1,0:T(8,128)(2,1)S(1)}, u32[]{:S(2)}, u32[]{:S(2)}) collective-permute-start(bf16[128,4096]{1,0:T(8,128)(2,1)S(1)} %fusion.1), channel_id=1, source_target_pairs={{0,1},{1,0},{2,3},{3,2},{4,5},{5,4},{6,7},{7,6},{8,9},{9,8},{10,11... | collective-permute-start | bytes 3145736 | tf_op jit(solution)/shard_map/ppermute | solution.py:80
  554.9 40.9 %collective-permute-start.32 = (bf16[8,2,32,128]{3,2,1,0:T(8,128)(2,1)S(1)}, bf16[8,2,32,128]{3,2,1,0:T(8,128)(2,1)S(1)}, u32[]{:S(2)}, u32[]{:S(2)}) collective-permute-start(bf16[8,2,32,128]{3,2,1,0:T(8,128)(2,1)S(1)} %get-tuple-element.172), channel_id=1, source_target_pairs={{0,1},{1,0},{2,3},{3,2},{4,5},{5,4},{6,7},{7,6},{8,9},{9,8},{10,11... | collective-permute-start | bytes 393224 | tf_op jit(solution)/shard_map/ppermute | solution.py:80
  557.3 47.3 %copy-start.37 = (bf16[256,1024]{1,0:T(8,128)(2,1)S(1)}, bf16[256,1024]{1,0:T(8,128)(2,1)}, u32[]{:S(2)}) copy-start(bf16[256,1024]{1,0:T(8,128)(2,1)} %pad_maximum_fusion.6) | copy-start | bytes 1572868
  557.3 47.3 %copy-start.39 = (bf16[256,1024]{1,0:T(8,128)(2,1)S(1)}, bf16[256,1024]{1,0:T(8,128)(2,1)}, u32[]{:S(2)}) copy-start(bf16[256,1024]{1,0:T(8,128)(2,1)} %pad_maximum_fusion.8) | copy-start | bytes 1572868
  557.3 47.8 %copy-start.14 = (bf16[128,2,4,128]{0,3,2,1:T(8,128)(2,1)S(1)}, bf16[128,2,4,128]{0,3,2,1:T(8,128)(2,1)}, u32[]{:S(2)}) copy-start(bf16[128,2,4,128]{0,3,2,1:T(8,128)(2,1)} %copy-done.13) | copy-start | bytes 786436
  557.3 47.8 %copy-start.16 = (bf16[128,2,4,128]{0,3,2,1:T(8,128)(2,1)S(1)}, bf16[128,2,4,128]{0,3,2,1:T(8,128)(2,1)}, u32[]{:S(2)}) copy-start(bf16[128,2,4,128]{0,3,2,1:T(8,128)(2,1)} %copy.199) | copy-start | bytes 786436
  557.3 48.0 %collective-permute-start.29 = (bf16[8,128,256]{2,1,0:T(8,128)(2,1)S(1)}, bf16[8,128,256]{2,1,0:T(8,128)(2,1)S(1)}, u32[]{:S(2)}, u32[]{:S(2)}) collective-permute-start(bf16[8,128,256]{2,1,0:T(8,128)(2,1)S(1)} %copy-done.41), channel_id=1, source_target_pairs={{0,2},{2,0},{4,6},{6,4},{8,10},{10,8},{12,14},{14,12},{16,18},{18,... | collective-permute-start | bytes 1572872 | tf_op jit(solution)/shard_map/ppermute | solution.py:80
  595.8 9.6 %collective-permute-start.15 = (bf16[256,1024]{1,0:T(8,128)(2,1)S(1)}, bf16[256,1024]{1,0:T(8,128)(2,1)S(1)}, u32[]{:S(2)}, u32[]{:S(2)}) collective-permute-start(bf16[256,1024]{1,0:T(8,128)(2,1)S(1)} %copy-done.38), channel_id=1, source_target_pairs={{0,2},{2,0},{4,6},{6,4},{8,10},{10,8},{12,14},{14,12},{16,18},{18,... | collective-permute-start | bytes 1572872 | tf_op jit(solution)/shard_map/ppermute | solution.py:80
  595.8 8.7 %collective-permute-start.30 = (bf16[128,1024]{1,0:T(8,128)(2,1)S(1)}, bf16[128,1024]{1,0:T(8,128)(2,1)S(1)}, u32[]{:S(2)}, u32[]{:S(2)}) collective-permute-start(bf16[128,1024]{1,0:T(8,128)(2,1)S(1)} %copy-done.35), channel_id=1, source_target_pairs={{0,1},{1,0},{2,3},{3,2},{4,5},{5,4},{6,7},{7,6},{8,9},{9,8},{10,11... | collective-permute-start | bytes 786440 | tf_op jit(solution)/shard_map/ppermute | solution.py:80
  604.5 1.9 collective-permute-start.7
  604.6 2.6 collective-permute-start.23
  605.3 2.8 collective-permute-start.5
  605.4 25.1 %collective-permute-start.11 = (bf16[256,4096]{1,0:T(8,128)(2,1)S(1)}, bf16[256,4096]{1,0:T(8,128)(2,1)S(1)}, u32[]{:S(2)}, u32[]{:S(2)}) collective-permute-start(bf16[256,4096]{1,0:T(8,128)(2,1)S(1)} %pad_maximum_fusion), channel_id=1, source_target_pairs={{0,2},{2,0},{4,6},{6,4},{8,10},{10,8},{12,14},{14,12},{16,18},{18,... | collective-permute-start | bytes 6291464 | tf_op jit(solution)/shard_map/ppermute | solution.py:80
  605.9 19.1 %collective-permute-start.27 = (bf16[256,3072]{0,1:T(8,128)(2,1)S(1)}, bf16[256,3072]{0,1:T(8,128)(2,1)S(1)}, u32[]{:S(2)}, u32[]{:S(2)}) collective-permute-start(bf16[256,3072]{0,1:T(8,128)(2,1)S(1)} %pad_maximum_fusion.2), channel_id=1, source_target_pairs={{0,2},{2,0},{4,6},{6,4},{8,10},{10,8},{12,14},{14,12},{16,18},{18,... | collective-permute-start | bytes 4718600 | tf_op jit(solution)/shard_map/ppermute | solution.py:80
  606.5 15.1 %collective-permute-start.19 = (bf16[256,2048]{1,0:T(8,128)(2,1)S(1)}, bf16[256,2048]{1,0:T(8,128)(2,1)S(1)}, u32[]{:S(2)}, u32[]{:S(2)}) collective-permute-start(bf16[256,2048]{1,0:T(8,128)(2,1)S(1)} %pad_maximum_fusion.3), channel_id=1, source_target_pairs={{0,2},{2,0},{4,6},{6,4},{8,10},{10,8},{12,14},{14,12},{16,18},{18,... | collective-permute-start | bytes 3145736 | tf_op jit(solution)/shard_map/ppermute | solution.py:80
  607.2 27.2 %collective-permute-start.35 = (bf16[256,4096]{1,0:T(8,128)(2,1)S(1)}, bf16[256,4096]{1,0:T(8,128)(2,1)S(1)}, u32[]{:S(2)}, u32[]{:S(2)}) collective-permute-start(bf16[256,4096]{1,0:T(8,128)(2,1)S(1)} %pad_maximum_fusion.1), channel_id=1, source_target_pairs={{0,2},{2,0},{4,6},{6,4},{8,10},{10,8},{12,14},{14,12},{16,18},{18,... | collective-permute-start | bytes 6291464 | tf_op jit(solution)/shard_map/ppermute | solution.py:80
  608.0 10.4 %collective-permute-start.31 = (bf16[256,1024]{1,0:T(8,128)(2,1)S(1)}, bf16[256,1024]{1,0:T(8,128)(2,1)S(1)}, u32[]{:S(2)}, u32[]{:S(2)}) collective-permute-start(bf16[256,1024]{1,0:T(8,128)(2,1)S(1)} %pad_maximum_fusion.9), channel_id=1, source_target_pairs={{0,2},{2,0},{4,6},{6,4},{8,10},{10,8},{12,14},{14,12},{16,18},{18,... | collective-permute-start | bytes 1572872 | tf_op jit(solution)/shard_map/ppermute | solution.py:80
  618.5 2.8 collective-permute-start.17
  621.2 3.3 collective-permute-start.25
  621.6 8.9 %collective-permute-start.9 = (bf16[8,32,256]{2,1,0:T(8,128)(2,1)S(1)}, bf16[8,32,256]{2,1,0:T(8,128)(2,1)S(1)}, u32[]{:S(2)}, u32[]{:S(2)}) collective-permute-start(bf16[8,32,256]{2,1,0:T(8,128)(2,1)S(1)} %copy-done.50), channel_id=1, source_target_pairs={{0,2},{2,0},{4,6},{6,4},{8,10},{10,8},{12,14},{14,12},{16,18},{18,... | collective-permute-start | bytes 393224 | tf_op jit(solution)/shard_map/ppermute | solution.py:80
  624.6 9.8 %collective-permute-start.33 = (bf16[8,32,256]{2,1,0:T(8,128)(2,1)S(1)}, bf16[8,32,256]{2,1,0:T(8,128)(2,1)S(1)}, u32[]{:S(2)}, u32[]{:S(2)}) collective-permute-start(bf16[8,32,256]{2,1,0:T(8,128)(2,1)S(1)} %get-tuple-element.171), channel_id=1, source_target_pairs={{0,2},{2,0},{4,6},{6,4},{8,10},{10,8},{12,14},{14,12},{16,18},{18,... | collective-permute-start | bytes 393224 | tf_op jit(solution)/shard_map/ppermute | solution.py:80
  (94 other events, 516.3 us)

commit v2 on v1

--- a/solution.py
+++ b/solution.py
@@ -377,9 +377,273 @@
     return gather_fast(shards, cube)
 
 
-def cube_of(shards):
+def distance_rows(group, left, right, backwards):
+    row = lax.broadcasted_iota(jnp.int32, (group, 128), 0)
+    row = group - 1 - row if backwards else row
+    distance = jnp.where(row >= group // 2, row - group, row)
+    index = jnp.clip(distance, -left, right) + left
+    hit = index == lax.broadcasted_iota(jnp.int32, (group, 128), 1)
+    return jnp.where(hit, 1.0, 0.0).astype(jnp.bfloat16)
+
+
+def halves(cube, rows, half):
+    mine = cube.bit(0)
+    return (
+        pl.ds(pl.multiple_of(mine * half, half), half),
+        pl.ds(pl.multiple_of((1 - mine) * half, half), half),
+        pl.ds(pl.multiple_of(mine * rows, rows), rows),
+        pl.ds(pl.multiple_of((1 - mine) * rows, rows), rows),
+    )
+
+
+def to_partner(cube, k, source, target, send, recv):
+    return pltpu.make_async_remote_copy(
+        src_ref=source,
+        dst_ref=target,
+        send_sem=send,
+        recv_sem=recv,
+        device_id=cube.partner(k),
+        device_id_type=MESH,
+    )
+
+
+def attend_kernel(cube, left, right, *refs):
+    hidden, before, same, table, query_w, key_w, value_w, out_w = refs[:8]
+    after, context, heads_out, probs_out = refs[8:12]
+    weights, heads_in, away, wide, context_away, load, send, recv, head_send, head_recv = refs[12:]
+    rows, width = hidden.shape
+    group, half = (2 * rows, width // 2)
+    heads = half // 128
+    scale = 1.0 / math.sqrt(128)
+    mine = cube.bit(0)
+    own_columns, away_columns, own_rows, away_rows = halves(cube, rows, half)
+    loads = []
+    for i, matrix in enumerate((query_w, key_w, value_w, out_w)):
+        loads.append(pltpu.make_async_copy(matrix, weights.at[i], load.at[i]))
+        loads[i].start()
+    greet(cube, [0])
+
+    def exchange(i):
+        return to_partner(
+            cube, 0, away.at[i], heads_in.at[i, own_rows], send.at[i], recv.at[i]
+        )
+
+    def context_copy(head):
+        column = pl.ds(pl.multiple_of(mine * half + head * 128, 128), 128)
+        return to_partner(
+            cube, 0, context_away.at[head], wide.at[:, column], head_send.at[head], head_recv.at[head]
+        )
+
+    for i in range(3):
+        loads[i].wait()
+        away[i] = matmul(hidden[...], weights[i, :, away_columns]).astype(jnp.bfloat16)
+        exchange(i).start()
+    for i in range(3):
+        heads_in[i, own_rows, :] = matmul(hidden[...], weights[i, :, own_columns]).astype(
+            jnp.bfloat16
+        )
+    spread = matmul(distance_rows(group, left, right, False), table[...]).astype(jnp.bfloat16)
+    loads[3].wait()
+    for i in range(3):
+        exchange(i).wait_recv()
+
+    def one_head(head, carry):
+        column = pl.ds(pl.multiple_of(head * 128, 128), 128)
+        place = pl.ds(pl.multiple_of(mine * half + head * 128, 128), 128)
+        query, keys, values = (heads_in[i, :, column] for i in range(3))
+        relative = pltpu.roll(transposed_right(query, spread), 0, 1, stride=1, stride_axis=0)
+        scores = scale * (transposed_right(query, keys) + relative)
+        scores = jnp.where(same[...] > 0, scores, masked_score)
+        weight = jnp.exp(scores - jnp.max(scores, axis=1, keepdims=True))
+        probs_out[head] = weight / jnp.sum(weight, axis=1, keepdims=True)
+        there = probs_out[head, away_rows, :].astype(jnp.bfloat16)
+        context_away[head] = matmul(there, values).astype(jnp.bfloat16)
+        context_copy(head).start()
+        here = probs_out[head, own_rows, :].astype(jnp.bfloat16)
+        wide[:, place] = matmul(here, values).astype(jnp.bfloat16)
+        return carry
+
+    lax.fori_loop(0, heads, one_head, 0)
+    heads_out[...] = heads_in[...]
+    after[...] = before[...] + matmul(wide[:, own_columns], weights[3, own_columns, :])
+    for head in range(heads):
+        context_copy(head).wait_recv()
+    after[...] += matmul(wide[:, away_columns], weights[3, away_columns, :])
+    context[...] = wide[...]
+    for i in range(3):
+        exchange(i).wait_send()
+    for head in range(heads):
+        context_copy(head).wait_send()
+
+
+def attend_fast(cube, hidden, before, same, table, matrices):
+    rows, width = hidden.shape
+    group, half = (2 * rows, width // 2)
+    heads = half // 128
+    vmem = pl.BlockSpec(memory_space=pltpu.VMEM)
+    return pl.pallas_call(
+        functools.partial(attend_kernel, cube, REL_LEFT, REL_RIGHT),
+        out_shape=[
+            jax.ShapeDtypeStruct((rows, width), jnp.float32),
+            jax.ShapeDtypeStruct((rows, width), jnp.bfloat16),
+            jax.ShapeDtypeStruct((3, group, half), jnp.bfloat16),
+            jax.ShapeDtypeStruct((heads, group, group), jnp.float32),
+        ],
+        in_specs=[vmem] * 4 + [pl.BlockSpec(memory_space=pl.ANY)] * 4,
+        out_specs=[vmem] * 4,
+        scratch_shapes=[
+            pltpu.VMEM((4, width, width), jnp.bfloat16),
+            pltpu.VMEM((3, group, half), jnp.bfloat16),
+            pltpu.VMEM((3, rows, half), jnp.bfloat16),
+            pltpu.VMEM((rows, width), jnp.bfloat16),
+            pltpu.VMEM((heads, rows, 128), jnp.bfloat16),
+            pltpu.SemaphoreType.DMA((4,)),
+            pltpu.SemaphoreType.DMA((3,)),
+            pltpu.SemaphoreType.DMA((3,)),
+            pltpu.SemaphoreType.DMA((heads,)),
+            pltpu.SemaphoreType.DMA((heads,)),
+        ],
+        compiler_params=pltpu.CompilerParams(
+            collective_id=5, has_side_effects=True, vmem_limit_bytes=48 * 1024 * 1024
+        ),
+        name="attend",
+    )(hidden, before, same, table, *matrices)
+
+
+def attend_back_kernel(cube, left, right, *refs):
+    branch, heads_in, probs_in, table, query_w, key_w, value_w, out_w = refs[:8]
+    d_hidden, d_heads, d_table = refs[8:11]
+    weights, d_context, d_context_away, wide, away, load, send, recv, head_send, head_recv = refs[
+        11:
+    ]
+    rows, width = branch.shape
+    group, half = (2 * rows, width // 2)
+    heads = half // 128
+    scale = 1.0 / math.sqrt(128)
+    mine = cube.bit(0)
+    own_columns, away_columns, own_rows, away_rows = halves(cube, rows, half)
+    loads = []
+    for i, matrix in enumerate((out_w, query_w, key_w, value_w)):
+        loads.append(pltpu.make_async_copy(matrix, weights.at[i], load.at[i]))
+        loads[i].start()
+    greet(cube, [0])
+    loads[0].wait()
+    exchange = to_partner(
+        cube, 0, d_context_away, d_context.at[own_rows], send.at[0], recv.at[0]
+    )
+    d_context_away[...] = transposed_right(branch[...], weights[0, away_columns, :]).astype(
+        jnp.bfloat16
+    )
+    exchange.start()
+    d_context[own_rows, :] = transposed_right(branch[...], weights[0, own_columns, :]).astype(
+        jnp.bfloat16
+    )
+    spread = distance_rows(group, left, right, True)
+    down = lax.broadcasted_iota(jnp.int32, (group, group), 0)
+    across = lax.broadcasted_iota(jnp.int32, (group, group), 1)
+    mirror = jnp.where(down + across == group - 1, 1.0, 0.0).astype(jnp.bfloat16)
+    d_table[...] = jnp.zeros_like(d_table)
+    exchange.wait_recv()
+
+    def head_copy(head, i):
+        column = pl.ds(pl.multiple_of(i * width + mine * half + head * 128, 128), 128)
+        return to_partner(
+            cube,
+            0,
+            away.at[head, i, away_rows],
+            wide.at[:, column],
+            head_send.at[head, i],
+            head_recv.at[head, i],
+        )
+
+    def one_head(head, carry):
+        column = pl.ds(pl.multiple_of(head * 128, 128), 128)
+        query, keys, values = (heads_in[i, :, column] for i in range(3))
+        d_rows = d_context[:, column]
+        probs = probs_in[head]
+        d_probs = transposed_right(d_rows, values)
+        weighted = jnp.sum(probs * d_probs, axis=1, keepdims=True)
+        d_scores = (probs * (d_probs - weighted)).astype(jnp.bfloat16)
+        away[head, 2] = transposed_left(probs.astype(jnp.bfloat16), d_rows).astype(jnp.bfloat16)
+        head_copy(head, 2).start()
+        away[head, 1] = (scale * transposed_left(d_scores, query)).astype(jnp.bfloat16)
+        head_copy(head, 1).start()
+        turned = pltpu.roll(matmul(d_scores, mirror), 0, 1, stride=1, stride_axis=0)
+        bins = (scale * matmul(turned.astype(jnp.bfloat16), spread)).astype(jnp.bfloat16)
+        away[head, 0] = (scale * matmul(d_scores, keys) + matmul(bins, table[...])).astype(
+            jnp.bfloat16
+        )
+        head_copy(head, 0).start()
+        d_table[...] += transposed_left(bins, query)
+        for i in range(3):
+            place = pl.ds(pl.multiple_of(i * width + mine * half + head * 128, 128), 128)
+            wide[:, place] = away[head, i, own_rows, :]
+        return carry
+
+    lax.fori_loop(0, heads, one_head, 0)
+    for i in range(3):
+        loads[1 + i].wait()
+
+    def part(i, offset, columns):
+        place = pl.ds(pl.multiple_of(i * width + offset * half, half), half)
+        return transposed_right(wide[:, place], weights[1 + i, :, columns])
+
+    total = part(0, mine, own_columns)
+    for i in range(1, 3):
+        total += part(i, mine, own_columns)
+    d_hidden[...] = total
+    for head in range(heads):
+        for i in range(3):
+            head_copy(head, i).wait_recv()
+    total = part(0, 1 - mine, away_columns)
+    for i in range(1, 3):
+        total += part(i, 1 - mine, away_columns)
+    d_hidden[...] += total
+    d_heads[...] = wide[...]
+    exchange.wait_send()
+    for head in range(heads):
+        for i in range(3):
+            head_copy(head, i).wait_send()
+
+
+def attend_back_fast(cube, branch, heads_in, probs, table, matrices):
+    rows, width = branch.shape
+    group, half = (2 * rows, width // 2)
+    heads = half // 128
+    vmem = pl.BlockSpec(memory_space=pltpu.VMEM)
+    return pl.pallas_call(
+        functools.partial(attend_back_kernel, cube, REL_LEFT, REL_RIGHT),
+        out_shape=[
+            jax.ShapeDtypeStruct((rows, width), jnp.float32),
+            jax.ShapeDtypeStruct((rows, 3 * width), jnp.bfloat16),
+            jax.ShapeDtypeStruct((128, 128), jnp.float32),
+        ],
+        in_specs=[vmem] * 4 + [pl.BlockSpec(memory_space=pl.ANY)] * 4,
+        out_specs=[vmem] * 3,
+        scratch_shapes=[
+            pltpu.VMEM((4, width, width), jnp.bfloat16),
+            pltpu.VMEM((group, half), jnp.bfloat16),
+            pltpu.VMEM((rows, half), jnp.bfloat16),
+            pltpu.VMEM((rows, 3 * width), jnp.bfloat16),
+            pltpu.VMEM((heads, 3, group, 128), jnp.bfloat16),
+            pltpu.SemaphoreType.DMA((4,)),
+            pltpu.SemaphoreType.DMA((1,)),
+            pltpu.SemaphoreType.DMA((1,)),
+            pltpu.SemaphoreType.DMA((heads, 3)),
+            pltpu.SemaphoreType.DMA((heads, 3)),
+        ],
+        compiler_params=pltpu.CompilerParams(
+            collective_id=6, has_side_effects=True, vmem_limit_bytes=48 * 1024 * 1024
+        ),
+        name="attend_back",
+    )(branch, heads_in, probs, table, *matrices)
+
+
+def cube_of(shards, rel_table):
     batch, seq = (lax.axis_size("batch"), lax.axis_size("seq"))
     if seq != 2 or batch < 8 or batch & (batch - 1):
+        return None
+    if rel_table.shape[0] > 128 or rel_table.shape[1] != 128:
         return None
     if any(shard.shape[0] % 32 or shard.shape[1] % 1024 for shard in shards):
         return None
@@ -597,7 +861,7 @@
         ffn2_in,
         ffn2_out,
     )
-    cube = cube_of(shards)
+    cube = cube_of(shards, rel_table)
     gathered = gather_all(shards, cube)
     start_values = frames.astype(jnp.float32)
     after_first, kept_first = ffn_forward(
@@ -605,43 +869,50 @@
     )
     attn_norm, attn_unit, attn_inverse = norm_forward(after_first, norm_gains[1], norm_biases[1])
     attn_hidden = attn_norm.astype(jnp.bfloat16)
-    query_heads, key_heads, value_heads = (
-        lax.all_to_all(
-            to_heads(attn_hidden, gathered[2], HEADS),
-            "seq",
-            split_axis=1,
-            concat_axis=0,
-            tiled=True,
-        ),
-        lax.all_to_all(
-            to_heads(attn_hidden, gathered[3], HEADS),
-            "seq",
-            split_axis=1,
-            concat_axis=0,
-            tiled=True,
-        ),
-        lax.all_to_all(
-            to_heads(attn_hidden, gathered[4], HEADS),
-            "seq",
-            split_axis=1,
-            concat_axis=0,
-            tiled=True,
-        ),
-    )
-    context_heads, log_total = attention_forward(
-        query_heads,
-        key_heads,
-        value_heads,
-        rel_table,
-        group_segment,
-        block_rows,
-        REL_LEFT,
-        REL_RIGHT,
-    )
-    context = lax.all_to_all(context_heads, "seq", split_axis=0, concat_axis=1, tiled=True).reshape(
-        frames_here, width
-    )
-    after_attn = after_first + matmul(context, gathered[5])
+    if cube is None:
+        query_heads, key_heads, value_heads = (
+            lax.all_to_all(
+                to_heads(attn_hidden, gathered[2], HEADS),
+                "seq",
+                split_axis=1,
+                concat_axis=0,
+                tiled=True,
+            ),
+            lax.all_to_all(
+                to_heads(attn_hidden, gathered[3], HEADS),
+                "seq",
+                split_axis=1,
+                concat_axis=0,
+                tiled=True,
+            ),
+            lax.all_to_all(
+                to_heads(attn_hidden, gathered[4], HEADS),
+                "seq",
+                split_axis=1,
+                concat_axis=0,
+                tiled=True,
+            ),
+        )
+        context_heads, log_total = attention_forward(
+            query_heads,
+            key_heads,
+            value_heads,
+            rel_table,
+            group_segment,
+            block_rows,
+            REL_LEFT,
+            REL_RIGHT,
+        )
+        context = lax.all_to_all(context_heads, "seq", split_axis=0, concat_axis=1, tiled=True).reshape(
+            frames_here, width
+        )
+        after_attn = after_first + matmul(context, gathered[5])
+    else:
+        table = jnp.pad(rel_table, ((0, 128 - rel_table.shape[0]), (0, 0)))
+        same = (group_segment[:, None] == group_segment[None, :]).astype(jnp.float32)
+        after_attn, context, heads_kept, probs_kept = attend_fast(
+            cube, attn_hidden, after_first, same, table, gathered[2:6]
+        )
     conv_norm, conv_unit, conv_inverse = norm_forward(after_attn, norm_gains[2], norm_biases[2])
     conv_hidden = conv_norm.astype(jnp.bfloat16)
     pointwise = matmul(conv_hidden, gathered[6])
@@ -722,37 +993,44 @@
     )
     d_attn_res = d_conv_res + d_conv_norm
     attn_branch = d_attn_res.astype(jnp.bfloat16)
-    d_context = (
-        transposed_right(attn_branch, gathered[5])
-        .astype(jnp.bfloat16)
-        .reshape(frames_here, HEADS, -1)
-    )
-    d_context_heads = lax.all_to_all(d_context, "seq", split_axis=1, concat_axis=0, tiled=True)
-    d_query_heads, d_key_heads, d_value_heads, d_table = attention_backward(
-        query_heads,
-        key_heads,
-        value_heads,
-        rel_table,
-        group_segment,
-        log_total,
-        d_context_heads,
-        block_rows,
-        REL_LEFT,
-        REL_RIGHT,
-    )
-    d_query, d_keys, d_values = (
-        lax.all_to_all(d_query_heads, "seq", split_axis=0, concat_axis=1, tiled=True),
-        lax.all_to_all(d_key_heads, "seq", split_axis=0, concat_axis=1, tiled=True),
-        lax.all_to_all(d_value_heads, "seq", split_axis=0, concat_axis=1, tiled=True),
-    )
-    d_query = d_query.reshape(frames_here, width)
-    d_keys = d_keys.reshape(frames_here, width)
-    d_values = d_values.reshape(frames_here, width)
-    d_attn_hidden = (
-        transposed_right(d_query, gathered[2])
-        + transposed_right(d_keys, gathered[3])
-        + transposed_right(d_values, gathered[4])
-    )
+    if cube is None:
+        d_context = (
+            transposed_right(attn_branch, gathered[5])
+            .astype(jnp.bfloat16)
+            .reshape(frames_here, HEADS, -1)
+        )
+        d_context_heads = lax.all_to_all(d_context, "seq", split_axis=1, concat_axis=0, tiled=True)
+        d_query_heads, d_key_heads, d_value_heads, d_table = attention_backward(
+            query_heads,
+            key_heads,
+            value_heads,
+            rel_table,
+            group_segment,
+            log_total,
+            d_context_heads,
+            block_rows,
+            REL_LEFT,
+            REL_RIGHT,
+        )
+        d_query, d_keys, d_values = (
+            lax.all_to_all(d_query_heads, "seq", split_axis=0, concat_axis=1, tiled=True),
+            lax.all_to_all(d_key_heads, "seq", split_axis=0, concat_axis=1, tiled=True),
+            lax.all_to_all(d_value_heads, "seq", split_axis=0, concat_axis=1, tiled=True),
+        )
+        d_query = d_query.reshape(frames_here, width)
+        d_keys = d_keys.reshape(frames_here, width)
+        d_values = d_values.reshape(frames_here, width)
+        d_attn_hidden = (
+            transposed_right(d_query, gathered[2])
+            + transposed_right(d_keys, gathered[3])
+            + transposed_right(d_values, gathered[4])
+        )
+        heads_in = jnp.concatenate([d_query, d_keys, d_values], axis=1)
+    else:
+        d_attn_hidden, heads_in, d_table = attend_back_fast(
+            cube, attn_branch, heads_kept, probs_kept, table, gathered[2:6]
+        )
+        d_table = d_table[: rel_table.shape[0]]
     d_attn_norm, gain_one, shift_one = norm_backward(
         d_attn_hidden, attn_unit, attn_inverse, norm_gains[1]
     )
@@ -760,7 +1038,6 @@
     d_input, grad_one_in, grad_one_out, gain_zero, shift_zero = ffn_backward(
         d_first_res, kept_first, norm_gains[0], gathered[0], gathered[1]
     )
-    heads_in = jnp.concatenate([d_query, d_keys, d_values], axis=1)
     two_out, two_in, conv_out, conv_in, attn_out, attn_in, one_out, one_in = gradient_shards(
         (
             grad_two_out,

time: 804 us -> 776 us (0.965)
  Pallas kernels: 431 us -> 467 us
  starting transfers between devices: 62.3 us -> 29 us
  waiting for transfers between devices: 75.2 us -> 105 us
  matrix products: 84.7 us -> 61.6 us
  local copies, waits for them, and re-layouts: 83.3 us -> 65 us
  other arithmetic: 53.2 us -> 35.3 us
    ppermute x32, waiting for transfers between devices: 57.7 us -> 105 us  [swap(): return lax.ppermute(values, axis, pairs)]
    pallas_call x0 -> x2, Pallas kernels: none -> 35.4 us  [the longest x1 19 us: attend_fast(): pl.pallas_call(functools.partial(attend_kernel, cube, REL_LEFT, REL_RIGHT...]
    all_to_all x8 -> x0, starting transfers between devices: 29.9 us -> none  [the longest x1 4.29 us: on_device(): lax.all_to_all(to_heads(attn_hidden, gathered[3], HEADS), 'seq', split_ax...]
    all_to_all x8 -> x0, waiting for transfers between devices: 16.9 us -> none  [the longest x1 5.61 us: on_device(): lax.all_to_all(d_key_heads, 'seq', split_axis=0, concat_axis=1, tiled=True)]
    dot_general x18 -> x14, matrix products: 50.9 us -> 40.1 us  [matmul(): return jnp.dot(left, right, preferred_element_type=jnp.float32)]
    reshape x8 -> x0, local copies, waits for them, and re-layouts: 10.4 us -> none  [the longest x2 3.5 us: spread_band(): padded.reshape(heads, rows * (band + 1))[:, :rows * band]]
    dot_general x10 -> x6, matrix products: 29.3 us -> 21.5 us  [transposed_right(): lax.dot_general(left, right, (((1,), (1,)), ((), ())), preferred_element_...]
    unnamed x242 -> x175, local copies, waits for them, and re-layouts: 22.1 us -> 23.1 us
  transfers between devices with their start and end apart: 44 -> 36, of which waited for: 12 -> 9; matrix products, arithmetic and copies ran while one was open for 24% -> 17% of each run, Pallas kernels for 7% -> 10%
where the time goes in v2:
time: 776 us; the launch traced here: 766 us
  Pallas kernels  467 us (60%)
  waiting for transfers between devices  105 us (14%)
  local copies, waits for them, and re-layouts  65 us (8%)
  matrix products  61.6 us (8%)
  other arithmetic  35.3 us (5%)
  starting transfers between devices  29 us (4%)
    pallas_call x1, Pallas kernels, gather_fast(): pl.pallas_call(functools.partial(gather_kernel, cube, orders, count, whic...  230 us
    pallas_call x1, Pallas kernels, reduce_fast(): pl.pallas_call(functools.partial(reduce_kernel, cube, order, rows, column...  144 us
    ppermute x32, waiting for transfers between devices, swap(): return lax.ppermute(values, axis, pairs)  105 us
    pallas_call x3, Pallas kernels, sum_fast(): pl.pallas_call(functools.partial(sum_kernel, cube), out_shape=jax.ShapeDt...  58.3 us
    dot_general x14, matrix products, matmul(): return jnp.dot(left, right, preferred_element_type=jnp.float32)  40.1 us
    unnamed x175, local copies, waits for them, and re-layouts  23.1 us
    dot_general x6, matrix products, transposed_right(): lax.dot_general(left, right, (((1,), (1,)), ((), ())), preferred_element_...  21.5 us
    ppermute x32, starting transfers between devices, swap(): return lax.ppermute(values, axis, pairs)  19.4 us
  transfers between devices with their start and end apart: 36, of which 9 were waited for; matrix products, arithmetic and copies ran while one was open for 17% of the time, Pallas kernels for 10%

profile of v2, /device:TPU:0, one launch (start us, length us, event | category | flops | bytes accessed | tf_op | source)
XLA Modules:
  0.0 766.2 jit_solution(6562720406856113598)
XLA Ops:
  4.9 229.5 %gather_weights.1 = (bf16[2,2,2,2,2,32,4096]{6,5,4,3,2,1,0:T(8,128)(2,1)}, bf16[2,2,2,2,2,128,1024]{6,5,4,3,2,1,0:T(8,128)(2,1)}, bf16[2,2,2,2,2,32,1024]{6,5,4,...) custom-call(bf16[32,4096]{1,0:T(8,128)(2,1)} %refs_0_.1, ...), custom_call_target="tpu_custom_call" | custom-call | tf_op jit(solution)/shard_map/gather_weights/pallas_call | solution.py:165
  234.4 6.0 fusion.31
  240.5 1.4 fusion.181
  242.9 19.0 %attend.1 = (f32[128,1024]{1,0:T(8,128)S(1)}, bf16[128,1024]{1,0:T(8,128)(2,1)S(1)}, bf16[3,256,512]{2,1,0:T(8,128)(2,1)S(1)}, f32[4,256,256]{2,1,0:T(8,128)S(1)}) custom-call(bf16[128,1024]{1,0:T(8,128)(2,1)S(1)} %add_convert_fusion.3.refs_0_, f32[128,1024]{1,0:T(8,128)S(1)} %get-tuple-element.172.refs_1_, f32[256,256]{1,0:T(8,128)S(1)} %compare_convert_fusion.refs_2_, ...), custom_call_target="tpu_custom_call" | custom-call | tf_op jit(solution)/shard_map/attend/pallas_call | solution.py:484
  264.1 3.0 fusion.165
  269.6 2.4 collective-permute-start
  272.0 1.3 collective-permute-start.1
  274.2 1.8 copy.58
  276.0 1.7 dynamic-slice_bitcast_fusion.2
  277.7 2.6 collective-permute-start.24
  281.1 1.7 dynamic-slice_bitcast_fusion.4
  283.8 3.0 reshape.411
  286.9 1.3 multiply_reduce_fusion.13
  289.5 17.1 %sum_over_devices.3 = f32[8,1024]{1,0:T(8,128)} custom-call(f32[8,1024]{1,0:T(8,128)} %reshape.392.value), custom_call_target="tpu_custom_call" | custom-call | tf_op jit(solution)/shard_map/sum_over_devices/pallas_call | solution.py:205
  308.6 2.1 multiply_divide_fusion
  311.3 1.9 fusion.205
  313.2 2.5 fusion.182
  316.0 6.0 fusion.30
  322.0 1.4 fusion.183
  325.4 4.1 fusion
  329.6 2.9 fusion.184
  332.5 1.6 multiply_reduce_fusion.1
  334.1 1.4 fusion.170
  335.5 2.7 multiply_reduce_fusion.7
  339.2 16.3 %sum_over_devices.4 = f32[8,1024]{1,0:T(8,128)} custom-call(f32[8,1024]{1,0:T(8,128)} %reshape.398.value), custom_call_target="tpu_custom_call" | custom-call | tf_op jit(solution)/shard_map/sum_over_devices/pallas_call | solution.py:205
  356.4 2.8 fusion.96
  361.2 4.5 collective-permute-start.3
  365.8 2.6 reshape.399
  369.2 1.7 dynamic-slice_bitcast_fusion.8
  372.0 7.7 %constant_dynamic-slice_fusion = (bf16[8,2,1,128,128]{3,2,1,0,4:T(2,128)(2,1)}, bf16[8,2,1,128,128]{3,2,1,0,4:T(2,128)(2,1)}, bf16[8,2,1,128,128]{3,2,1,0,4:T(2,128)(2,1)}, bf16[8,2,1,128,128]{3,2,1,0,4:T(2,128)(2,1)}) fusion(bf16[8,2,2,128,128]{3,2,1,0,4:T(2,128)(2,1)} %reshape.411, s32[]{:T(128)S(6)} %select_n.97, s32[]{:T(128)S(6)} %select_n.96, ...), kind=kLoop, calls=%fused_computation.311 | loop fusion | bytes 4194312 | tf_op jit(solution)/shard_map/jit(dynamic_index_in_dim)/dynamic_slice | solution.py:354
  380.5 3.5 copy.69
  384.0 3.6 copy.68
  387.5 3.5 copy.67
  391.0 3.5 copy.66
  394.6 2.0 collective-permute-start.8
  396.6 1.6 multiply_convert_fusion.6
  398.5 3.8 fusion.163
  404.7 16.4 %attend_back.1 = (f32[128,1024]{1,0:T(8,128)S(1)}, bf16[128,3072]{1,0:T(8,128)(2,1)S(1)}, f32[128,128]{1,0:T(8,128)S(1)}) custom-call(bf16[128,1024]{1,0:T(8,128)(2,1)S(1)} %get-tuple-element.90.refs_0_, bf16[3,256,512]{2,1,0:T(8,128)(2,1)S(1)} %copy-done.4, f32[4,256,256]{2,1,0:T(8,128)S(1)} %copy-done.2, bf16[128,128]{1,0:T(8,128)(2,1)S(1)} %pad.16.refs_3_, ...), custom_call_target="tpu_custom_call" | custom-call | tf_op jit(solution)/shard_map/attend_back/pallas_call | solution.py:614
  422.6 5.1 fusion.1
  427.8 2.9 fusion.185
  432.0 24.9 %sum_over_devices.5 = f32[32,1024]{1,0:T(8,128)} custom-call(f32[32,1024]{1,0:T(8,128)} %reshape.427.value), custom_call_target="tpu_custom_call" | custom-call | tf_op jit(solution)/shard_map/sum_over_devices/pallas_call | solution.py:205
  456.9 2.1 fusion.74
  459.0 1.6 fusion.176
  461.6 1.6 collective-permute-start.32
  466.0 1.6 collective-permute-start.28
  468.1 1.6 collective-permute-start.26
  472.5 1.6 collective-permute-done.6
  475.9 15.0 %collective-permute-done.30 = bf16[128,1024]{1,0:T(8,128)(2,1)S(1)} collective-permute-done((bf16[128,1024]{1,0:T(8,128)(2,1)}, bf16[128,1024]{1,0:T(8,128)(2,1)S(1)}, u32[]{:S(2)}, u32[]{:S(2)}) %collective-permute-start.30) | collective-permute-done | bytes 262176 | tf_op jit(solution)/shard_map/ppermute | solution.py:80
  493.8 43.6 %collective-permute-done.16 = bf16[8,2,32,128]{3,2,1,0:T(8,128)(2,1)S(1)} collective-permute-done((bf16[8,2,32,128]{3,2,1,0:T(8,128)(2,1)S(1)}, bf16[8,2,32,128]{3,2,1,0:T(8,128)(2,1)S(1)}, u32[]{:S(2)}, u32[]{:S(2)}) %collective-permute-start.16) | collective-permute-done | bytes 131104 | tf_op jit(solution)/shard_map/ppermute | solution.py:80
  537.3 1.3 collective-permute-start.4
  540.7 1.3 collective-permute-start.18
  543.5 8.6 %collective-permute-done.4 = bf16[8,2,128,128]{3,2,1,0:T(8,128)(2,1)S(1)} collective-permute-done((bf16[8,2,128,128]{3,2,1,0:T(8,128)(2,1)S(1)}, bf16[8,2,128,128]{3,2,1,0:T(8,128)(2,1)S(1)}, u32[]{:S(2)}, u32[]{:S(2)}) %collective-permute-start.4) | collective-permute-done | bytes 524320 | tf_op jit(solution)/shard_map/ppermute | solution.py:80
  552.9 30.8 %collective-permute-done.18 = bf16[128,2048]{1,0:T(8,128)(2,1)S(1)} collective-permute-done((bf16[128,2048]{1,0:T(8,128)(2,1)S(1)}, bf16[128,2048]{1,0:T(8,128)(2,1)S(1)}, u32[]{:S(2)}, u32[]{:S(2)}) %collective-permute-start.18) | collective-permute-done | bytes 524320 | tf_op jit(solution)/shard_map/ppermute | solution.py:80
  586.9 2.5 collective-permute-done.29
  589.6 2.3 convolution_convert_fusion.7
  593.1 3.8 convolution_convert_fusion.4
  597.3 3.5 convolution_convert_fusion.5
  601.3 1.7 convolution_convert_fusion.3
  603.1 2.2 convolution_convert_fusion.2
  605.4 2.5 convolution_convert_fusion.1
  607.9 2.5 convolution_convert_fusion
  610.4 143.9 %reduce_gradients.1 = f32[23,32,1024]{2,1,0:T(8,128)} custom-call(bf16[2,2,2,128,1024]{4,3,2,1,0:T(8,128)(2,1)} %bitcast.242, bf16[2,2,2,32,4096]{4,3,2,1,0:T(8,128)(2,1)} %bitcast.243, bf16[2,2,2,32,1024]{4,3,2,1,0:T(8,128)(2,1)} %bitcast.262, bf16[2,2,2,32,2048]{4,3,2,1,0:T(8,128)(2,1)} %bitcast.252, bf16[2,2,2,32,1024]{4,3,2,1,0:T(8,128)(2,1)} %bitcast.263, ...), custom_call_target="tpu_custom_call" | custom-call | tf_op jit(solution)/shard_map/reduce_gradients/pallas_call | solution.py:319
  754.3 2.7 fusion.172
  759.0 1.7 slice_bitcast_fusion.4
  (335 shorter events, 58.0 us)
Async XLA Ops:
  0.7 233.8 %copy-start.14 = (bf16[128,1024]{1,0:T(8,128)(2,1)S(1)}, bf16[128,1024]{1,0:T(8,128)(2,1)}, u32[]{:S(2)}) copy-start(bf16[128,1024]{1,0:T(8,128)(2,1)} %param.19) | copy-start | bytes 786436
  3.7 236.8 %copy-start.64 = (f32[128]{0:T(128)}, f32[128]{0:T(128)S(1)}, u32[]{:S(2)}) copy-start(f32[128]{0:T(128)S(1)} %broadcast_multiply_fusion.14) | copy-start | bytes 1540
  4.9 235.6 %copy-start.69 = (f32[128]{0:T(128)}, f32[128]{0:T(128)S(1)}, u32[]{:S(2)}) copy-start(f32[128]{0:T(128)S(1)} %add_rsqrt_fusion.5) | copy-start | bytes 1540
  242.0 31.4 %copy-start.50 = (f32[128]{0:T(128)}, f32[128]{0:T(128)S(1)}, u32[]{:S(2)}) copy-start(f32[128]{0:T(128)S(1)} %broadcast_multiply_fusion.13) | copy-start | bytes 1540
  242.2 31.1 %copy-start.60 = (f32[128]{0:T(128)}, f32[128]{0:T(128)S(1)}, u32[]{:S(2)}) copy-start(f32[128]{0:T(128)S(1)} %add_rsqrt_fusion.4) | copy-start | bytes 1540
  268.1 15.0 %copy-start.40 = (bf16[5,1024]{1,0:T(8,128)(2,1)S(1)}, bf16[5,1024]{1,0:T(8,128)(2,1)}, u32[]{:S(2)}) copy-start(bf16[5,1024]{1,0:T(8,128)(2,1)} %param.32) | copy-start | bytes 30724
  269.6 17.3 %collective-permute-start = (bf16[2,1024]{1,0:T(2,128)(2,1)}, bf16[2,1024]{1,0:T(2,128)(2,1)S(1)}, u32[]{:S(2)}, u32[]{:S(2)}) collective-permute-start(bf16[2,1024]{1,0:T(2,128)(2,1)} %get-tuple-element.144), channel_id=1, source_target_pairs={{0,1},{2,3},{4,5},{6,7},{8,9},{10,11},{12,13},{14,15},{16,17},{18,... | collective-permute-start | bytes 12296 | tf_op jit(solution)/shard_map/ppermute | solution.py:30
  272.0 14.8 %collective-permute-start.1 = (bf16[2,1024]{1,0:T(2,128)(2,1)S(1)}, bf16[2,1024]{1,0:T(2,128)(2,1)S(1)}, u32[]{:S(2)}, u32[]{:S(2)}) collective-permute-start(bf16[2,1024]{1,0:T(2,128)(2,1)S(1)} %get-tuple-element.145), channel_id=1, source_target_pairs={{1,0},{3,2},{5,4},{7,6},{9,8},{11,10},{13,12},{15,14},{17,16},{19,... | collective-permute-start | bytes 12296 | tf_op jit(solution)/shard_map/ppermute | solution.py:31
  277.7 183.9 %collective-permute-start.24 = (bf16[8,2,32,128]{3,2,1,0:T(8,128)(2,1)}, bf16[8,2,32,128]{3,2,1,0:T(8,128)(2,1)}, u32[]{:S(2)}, u32[]{:S(2)}) collective-permute-start(bf16[8,2,32,128]{3,2,1,0:T(8,128)(2,1)} %get-tuple-element.124), channel_id=1, source_target_pairs={{0,1},{1,0},{2,3},{3,2},{4,5},{5,4},{6,7},{7,6},{8,9},{9,8},{10,11... | collective-permute-start | bytes 393224 | tf_op jit(solution)/shard_map/ppermute | solution.py:80
  280.3 30.4 %copy-start.42 = (f32[1024]{0:T(1024)S(1)}, f32[1024]{0:T(1024)}, u32[]{:S(2)}) copy-start(f32[1024]{0:T(1024)} %param.36) | copy-start | bytes 12292
  282.9 181.8 %collective-permute-start.20 = (bf16[8,2,32,128]{3,2,1,0:T(8,128)(2,1)}, bf16[8,2,32,128]{3,2,1,0:T(8,128)(2,1)}, u32[]{:S(2)}, u32[]{:S(2)}) collective-permute-start(bf16[8,2,32,128]{3,2,1,0:T(8,128)(2,1)} %get-tuple-element.128), channel_id=1, source_target_pairs={{0,1},{1,0},{2,3},{3,2},{4,5},{5,4},{6,7},{7,6},{8,9},{9,8},{10,11... | collective-permute-start | bytes 393224 | tf_op jit(solution)/shard_map/ppermute | solution.py:80
  335.5 20.9 %copy-start.43 = (f32[1024]{0:T(1024)S(1)}, f32[1024]{0:T(1024)}, u32[]{:S(2)}) copy-start(f32[1024]{0:T(1024)} %mul.676) | copy-start | bytes 12292
  335.5 20.9 %copy-start.53 = (f32[128]{0:T(128)S(1)}, f32[128]{0:T(128)}, u32[]{:S(2)}) copy-start(f32[128]{0:T(128)} %copy-done.52) | copy-start | bytes 1540
  335.5 20.9 %copy-start.55 = (f32[128]{0:T(128)S(1)}, f32[128]{0:T(128)}, u32[]{:S(2)}) copy-start(f32[128]{0:T(128)} %copy-done.54) | copy-start | bytes 1540
  338.3 132.6 %collective-permute-start.14 = (bf16[128,1024]{1,0:T(8,128)(2,1)}, bf16[128,1024]{1,0:T(8,128)(2,1)}, u32[]{:S(2)}, u32[]{:S(2)}) collective-permute-start(bf16[128,1024]{1,0:T(8,128)(2,1)} %get-tuple-element.94), channel_id=1, source_target_pairs={{0,1},{1,0},{2,3},{3,2},{4,5},{5,4},{6,7},{7,6},{8,9},{9,8},{10,11... | collective-permute-start | bytes 786440 | tf_op jit(solution)/shard_map/ppermute | solution.py:80
  356.4 12.8 %copy-start.44 = (f32[1,1024]{1,0:T(1,128)}, f32[1,1024]{1,0:T(1,128)S(1)}, u32[]{:S(2)}) copy-start(f32[1,1024]{1,0:T(1,128)S(1)} %get-tuple-element.149) | copy-start | bytes 12292
  356.4 12.8 %copy-start.45 = (f32[1,1024]{1,0:T(1,128)}, f32[1,1024]{1,0:T(1,128)S(1)}, u32[]{:S(2)}) copy-start(f32[1,1024]{1,0:T(1,128)S(1)} %get-tuple-element.150) | copy-start | bytes 12292
  359.9 34.6 %collective-permute-start.2 = (bf16[2,1024]{1,0:T(2,128)(2,1)S(1)}, bf16[2,1024]{1,0:T(2,128)(2,1)S(1)}, u32[]{:S(2)}, u32[]{:S(2)}) collective-permute-start(bf16[2,1024]{1,0:T(2,128)(2,1)S(1)} %get-tuple-element.142), channel_id=1, source_target_pairs={{1,0},{3,2},{5,4},{7,6},{9,8},{11,10},{13,12},{15,14},{17,16},{19,... | collective-permute-start | bytes 12296 | tf_op jit(solution)/shard_map/ppermute | solution.py:31
  361.2 33.3 %collective-permute-start.3 = (bf16[2,1024]{1,0:T(2,128)(2,1)S(1)}, bf16[2,1024]{1,0:T(2,128)(2,1)S(1)}, u32[]{:S(2)}, u32[]{:S(2)}) collective-permute-start(bf16[2,1024]{1,0:T(2,128)(2,1)S(1)} %get-tuple-element.143), channel_id=1, source_target_pairs={{0,1},{2,3},{4,5},{6,7},{8,9},{10,11},{12,13},{14,15},{16,17},{18,... | collective-permute-start | bytes 12296 | tf_op jit(solution)/shard_map/ppermute | solution.py:30
  384.0 12.6 %copy-start.27 = (bf16[128,1024]{1,0:T(8,128)(2,1)S(1)}, bf16[128,1024]{1,0:T(8,128)(2,1)}, u32[]{:S(2)}) copy-start(bf16[128,1024]{1,0:T(8,128)(2,1)} %copy-done.26) | copy-start | bytes 786436
  384.0 12.6 %copy-start.57 = (f32[128]{0:T(128)S(1)}, f32[128]{0:T(128)}, u32[]{:S(2)}) copy-start(f32[128]{0:T(128)} %copy-done.56) | copy-start | bytes 1540
  384.0 12.6 %copy-start.59 = (f32[128]{0:T(128)S(1)}, f32[128]{0:T(128)}, u32[]{:S(2)}) copy-start(f32[128]{0:T(128)} %copy-done.58) | copy-start | bytes 1540
  394.5 71.5 %collective-permute-start.12 = (bf16[8,2,32,128]{3,2,1,0:T(8,128)(2,1)}, bf16[8,2,32,128]{3,2,1,0:T(8,128)(2,1)}, u32[]{:S(2)}, u32[]{:S(2)}) collective-permute-start(bf16[8,2,32,128]{3,2,1,0:T(8,128)(2,1)} %get-tuple-element.136), channel_id=1, source_target_pairs={{0,1},{1,0},{2,3},{3,2},{4,5},{5,4},{6,7},{7,6},{8,9},{9,8},{10,11... | collective-permute-start | bytes 393224 | tf_op jit(solution)/shard_map/ppermute | solution.py:80
  394.6 73.1 %collective-permute-start.8 = (bf16[8,2,32,128]{3,2,1,0:T(8,128)(2,1)}, bf16[8,2,32,128]{3,2,1,0:T(8,128)(2,1)}, u32[]{:S(2)}, u32[]{:S(2)}) collective-permute-start(bf16[8,2,32,128]{3,2,1,0:T(8,128)(2,1)} %get-tuple-element.140), channel_id=1, source_target_pairs={{0,1},{1,0},{2,3},{3,2},{4,5},{5,4},{6,7},{7,6},{8,9},{9,8},{10,11... | collective-permute-start | bytes 393224 | tf_op jit(solution)/shard_map/ppermute | solution.py:80
  404.1 18.5 %slice-start.4 = ((s8[8388608]{0:T(1024)(128)(4,1)}), s8[4194304]{0:T(1024)(128)(4,1)S(1)}, s32[]{:S(2)}) async-start(s8[8388608]{0:T(1024)(128)(4,1)} %bitcast.346), calls=%async_computation.4 | async-start | bytes 8388608
  404.7 16.5 %copy-start.51 = (f32[128]{0:T(128)S(1)}, f32[128]{0:T(128)}, u32[]{:S(2)}) copy-start(f32[128]{0:T(128)} %copy-done.50) | copy-start | bytes 1540
  404.7 16.5 %copy-start.61 = (f32[128]{0:T(128)S(1)}, f32[128]{0:T(128)}, u32[]{:S(2)}) copy-start(f32[128]{0:T(128)} %copy-done.60) | copy-start | bytes 1540
  404.7 17.9 %slice-start.5 = ((s8[8388608]{0:T(1024)(128)(4,1)}), s8[4194304]{0:T(1024)(128)(4,1)S(1)}, s32[]{:S(2)}) async-start(s8[8388608]{0:T(1024)(128)(4,1)} %bitcast.346), calls=%async_computation.5 | async-start | bytes 8388608
  431.1 30.3 %copy-start.29 = (bf16[1024,128]{0,1:T(8,128)(2,1)S(1)}, bf16[1024,128]{0,1:T(8,128)(2,1)}, u32[]{:S(2)}) copy-start(bf16[1024,128]{0,1:T(8,128)(2,1)} %get-tuple-element.111) | copy-start | bytes 786436
  459.0 11.9 %copy-start.11 = (bf16[128,4096]{1,0:T(8,128)(2,1)S(1)}, bf16[128,4096]{1,0:T(8,128)(2,1)}, u32[]{:S(2)}) copy-start(bf16[128,4096]{1,0:T(8,128)(2,1)} %copy-done.10) | copy-start | bytes 3145732
  461.6 6.5 collective-permute-start.32
  464.0 26.9 %copy-start.39 = (bf16[8,2,32,128]{3,2,1,0:T(8,128)(2,1)S(1)}, bf16[8,2,32,128]{3,2,1,0:T(8,128)(2,1)}, u32[]{:S(2)}) copy-start(bf16[8,2,32,128]{3,2,1,0:T(8,128)(2,1)} %get-tuple-element.132) | copy-start | bytes 393220
  464.6 9.5 %collective-permute-start.6 = (bf16[128,1024]{1,0:T(8,128)(2,1)}, bf16[128,1024]{1,0:T(8,128)(2,1)S(1)}, u32[]{:S(2)}, u32[]{:S(2)}) collective-permute-start(bf16[128,1024]{1,0:T(8,128)(2,1)} %multiply_convert_fusion.8), channel_id=1, source_target_pairs={{0,1},{1,0},{2,3},{3,2},{4,5},{5,4},{6,7},{7,6},{8,9},{9,8},{10,11... | collective-permute-start | bytes 786440 | tf_op jit(solution)/shard_map/ppermute | solution.py:80
  466.0 73.3 %collective-permute-start.28 = (bf16[8,2,128,128]{3,2,1,0:T(8,128)(2,1)}, bf16[8,2,128,128]{3,2,1,0:T(8,128)(2,1)S(1)}, u32[]{:S(2)}, u32[]{:S(2)}) collective-permute-start(bf16[8,2,128,128]{3,2,1,0:T(8,128)(2,1)} %bitcast.261), channel_id=1, source_target_pairs={{0,1},{1,0},{2,3},{3,2},{4,5},{5,4},{6,7},{7,6},{8,9},{9,8},{10,11... | collective-permute-start | bytes 1572872 | tf_op jit(solution)/shard_map/ppermute | solution.py:80
  467.6 23.3 %collective-permute-start.30 = (bf16[128,1024]{1,0:T(8,128)(2,1)}, bf16[128,1024]{1,0:T(8,128)(2,1)S(1)}, u32[]{:S(2)}, u32[]{:S(2)}) collective-permute-start(bf16[128,1024]{1,0:T(8,128)(2,1)} %get-tuple-element.88), channel_id=1, source_target_pairs={{0,1},{1,0},{2,3},{3,2},{4,5},{5,4},{6,7},{7,6},{8,9},{9,8},{10,11... | collective-permute-start | bytes 786440 | tf_op jit(solution)/shard_map/ppermute | solution.py:80
  468.1 73.9 %collective-permute-start.26 = (bf16[128,3072]{1,0:T(8,128)(2,1)S(1)}, bf16[128,3072]{1,0:T(8,128)(2,1)S(1)}, u32[]{:S(2)}, u32[]{:S(2)}) collective-permute-start(bf16[128,3072]{1,0:T(8,128)(2,1)S(1)} %copy-done.6), channel_id=1, source_target_pairs={{0,1},{1,0},{2,3},{3,2},{4,5},{5,4},{6,7},{7,6},{8,9},{9,8},{10,11... | collective-permute-start | bytes 2359304 | tf_op jit(solution)/shard_map/ppermute | solution.py:80
  469.7 67.6 %copy-start.31 = (bf16[8,2,1,128,128]{4,3,1,0,2:T(8,128)(2,1)S(1)}, bf16[8,2,1,128,128]{4,3,1,0,2:T(8,128)(2,1)}, u32[]{:S(2)}) copy-start(bf16[8,2,1,128,128]{4,3,1,0,2:T(8,128)(2,1)} %copy.67) | copy-start | bytes 1572868
  469.8 68.9 %copy-start.13 = (bf16[128,4096]{1,0:T(8,128)(2,1)S(1)}, bf16[128,4096]{1,0:T(8,128)(2,1)}, u32[]{:S(2)}) copy-start(bf16[128,4096]{1,0:T(8,128)(2,1)} %copy-done.12) | copy-start | bytes 3145732
  470.9 81.3 %collective-permute-start.10 = (bf16[128,4096]{1,0:T(8,128)(2,1)S(1)}, bf16[128,4096]{1,0:T(8,128)(2,1)S(1)}, u32[]{:S(2)}, u32[]{:S(2)}) collective-permute-start(bf16[128,4096]{1,0:T(8,128)(2,1)S(1)} %copy-done.11), channel_id=1, source_target_pairs={{0,1},{1,0},{2,3},{3,2},{4,5},{5,4},{6,7},{7,6},{8,9},{9,8},{10,11... | collective-permute-start | bytes 3145736 | tf_op jit(solution)/shard_map/ppermute | solution.py:80
  472.5 66.9 %copy-start.24 = (bf16[8,2,1,128,128]{4,3,1,0,2:T(8,128)(2,1)S(1)}, bf16[8,2,1,128,128]{4,3,1,0,2:T(8,128)(2,1)}, u32[]{:S(2)}) copy-start(bf16[8,2,1,128,128]{4,3,1,0,2:T(8,128)(2,1)} %copy.68) | copy-start | bytes 1572868
  474.1 64.6 %collective-permute-start.22 = (bf16[128,1024]{1,0:T(8,128)(2,1)S(1)}, bf16[128,1024]{1,0:T(8,128)(2,1)S(1)}, u32[]{:S(2)}, u32[]{:S(2)}) collective-permute-start(bf16[128,1024]{1,0:T(8,128)(2,1)S(1)} %get-tuple-element.90.refs_0_), channel_id=1, source_target_pairs={{0,1},{1,0},{2,3},{3,2},{4,5},{5,4},{6,7},{7,6},{8,9},{9,8},{10,11... | collective-permute-start | bytes 786440 | tf_op jit(solution)/shard_map/ppermute | solution.py:80
  490.9 46.4 %collective-permute-start.16 = (bf16[8,2,32,128]{3,2,1,0:T(8,128)(2,1)S(1)}, bf16[8,2,32,128]{3,2,1,0:T(8,128)(2,1)S(1)}, u32[]{:S(2)}, u32[]{:S(2)}) collective-permute-start(bf16[8,2,32,128]{3,2,1,0:T(8,128)(2,1)S(1)} %copy-done.39), channel_id=1, source_target_pairs={{0,1},{1,0},{2,3},{3,2},{4,5},{5,4},{6,7},{7,6},{8,9},{9,8},{10,11... | collective-permute-start | bytes 393224 | tf_op jit(solution)/shard_map/ppermute | solution.py:80
  492.7 48.0 %copy-start.32 = (bf16[128,2048]{1,0:T(8,128)(2,1)S(1)}, bf16[128,2048]{1,0:T(8,128)(2,1)}, u32[]{:S(2)}) copy-start(bf16[128,2048]{1,0:T(8,128)(2,1)} %pad_maximum_fusion.4) | copy-start | bytes 1572868
  537.3 14.9 %collective-permute-start.4 = (bf16[8,2,128,128]{3,2,1,0:T(8,128)(2,1)S(1)}, bf16[8,2,128,128]{3,2,1,0:T(8,128)(2,1)S(1)}, u32[]{:S(2)}, u32[]{:S(2)}) collective-permute-start(bf16[8,2,128,128]{3,2,1,0:T(8,128)(2,1)S(1)} %bitcast.260), channel_id=1, source_target_pairs={{0,1},{1,0},{2,3},{3,2},{4,5},{5,4},{6,7},{7,6},{8,9},{9,8},{10,11... | collective-permute-start | bytes 1572872 | tf_op jit(solution)/shard_map/ppermute | solution.py:80
  538.6 45.1 %collective-permute-start.34 = (bf16[128,4096]{1,0:T(8,128)(2,1)S(1)}, bf16[128,4096]{1,0:T(8,128)(2,1)S(1)}, u32[]{:S(2)}, u32[]{:S(2)}) collective-permute-start(bf16[128,4096]{1,0:T(8,128)(2,1)S(1)} %copy-done.13), channel_id=1, source_target_pairs={{0,1},{1,0},{2,3},{3,2},{4,5},{5,4},{6,7},{7,6},{8,9},{9,8},{10,11... | collective-permute-start | bytes 3145736 | tf_op jit(solution)/shard_map/ppermute | solution.py:80
  539.4 1.3 collective-permute-start.21
  540.7 43.0 %collective-permute-start.18 = (bf16[128,2048]{1,0:T(8,128)(2,1)S(1)}, bf16[128,2048]{1,0:T(8,128)(2,1)S(1)}, u32[]{:S(2)}, u32[]{:S(2)}) collective-permute-start(bf16[128,2048]{1,0:T(8,128)(2,1)S(1)} %copy-done.32), channel_id=1, source_target_pairs={{0,1},{1,0},{2,3},{3,2},{4,5},{5,4},{6,7},{7,6},{8,9},{9,8},{10,11... | collective-permute-start | bytes 1572872 | tf_op jit(solution)/shard_map/ppermute | solution.py:80
  542.0 1.3 collective-permute-start.13
  543.4 41.1 %collective-permute-start.15 = (bf16[256,1024]{1,0:T(8,128)(2,1)S(1)}, bf16[256,1024]{1,0:T(8,128)(2,1)S(1)}, u32[]{:S(2)}, u32[]{:S(2)}) collective-permute-start(bf16[256,1024]{1,0:T(8,128)(2,1)S(1)} %pad_maximum_fusion.6), channel_id=1, source_target_pairs={{0,2},{2,0},{4,6},{6,4},{8,10},{10,8},{12,14},{14,12},{16,18},{18,... | collective-permute-start | bytes 1572872 | tf_op jit(solution)/shard_map/ppermute | solution.py:80
  552.2 32.4 %collective-permute-start.7 = (bf16[256,1024]{1,0:T(8,128)(2,1)S(1)}, bf16[256,1024]{1,0:T(8,128)(2,1)S(1)}, u32[]{:S(2)}, u32[]{:S(2)}) collective-permute-start(bf16[256,1024]{1,0:T(8,128)(2,1)S(1)} %pad_maximum_fusion.5), channel_id=1, source_target_pairs={{0,2},{2,0},{4,6},{6,4},{8,10},{10,8},{12,14},{14,12},{16,18},{18,... | collective-permute-start | bytes 1572872 | tf_op jit(solution)/shard_map/ppermute | solution.py:80
  552.2 32.9 %collective-permute-start.31 = (bf16[256,1024]{1,0:T(8,128)(2,1)S(1)}, bf16[256,1024]{1,0:T(8,128)(2,1)S(1)}, u32[]{:S(2)}, u32[]{:S(2)}) collective-permute-start(bf16[256,1024]{1,0:T(8,128)(2,1)S(1)} %pad_maximum_fusion.8), channel_id=1, source_target_pairs={{0,2},{2,0},{4,6},{6,4},{8,10},{10,8},{12,14},{14,12},{16,18},{18,... | collective-permute-start | bytes 1572872 | tf_op jit(solution)/shard_map/ppermute | solution.py:80
  552.9 32.3 %copy-start.17 = (bf16[128,1024]{1,0:T(8,128)(2,1)S(1)}, bf16[128,1024]{1,0:T(8,128)(2,1)}, u32[]{:S(2)}) copy-start(bf16[128,1024]{1,0:T(8,128)(2,1)} %copy-done.16) | copy-start | bytes 786436
  552.9 32.3 %copy-start.19 = (bf16[128,1024]{1,0:T(8,128)(2,1)S(1)}, bf16[128,1024]{1,0:T(8,128)(2,1)}, u32[]{:S(2)}) copy-start(bf16[128,1024]{1,0:T(8,128)(2,1)} %copy-done.18) | copy-start | bytes 786436
  583.7 1.9 collective-permute-start.23
  583.7 21.6 %collective-permute-start.11 = (bf16[256,4096]{1,0:T(8,128)(2,1)S(1)}, bf16[256,4096]{1,0:T(8,128)(2,1)S(1)}, u32[]{:S(2)}, u32[]{:S(2)}) collective-permute-start(bf16[256,4096]{1,0:T(8,128)(2,1)S(1)} %pad_maximum_fusion), channel_id=1, source_target_pairs={{0,2},{2,0},{4,6},{6,4},{8,10},{10,8},{12,14},{14,12},{16,18},{18,... | collective-permute-start | bytes 6291464 | tf_op jit(solution)/shard_map/ppermute | solution.py:80
  584.5 4.9 collective-permute-start.29
  584.6 18.6 %collective-permute-start.27 = (bf16[256,3072]{1,0:T(8,128)(2,1)S(1)}, bf16[256,3072]{1,0:T(8,128)(2,1)S(1)}, u32[]{:S(2)}, u32[]{:S(2)}) collective-permute-start(bf16[256,3072]{1,0:T(8,128)(2,1)S(1)} %pad_maximum_fusion.2), channel_id=1, source_target_pairs={{0,2},{2,0},{4,6},{6,4},{8,10},{10,8},{12,14},{14,12},{16,18},{18,... | collective-permute-start | bytes 4718600 | tf_op jit(solution)/shard_map/ppermute | solution.py:80
  585.1 22.8 %collective-permute-start.35 = (bf16[256,4096]{1,0:T(8,128)(2,1)S(1)}, bf16[256,4096]{1,0:T(8,128)(2,1)S(1)}, u32[]{:S(2)}, u32[]{:S(2)}) collective-permute-start(bf16[256,4096]{1,0:T(8,128)(2,1)S(1)} %pad_maximum_fusion.1), channel_id=1, source_target_pairs={{0,2},{2,0},{4,6},{6,4},{8,10},{10,8},{12,14},{14,12},{16,18},{18,... | collective-permute-start | bytes 6291464 | tf_op jit(solution)/shard_map/ppermute | solution.py:80
  585.6 15.3 %collective-permute-start.19 = (bf16[256,2048]{1,0:T(8,128)(2,1)S(1)}, bf16[256,2048]{1,0:T(8,128)(2,1)S(1)}, u32[]{:S(2)}, u32[]{:S(2)}) collective-permute-start(bf16[256,2048]{1,0:T(8,128)(2,1)S(1)} %pad_maximum_fusion.3), channel_id=1, source_target_pairs={{0,2},{2,0},{4,6},{6,4},{8,10},{10,8},{12,14},{14,12},{16,18},{18,... | collective-permute-start | bytes 3145736 | tf_op jit(solution)/shard_map/ppermute | solution.py:80
  589.4 7.5 collective-permute-start.5
  596.9 3.9 collective-permute-start.17
  600.8 2.2 collective-permute-start.25
  600.9 4.4 collective-permute-start.9
  603.0 4.9 collective-permute-start.33
  (55 other events, 205.7 us)

commit v3 on v2

--- a/solution.py
+++ b/solution.py
@@ -70,14 +70,6 @@
         if k < self.seq_bits:
             return (batch, seq + step * (1 << k))
         return (batch + step * (1 << (k - self.seq_bits)), seq)
-
-    def swap(self, values, k):
-        if k < self.seq_bits:
-            axis, step = ("seq", 1 << k)
-        else:
-            axis, step = ("batch", 1 << (k - self.seq_bits))
-        pairs = [(i, i ^ step) for i in range(lax.axis_size(axis))]
-        return lax.ppermute(values, axis, pairs)
 
 
 def greet(cube, bits):
@@ -232,131 +224,213 @@
     return tuple(out)
 
 
-def reduce_kernel(cube, order, rows, columns, count, places, *refs):
-    parts, out, refs = (refs[:count], refs[count], refs[count + 1 :])
-    stages, number = (len(order), len(places))
-    own, refs = (refs[0], refs[1:])
-    recv_at, refs = (refs[:stages], refs[stages:])
-    send_at, refs = ((None,) + refs[: stages - 1], refs[stages - 1 :])
-    keep_at, refs = ((None,) + refs[: stages - 1], refs[stages - 1 :])
-    send, recv, local = refs
+def gradient_kernel(cube, count, shapes, tile, *refs):
+    lefts, rights, out, refs = (
+        refs[:count],
+        refs[count : 2 * count],
+        refs[2 * count],
+        refs[2 * count + 1 :],
+    )
+    near, far, whole = (refs[:count], refs[count : 2 * count], refs[2 * count : 3 * count])
+    refs = refs[3 * count :]
+    order = cube.y + cube.z[::-1]
+    stages = len(order)
+    total, sent, recv_at, refs = (refs[0], refs[1 : 1 + stages], refs[1 + stages : 1 + 2 * stages], refs[1 + 2 * stages :])
+    x_send, x_recv, local, c_send, c_recv, send, recv = refs
+    rows, columns = tile
+    number, depth = (out.shape[0], total.shape[0])
+    lags = [3 + 2 * stage for stage in range(stages)]
+    x, c = (cube.bit(0), cube.bit(cube.core))
+    dims = sorted(order, reverse=True)
     bits = [cube.bit(k) for k in order]
-    dims = sorted(order, reverse=True)
+    every = (slice(None),) * stages
+    tokens = near[0].shape[-1] // 2
+    own_lanes = pl.ds(pl.multiple_of(x * tokens, tokens), tokens)
 
     def spot(stage, flip):
         left = [k for k in dims if k not in order[:stage]]
-        side = bits[stage]
-        side = 1 - side if flip else side
+        side = 1 - bits[stage] if flip else bits[stage]
         return tuple(side if k == order[stage] else slice(None) for k in left)
 
-    def remote(stage, chunk, source):
-        return pltpu.make_async_remote_copy(
-            src_ref=source,
-            dst_ref=recv_at[stage].at[chunk],
-            send_sem=send.at[stage, chunk],
-            recv_sem=recv.at[stage, chunk],
-            device_id=cube.partner(order[stage]),
-            device_id_type=MESH,
-        )
-
-    greet(cube, order)
-    for chunk, (m, row, column) in enumerate(places):
-        block = (pl.ds(row, rows), pl.ds(column, columns))
-        remote(0, chunk, parts[m].at[spot(0, True) + block]).start()
-        pltpu.make_async_copy(
-            parts[m].at[spot(0, False) + block], own.at[chunk], local.at[chunk]
-        ).start()
-
-    def turn(step, carry):
+    def along_x(m):
+        return [
+            to_partner(
+                cube,
+                0,
+                lefts[m].at[every + (slice(None), 1 - x)],
+                near[m].at[every + (slice(None), slice(None), own_lanes)],
+                x_send.at[m, 0],
+                x_recv.at[m, 0],
+            ),
+            to_partner(
+                cube, 0, rights[m], whole[m].at[c, own_lanes], x_send.at[m, 1], x_recv.at[m, 1]
+            ),
+        ]
+
+    def at_home(m):
+        return [
+            pltpu.make_async_copy(
+                lefts[m].at[every + (slice(None), x)],
+                near[m].at[every + (slice(None), slice(None), own_lanes)],
+                local.at[m, 0],
+            ),
+            pltpu.make_async_copy(rights[m], whole[m].at[c, own_lanes], local.at[m, 1]),
+        ]
+
+    def along_core(m):
+        return [
+            to_partner(
+                cube,
+                cube.core,
+                near[m].at[every + (1 - c,)],
+                far[m],
+                c_send.at[m, 0],
+                c_recv.at[m, 0],
+            ),
+            to_partner(
+                cube, cube.core, whole[m].at[c], whole[m].at[c], c_send.at[m, 1], c_recv.at[m, 1]
+            ),
+        ]
+
+    def remote(stage, chunk):
+        return to_partner(
+            cube,
+            order[stage],
+            sent[stage].at[chunk],
+            recv_at[stage].at[chunk],
+            send.at[stage, chunk],
+            recv.at[stage, chunk],
+        )
+
+    def reduce(step):
         for stage in range(stages):
-            chunk = step - stage
+            chunk = step - lags[stage]
 
             @pl.when((chunk >= 0) & (chunk < number))
-            def _():
-                source = own if stage == 0 else keep_at[stage]
-                if stage == 0:
-                    pltpu.make_async_copy(own.at[chunk], own.at[chunk], local.at[chunk]).wait()
-                remote(stage, chunk, recv_at[stage].at[chunk]).wait_recv()
+            def _(stage=stage, chunk=chunk):
+                slot = lax.rem(chunk, depth)
+                remote(stage, chunk).wait_recv()
+                mine = tuple(
+                    bits[order.index(k)] if k in order[: stage + 1] else slice(None) for k in dims
+                )
                 arrived = recv_at[stage]
                 if stage + 1 == stages:
-                    out[chunk] = source[chunk] + arrived[chunk].astype(jnp.float32)
+                    out[chunk] = total[(slot,) + mine] + arrived[chunk].astype(jnp.float32)
                 else:
                     away, home = (spot(stage + 1, True), spot(stage + 1, False))
-                    send_at[stage + 1][chunk] = (
-                        source[(chunk,) + away].astype(jnp.float32)
+                    full = list(mine)
+                    full[dims.index(order[stage + 1])] = 1 - bits[stage + 1]
+                    sent[stage + 1][chunk] = (
+                        total[(slot,) + tuple(full)]
                         + arrived[(chunk,) + away].astype(jnp.float32)
                     ).astype(jnp.bfloat16)
-                    remote(stage + 1, chunk, send_at[stage + 1].at[chunk]).start()
-                    keep_at[stage + 1][chunk] = source[(chunk,) + home].astype(
-                        jnp.float32
-                    ) + arrived[(chunk,) + home].astype(jnp.float32)
-
+                    remote(stage + 1, chunk).start()
+                    full[dims.index(order[stage + 1])] = bits[stage + 1]
+                    total[(slot,) + tuple(full)] += arrived[(chunk,) + home].astype(jnp.float32)
+
+    greet(cube, range(cube.count))
+    for m in range(count):
+        for copy in along_x(m) + at_home(m):
+            copy.start()
+    first = 0
+    for m in range(count):
+        for copy in at_home(m):
+            copy.wait()
+        for copy in along_x(m):
+            copy.wait_recv()
+        for copy in along_core(m):
+            copy.start()
+        for copy in along_core(m):
+            copy.wait_recv()
+        down, across = shapes[m]
+
+        def one(j, carry, m=m, first=first, down=down, across=across):
+            chunk = first + j
+            slot = lax.rem(chunk, depth)
+            row = pl.ds(pl.multiple_of((j // across) * rows, rows), rows)
+            column = pl.ds(pl.multiple_of(lax.rem(j, across) * columns, columns), columns)
+
+            def half(flip):
+                place = spot(0, flip)
+                one_left = near[m][place + (c, row, slice(None))]
+                two_left = far[m][place + (row, slice(None))]
+                shape = one_left.shape[:-1] + (columns,)
+                one_left = one_left.reshape(-1, 2 * tokens)
+                two_left = two_left.reshape(-1, 2 * tokens)
+                result = matmul(one_left, whole[m][c, :, column]) + matmul(
+                    two_left, whole[m][1 - c, :, column]
+                )
+                return result.reshape(shape)
+
+            sent[0][chunk] = half(True).astype(jnp.bfloat16)
+            remote(0, chunk).start()
+            total[(slot,) + spot(0, False)] = half(False)
+            reduce(chunk)
+            return carry
+
+        lax.fori_loop(0, down * across, one, 0)
+        first += down * across
+
+    def drain(step, carry):
+        reduce(step)
         return carry
 
-    lax.fori_loop(0, number + stages, turn, 0)
+    lax.fori_loop(number, number + lags[-1] + 1, drain, 0)
+    for m in range(count):
+        for copy in along_x(m) + along_core(m):
+            copy.wait_send()
 
     def finish(chunk, carry):
         for stage in range(stages):
-            remote(stage, chunk, recv_at[stage].at[chunk]).wait_send()
+            remote(stage, chunk).wait_send()
         return carry
 
     lax.fori_loop(0, number, finish, 0)
 
 
-def reduce_fast(parts, cube, rows, columns):
+def gradients_fast(pairs, cube, rows, columns):
     order = cube.y + cube.z[::-1]
-    stages, count = (len(order), len(parts))
-    places = []
-    for m, part in enumerate(parts):
-        for row in range(0, part.shape[-2], rows):
-            for column in range(0, part.shape[-1], columns):
-                places.append((m, row, column))
-    number, tile = (len(places), (rows, columns))
-
-    def held(stage, dtype):
-        return pltpu.VMEM((number,) + (2,) * (stages - 1 - stage) + tile, dtype)
-
+    stages, count, tokens = (len(order), len(pairs), pairs[0][0].shape[0])
+    lefts, rights, shapes, near, far, whole = ([], [], [], [], [], [])
+    for left, right in pairs:
+        block = left.shape[1] >> cube.count
+        lead = (2,) * stages
+        lefts.append(left.T.reshape(lead + (2, 2, block, tokens)))
+        rights.append(right)
+        shapes.append((block // rows, right.shape[1] // columns))
+        near.append(pltpu.VMEM(lead + (2, block, 2 * tokens), jnp.bfloat16))
+        far.append(pltpu.VMEM(lead + (block, 2 * tokens), jnp.bfloat16))
+        whole.append(pltpu.VMEM((2, 2 * tokens, right.shape[1]), jnp.bfloat16))
+    number, tile = (sum(down * across for down, across in shapes), (rows, columns))
+    held = [
+        pltpu.VMEM((number,) + (2,) * (stages - 1 - stage) + tile, jnp.bfloat16)
+        for stage in range(stages)
+    ]
+    depth = 3 + 2 * (stages - 1) + 1
     out = pl.pallas_call(
-        functools.partial(reduce_kernel, cube, order, rows, columns, count, places),
+        functools.partial(gradient_kernel, cube, count, shapes, tile),
         out_shape=jax.ShapeDtypeStruct((number,) + tile, jnp.float32),
-        in_specs=[pl.BlockSpec(memory_space=pl.ANY)] * count,
+        in_specs=[pl.BlockSpec(memory_space=pl.ANY)] * (2 * count),
         out_specs=pl.BlockSpec(memory_space=pltpu.VMEM),
-        scratch_shapes=[held(0, jnp.bfloat16)]
-        + [held(stage, jnp.bfloat16) for stage in range(stages)]
-        + [held(stage, jnp.bfloat16) for stage in range(1, stages)]
-        + [held(stage, jnp.float32) for stage in range(1, stages)]
-        + [
-            pltpu.SemaphoreType.DMA((stages, number)),
-            pltpu.SemaphoreType.DMA((stages, number)),
-            pltpu.SemaphoreType.DMA((number,)),
-        ],
+        scratch_shapes=near
+        + far
+        + whole
+        + [pltpu.VMEM((depth,) + (2,) * stages + tile, jnp.float32)]
+        + held
+        + held
+        + [pltpu.SemaphoreType.DMA((count, 2))] * 5
+        + [pltpu.SemaphoreType.DMA((stages, number))] * 2,
         compiler_params=pltpu.CompilerParams(
-            collective_id=4, has_side_effects=True, vmem_limit_bytes=56 * 1024 * 1024
+            collective_id=4, has_side_effects=True, vmem_limit_bytes=60 * 1024 * 1024
         ),
         name="reduce_gradients",
-    )(*parts)
+    )(*lefts, *rights)
     results, at = ([], 0)
-    for part in parts:
-        down, across = (part.shape[-2] // rows, part.shape[-1] // columns)
+    for (down, across), right in zip(shapes, rights):
         piece = out[at : at + down * across].reshape(down, across, rows, columns)
-        results.append(piece.transpose(0, 2, 1, 3).reshape(part.shape[-2], part.shape[-1]))
+        results.append(piece.transpose(0, 2, 1, 3).reshape(down * rows, right.shape[1]))
         at += down * across
     return results
-
-
-def near_sum(left, right, cube):
-    near = cube.seq_bits + 1
-    flipped = left.T
-    rows = flipped.shape[0] >> cube.count
-    flipped = flipped.reshape((-1,) + (2,) * near + (rows, left.shape[0]))
-    for k in range(near):
-        axis = flipped.ndim - 3
-        away = lax.dynamic_index_in_dim(flipped, 1 - cube.bit(k), axis, keepdims=False)
-        home = lax.dynamic_index_in_dim(flipped, cube.bit(k), axis, keepdims=False)
-        flipped = jnp.concatenate([home, cube.swap(away, k)], axis=-1)
-        right = jnp.concatenate([right, cube.swap(right, k)], axis=0)
-    sums = matmul(flipped.reshape(-1, flipped.shape[-1]), right).astype(jnp.bfloat16)
-    return sums.reshape((2,) * (cube.count - near) + (rows, right.shape[1]))
 
 
 def gradient_shards(pairs, cube):
@@ -368,7 +442,7 @@
             shard = lax.psum_scatter(flat, AXES, scatter_dimension=0, tiled=True)
             results.append(shard.reshape(-1, whole.shape[1]))
         return results
-    return reduce_fast([near_sum(left, right, cube) for left, right in pairs], cube, 32, 1024)
+    return gradients_fast(pairs, cube, 32, 1024)
 
 
 def gather_all(shards, cube):
@@ -1038,16 +1112,16 @@
     d_input, grad_one_in, grad_one_out, gain_zero, shift_zero = ffn_backward(
         d_first_res, kept_first, norm_gains[0], gathered[0], gathered[1]
     )
-    two_out, two_in, conv_out, conv_in, attn_out, attn_in, one_out, one_in = gradient_shards(
+    attn_out, conv_out, conv_in, two_out, two_in, one_in, one_out, attn_in = gradient_shards(
         (
+            (context, attn_branch),
+            (conv_swish, conv_branch),
+            (conv_hidden, d_pointwise),
             grad_two_out,
             grad_two_in,
-            (conv_swish, conv_branch),
-            (conv_hidden, d_pointwise),
-            (context, attn_branch),
+            grad_one_in,
+            grad_one_out,
             (attn_hidden, heads_in),
-            grad_one_out,
-            grad_one_in,
         ),
         cube,
     )

time: 776 us -> 639 us (0.82)
  waiting for transfers between devices: 105 us -> 0.01 us
  Pallas kernels: 467 us -> 505 us
  local copies, waits for them, and re-layouts: 65 us -> 39.4 us
  matrix products: 61.6 us -> 40 us
  other arithmetic: 35.3 us -> 25.8 us
    ppermute x32 -> x0, waiting for transfers between devices: 105 us -> none  [swap(): return lax.ppermute(values, axis, pairs)]
    pallas_call x1, Pallas kernels: 144 us -> 183 us  [gradients_fast(): pl.pallas_call(functools.partial(gradient_kernel, cube, count, shapes, ti...]
    dot_general x14 -> x6, matrix products: 40.1 us -> 20.4 us  [matmul(): return jnp.dot(left, right, preferred_element_type=jnp.float32)]
    ppermute x32 -> x0, starting transfers between devices: 19.4 us -> none  [swap(): return lax.ppermute(values, axis, pairs)]
    unnamed x175 -> x139, local copies, waits for them, and re-layouts: 23.1 us -> 8.86 us
    ppermute x2, starting transfers between devices: 6.97 us -> 19.6 us  [padded_2(): before = lax.ppermute(last, axis, up)]
    concatenate x16 -> x0, other arithmetic: 7.89 us -> none  [the longest x8 4.24 us: near_sum(): flipped = jnp.concatenate([home, cube.swap(away, k)], axis=-1)]
  transfers between devices with their start and end apart: 36 -> 4, of which waited for: 9 -> 0; matrix products, arithmetic and copies ran while one was open for 17% -> 2% of each run, Pallas kernels for 10% -> 0%
where the time goes in v3:
time: 639 us; the launch traced here: 635 us
  Pallas kernels  505 us (79%)
  matrix products  40 us (6%)
  local copies, waits for them, and re-layouts  39.4 us (6%)
  other arithmetic  25.8 us (4%)
  starting transfers between devices  22.2 us (3%)
    pallas_call x1, Pallas kernels, gather_fast(): pl.pallas_call(functools.partial(gather_kernel, cube, orders, count, whic...  230 us
    pallas_call x1, Pallas kernels, gradients_fast(): pl.pallas_call(functools.partial(gradient_kernel, cube, count, shapes, ti...  183 us
    pallas_call x3, Pallas kernels, sum_fast(): pl.pallas_call(functools.partial(sum_kernel, cube), out_shape=jax.ShapeDt...  57.5 us
    dot_general x6, matrix products, matmul(): return jnp.dot(left, right, preferred_element_type=jnp.float32)  20.4 us
    dot_general x6, matrix products, transposed_right(): lax.dot_general(left, right, (((1,), (1,)), ((), ())), preferred_element_...  19.6 us
    ppermute x2, starting transfers between devices, padded_2(): before = lax.ppermute(last, axis, up)  19.6 us
    pallas_call x1, Pallas kernels, attend_fast(): pl.pallas_call(functools.partial(attend_kernel, cube, REL_LEFT, REL_RIGHT...  19 us
    pallas_call x1, Pallas kernels, attend_back_fast(): pl.pallas_call(functools.partial(attend_back_kernel, cube, REL_LEFT, REL_...  16.5 us
  transfers between devices with their start and end apart: 4, of which 0 were waited for; matrix products, arithmetic and copies ran while one was open for 2% of the time, Pallas kernels for 0%

profile of v3, /device:TPU:0, one launch (start us, length us, event | category | flops | bytes accessed | tf_op | source)
XLA Modules:
  0.0 635.4 jit_solution(8523306737344378227)
XLA Ops:
  0.7 1.0 fusion.80
  1.6 1.0 fusion.81
  2.6 1.1 convert_reduce_fusion
  3.7 1.2 fusion.28
  4.9 229.5 %gather_weights.1 = (bf16[2,2,2,2,2,32,4096]{6,5,4,3,2,1,0:T(8,128)(2,1)}, bf16[2,2,2,2,2,128,1024]{6,5,4,3,2,1,0:T(8,128)(2,1)}, bf16[2,2,2,2,2,32,1024]{6,5,4,...) custom-call(bf16[32,4096]{1,0:T(8,128)(2,1)} %refs_0_.1, ...), custom_call_target="tpu_custom_call" | custom-call | tf_op jit(solution)/shard_map/gather_weights/pallas_call | solution.py:157
  234.4 6.0 fusion.9
  240.5 1.5 fusion.83
  242.9 19.0 %attend.1 = (f32[128,1024]{1,0:T(8,128)S(1)}, bf16[128,1024]{1,0:T(8,128)(2,1)S(1)}, bf16[3,256,512]{2,1,0:T(8,128)(2,1)S(1)}, f32[4,256,256]{2,1,0:T(8,128)S(1)}) custom-call(bf16[128,1024]{1,0:T(8,128)(2,1)S(1)} %add_convert_fusion.3.refs_0_, f32[128,1024]{1,0:T(8,128)S(1)} %get-tuple-element.140.refs_1_, f32[256,256]{1,0:T(8,128)S(1)} %compare_convert_fusion.refs_2_, ...), custom_call_target="tpu_custom_call" | custom-call | tf_op jit(solution)/shard_map/attend/pallas_call | solution.py:558
  261.9 1.0 copy-done.2
  262.9 0.9 copy-done.4
  264.1 3.0 fusion.67
  267.1 1.0 copy-done.7
  269.6 2.4 collective-permute-start
  272.0 1.3 collective-permute-start.1
  273.3 0.9 fusion.106
  275.1 0.8 copy.58
  275.9 1.8 copy.65
  277.8 2.5 copy.64
  280.3 1.3 multiply_reduce_fusion.13
  282.9 17.7 %sum_over_devices.3 = f32[8,1024]{1,0:T(8,128)} custom-call(f32[8,1024]{1,0:T(8,128)} %reshape.336.value), custom_call_target="tpu_custom_call" | custom-call | tf_op jit(solution)/shard_map/sum_over_devices/pallas_call | solution.py:197
  300.7 0.8 copy.76
  302.6 2.1 multiply_divide_fusion
  305.3 2.5 fusion.84
  308.1 6.0 fusion.8
  314.1 1.4 fusion.85
  315.7 0.9 multiply_reduce_fusion
  316.9 3.0 fusion.refs_12_
  320.0 2.9 fusion.86
  322.9 1.6 multiply_reduce_fusion.1
  324.4 1.3 fusion.72
  325.8 1.8 multiply_reduce_fusion.7
  328.2 14.7 %sum_over_devices.4 = f32[8,1024]{1,0:T(8,128)} custom-call(f32[8,1024]{1,0:T(8,128)} %reshape.342.value), custom_call_target="tpu_custom_call" | custom-call | tf_op jit(solution)/shard_map/sum_over_devices/pallas_call | solution.py:197
  342.9 0.8 fusion.79
  343.8 3.2 fusion.48
  348.3 1.3 collective-permute-start.2
  349.6 17.2 %collective-permute-start.3 = (bf16[2,1024]{1,0:T(2,128)(2,1)}, bf16[2,1024]{1,0:T(2,128)(2,1)}, u32[]{:S(2)}, u32[]{:S(2)}) collective-permute-start(bf16[2,1024]{1,0:T(2,128)(2,1)} %get-tuple-element.111), channel_id=1, source_target_pairs={{0,1},{2,3},{4,5},{6,7},{8,9},{10,11},{12,13},{14,15},{16,17},{18,... | collective-permute-start | bytes 12296 | tf_op jit(solution)/shard_map/ppermute | solution.py:30
  366.8 1.2 fusion.107
  368.0 0.8 stack.71
  368.8 0.8 copy.59
  369.7 1.8 copy.62
  371.5 2.3 copy.61
  373.8 2.4 multiply_convert_fusion.6
  376.5 3.8 fusion.65
  380.3 1.0 multiply_reduce_fusion.2
  381.8 16.5 %attend_back.1 = (f32[128,1024]{1,0:T(8,128)S(1)}, bf16[128,3072]{1,0:T(8,128)(2,1)S(1)}, f32[128,128]{1,0:T(8,128)S(1)}) custom-call(bf16[128,1024]{1,0:T(8,128)(2,1)S(1)} %get-tuple-element.90.refs_0_.refs_8_, bf16[3,256,512]{2,1,0:T(8,128)(2,1)S(1)} %copy-done.5, f32[4,256,256]{2,1,0:T(8,128)S(1)} %copy-done.3, bf16[128,128]{1,0:T(8,128)(2,1)S(1)} %pad.16.refs_3_, ...), custom_call_target="tpu_custom_call" | custom-call | tf_op jit(solution)/shard_map/attend_back/pallas_call | solution.py:688
  399.0 5.3 fusion.1.refs_13_
  404.4 2.9 fusion.87
  407.4 1.0 fusion.27
  409.2 25.0 %sum_over_devices.5 = f32[32,1024]{1,0:T(8,128)} custom-call(f32[32,1024]{1,0:T(8,128)} %reshape.363.value), custom_call_target="tpu_custom_call" | custom-call | tf_op jit(solution)/shard_map/sum_over_devices/pallas_call | solution.py:197
  434.2 0.9 slice.260
  435.1 1.6 fusion.78
  436.7 0.8 pad_maximum_fusion.refs_10_
  437.5 0.8 copy.63
  438.4 0.8 copy.60
  439.2 182.8 %reduce_gradients.1 = f32[23,32,1024]{2,1,0:T(8,128)} custom-call(bf16[2,2,2,2,2,32,128]{6,5,4,3,2,1,0:T(8,128)(2,1)} %bitcast.177, bf16[2,2,2,2,2,32,128]{6,5,4,3,2,1,0:T(8,128)(2,1)} %bitcast.179, bf16[2,2,2,2,2,32,128]{6,5,4,3,2,1,0:T(8,128)(2,1)} %bitcast.182, bf16[2,2,2,2,2,128,128]{6,5,4,3,2,1,0:T(8,128)(2,1)} %bitcast.172, ...), custom_call_target="tpu_custom_call" | custom-call | tf_op jit(solution)/shard_map/reduce_gradients/pallas_call | solution.py:410
  622.0 2.7 fusion.74
  624.7 1.0 slice_bitcast_fusion.2
  625.7 1.0 slice_bitcast_fusion.3
  626.7 1.7 slice_bitcast_fusion.4
  629.4 1.1 copy.71
  630.8 1.1 copy.74
  632.4 0.8 fusion.75
  633.4 0.8 copy.73
  634.2 1.0 fusion.26
  (204 shorter events, 12.9 us)
Async XLA Ops:
  0.7 233.8 %copy-start.10 = (bf16[128,1024]{1,0:T(8,128)(2,1)S(1)}, bf16[128,1024]{1,0:T(8,128)(2,1)}, u32[]{:S(2)}) copy-start(bf16[128,1024]{1,0:T(8,128)(2,1)} %param.19) | copy-start | bytes 786436
  3.7 236.8 %copy-start.48 = (f32[128]{0:T(128)}, f32[128]{0:T(128)S(1)}, u32[]{:S(2)}) copy-start(f32[128]{0:T(128)S(1)} %broadcast_multiply_fusion.14) | copy-start | bytes 1540
  4.9 235.6 %copy-start.53 = (f32[128]{0:T(128)}, f32[128]{0:T(128)S(1)}, u32[]{:S(2)}) copy-start(f32[128]{0:T(128)S(1)} %add_rsqrt_fusion.5) | copy-start | bytes 1540
  234.4 6.1 copy-start.55
  240.5 1.7 copy-start.57
  240.5 2.1 copy-start.27
  240.5 2.4 copy-start
  242.0 31.3 %copy-start.36 = (f32[128]{0:T(128)}, f32[128]{0:T(128)S(1)}, u32[]{:S(2)}) copy-start(f32[128]{0:T(128)S(1)} %broadcast_multiply_fusion.13) | copy-start | bytes 1540
  242.2 31.1 %copy-start.44 = (f32[128]{0:T(128)}, f32[128]{0:T(128)S(1)}, u32[]{:S(2)}) copy-start(f32[128]{0:T(128)S(1)} %add_rsqrt_fusion.4) | copy-start | bytes 1540
  263.9 3.2 copy-start.46
  264.1 3.0 copy-start.50
  268.1 6.3 copy-start.26
  269.6 10.7 %collective-permute-start = (bf16[2,1024]{1,0:T(2,128)(2,1)}, bf16[2,1024]{1,0:T(2,128)(2,1)S(1)}, u32[]{:S(2)}, u32[]{:S(2)}) collective-permute-start(bf16[2,1024]{1,0:T(2,128)(2,1)} %get-tuple-element.112), channel_id=1, source_target_pairs={{0,1},{2,3},{4,5},{6,7},{8,9},{10,11},{12,13},{14,15},{16,17},{18,... | collective-permute-start | bytes 12296 | tf_op jit(solution)/shard_map/ppermute | solution.py:30
  272.0 8.3 %collective-permute-start.1 = (bf16[2,1024]{1,0:T(2,128)(2,1)S(1)}, bf16[2,1024]{1,0:T(2,128)(2,1)S(1)}, u32[]{:S(2)}, u32[]{:S(2)}) collective-permute-start(bf16[2,1024]{1,0:T(2,128)(2,1)S(1)} %get-tuple-element.113), channel_id=1, source_target_pairs={{1,0},{3,2},{5,4},{7,6},{9,8},{11,10},{13,12},{15,14},{17,16},{19,... | collective-permute-start | bytes 12296 | tf_op jit(solution)/shard_map/ppermute | solution.py:31
  274.4 7.3 %copy-start.38 = (f32[128]{0:T(128)}, f32[128]{0:T(128)S(1)}, u32[]{:S(2)}) copy-start(f32[128]{0:T(128)S(1)} %get-tuple-element.134) | copy-start | bytes 1540
  274.4 7.3 %copy-start.40 = (f32[128]{0:T(128)}, f32[128]{0:T(128)S(1)}, u32[]{:S(2)}) copy-start(f32[128]{0:T(128)S(1)} %get-tuple-element.135) | copy-start | bytes 1540
  274.4 7.3 %copy-start.42 = (f32[128]{0:T(128)}, f32[128]{0:T(128)S(1)}, u32[]{:S(2)}) copy-start(f32[128]{0:T(128)S(1)} %get-tuple-element.136) | copy-start | bytes 1540
  274.4 7.3 %copy-start.43 = (f32[128]{0:T(128)}, f32[128]{0:T(128)S(1)}, u32[]{:S(2)}) copy-start(f32[128]{0:T(128)S(1)} %get-tuple-element.137) | copy-start | bytes 1540
  275.1 29.6 %copy-start.28 = (f32[1024]{0:T(1024)S(1)}, f32[1024]{0:T(1024)}, u32[]{:S(2)}) copy-start(f32[1024]{0:T(1024)} %param.36) | copy-start | bytes 12292
  275.9 4.4 copy-start.15
  305.3 8.7 %slice-start.6 = ((s8[8388608]{0:T(1024)(128)(4,1)}), s8[4194304]{0:T(1024)(128)(4,1)S(1)}, s32[]{:S(2)}) async-start(s8[8388608]{0:T(1024)(128)(4,1)} %bitcast.261), calls=%async_computation.6 | async-start | bytes 8388608
  308.1 6.0 slice-start.7
  314.1 1.6 copy-start.18
  315.7 4.2 slice-start.2
  316.9 3.1 copy-start.22
  316.9 3.1 slice-start.3
  319.9 2.9 copy-start.12
  322.8 2.9 copy-start.9
  322.9 2.9 copy-start.52
  322.9 2.9 copy-start.56
  325.7 1.8 copy-start.21
  325.8 18.0 %copy-start.29 = (f32[1024]{0:T(1024)S(1)}, f32[1024]{0:T(1024)}, u32[]{:S(2)}) copy-start(f32[1024]{0:T(1024)} %mul.676) | copy-start | bytes 12292
  343.8 29.9 %copy-start.30 = (f32[1,1024]{1,0:T(1,128)}, f32[1,1024]{1,0:T(1,128)S(1)}, u32[]{:S(2)}) copy-start(f32[1,1024]{1,0:T(1,128)S(1)} %get-tuple-element.117) | copy-start | bytes 12292
  343.8 29.9 %copy-start.31 = (f32[1,1024]{1,0:T(1,128)}, f32[1,1024]{1,0:T(1,128)S(1)}, u32[]{:S(2)}) copy-start(f32[1,1024]{1,0:T(1,128)S(1)} %get-tuple-element.118) | copy-start | bytes 12292
  347.0 26.7 %copy-start.39 = (f32[128]{0:T(128)S(1)}, f32[128]{0:T(128)}, u32[]{:S(2)}) copy-start(f32[128]{0:T(128)} %copy-done.38) | copy-start | bytes 1540
  347.0 26.7 %copy-start.41 = (f32[128]{0:T(128)S(1)}, f32[128]{0:T(128)}, u32[]{:S(2)}) copy-start(f32[128]{0:T(128)} %copy-done.40) | copy-start | bytes 1540
  348.3 25.4 %collective-permute-start.2 = (bf16[2,1024]{1,0:T(2,128)(2,1)}, bf16[2,1024]{1,0:T(2,128)(2,1)}, u32[]{:S(2)}, u32[]{:S(2)}) collective-permute-start(bf16[2,1024]{1,0:T(2,128)(2,1)} %get-tuple-element.110), channel_id=1, source_target_pairs={{1,0},{3,2},{5,4},{7,6},{9,8},{11,10},{13,12},{15,14},{17,16},{19,... | collective-permute-start | bytes 12296 | tf_op jit(solution)/shard_map/ppermute | solution.py:31
  349.6 24.1 %collective-permute-start.3 = (bf16[2,1024]{1,0:T(2,128)(2,1)}, bf16[2,1024]{1,0:T(2,128)(2,1)}, u32[]{:S(2)}, u32[]{:S(2)}) collective-permute-start(bf16[2,1024]{1,0:T(2,128)(2,1)} %get-tuple-element.111), channel_id=1, source_target_pairs={{0,1},{2,3},{4,5},{6,7},{8,9},{10,11},{12,13},{14,15},{16,17},{18,... | collective-permute-start | bytes 12296 | tf_op jit(solution)/shard_map/ppermute | solution.py:30
  373.7 2.5 copy-start.8
  376.4 3.8 copy-start.16
  376.4 3.8 copy-start.47
  376.4 3.8 copy-start.51
  376.4 4.8 copy-start.19
  380.3 1.5 copy-start.5
  381.3 17.7 %slice-start.4 = ((s8[8388608]{0:T(1024)(128)(4,1)}), s8[4194304]{0:T(1024)(128)(4,1)S(1)}, s32[]{:S(2)}) async-start(s8[8388608]{0:T(1024)(128)(4,1)} %bitcast.258), calls=%async_computation.4 | async-start | bytes 8388608
  381.5 16.8 %copy-start.1 = (bf16[128,1024]{1,0:T(8,128)(2,1)}, bf16[128,1024]{1,0:T(8,128)(2,1)S(1)}, u32[]{:S(2)}) copy-start(bf16[128,1024]{1,0:T(8,128)(2,1)S(1)} %get-tuple-element.90.refs_0_.refs_8_) | copy-start | bytes 786436
  381.8 16.5 %copy-start.37 = (f32[128]{0:T(128)S(1)}, f32[128]{0:T(128)}, u32[]{:S(2)}) copy-start(f32[128]{0:T(128)} %copy-done.36) | copy-start | bytes 1540
  381.8 16.5 %copy-start.45 = (f32[128]{0:T(128)S(1)}, f32[128]{0:T(128)}, u32[]{:S(2)}) copy-start(f32[128]{0:T(128)} %copy-done.44) | copy-start | bytes 1540
  381.8 17.1 %slice-start.5 = ((s8[8388608]{0:T(1024)(128)(4,1)}), s8[4194304]{0:T(1024)(128)(4,1)S(1)}, s32[]{:S(2)}) async-start(s8[8388608]{0:T(1024)(128)(4,1)} %bitcast.258), calls=%async_computation.5 | async-start | bytes 8388608
  398.3 5.9 copy-start.6
  398.4 5.9 slice-start
  398.9 5.4 copy-start.25
  399.0 5.3 slice-start.1
  404.3 3.0 copy-start.13
  404.3 3.0 copy-start.11
  404.3 3.0 copy-start.49
  404.4 3.0 copy-start.54
  404.4 4.0 copy-start.33
  404.4 4.0 copy-start.35
  404.4 4.0 copy-start.32
  404.4 4.0 copy-start.34
  407.3 29.4 %copy-start.17 = (bf16[128,1024]{1,0:T(8,128)(2,1)S(1)}, bf16[128,1024]{1,0:T(8,128)(2,1)}, u32[]{:S(2)}) copy-start(bf16[128,1024]{1,0:T(8,128)(2,1)} %copy-done.16) | copy-start | bytes 786436
  407.3 31.0 %copy-start.23 = (bf16[1024,128]{0,1:T(8,128)(2,1)S(1)}, bf16[1024,128]{0,1:T(8,128)(2,1)}, u32[]{:S(2)}) copy-start(bf16[1024,128]{0,1:T(8,128)(2,1)} %get-tuple-element.104) | copy-start | bytes 786436
  408.3 29.2 %copy-start.24 = (bf16[1024,128]{0,1:T(8,128)(2,1)S(1)}, bf16[1024,128]{0,1:T(8,128)(2,1)}, u32[]{:S(2)}) copy-start(bf16[1024,128]{0,1:T(8,128)(2,1)} %get-tuple-element.109) | copy-start | bytes 786436
  (7 other events, 7.1 us)

commit v4 on v3

--- a/solution.py
+++ b/solution.py
@@ -79,53 +79,61 @@
     pl.semaphore_wait(barrier, len(bits))
 
 
-def gather_kernel(cube, orders, count, which, cuts, *refs):
+def gather_kernel(cube, plans, items, *refs):
+    count = len(plans)
     shards, outs = (refs[:count], refs[count : 2 * count])
     send, recv, local = refs[2 * count :]
-    bits = range(cube.count)
-    own = [cube.bit(k) for k in bits]
+    own = [cube.bit(k) for k in range(cube.count)]
     kept = []
-    for m in range(count):
+    for m, (bits, paired) in enumerate(plans):
         kept.append(
-            pltpu.make_async_copy(shards[m], outs[m].at[tuple(own[::-1])], local.at[m])
+            pltpu.make_async_copy(
+                shards[m].at[own[0]] if paired else shards[m],
+                outs[m].at[tuple(own[k] for k in bits)],
+                local.at[m],
+            )
         )
         kept[m].start()
-    greet(cube, bits)
-    lanes = len(orders)
-
-    def copy(chunk, lane, stage):
-        m, order = (which[chunk], orders[lane])
-        row, rows, column, columns = cuts[chunk][lane]
-        block = (pl.ds(row, rows), pl.ds(column, columns))
-        lead = tuple(slice(None) if k in order[:stage] else own[k] for k in reversed(bits))
+    greet(cube, range(cube.count))
+
+    def copy(number, stage):
+        m, order, block = flat[number]
+        bits, paired = plans[m]
+        lead = tuple(slice(None) if k in order[:stage] else own[k] for k in bits)
         place = outs[m].at[lead + block]
-        return pltpu.make_async_remote_copy(
-            src_ref=shards[m].at[block] if stage == 0 else place,
-            dst_ref=place,
-            send_sem=send.at[chunk * lanes + lane, stage],
-            recv_sem=recv.at[chunk * lanes + lane, stage],
-            device_id=cube.partner(order[stage]),
-            device_id_type=MESH,
-        )
-
-    for chunk in range(len(cuts)):
-        for lane in range(lanes):
-            copy(chunk, lane, 0).start()
+        source = place
+        if stage == 0:
+            source = shards[m].at[(1 - own[0],) + block] if paired else shards[m].at[block]
+        return to_partner(
+            cube, order[stage], source, place, send.at[number, stage], recv.at[number, stage]
+        )
+
+    flat = [item for chunk in items for item in chunk]
+    numbers, at = ([], 0)
+    for chunk in items:
+        numbers.append(range(at, at + len(chunk)))
+        at += len(chunk)
+    for number in range(len(flat)):
+        copy(number, 0).start()
     for one in kept:
         one.wait()
-    stages = cube.count
-    for turn in range(len(cuts) + stages):
-        for stage in range(stages):
-            chunk = turn - stage - (stage == stages - 1)
-            if 0 <= chunk < len(cuts):
-                for lane in range(lanes):
-                    copy(chunk, lane, stage).wait_recv()
+    most = max(len(order) for _, order, _ in flat)
+    for turn in range(len(items) + most):
+        for stage in range(most):
+            for late in (0, 1):
+                chunk = turn - stage - late
+                if not 0 <= chunk < len(items):
+                    continue
+                for number in numbers[chunk]:
+                    stages = len(flat[number][1])
+                    if stage >= stages or late != (stage == stages - 1):
+                        continue
+                    copy(number, stage).wait_recv()
                     if stage + 1 < stages:
-                        copy(chunk, lane, stage + 1).start()
-    for chunk in range(len(cuts)):
-        for lane in range(lanes):
-            for stage in range(stages):
-                copy(chunk, lane, stage).wait_send()
+                        copy(number, stage + 1).start()
+    for number, (_, order, _) in enumerate(flat):
+        for stage in range(len(order)):
+            copy(number, stage).wait_send()
 
 
 def column_parts(width, shares):
@@ -137,39 +145,46 @@
     return parts
 
 
-def gather_fast(shards, cube):
-    core = [cube.core]
-    orders = [
-        cube.z + cube.y + cube.x + core,
-        cube.z + cube.x + cube.y + core,
-        cube.x + cube.y + cube.z + core,
-    ]
-    which, cuts = ([], [])
-    for m, shard in enumerate(shards):
-        rows, columns = (min(64, shard.shape[0]), min(2048, shard.shape[1]))
-        for row in range(0, shard.shape[0], rows):
-            for column in range(0, shard.shape[1], columns):
-                which.append(m)
-                cuts.append(
-                    [(row, rows, column + a, w) for a, w in column_parts(columns, (3, 3, 2))]
+def gather_fast(shards, kinds, cube):
+    core, x, y, z = ([cube.core], cube.x, cube.y, cube.z)
+    every = list(range(cube.count))[::-1]
+    plans, items, shapes = ([], [], [])
+    for m, (shard, kind) in enumerate(zip(shards, kinds)):
+        if kind == "all":
+            bits, shares = (every, (3, 3, 2))
+            orders = [z + y + x + core, z + x + y + core, x + y + z + core]
+        else:
+            bits = every if kind == "pair" else every[:-1]
+            first = x if kind == "pair" else []
+            orders, shares = ([first + z + y + core, first + y + z + core], (7, 1))
+        plans.append((bits, kind == "pair"))
+        shapes.append((2,) * len(bits) + shard.shape[-2:])
+        rows, columns = (min(64, shard.shape[-2]), min(2048, shard.shape[-1]))
+        for row in range(0, shard.shape[-2], rows):
+            for column in range(0, shard.shape[-1], columns):
+                items.append(
+                    [
+                        (m, order, (pl.ds(row, rows), pl.ds(column + a, w)))
+                        for order, (a, w) in zip(orders, column_parts(columns, shares))
+                    ]
                 )
-    count, items = (len(shards), len(cuts) * len(orders))
+    count, copies = (len(shards), sum(len(chunk) for chunk in items))
     outs = pl.pallas_call(
-        functools.partial(gather_kernel, cube, orders, count, which, cuts),
+        functools.partial(gather_kernel, cube, plans, items),
         out_shape=[
-            jax.ShapeDtypeStruct((2,) * cube.count + shard.shape, shard.dtype) for shard in shards
+            jax.ShapeDtypeStruct(shape, shard.dtype) for shape, shard in zip(shapes, shards)
         ],
         in_specs=[pl.BlockSpec(memory_space=pl.ANY)] * count,
         out_specs=[pl.BlockSpec(memory_space=pl.ANY)] * count,
         scratch_shapes=[
-            pltpu.SemaphoreType.DMA((items, cube.count)),
-            pltpu.SemaphoreType.DMA((items, cube.count)),
+            pltpu.SemaphoreType.DMA((copies, cube.count)),
+            pltpu.SemaphoreType.DMA((copies, cube.count)),
             pltpu.SemaphoreType.DMA((count,)),
         ],
         compiler_params=pltpu.CompilerParams(collective_id=0, has_side_effects=True),
         name="gather_weights",
     )(*shards)
-    return tuple(out.reshape(-1, shard.shape[1]) for out, shard in zip(outs, shards))
+    return tuple(out.reshape(-1, shard.shape[-1]) for out, shard in zip(outs, shards))
 
 
 def sum_kernel(cube, value, out, held, sent, send, recv):
@@ -213,30 +228,20 @@
 def sum_everywhere(values, cube, number):
     if cube is None:
         return lax.psum(values, AXES)
-    flat = jnp.concatenate([value.reshape(-1) for value in values])
-    size = -(-flat.shape[0] // 8192) * 8192
-    flat = jnp.pad(flat, (0, size - flat.shape[0])).reshape(-1, 1024)
-    flat = sum_fast(flat, cube, number).reshape(-1)
-    out, at = ([], 0)
-    for value in values:
-        out.append(flat[at : at + value.size].reshape(value.shape))
-        at += value.size
-    return tuple(out)
-
-
-def gradient_kernel(cube, count, shapes, tile, *refs):
-    lefts, rights, out, refs = (
-        refs[:count],
-        refs[count : 2 * count],
-        refs[2 * count],
-        refs[2 * count + 1 :],
-    )
+    return flat_unpack(sum_fast(flat_pack(values), cube, number), values)
+
+
+def gradient_kernel(cube, shapes, kinds, tile, *refs):
+    count = len(shapes)
+    lefts, rights, refs = (refs[:count], refs[count : 2 * count], refs[2 * count :])
+    value, out, crossed, value_out, refs = (refs[0], refs[1], refs[2], refs[3], refs[4:])
     near, far, whole = (refs[:count], refs[count : 2 * count], refs[2 * count : 3 * count])
     refs = refs[3 * count :]
     order = cube.y + cube.z[::-1]
     stages = len(order)
     total, sent, recv_at, refs = (refs[0], refs[1 : 1 + stages], refs[1 + stages : 1 + 2 * stages], refs[1 + 2 * stages :])
-    x_send, x_recv, local, c_send, c_recv, send, recv = refs
+    cross, value_sent, value_held, refs = (refs[0], refs[1], refs[2], refs[3:])
+    x_send, x_recv, local, c_send, c_recv, send, recv, cross_send, cross_recv, v_send, v_recv = refs
     rows, columns = tile
     number, depth = (out.shape[0], total.shape[0])
     lags = [3 + 2 * stage for stage in range(stages)]
@@ -245,6 +250,7 @@
     bits = [cube.bit(k) for k in order]
     every = (slice(None),) * stages
     tokens = near[0].shape[-1] // 2
+    pairs = [m for m in range(count) if kinds[m] == "pair"]
     own_lanes = pl.ds(pl.multiple_of(x * tokens, tokens), tokens)
 
     def spot(stage, flip):
@@ -253,6 +259,8 @@
         return tuple(side if k == order[stage] else slice(None) for k in left)
 
     def along_x(m):
+        if kinds[m] != "all":
+            return []
         return [
             to_partner(
                 cube,
@@ -268,6 +276,11 @@
         ]
 
     def at_home(m):
+        if kinds[m] != "all":
+            return [
+                pltpu.make_async_copy(lefts[m], near[m], local.at[m, 0]),
+                pltpu.make_async_copy(rights[m], whole[m].at[c], local.at[m, 1]),
+            ]
         return [
             pltpu.make_async_copy(
                 lefts[m].at[every + (slice(None), x)],
@@ -328,12 +341,38 @@
                     full[dims.index(order[stage + 1])] = bits[stage + 1]
                     total[(slot,) + tuple(full)] += arrived[(chunk,) + home].astype(jnp.float32)
 
+    def value_copy(k):
+        return to_partner(
+            cube, k, value_sent.at[k], value_held.at[k], v_send.at[k], v_recv.at[k]
+        )
+
+    def value_turn(k):
+        if k == 0:
+            value_sent[0] = value[...]
+        elif k <= cube.count:
+            value_copy(k - 1).wait_recv()
+            sum_here = value_sent[k - 1] + value_held[k - 1]
+            if k < cube.count:
+                value_sent[k] = sum_here
+            else:
+                value_out[...] = sum_here
+        if k < cube.count:
+            value_copy(k).start()
+
+    def cross_copy(i, first):
+        away = pl.ds(first + (1 - x) * 2, 2)
+        return to_partner(cube, 0, out.at[away], cross.at[i], cross_send.at[i], cross_recv.at[i])
+
     greet(cube, range(cube.count))
+    value_turn(0)
     for m in range(count):
         for copy in along_x(m) + at_home(m):
             copy.start()
-    first = 0
+    first, firsts = (0, {})
     for m in range(count):
+        firsts[m] = first
+        if m > 0:
+            value_turn(m)
         for copy in at_home(m):
             copy.wait()
         for copy in along_x(m):
@@ -375,7 +414,18 @@
         reduce(step)
         return carry
 
+    for k in range(count, cube.count + 1):
+        value_turn(k)
+    for i, m in enumerate(pairs):
+        cross_copy(i, firsts[m]).start()
     lax.fori_loop(number, number + lags[-1] + 1, drain, 0)
+    for i, m in enumerate(pairs):
+        cross_copy(i, firsts[m]).wait_recv()
+        crossed[i, x] = out[pl.ds(firsts[m] + x * 2, 2)]
+        crossed[i, 1 - x] = cross[i]
+        cross_copy(i, firsts[m]).wait_send()
+    for k in range(cube.count):
+        value_copy(k).wait_send()
     for m in range(count):
         for copy in along_x(m) + along_core(m):
             copy.wait_send()
@@ -388,14 +438,18 @@
     lax.fori_loop(0, number, finish, 0)
 
 
-def gradients_fast(pairs, cube, rows, columns):
+def gradients_fast(pairs, kinds, value, cube, rows, columns):
     order = cube.y + cube.z[::-1]
-    stages, count, tokens = (len(order), len(pairs), pairs[0][0].shape[0])
+    stages, count = (len(order), len(pairs))
     lefts, rights, shapes, near, far, whole = ([], [], [], [], [], [])
-    for left, right in pairs:
-        block = left.shape[1] >> cube.count
+    for (left, right), kind in zip(pairs, kinds):
         lead = (2,) * stages
-        lefts.append(left.T.reshape(lead + (2, 2, block, tokens)))
+        if kind == "all":
+            block, tokens = (left.shape[1] >> cube.count, left.shape[0])
+            lefts.append(left.T.reshape(lead + (2, 2, block, tokens)))
+        else:
+            block, tokens = (left.shape[1] >> (cube.count - 1), left.shape[0] // 2)
+            lefts.append(left.T.reshape(lead + (2, block, 2 * tokens)))
         rights.append(right)
         shapes.append((block // rows, right.shape[1] // columns))
         near.append(pltpu.VMEM(lead + (2, block, 2 * tokens), jnp.bfloat16))
@@ -407,33 +461,62 @@
         for stage in range(stages)
     ]
     depth = 3 + 2 * (stages - 1) + 1
-    out = pl.pallas_call(
-        functools.partial(gradient_kernel, cube, count, shapes, tile),
-        out_shape=jax.ShapeDtypeStruct((number,) + tile, jnp.float32),
-        in_specs=[pl.BlockSpec(memory_space=pl.ANY)] * (2 * count),
-        out_specs=pl.BlockSpec(memory_space=pltpu.VMEM),
+    paired = kinds.count("pair")
+    vmem = pl.BlockSpec(memory_space=pltpu.VMEM)
+    values = pltpu.VMEM((cube.count,) + value.shape, value.dtype)
+    out, crossed, value = pl.pallas_call(
+        functools.partial(gradient_kernel, cube, shapes, kinds, tile),
+        out_shape=[
+            jax.ShapeDtypeStruct((number,) + tile, jnp.float32),
+            jax.ShapeDtypeStruct((paired, 2, 2) + tile, jnp.float32),
+            jax.ShapeDtypeStruct(value.shape, value.dtype),
+        ],
+        in_specs=[pl.BlockSpec(memory_space=pl.ANY)] * (2 * count) + [vmem],
+        out_specs=[vmem] * 3,
         scratch_shapes=near
         + far
         + whole
         + [pltpu.VMEM((depth,) + (2,) * stages + tile, jnp.float32)]
         + held
         + held
+        + [pltpu.VMEM((paired, 2) + tile, jnp.float32), values, values]
         + [pltpu.SemaphoreType.DMA((count, 2))] * 5
-        + [pltpu.SemaphoreType.DMA((stages, number))] * 2,
+        + [pltpu.SemaphoreType.DMA((stages, number))] * 2
+        + [pltpu.SemaphoreType.DMA((paired,))] * 2
+        + [pltpu.SemaphoreType.DMA((cube.count,))] * 2,
         compiler_params=pltpu.CompilerParams(
             collective_id=4, has_side_effects=True, vmem_limit_bytes=60 * 1024 * 1024
         ),
         name="reduce_gradients",
-    )(*lefts, *rights)
-    results, at = ([], 0)
-    for (down, across), right in zip(shapes, rights):
-        piece = out[at : at + down * across].reshape(down, across, rows, columns)
-        results.append(piece.transpose(0, 2, 1, 3).reshape(down * rows, right.shape[1]))
+    )(*lefts, *rights, value)
+    results, at, pair = ([], 0, 0)
+    for (down, across), right, kind in zip(shapes, rights, kinds):
+        if kind == "pair":
+            piece = crossed[pair].reshape(2, 2, rows, columns // 128, 128)
+            results.append(piece.transpose(2, 1, 3, 0, 4).reshape(rows, 4 * columns))
+            pair += 1
+        else:
+            piece = out[at : at + down * across].reshape(down, across, rows, columns)
+            results.append(piece.transpose(0, 2, 1, 3).reshape(down * rows, right.shape[1]))
         at += down * across
-    return results
-
-
-def gradient_shards(pairs, cube):
+    return results, value
+
+
+def flat_pack(values):
+    flat = jnp.concatenate([value.reshape(-1) for value in values])
+    size = -(-flat.shape[0] // 8192) * 8192
+    return jnp.pad(flat, (0, size - flat.shape[0])).reshape(-1, 1024)
+
+
+def flat_unpack(flat, values):
+    flat, out, at = (flat.reshape(-1), [], 0)
+    for value in values:
+        out.append(flat[at : at + value.size].reshape(value.shape))
+        at += value.size
+    return tuple(out)
+
+
+def gradient_shards(pairs, values, cube):
     if cube is None:
         results = []
         for left, right in pairs:
@@ -441,14 +524,23 @@
             flat = whole.reshape(-1, 128)
             shard = lax.psum_scatter(flat, AXES, scatter_dimension=0, tiled=True)
             results.append(shard.reshape(-1, whole.shape[1]))
-        return results
-    return gradients_fast(pairs, cube, 32, 1024)
+        return results, lax.psum(values, AXES)
+    kinds = ["all"] * 3 + ["half", "pair", "pair", "half", "all"]
+    results, flat = gradients_fast(pairs, kinds, flat_pack(values), cube, 32, 1024)
+    return results, flat_unpack(flat, values)
+
+
+def parities(shard):
+    rows, columns = shard.shape
+    return shard.reshape(rows, columns // 256, 2, 128).transpose(2, 0, 1, 3).reshape(2, rows, -1)
 
 
 def gather_all(shards, cube):
     if cube is None:
         return tuple(lax.all_gather(shard, AXES, axis=0, tiled=True) for shard in shards)
-    return gather_fast(shards, cube)
+    kinds = ("pair", "half") + ("all",) * 6 + ("pair", "half")
+    shards = [parities(shard) if kind == "pair" else shard for shard, kind in zip(shards, kinds)]
+    return gather_fast(shards, kinds, cube)
 
 
 def distance_rows(group, left, right, backwards):
@@ -713,6 +805,158 @@
     )(branch, heads_in, probs, table, *matrices)
 
 
+def ffn_kernel(cube, *refs):
+    hidden, before, weight_in, weight_out = refs[:4]
+    after, act, swish, hidden_out = refs[4:8]
+    into, outof, both, away, arrived, load, send, recv = refs[8:]
+    rows, width = hidden.shape
+    wide = into.shape[1]
+    step = wide // 4
+    own_columns, away_columns, own_rows, away_rows = halves(cube, rows, width // 2)
+    loads = []
+    for q in range(4):
+        part = pl.ds(q * step, step)
+        loads.append(
+            pltpu.make_async_copy(weight_in.at[:, part], into.at[:, part], load.at[q])
+        )
+    loads.append(pltpu.make_async_copy(weight_out, outof, load.at[4]))
+    for one in loads:
+        one.start()
+    both[own_rows, :] = hidden[...]
+    greet(cube, [0])
+    exchange = to_partner(
+        cube, 0, both.at[own_rows], both.at[own_rows], send.at[0], recv.at[0]
+    )
+    exchange.start()
+
+    def activate(q, rows_here):
+        part = pl.ds(q * step, step)
+        value = matmul(both[rows_here, :], into[:, part])
+        act[rows_here, part] = value
+        swish[rows_here, part] = jax.nn.silu(value).astype(jnp.bfloat16)
+
+    for q in range(4):
+        loads[q].wait()
+        activate(q, own_rows)
+    loads[4].wait()
+    exchange.wait_recv()
+    for q in range(4):
+        activate(q, away_rows)
+    half = width // 2
+    back = []
+    for q in range(2):
+        part = pl.ds(q * half, half)
+        away[:, part] = matmul(swish[away_rows, :], outof[:, part]).astype(jnp.bfloat16)
+        back.append(
+            to_partner(
+                cube, 0, away.at[:, part], arrived.at[:, part], send.at[1 + q], recv.at[1 + q]
+            )
+        )
+        back[q].start()
+    hidden_out[...] = both[...]
+    for q in range(2):
+        part = pl.ds(q * half, half)
+        after[:, part] = before[:, part] + 0.5 * matmul(swish[own_rows, :], outof[:, part])
+    for q in range(2):
+        part = pl.ds(q * half, half)
+        back[q].wait_recv()
+        after[:, part] += 0.5 * arrived[:, part].astype(jnp.float32)
+    for one in [exchange] + back:
+        one.wait_send()
+
+
+def ffn_back_kernel(cube, *refs):
+    branch, act, weight_in, weight_out = refs[:4]
+    d_hidden, d_act, branch_out = refs[4:7]
+    into, outof, both, away, arrived, load, send, recv = refs[7:]
+    rows, width = branch.shape
+    wide = into.shape[1]
+    step = wide // 4
+    own_columns, away_columns, own_rows, away_rows = halves(cube, rows, width // 2)
+    loads = []
+    for q in range(4):
+        part = pl.ds(q * step, step)
+        loads.append(
+            pltpu.make_async_copy(weight_out.at[part], outof.at[part], load.at[q])
+        )
+    loads.append(pltpu.make_async_copy(weight_in, into, load.at[4]))
+    for one in loads:
+        one.start()
+    both[own_rows, :] = branch[...]
+    greet(cube, [0])
+    exchange = to_partner(
+        cube, 0, both.at[own_rows], both.at[own_rows], send.at[0], recv.at[0]
+    )
+    exchange.start()
+
+    def deactivate(q, rows_here):
+        part = pl.ds(q * step, step)
+        value = transposed_right(both[rows_here, :], outof[part, :])
+        d_act[rows_here, part] = (value * swish_slope(act[rows_here, part])).astype(jnp.bfloat16)
+
+    for q in range(4):
+        loads[q].wait()
+        deactivate(q, own_rows)
+    loads[4].wait()
+    exchange.wait_recv()
+    for q in range(4):
+        deactivate(q, away_rows)
+    half = width // 2
+    back = []
+    for q in range(2):
+        part = pl.ds(q * half, half)
+        away[:, part] = transposed_right(d_act[away_rows, :], into[part, :]).astype(jnp.bfloat16)
+        back.append(
+            to_partner(
+                cube, 0, away.at[:, part], arrived.at[:, part], send.at[1 + q], recv.at[1 + q]
+            )
+        )
+        back[q].start()
+    branch_out[...] = both[...]
+    for q in range(2):
+        part = pl.ds(q * half, half)
+        d_hidden[:, part] = transposed_right(d_act[own_rows, :], into[part, :])
+    for q in range(2):
+        part = pl.ds(q * half, half)
+        back[q].wait_recv()
+        d_hidden[:, part] += arrived[:, part].astype(jnp.float32)
+    for one in [exchange] + back:
+        one.wait_send()
+
+
+def ffn_fast(cube, first, second, weight_in, weight_out, number, backward):
+    rows, width = first.shape
+    wide = weight_in.shape[1]
+    vmem = pl.BlockSpec(memory_space=pltpu.VMEM)
+    both = jax.ShapeDtypeStruct((2 * rows, width), jnp.bfloat16)
+    result = jax.ShapeDtypeStruct((rows, width), jnp.float32)
+    inner = jax.ShapeDtypeStruct((2 * rows, wide), jnp.bfloat16)
+    if backward:
+        shapes = [result, inner, both]
+    else:
+        shapes = [result, jax.ShapeDtypeStruct((2 * rows, wide), jnp.float32), inner, both]
+    return pl.pallas_call(
+        functools.partial(ffn_back_kernel if backward else ffn_kernel, cube),
+        out_shape=shapes,
+        in_specs=[vmem] * 2 + [pl.BlockSpec(memory_space=pl.ANY)] * 2,
+        out_specs=[vmem] * len(shapes),
+        scratch_shapes=[
+            pltpu.VMEM(weight_in.shape, jnp.bfloat16),
+            pltpu.VMEM(weight_out.shape, jnp.bfloat16),
+            pltpu.VMEM((2 * rows, width), jnp.bfloat16),
+            pltpu.VMEM((rows, width), jnp.bfloat16),
+            pltpu.VMEM((rows, width), jnp.bfloat16),
+            pltpu.SemaphoreType.DMA((5,)),
+            pltpu.SemaphoreType.DMA((3,)),
+            pltpu.SemaphoreType.DMA((3,)),
+        ],
+        compiler_params=pltpu.CompilerParams(
+            collective_id=number, has_side_effects=True, vmem_limit_bytes=48 * 1024 * 1024
+        ),
+        name="ffn_back" if backward else "ffn",
+    )(first, second, weight_in, weight_out)
+
+
 def cube_of(shards, rel_table):
     batch, seq = (lax.axis_size("batch"), lax.axis_size("seq"))
     if seq != 2 or batch < 8 or batch & (batch - 1):
@@ -747,19 +991,30 @@
     return (d_values, jnp.sum(d_out * unit, axis=0), jnp.sum(d_out, axis=0))
 
 
-def ffn_forward(values, gain, shift, weight_in, weight_out):
+def ffn_forward(values, gain, shift, weight_in, weight_out, cube, number):
     normed, unit, inverse = norm_forward(values, gain, shift)
     hidden = normed.astype(jnp.bfloat16)
+    if cube is not None:
+        after, act, swish, hidden = ffn_fast(
+            cube, hidden, values, weight_in, weight_out, number, False
+        )
+        return (after, (hidden, act, swish, unit, inverse))
     act = matmul(hidden, weight_in)
     swish = jax.nn.silu(act).astype(jnp.bfloat16)
     return (values + 0.5 * matmul(swish, weight_out), (hidden, act, swish, unit, inverse))
 
 
-def ffn_backward(d_out, kept, gain, weight_in, weight_out):
+def ffn_backward(d_out, kept, gain, weight_in, weight_out, cube, number):
     hidden, act, swish, unit, inverse = kept
     d_branch = (0.5 * d_out).astype(jnp.bfloat16)
-    d_act = (transposed_right(d_branch, weight_out) * swish_slope(act)).astype(jnp.bfloat16)
-    d_norm, d_gain, d_shift = norm_backward(transposed_right(d_act, weight_in), unit, inverse, gain)
+    if cube is not None:
+        d_hidden, d_act, d_branch = ffn_fast(
+            cube, d_branch, act, weight_in, weight_out, number, True
+        )
+    else:
+        d_act = (transposed_right(d_branch, weight_out) * swish_slope(act)).astype(jnp.bfloat16)
+        d_hidden = transposed_right(d_act, weight_in)
+    d_norm, d_gain, d_shift = norm_backward(d_hidden, unit, inverse, gain)
     return (d_out + d_norm, (hidden, d_act), (swish, d_branch), d_gain, d_shift)
 
 
@@ -939,7 +1194,7 @@
     gathered = gather_all(shards, cube)
     start_values = frames.astype(jnp.float32)
     after_first, kept_first = ffn_forward(
-        start_values, norm_gains[0], norm_biases[0], gathered[0], gathered[1]
+        start_values, norm_gains[0], norm_biases[0], gathered[0], gathered[1], cube, 7
     )
     attn_norm, attn_unit, attn_inverse = norm_forward(after_first, norm_gains[1], norm_biases[1])
     attn_hidden = attn_norm.astype(jnp.bfloat16)
@@ -1017,7 +1272,7 @@
     conv_swish = jax.nn.silu(bn_out).astype(jnp.bfloat16)
     after_conv = after_attn + matmul(conv_swish, gathered[7])
     after_second, kept_second = ffn_forward(
-        after_conv, norm_gains[3], norm_biases[3], gathered[8], gathered[9]
+        after_conv, norm_gains[3], norm_biases[3], gathered[8], gathered[9], cube, 8
     )
     final_norm, final_unit, final_inverse = norm_forward(
         after_second, norm_gains[4], norm_biases[4]
@@ -1028,7 +1283,7 @@
         d_final, final_unit, final_inverse, norm_gains[4]
     )
     d_conv_res, grad_two_in, grad_two_out, gain_three, shift_three = ffn_backward(
-        d_second, kept_second, norm_gains[3], gathered[8], gathered[9]
+        d_second, kept_second, norm_gains[3], gathered[8], gathered[9], cube, 9
     )
     conv_branch = d_conv_res.astype(jnp.bfloat16)
     d_bn_out = transposed_right(conv_branch, gathered[7]) * swish_slope(bn_out)
@@ -1110,9 +1365,12 @@
     )
     d_first_res = d_attn_res + d_attn_norm
     d_input, grad_one_in, grad_one_out, gain_zero, shift_zero = ffn_backward(
-        d_first_res, kept_first, norm_gains[0], gathered[0], gathered[1]
-    )
-    attn_out, conv_out, conv_in, two_out, two_in, one_in, one_out, attn_in = gradient_shards(
+        d_first_res, kept_first, norm_gains[0], gathered[0], gathered[1], cube, 10
+    )
+    gains_local = jnp.stack([gain_zero, gain_one, gain_two, gain_three, gain_four])
+    shifts_local = jnp.stack([shift_zero, shift_one, shift_two, shift_three, shift_four])
+    kernel_local = jnp.stack(kernel_rows)
+    shards, (grad_gains, grad_biases, grad_depth, grad_rel) = gradient_shards(
         (
             (context, attn_branch),
             (conv_swish, conv_branch),
@@ -1123,14 +1381,10 @@
             grad_one_out,
             (attn_hidden, heads_in),
         ),
+        (gains_local, shifts_local, kernel_local, d_table),
         cube,
     )
-    gains_local = jnp.stack([gain_zero, gain_one, gain_two, gain_three, gain_four])
-    shifts_local = jnp.stack([shift_zero, shift_one, shift_two, shift_three, shift_four])
-    kernel_local = jnp.stack(kernel_rows)
-    grad_gains, grad_biases, grad_depth, grad_rel = sum_everywhere(
-        (gains_local, shifts_local, kernel_local, d_table), cube, 3
-    )
+    attn_out, conv_out, conv_in, two_out, two_in, one_in, one_out, attn_in = shards
     return (
         final_norm.astype(jnp.bfloat16),
         d_input.astype(jnp.bfloat16),

time: 639 us -> 599 us (0.937)
  matrix products: 40 us -> 10.7 us
  Pallas kernels: 505 us -> 494 us
  starting transfers between devices: 22.2 us -> 11.7 us
  local copies, waits for them, and re-layouts: 39.4 us -> 47.7 us
    pallas_call x3 -> x2, Pallas kernels: 57.5 us -> 32 us  [sum_fast(): pl.pallas_call(functools.partial(sum_kernel, cube), out_shape=jax.ShapeDt...]
    pallas_call x2 -> x6, Pallas kernels: 412 us -> 429 us  [the longest x1 193 us: gather_fast(): pl.pallas_call(functools.partial(gather_kernel, cube, plans, items), out_...]
    dot_general x6 -> x2, matrix products: 20.4 us -> 5.21 us  [matmul(): return jnp.dot(left, right, preferred_element_type=jnp.float32)]
    dot_general x6 -> x2, matrix products: 19.6 us -> 5.53 us  [transposed_right(): lax.dot_general(left, right, (((1,), (1,)), ((), ())), preferred_element_...]
    ppermute x2, starting transfers between devices: 19.6 us -> 9.08 us  [padded_2(): before = lax.ppermute(last, axis, up)]
    unnamed x139 -> x135, local copies, waits for them, and re-layouts: 8.86 us -> 15.3 us
where the time goes in v4:
time: 599 us; the launch traced here: 590 us
  Pallas kernels  494 us (82%)
  local copies, waits for them, and re-layouts  47.7 us (8%)
  other arithmetic  23 us (4%)
  starting transfers between devices  11.7 us (2%)
  matrix products  10.7 us (2%)
    pallas_call x1, Pallas kernels, gather_fast(): pl.pallas_call(functools.partial(gather_kernel, cube, plans, items), out_...  193 us
    pallas_call x1, Pallas kernels, gradients_fast(): pl.pallas_call(functools.partial(gradient_kernel, cube, shapes, kinds, ti...  174 us
    pallas_call x4, Pallas kernels, ffn_fast(): pl.pallas_call(functools.partial(ffn_back_kernel if backward else ffn_ker...  61.9 us
    pallas_call x2, Pallas kernels, sum_fast(): pl.pallas_call(functools.partial(sum_kernel, cube), out_shape=jax.ShapeDt...  32 us
    pallas_call x1, Pallas kernels, attend_fast(): pl.pallas_call(functools.partial(attend_kernel, cube, REL_LEFT, REL_RIGHT...  16.6 us
    pallas_call x1, Pallas kernels, attend_back_fast(): pl.pallas_call(functools.partial(attend_back_kernel, cube, REL_LEFT, REL_...  16.2 us
    unnamed x135, local copies, waits for them, and re-layouts  15.3 us
  transfers between devices with their start and end apart: 4, of which 0 were waited for; matrix products, arithmetic and copies ran while one was open for 2% of the time, Pallas kernels for 0%

profile of v4, /device:TPU:0, one launch (start us, length us, event | category | flops | bytes accessed | tf_op | source)
XLA Modules:
  0.0 590.0 jit_solution(11154067702225075217)
XLA Ops:
  0.7 1.1 convert_reduce_fusion
  1.8 1.0 convert_element_type.130.refs_1_
  2.8 1.0 fusion.45
  3.8 1.2 multiply_reduce_fusion.18
  5.0 1.0 fusion.46
  5.9 1.1 reshape.332
  7.1 0.8 reshape.333.refs_0_
  8.2 0.8 reshape.335.refs_8_
  9.2 193.2 %gather_weights.1 = (bf16[2,2,2,2,2,32,2048]{6,5,4,3,2,1,0:T(8,128)(2,1)}, bf16[2,2,2,2,128,1024]{5,4,3,2,1,0:T(8,128)(2,1)}, bf16[2,2,2,2,2,32,1024]{6,5,4,3,2,...) custom-call(bf16[2,32,2048]{2,1,0:T(8,128)(2,1)} %reshape.333.refs_0, ...), custom_call_target="tpu_custom_call" | custom-call | tf_op jit(solution)/shard_map/gather_weights/pallas_call | solution.py:172
  202.5 17.8 %ffn.2 = (f32[128,1024]{1,0:T(8,128)S(1)}, f32[256,2048]{1,0:T(8,128)S(1)}, bf16[256,2048]{1,0:T(8,128)(2,1)S(1)}, bf16[256,1024]{1,0:T(8,128)(2,1)S(1)}) custom-call(bf16[128,1024]{1,0:T(8,128)(2,1)S(1)} %add_convert_fusion.5.refs_0_, f32[128,1024]{1,0:T(8,128)S(1)} %convert_element_type.130.refs_1_, bf16[1024,2048]{1,0:T(8,128)(2,1)} %bitcast.133, ...), custom_call_target="tpu_custom_call" | custom-call | tf_op jit(solution)/shard_map/ffn/pallas_call | solution.py:938
  220.3 1.3 copy-done.3
  221.6 1.0 copy-done.11
  222.6 0.8 copy-done.20
  225.0 16.6 %attend.1 = (f32[128,1024]{1,0:T(8,128)S(1)}, bf16[128,1024]{1,0:T(8,128)(2,1)S(1)}, bf16[3,256,512]{2,1,0:T(8,128)(2,1)S(1)}, f32[4,256,256]{2,1,0:T(8,128)S(1)}) custom-call(bf16[128,1024]{1,0:T(8,128)(2,1)S(1)} %add_convert_fusion.4.refs_0_, f32[128,1024]{1,0:T(8,128)S(1)} %get-tuple-element.55.refs_1_, f32[256,256]{1,0:T(8,128)S(1)} %compare_convert_fusion.refs_2_, ...), custom_call_target="tpu_custom_call" | custom-call | tf_op jit(solution)/shard_map/attend/pallas_call | solution.py:650
  241.6 1.0 copy-done.7
  242.7 0.9 copy-done.13
  243.9 3.0 fusion.33
  246.9 1.0 copy-done.22
  248.6 3.4 collective-permute-start
  252.0 1.3 collective-permute-start.1
  254.5 0.8 copy.66
  255.3 0.9 copy.73
  256.2 1.5 copy.72
  257.6 1.0 copy.71
  260.5 16.8 %sum_over_devices.2 = f32[8,1024]{1,0:T(8,128)} custom-call(f32[8,1024]{1,0:T(8,128)} %reshape.346.value), custom_call_target="tpu_custom_call" | custom-call | tf_op jit(solution)/shard_map/sum_over_devices/pallas_call | solution.py:212
  279.3 2.1 multiply_divide_fusion
  281.4 2.2 fusion.48
  284.1 12.4 %ffn.3 = (f32[128,1024]{1,0:T(8,128)S(1)}, f32[256,2048]{1,0:T(8,128)S(1)}, bf16[256,2048]{1,0:T(8,128)(2,1)S(1)}, bf16[256,1024]{1,0:T(8,128)(2,1)S(1)}) custom-call(bf16[128,1024]{1,0:T(8,128)(2,1)S(1)} %add_convert_fusion.2.refs_0_, f32[128,1024]{1,0:T(8,128)S(1)} %get-tuple-element.172.refs_1_, bf16[1024,2048]{1,0:T(8,128)(2,1)} %bitcast.137, ...), custom_call_target="tpu_custom_call" | custom-call | tf_op jit(solution)/shard_map/ffn/pallas_call | solution.py:938
  296.5 1.3 copy-done.5
  297.8 0.8 copy-done.18
  298.9 1.4 multiply_reduce_fusion
  300.3 1.2 multiply_convert_fusion.4.refs_0_
  301.6 17.0 %ffn_back.2 = (f32[128,1024]{1,0:T(8,128)S(1)}, bf16[256,2048]{1,0:T(8,128)(2,1)S(1)}, bf16[256,1024]{1,0:T(8,128)(2,1)S(1)}) custom-call(bf16[128,1024]{1,0:T(8,128)(2,1)S(1)} %multiply_convert_fusion.4.refs_0_, f32[256,2048]{1,0:T(8,128)S(1)} %copy-done.6, bf16[1024,2048]{1,0:T(8,128)(2,1)} %bitcast.138, bf16[2048,1024]{1,0:T(8,128)(2,1)} %bitcast.140), custom_call_target="tpu_custom_call" | custom-call | tf_op jit(solution)/shard_map/ffn_back/pallas_call | solution.py:938
  319.4 1.3 fusion.36
  321.2 1.8 multiply_reduce_fusion.9
  323.7 15.2 %sum_over_devices.3 = f32[8,1024]{1,0:T(8,128)} custom-call(f32[8,1024]{1,0:T(8,128)} %reshape.352.value), custom_call_target="tpu_custom_call" | custom-call | tf_op jit(solution)/shard_map/sum_over_devices/pallas_call | solution.py:212
  338.8 0.8 fusion.44
  339.7 2.5 fusion.19
  343.1 1.3 collective-permute-start.2
  344.3 5.7 collective-permute-start.3
  350.1 0.9 fusion.56
  351.0 0.9 copy.67
  351.9 1.3 copy.69
  353.2 1.0 copy.70
  354.2 1.6 multiply_convert_fusion.2
  356.1 3.8 fusion.31
  359.9 0.8 pad_maximum_fusion.refs_10_
  362.1 16.2 %attend_back.1 = (f32[128,1024]{1,0:T(8,128)S(1)}, bf16[128,3072]{1,0:T(8,128)(2,1)S(1)}, f32[128,128]{1,0:T(8,128)S(1)}) custom-call(bf16[128,1024]{1,0:T(8,128)(2,1)S(1)} %get-tuple-element.124.refs_0_.refs_8_, bf16[3,256,512]{2,1,0:T(8,128)(2,1)S(1)} %copy-done.14, f32[4,256,256]{2,1,0:T(8,128)S(1)} %copy-done.8, bf16[128,128]{1,0:T(8,128)(2,1)S(1)} %pad.16.refs_3_, ...), custom_call_target="tpu_custom_call" | custom-call | tf_op jit(solution)/shard_map/attend_back/pallas_call | solution.py:780
  379.2 1.0 copy-done.4
  380.2 14.8 %ffn_back.3 = (f32[128,1024]{1,0:T(8,128)S(1)}, bf16[256,2048]{1,0:T(8,128)(2,1)S(1)}, bf16[256,1024]{1,0:T(8,128)(2,1)S(1)}) custom-call(bf16[128,1024]{1,0:T(8,128)(2,1)S(1)} %get-tuple-element.122.refs_0_, f32[256,2048]{1,0:T(8,128)S(1)} %copy-done.4, bf16[1024,2048]{1,0:T(8,128)(2,1)} %bitcast.134, bf16[2048,1024]{1,0:T(8,128)(2,1)} %bitcast.136), custom_call_target="tpu_custom_call" | custom-call | tf_op jit(solution)/shard_map/ffn_back/pallas_call | solution.py:938
  395.0 1.0 copy-done.10
  396.0 0.8 copy-done.17
  397.9 0.8 copy.68
  398.7 173.9 %reduce_gradients.1 = (f32[23,32,1024]{2,1,0:T(8,128)}, f32[2,2,2,32,1024]{4,3,2,1,0:T(8,128)}, f32[32,1024]{1,0:T(8,128)}) custom-call(bf16[2,2,2,2,2,32,128]{6,5,4,3,2,1,0:T(8,128)(2,1)} %bitcast.157, bf16[2,2,2,2,2,32,128]{6,5,4,3,2,1,0:T(8,128)(2,1)} %bitcast.159, bf16[2,2,2,2,2,32,128]{6,5,4,3,2,1,0:T(8,128)(2,1)} %bitcast.160, ...), custom_call_target="tpu_custom_call" | custom-call | tf_op jit(solution)/shard_map/reduce_gradients/pallas_call | solution.py:467
  572.6 1.1 slice_bitcast_fusion
  573.7 2.3 fusion.38
  576.0 1.7 slice_bitcast_fusion.1
  577.6 1.7 slice_bitcast_fusion.2
  580.0 1.3 fusion.39
  581.8 1.2 reshape.366
  583.5 1.2 reshape.371
  586.0 1.2 copy.76
  587.2 0.8 copy.81
  588.6 1.0 add_convert_fusion
  (205 shorter events, 17.9 us)
Async XLA Ops:
  0.7 8.3 %copy-start.24 = (bf16[128,1024]{1,0:T(8,128)(2,1)S(1)}, bf16[128,1024]{1,0:T(8,128)(2,1)}, u32[]{:S(2)}) copy-start(bf16[128,1024]{1,0:T(8,128)(2,1)} %param.19) | copy-start | bytes 786436
  0.7 7.3 %copy-start.35 = (bf16[32,4096]{1,0:T(8,128)(2,1)S(1)}, bf16[32,4096]{1,0:T(8,128)(2,1)}, u32[]{:S(2)}) copy-start(bf16[32,4096]{1,0:T(8,128)(2,1)} %param.30) | copy-start | bytes 786436
  3.8 198.7 %copy-start.44 = (f32[128]{0:T(128)}, f32[128]{0:T(128)S(1)}, u32[]{:S(2)}) copy-start(f32[128]{0:T(128)S(1)} %broadcast_multiply_fusion.14) | copy-start | bytes 1540
  5.0 197.5 %copy-start.58 = (f32[128]{0:T(128)}, f32[128]{0:T(128)S(1)}, u32[]{:S(2)}) copy-start(f32[128]{0:T(128)S(1)} %add_rsqrt_fusion.5) | copy-start | bytes 1540
  202.5 21.3 %copy-start.64 = (s32[1,4]{1,0:T(1,128)S(1)}, s32[1,4]{1,0:T(1,128)}, u32[]{:S(2)}) copy-start(s32[1,4]{1,0:T(1,128)} %param.20) | copy-start | bytes 52
  202.5 21.7 %copy-start.37 = (bf16[73,128]{1,0:T(8,128)(2,1)S(1)}, bf16[73,128]{1,0:T(8,128)(2,1)}, u32[]{:S(2)}) copy-start(bf16[73,128]{1,0:T(8,128)(2,1)} %param.33) | copy-start | bytes 56068
  220.3 1.3 copy-start.3
  221.6 1.0 copy-start.11
  223.4 1.6 copy-start
  223.5 29.8 %copy-start.42 = (f32[128]{0:T(128)}, f32[128]{0:T(128)S(1)}, u32[]{:S(2)}) copy-start(f32[128]{0:T(128)S(1)} %broadcast_multiply_fusion.13) | copy-start | bytes 1540
  223.7 29.6 %copy-start.54 = (f32[128]{0:T(128)}, f32[128]{0:T(128)S(1)}, u32[]{:S(2)}) copy-start(f32[128]{0:T(128)S(1)} %add_rsqrt_fusion.4) | copy-start | bytes 1540
  241.6 1.0 copy-start.7
  243.7 3.2 copy-start.56
  243.9 4.2 copy-start.60
  243.9 9.8 %copy-start.36 = (bf16[5,1024]{1,0:T(8,128)(2,1)S(1)}, bf16[5,1024]{1,0:T(8,128)(2,1)}, u32[]{:S(2)}) copy-start(bf16[5,1024]{1,0:T(8,128)(2,1)} %param.32) | copy-start | bytes 30724
  246.9 1.0 copy-start.22
  247.9 8.3 %copy-start.12 = (bf16[256,2048]{1,0:T(8,128)(2,1)S(1)}, bf16[256,2048]{1,0:T(8,128)(2,1)}, u32[]{:S(2)}) copy-start(bf16[256,2048]{1,0:T(8,128)(2,1)} %copy-done.11) | copy-start | bytes 3145732
  247.9 9.8 %copy-start.21 = (bf16[256,1024]{1,0:T(8,128)(2,1)S(1)}, bf16[256,1024]{1,0:T(8,128)(2,1)}, u32[]{:S(2)}) copy-start(bf16[256,1024]{1,0:T(8,128)(2,1)} %copy-done.20) | copy-start | bytes 1572868
  248.6 10.0 %collective-permute-start = (bf16[2,1024]{1,0:T(2,128)(2,1)}, bf16[2,1024]{1,0:T(2,128)(2,1)S(1)}, u32[]{:S(2)}, u32[]{:S(2)}) collective-permute-start(bf16[2,1024]{1,0:T(2,128)(2,1)} %get-tuple-element.144), channel_id=1, source_target_pairs={{0,1},{2,3},{4,5},{6,7},{8,9},{10,11},{12,13},{14,15},{16,17},{18,... | collective-permute-start | bytes 12296 | tf_op jit(solution)/shard_map/ppermute | solution.py:30
  252.0 6.6 %collective-permute-start.1 = (bf16[2,1024]{1,0:T(2,128)(2,1)S(1)}, bf16[2,1024]{1,0:T(2,128)(2,1)S(1)}, u32[]{:S(2)}, u32[]{:S(2)}) collective-permute-start(bf16[2,1024]{1,0:T(2,128)(2,1)S(1)} %get-tuple-element.145), channel_id=1, source_target_pairs={{1,0},{3,2},{5,4},{7,6},{9,8},{11,10},{13,12},{15,14},{17,16},{19,... | collective-permute-start | bytes 12296 | tf_op jit(solution)/shard_map/ppermute | solution.py:31
  253.3 28.1 %copy-start.38 = (f32[1024]{0:T(1024)S(1)}, f32[1024]{0:T(1024)}, u32[]{:S(2)}) copy-start(f32[1024]{0:T(1024)} %param.36) | copy-start | bytes 12292
  253.7 27.7 %copy-start.46 = (f32[128]{0:T(128)}, f32[128]{0:T(128)S(1)}, u32[]{:S(2)}) copy-start(f32[128]{0:T(128)S(1)} %get-tuple-element.166) | copy-start | bytes 1540
  253.7 29.9 %copy-start.48 = (f32[128]{0:T(128)}, f32[128]{0:T(128)S(1)}, u32[]{:S(2)}) copy-start(f32[128]{0:T(128)S(1)} %get-tuple-element.167) | copy-start | bytes 1540
  253.7 29.9 %copy-start.50 = (f32[128]{0:T(128)}, f32[128]{0:T(128)S(1)}, u32[]{:S(2)}) copy-start(f32[128]{0:T(128)S(1)} %get-tuple-element.168) | copy-start | bytes 1540
  253.7 29.9 %copy-start.52 = (f32[128]{0:T(128)}, f32[128]{0:T(128)S(1)}, u32[]{:S(2)}) copy-start(f32[128]{0:T(128)S(1)} %get-tuple-element.169) | copy-start | bytes 1540
  259.2 24.9 %copy-start.26 = (f32[128,1024]{1,0:T(8,128)}, f32[128,1024]{1,0:T(8,128)S(1)}, u32[]{:S(2)}) copy-start(f32[128,1024]{1,0:T(8,128)S(1)} %get-tuple-element.130) | copy-start | bytes 1572868
  296.4 1.3 copy-start.5
  298.7 2.9 copy-start.6
  301.6 17.9 %copy-start.29 = (bf16[128,1024]{1,0:T(8,128)(2,1)S(1)}, bf16[128,1024]{1,0:T(8,128)(2,1)}, u32[]{:S(2)}) copy-start(bf16[128,1024]{1,0:T(8,128)(2,1)} %param.21) | copy-start | bytes 786436
  318.6 4.4 copy-start.9
  318.6 4.4 copy-start.16
  318.6 2.1 copy-start.27
  318.6 2.1 copy-start.62
  318.6 2.6 copy-start.63
  320.7 2.3 copy-start.33
  321.2 18.5 %copy-start.28 = (f32[128,1024]{1,0:T(8,128)S(1)}, f32[128,1024]{1,0:T(8,128)}, u32[]{:S(2)}) copy-start(f32[128,1024]{1,0:T(8,128)} %copy-done.26) | copy-start | bytes 1572868
  323.0 30.1 %copy-start.19 = (bf16[256,1024]{1,0:T(8,128)(2,1)S(1)}, bf16[256,1024]{1,0:T(8,128)(2,1)}, u32[]{:S(2)}) copy-start(bf16[256,1024]{1,0:T(8,128)(2,1)} %copy-done.18) | copy-start | bytes 1572868
  339.7 14.5 %copy-start.39 = (f32[1,1024]{1,0:T(1,128)}, f32[1,1024]{1,0:T(1,128)S(1)}, u32[]{:S(2)}) copy-start(f32[1,1024]{1,0:T(1,128)S(1)} %get-tuple-element.149) | copy-start | bytes 12292
  339.7 14.5 %copy-start.40 = (f32[1,1024]{1,0:T(1,128)}, f32[1,1024]{1,0:T(1,128)S(1)}, u32[]{:S(2)}) copy-start(f32[1,1024]{1,0:T(1,128)S(1)} %get-tuple-element.150) | copy-start | bytes 12292
  342.2 8.7 %copy-start.31 = (bf16[128,1024]{1,0:T(8,128)(2,1)}, bf16[128,1024]{1,0:T(8,128)(2,1)S(1)}, u32[]{:S(2)}) copy-start(bf16[128,1024]{1,0:T(8,128)(2,1)S(1)} %get-tuple-element.121) | copy-start | bytes 786436
  342.2 12.0 %copy-start.47 = (f32[128]{0:T(128)S(1)}, f32[128]{0:T(128)}, u32[]{:S(2)}) copy-start(f32[128]{0:T(128)} %copy-done.46) | copy-start | bytes 1540
  342.4 11.8 %copy-start.49 = (f32[128]{0:T(128)S(1)}, f32[128]{0:T(128)}, u32[]{:S(2)}) copy-start(f32[128]{0:T(128)} %copy-done.48) | copy-start | bytes 1540
  342.4 11.8 %copy-start.51 = (f32[128]{0:T(128)S(1)}, f32[128]{0:T(128)}, u32[]{:S(2)}) copy-start(f32[128]{0:T(128)} %copy-done.50) | copy-start | bytes 1540
  342.4 11.8 %copy-start.53 = (f32[128]{0:T(128)S(1)}, f32[128]{0:T(128)}, u32[]{:S(2)}) copy-start(f32[128]{0:T(128)} %copy-done.52) | copy-start | bytes 1540
  343.1 11.1 %collective-permute-start.2 = (bf16[2,1024]{1,0:T(2,128)(2,1)}, bf16[2,1024]{1,0:T(2,128)(2,1)}, u32[]{:S(2)}, u32[]{:S(2)}) collective-permute-start(bf16[2,1024]{1,0:T(2,128)(2,1)} %get-tuple-element.142), channel_id=1, source_target_pairs={{1,0},{3,2},{5,4},{7,6},{9,8},{11,10},{13,12},{15,14},{17,16},{19,... | collective-permute-start | bytes 12296 | tf_op jit(solution)/shard_map/ppermute | solution.py:31
  344.3 9.8 %collective-permute-start.3 = (bf16[2,1024]{1,0:T(2,128)(2,1)}, bf16[2,1024]{1,0:T(2,128)(2,1)}, u32[]{:S(2)}, u32[]{:S(2)}) collective-permute-start(bf16[2,1024]{1,0:T(2,128)(2,1)} %get-tuple-element.143), channel_id=1, source_target_pairs={{0,1},{2,3},{4,5},{6,7},{8,9},{10,11},{12,13},{14,15},{16,17},{18,... | collective-permute-start | bytes 12296 | tf_op jit(solution)/shard_map/ppermute | solution.py:30
  350.9 3.3 copy-start.32
  353.1 2.7 copy-start.23
  356.1 4.7 copy-start.57
  356.1 4.7 copy-start.61
  356.1 5.0 copy-start.30
  359.9 1.8 copy-start.1
  359.9 2.0 copy-start.8
  359.9 2.2 copy-start.14
  361.3 17.0 %copy-start.2 = (bf16[128,1024]{1,0:T(8,128)(2,1)}, bf16[128,1024]{1,0:T(8,128)(2,1)S(1)}, u32[]{:S(2)}) copy-start(bf16[128,1024]{1,0:T(8,128)(2,1)S(1)} %get-tuple-element.124.refs_0_.refs_8_) | copy-start | bytes 786436
  362.1 16.2 %copy-start.43 = (f32[128]{0:T(128)S(1)}, f32[128]{0:T(128)}, u32[]{:S(2)}) copy-start(f32[128]{0:T(128)} %copy-done.42) | copy-start | bytes 1540
  362.1 16.2 %copy-start.55 = (f32[128]{0:T(128)S(1)}, f32[128]{0:T(128)}, u32[]{:S(2)}) copy-start(f32[128]{0:T(128)} %copy-done.54) | copy-start | bytes 1540
  378.4 1.9 copy-start.4
  380.2 16.5 %copy-start.25 = (bf16[128,1024]{1,0:T(8,128)(2,1)S(1)}, bf16[128,1024]{1,0:T(8,128)(2,1)}, u32[]{:S(2)}) copy-start(bf16[128,1024]{1,0:T(8,128)(2,1)} %param.19) | copy-start | bytes 786436
  380.2 16.5 %copy-start.45 = (f32[128]{0:T(128)S(1)}, f32[128]{0:T(128)}, u32[]{:S(2)}) copy-start(f32[128]{0:T(128)} %copy-done.44) | copy-start | bytes 1540
  380.2 16.5 %copy-start.59 = (f32[128]{0:T(128)S(1)}, f32[128]{0:T(128)}, u32[]{:S(2)}) copy-start(f32[128]{0:T(128)} %copy-done.58) | copy-start | bytes 1540
  380.2 16.8 %copy-start.41 = (f32[1024]{0:T(1024)S(1)}, f32[1024]{0:T(1024)}, u32[]{:S(2)}) copy-start(f32[1024]{0:T(1024)} %get-tuple-element.87) | copy-start | bytes 12292
  395.0 1.0 copy-start.10
  572.6 6.7 %copy-start.34 = (f32[32,1024]{1,0:T(8,128)S(1)}, f32[32,1024]{1,0:T(8,128)}, u32[]{:S(2)}) copy-start(f32[32,1024]{1,0:T(8,128)} %get-tuple-element.86) | copy-start | bytes 393220
  (5 other events, 4.1 us)

commit v5 on v4

--- a/solution.py
+++ b/solution.py
@@ -10,6 +10,10 @@
 
 MESH = pl.DeviceIdType.MESH
 AXES = ("batch", "seq")
+ALL_SHARES = (3, 1, 0)
+ROWS = 64
+HALF_SHARES = (5, 3)
+PAIR_SHARES = (2, 2)
 
 HEADS = 8
 REL_LEFT = 64
@@ -136,12 +140,13 @@
             copy(number, stage).wait_send()
 
 
-def column_parts(width, shares):
-    units, total, at, parts = (width // 128, sum(shares), 0, [])
+def row_parts(rows, shares):
+    units, total, at, upto, parts = (rows // 8, sum(shares), 0, 0, [])
     for share in shares:
-        size = units * share // total
-        parts.append((at * 128, size * 128))
-        at += size
+        upto += share
+        end = (units * upto + total // 2) // total
+        parts.append((at * 8, (end - at) * 8))
+        at = end
     return parts
 
 
@@ -151,21 +156,23 @@
     plans, items, shapes = ([], [], [])
     for m, (shard, kind) in enumerate(zip(shards, kinds)):
         if kind == "all":
-            bits, shares = (every, (3, 3, 2))
+            bits, shares = (every, ALL_SHARES)
             orders = [z + y + x + core, z + x + y + core, x + y + z + core]
         else:
             bits = every if kind == "pair" else every[:-1]
             first = x if kind == "pair" else []
-            orders, shares = ([first + z + y + core, first + y + z + core], (7, 1))
+            orders = [first + z + y + core, first + y + z + core]
+            shares = PAIR_SHARES if kind == "pair" else HALF_SHARES
         plans.append((bits, kind == "pair"))
         shapes.append((2,) * len(bits) + shard.shape[-2:])
-        rows, columns = (min(64, shard.shape[-2]), min(2048, shard.shape[-1]))
+        rows, columns = (min(ROWS, shard.shape[-2]), min(2048, shard.shape[-1]))
         for row in range(0, shard.shape[-2], rows):
             for column in range(0, shard.shape[-1], columns):
                 items.append(
                     [
-                        (m, order, (pl.ds(row, rows), pl.ds(column + a, w)))
-                        for order, (a, w) in zip(orders, column_parts(columns, shares))
+                        (m, order, (pl.ds(row + a, w), pl.ds(column, columns)))
+                        for order, (a, w) in zip(orders, row_parts(rows, shares))
+                        if w
                     ]
                 )
     count, copies = (len(shards), sum(len(chunk) for chunk in items))
@@ -368,19 +375,24 @@
     for m in range(count):
         for copy in along_x(m) + at_home(m):
             copy.start()
-    first, firsts = (0, {})
-    for m in range(count):
-        firsts[m] = first
-        if m > 0:
-            value_turn(m)
+    def to_core(m):
         for copy in at_home(m):
             copy.wait()
         for copy in along_x(m):
             copy.wait_recv()
         for copy in along_core(m):
             copy.start()
+
+    first, firsts = (0, {})
+    to_core(0)
+    for m in range(count):
+        firsts[m] = first
+        if m > 0:
+            value_turn(m)
         for copy in along_core(m):
             copy.wait_recv()
+        if m + 1 < count:
+            to_core(m + 1)
         down, across = shapes[m]
 
         def one(j, carry, m=m, first=first, down=down, across=across):
@@ -525,7 +537,7 @@
             shard = lax.psum_scatter(flat, AXES, scatter_dimension=0, tiled=True)
             results.append(shard.reshape(-1, whole.shape[1]))
         return results, lax.psum(values, AXES)
-    kinds = ["all"] * 3 + ["half", "pair", "pair", "half", "all"]
+    kinds = ["half", "pair", "pair", "half"] + ["all"] * 4
     results, flat = gradients_fast(pairs, kinds, flat_pack(values), cube, 32, 1024)
     return results, flat_unpack(flat, values)
 
@@ -540,7 +552,9 @@
         return tuple(lax.all_gather(shard, AXES, axis=0, tiled=True) for shard in shards)
     kinds = ("pair", "half") + ("all",) * 6 + ("pair", "half")
     shards = [parities(shard) if kind == "pair" else shard for shard, kind in zip(shards, kinds)]
-    return gather_fast(shards, kinds, cube)
+    turns = (2, 6, 0, 3, 4, 8, 5, 7, 1, 9)
+    outs = gather_fast([shards[m] for m in turns], [kinds[m] for m in turns], cube)
+    return tuple(outs[turns.index(m)] for m in range(len(shards)))
 
 
 def distance_rows(group, left, right, backwards):
@@ -1372,19 +1386,19 @@
     kernel_local = jnp.stack(kernel_rows)
     shards, (grad_gains, grad_biases, grad_depth, grad_rel) = gradient_shards(
         (
-            (context, attn_branch),
-            (conv_swish, conv_branch),
-            (conv_hidden, d_pointwise),
             grad_two_out,
             grad_two_in,
             grad_one_in,
             grad_one_out,
+            (conv_hidden, d_pointwise),
             (attn_hidden, heads_in),
+            (conv_swish, conv_branch),
+            (context, attn_branch),
         ),
         (gains_local, shifts_local, kernel_local, d_table),
         cube,
     )
-    attn_out, conv_out, conv_in, two_out, two_in, one_in, one_out, attn_in = shards
+    two_out, two_in, one_in, one_out, conv_in, attn_in, conv_out, attn_out = shards
     return (
         final_norm.astype(jnp.bfloat16),
         d_input.astype(jnp.bfloat16),

time: 599 us -> 549 us (0.917)
  Pallas kernels: 494 us -> 444 us
    pallas_call x1, Pallas kernels: 193 us -> 162 us  [gather_fast(): pl.pallas_call(functools.partial(gather_kernel, cube, plans, items), out_...]
    pallas_call x1, Pallas kernels: 174 us -> 154 us  [gradients_fast(): pl.pallas_call(functools.partial(gradient_kernel, cube, shapes, kinds, ti...]
where the time goes in v5:
time: 549 us; the launch traced here: 539 us
  Pallas kernels  444 us (81%)
  local copies, waits for them, and re-layouts  47.7 us (9%)
  other arithmetic  23 us (4%)
  starting transfers between devices  11.2 us (2%)
  matrix products  10.7 us (2%)
    pallas_call x1, Pallas kernels, gather_fast(): pl.pallas_call(functools.partial(gather_kernel, cube, plans, items), out_...  162 us
    pallas_call x1, Pallas kernels, gradients_fast(): pl.pallas_call(functools.partial(gradient_kernel, cube, shapes, kinds, ti...  154 us
    pallas_call x4, Pallas kernels, ffn_fast(): pl.pallas_call(functools.partial(ffn_back_kernel if backward else ffn_ker...  61.2 us
    pallas_call x2, Pallas kernels, sum_fast(): pl.pallas_call(functools.partial(sum_kernel, cube), out_shape=jax.ShapeDt...  33.4 us
    pallas_call x1, Pallas kernels, attend_fast(): pl.pallas_call(functools.partial(attend_kernel, cube, REL_LEFT, REL_RIGHT...  17.1 us
    pallas_call x1, Pallas kernels, attend_back_fast(): pl.pallas_call(functools.partial(attend_back_kernel, cube, REL_LEFT, REL_...  16.1 us
    unnamed x135, local copies, waits for them, and re-layouts  15.3 us
  transfers between devices with their start and end apart: 4, of which 0 were waited for; matrix products, arithmetic and copies ran while one was open for 2% of the time, Pallas kernels for 0%

profile of v5, /device:TPU:0, one launch (start us, length us, event | category | flops | bytes accessed | tf_op | source)
XLA Modules:
  0.0 539.2 jit_solution(9802192693230908682)
XLA Ops:
  0.7 1.1 convert_reduce_fusion
  1.8 1.0 convert_element_type.130.refs_1_
  2.8 1.0 fusion.45
  3.8 1.2 multiply_reduce_fusion.18
  5.0 1.0 fusion.46
  5.9 1.1 reshape.332
  7.1 0.8 reshape.333.refs_2_
  8.2 0.8 reshape.335.refs_5_
  9.2 162.1 %gather_weights.1 = (bf16[2,2,2,2,2,32,1024]{6,5,4,3,2,1,0:T(8,128)(2,1)}, bf16[2,2,2,2,2,32,2048]{6,5,4,3,2,1,0:T(8,128)(2,1)}, bf16[2,2,2,2,2,32,2048]{6,5,4,3...) custom-call(bf16[32,1024]{1,0:T(8,128)(2,1)} %refs_0_.1, ...), custom_call_target="tpu_custom_call" | custom-call | tf_op jit(solution)/shard_map/gather_weights/pallas_call | solution.py:179
  171.3 17.2 %ffn.2 = (f32[128,1024]{1,0:T(8,128)S(1)}, f32[256,2048]{1,0:T(8,128)S(1)}, bf16[256,2048]{1,0:T(8,128)(2,1)S(1)}, bf16[256,1024]{1,0:T(8,128)(2,1)S(1)}) custom-call(bf16[128,1024]{1,0:T(8,128)(2,1)S(1)} %add_convert_fusion.5.refs_0_, f32[128,1024]{1,0:T(8,128)S(1)} %convert_element_type.130.refs_1_, bf16[1024,2048]{1,0:T(8,128)(2,1)} %bitcast.133, ...), custom_call_target="tpu_custom_call" | custom-call | tf_op jit(solution)/shard_map/ffn/pallas_call | solution.py:952
  188.6 1.3 copy-done.3
  189.9 1.0 copy-done.11
  190.9 0.8 copy-done.20
  193.2 17.1 %attend.1 = (f32[128,1024]{1,0:T(8,128)S(1)}, bf16[128,1024]{1,0:T(8,128)(2,1)S(1)}, bf16[3,256,512]{2,1,0:T(8,128)(2,1)S(1)}, f32[4,256,256]{2,1,0:T(8,128)S(1)}) custom-call(bf16[128,1024]{1,0:T(8,128)(2,1)S(1)} %add_convert_fusion.4.refs_0_, f32[128,1024]{1,0:T(8,128)S(1)} %get-tuple-element.55.refs_1_, f32[256,256]{1,0:T(8,128)S(1)} %compare_convert_fusion.refs_2_, ...), custom_call_target="tpu_custom_call" | custom-call | tf_op jit(solution)/shard_map/attend/pallas_call | solution.py:664
  210.3 1.0 copy-done.7
  211.3 0.9 copy-done.13
  212.6 3.0 fusion.33
  215.6 1.0 copy-done.22
  217.3 2.9 collective-permute-start
  220.2 1.3 collective-permute-start.1
  222.7 0.9 copy.73
  223.5 0.8 copy.71
  224.4 1.5 copy.69
  225.8 1.0 copy.68
  228.7 17.5 %sum_over_devices.2 = f32[8,1024]{1,0:T(8,128)} custom-call(f32[8,1024]{1,0:T(8,128)} %reshape.346.value), custom_call_target="tpu_custom_call" | custom-call | tf_op jit(solution)/shard_map/sum_over_devices/pallas_call | solution.py:219
  248.2 2.1 multiply_divide_fusion
  250.3 2.2 fusion.48
  253.0 12.4 %ffn.3 = (f32[128,1024]{1,0:T(8,128)S(1)}, f32[256,2048]{1,0:T(8,128)S(1)}, bf16[256,2048]{1,0:T(8,128)(2,1)S(1)}, bf16[256,1024]{1,0:T(8,128)(2,1)S(1)}) custom-call(bf16[128,1024]{1,0:T(8,128)(2,1)S(1)} %add_convert_fusion.2.refs_0_, f32[128,1024]{1,0:T(8,128)S(1)} %get-tuple-element.172.refs_1_, bf16[1024,2048]{1,0:T(8,128)(2,1)} %bitcast.137, ...), custom_call_target="tpu_custom_call" | custom-call | tf_op jit(solution)/shard_map/ffn/pallas_call | solution.py:952
  265.4 1.3 copy-done.5
  266.7 0.8 copy-done.18
  267.8 1.4 multiply_reduce_fusion
  269.3 1.2 multiply_convert_fusion.4.refs_0_
  270.5 17.0 %ffn_back.2 = (f32[128,1024]{1,0:T(8,128)S(1)}, bf16[256,2048]{1,0:T(8,128)(2,1)S(1)}, bf16[256,1024]{1,0:T(8,128)(2,1)S(1)}) custom-call(bf16[128,1024]{1,0:T(8,128)(2,1)S(1)} %multiply_convert_fusion.4.refs_0_, f32[256,2048]{1,0:T(8,128)S(1)} %copy-done.6, bf16[1024,2048]{1,0:T(8,128)(2,1)} %bitcast.138, bf16[2048,1024]{1,0:T(8,128)(2,1)} %bitcast.140), custom_call_target="tpu_custom_call" | custom-call | tf_op jit(solution)/shard_map/ffn_back/pallas_call | solution.py:952
  288.3 1.3 fusion.36
  290.1 1.8 multiply_reduce_fusion.9
  292.5 15.9 %sum_over_devices.3 = f32[8,1024]{1,0:T(8,128)} custom-call(f32[8,1024]{1,0:T(8,128)} %reshape.352.value), custom_call_target="tpu_custom_call" | custom-call | tf_op jit(solution)/shard_map/sum_over_devices/pallas_call | solution.py:219
  308.5 0.8 fusion.44
  309.3 2.5 fusion.19
  312.7 1.3 collective-permute-start.2
  314.0 5.7 %collective-permute-start.3 = (bf16[2,1024]{1,0:T(2,128)(2,1)}, bf16[2,1024]{1,0:T(2,128)(2,1)}, u32[]{:S(2)}, u32[]{:S(2)}) collective-permute-start(bf16[2,1024]{1,0:T(2,128)(2,1)} %get-tuple-element.143), channel_id=1, source_target_pairs={{0,1},{2,3},{4,5},{6,7},{8,9},{10,11},{12,13},{14,15},{16,17},{18,... | collective-permute-start | bytes 12296 | tf_op jit(solution)/shard_map/ppermute | solution.py:34
  319.7 0.9 fusion.55
  320.6 0.9 copy.72
  321.5 1.3 copy.66
  322.8 1.0 copy.67
  323.9 1.6 multiply_convert_fusion.2
  325.8 3.8 fusion.31
  329.6 0.8 pad_maximum_fusion.refs_12_
  331.8 16.1 %attend_back.1 = (f32[128,1024]{1,0:T(8,128)S(1)}, bf16[128,3072]{1,0:T(8,128)(2,1)S(1)}, f32[128,128]{1,0:T(8,128)S(1)}) custom-call(bf16[128,1024]{1,0:T(8,128)(2,1)S(1)} %get-tuple-element.124.refs_0_.refs_15_, bf16[3,256,512]{2,1,0:T(8,128)(2,1)S(1)} %copy-done.14, f32[4,256,256]{2,1,0:T(8,128)S(1)} %copy-done.8, bf16[128,128]{1,0:T(8,128)(2,1)S(1)} %pad.16.refs_3_, ...), custom_call_target="tpu_custom_call" | custom-call | tf_op jit(solution)/shard_map/attend_back/pallas_call | solution.py:794
  348.8 1.0 copy-done.4
  349.8 14.6 %ffn_back.3 = (f32[128,1024]{1,0:T(8,128)S(1)}, bf16[256,2048]{1,0:T(8,128)(2,1)S(1)}, bf16[256,1024]{1,0:T(8,128)(2,1)S(1)}) custom-call(bf16[128,1024]{1,0:T(8,128)(2,1)S(1)} %get-tuple-element.122.refs_0_, f32[256,2048]{1,0:T(8,128)S(1)} %copy-done.4, bf16[1024,2048]{1,0:T(8,128)(2,1)} %bitcast.134, bf16[2048,1024]{1,0:T(8,128)(2,1)} %bitcast.136), custom_call_target="tpu_custom_call" | custom-call | tf_op jit(solution)/shard_map/ffn_back/pallas_call | solution.py:952
  364.5 1.0 copy-done.10
  365.5 0.8 copy-done.17
  367.4 0.8 copy.70
  368.2 153.6 %reduce_gradients.1 = (f32[23,32,1024]{2,1,0:T(8,128)}, f32[2,2,2,32,1024]{4,3,2,1,0:T(8,128)}, f32[32,1024]{1,0:T(8,128)}) custom-call(bf16[2,2,2,2,128,256]{5,4,3,2,1,0:T(8,128)(2,1)} %bitcast.148, bf16[2,2,2,2,64,256]{5,4,3,2,1,0:T(8,128)(2,1)} %bitcast.150, bf16[2,2,2,2,64,256]{5,4,3,2,1,0:T(8,128)(2,1)} %bitcast.149, ...), custom_call_target="tpu_custom_call" | custom-call | tf_op jit(solution)/shard_map/reduce_gradients/pallas_call | solution.py:479
  521.9 1.1 slice_bitcast_fusion
  522.9 2.3 fusion.38
  525.2 1.7 slice_bitcast_fusion.1
  526.9 1.7 slice_bitcast_fusion.2
  529.2 1.3 fusion.39
  531.0 1.2 reshape.366
  532.7 1.2 reshape.371
  535.2 1.2 copy.76
  536.4 0.8 copy.81
  537.8 1.0 add_convert_fusion
  (205 shorter events, 17.9 us)
Async XLA Ops:
  0.7 8.3 %copy-start.24 = (bf16[128,1024]{1,0:T(8,128)(2,1)S(1)}, bf16[128,1024]{1,0:T(8,128)(2,1)}, u32[]{:S(2)}) copy-start(bf16[128,1024]{1,0:T(8,128)(2,1)} %param.19) | copy-start | bytes 786436
  0.7 7.3 %copy-start.35 = (bf16[32,4096]{1,0:T(8,128)(2,1)S(1)}, bf16[32,4096]{1,0:T(8,128)(2,1)}, u32[]{:S(2)}) copy-start(bf16[32,4096]{1,0:T(8,128)(2,1)} %param.30) | copy-start | bytes 786436
  3.8 167.5 %copy-start.44 = (f32[128]{0:T(128)}, f32[128]{0:T(128)S(1)}, u32[]{:S(2)}) copy-start(f32[128]{0:T(128)S(1)} %broadcast_multiply_fusion.14) | copy-start | bytes 1540
  5.0 166.3 %copy-start.58 = (f32[128]{0:T(128)}, f32[128]{0:T(128)S(1)}, u32[]{:S(2)}) copy-start(f32[128]{0:T(128)S(1)} %add_rsqrt_fusion.5) | copy-start | bytes 1540
  171.3 20.7 %copy-start.64 = (s32[1,4]{1,0:T(1,128)S(1)}, s32[1,4]{1,0:T(1,128)}, u32[]{:S(2)}) copy-start(s32[1,4]{1,0:T(1,128)} %param.20) | copy-start | bytes 52
  171.3 21.1 %copy-start.37 = (bf16[73,128]{1,0:T(8,128)(2,1)S(1)}, bf16[73,128]{1,0:T(8,128)(2,1)}, u32[]{:S(2)}) copy-start(bf16[73,128]{1,0:T(8,128)(2,1)} %param.33) | copy-start | bytes 56068
  188.5 1.3 copy-start.3
  189.9 1.0 copy-start.11
  191.7 1.6 copy-start
  191.8 29.8 %copy-start.42 = (f32[128]{0:T(128)}, f32[128]{0:T(128)S(1)}, u32[]{:S(2)}) copy-start(f32[128]{0:T(128)S(1)} %broadcast_multiply_fusion.13) | copy-start | bytes 1540
  192.0 29.5 %copy-start.54 = (f32[128]{0:T(128)}, f32[128]{0:T(128)S(1)}, u32[]{:S(2)}) copy-start(f32[128]{0:T(128)S(1)} %add_rsqrt_fusion.4) | copy-start | bytes 1540
  210.3 1.0 copy-start.7
  212.3 3.2 copy-start.56
  212.6 4.1 copy-start.60
  212.6 9.4 %copy-start.36 = (bf16[5,1024]{1,0:T(8,128)(2,1)S(1)}, bf16[5,1024]{1,0:T(8,128)(2,1)}, u32[]{:S(2)}) copy-start(bf16[5,1024]{1,0:T(8,128)(2,1)} %param.32) | copy-start | bytes 30724
  215.6 1.0 copy-start.22
  216.5 7.8 %copy-start.12 = (bf16[256,2048]{1,0:T(8,128)(2,1)S(1)}, bf16[256,2048]{1,0:T(8,128)(2,1)}, u32[]{:S(2)}) copy-start(bf16[256,2048]{1,0:T(8,128)(2,1)} %copy-done.11) | copy-start | bytes 3145732
  216.6 9.3 %copy-start.21 = (bf16[256,1024]{1,0:T(8,128)(2,1)S(1)}, bf16[256,1024]{1,0:T(8,128)(2,1)}, u32[]{:S(2)}) copy-start(bf16[256,1024]{1,0:T(8,128)(2,1)} %copy-done.20) | copy-start | bytes 1572868
  217.3 9.5 %collective-permute-start = (bf16[2,1024]{1,0:T(2,128)(2,1)}, bf16[2,1024]{1,0:T(2,128)(2,1)S(1)}, u32[]{:S(2)}, u32[]{:S(2)}) collective-permute-start(bf16[2,1024]{1,0:T(2,128)(2,1)} %get-tuple-element.144), channel_id=1, source_target_pairs={{0,1},{2,3},{4,5},{6,7},{8,9},{10,11},{12,13},{14,15},{16,17},{18,... | collective-permute-start | bytes 12296 | tf_op jit(solution)/shard_map/ppermute | solution.py:34
  220.2 6.6 %collective-permute-start.1 = (bf16[2,1024]{1,0:T(2,128)(2,1)S(1)}, bf16[2,1024]{1,0:T(2,128)(2,1)S(1)}, u32[]{:S(2)}, u32[]{:S(2)}) collective-permute-start(bf16[2,1024]{1,0:T(2,128)(2,1)S(1)} %get-tuple-element.145), channel_id=1, source_target_pairs={{1,0},{3,2},{5,4},{7,6},{9,8},{11,10},{13,12},{15,14},{17,16},{19,... | collective-permute-start | bytes 12296 | tf_op jit(solution)/shard_map/ppermute | solution.py:35
  221.6 28.8 %copy-start.38 = (f32[1024]{0:T(1024)S(1)}, f32[1024]{0:T(1024)}, u32[]{:S(2)}) copy-start(f32[1024]{0:T(1024)} %param.36) | copy-start | bytes 12292
  221.9 28.4 %copy-start.46 = (f32[128]{0:T(128)}, f32[128]{0:T(128)S(1)}, u32[]{:S(2)}) copy-start(f32[128]{0:T(128)S(1)} %get-tuple-element.166) | copy-start | bytes 1540
  221.9 30.6 %copy-start.48 = (f32[128]{0:T(128)}, f32[128]{0:T(128)S(1)}, u32[]{:S(2)}) copy-start(f32[128]{0:T(128)S(1)} %get-tuple-element.167) | copy-start | bytes 1540
  221.9 30.6 %copy-start.50 = (f32[128]{0:T(128)}, f32[128]{0:T(128)S(1)}, u32[]{:S(2)}) copy-start(f32[128]{0:T(128)S(1)} %get-tuple-element.168) | copy-start | bytes 1540
  221.9 30.6 %copy-start.52 = (f32[128]{0:T(128)}, f32[128]{0:T(128)S(1)}, u32[]{:S(2)}) copy-start(f32[128]{0:T(128)S(1)} %get-tuple-element.169) | copy-start | bytes 1540
  227.4 25.6 %copy-start.26 = (f32[128,1024]{1,0:T(8,128)}, f32[128,1024]{1,0:T(8,128)S(1)}, u32[]{:S(2)}) copy-start(f32[128,1024]{1,0:T(8,128)S(1)} %get-tuple-element.130) | copy-start | bytes 1572868
  265.4 1.3 copy-start.5
  267.6 2.9 copy-start.6
  270.5 17.8 %copy-start.29 = (bf16[128,1024]{1,0:T(8,128)(2,1)S(1)}, bf16[128,1024]{1,0:T(8,128)(2,1)}, u32[]{:S(2)}) copy-start(bf16[128,1024]{1,0:T(8,128)(2,1)} %param.21) | copy-start | bytes 786436
  287.5 4.4 copy-start.9
  287.5 4.4 copy-start.16
  287.5 2.1 copy-start.27
  287.5 2.1 copy-start.62
  287.5 2.6 copy-start.63
  289.6 2.3 copy-start.33
  290.1 19.2 %copy-start.28 = (f32[128,1024]{1,0:T(8,128)S(1)}, f32[128,1024]{1,0:T(8,128)}, u32[]{:S(2)}) copy-start(f32[128,1024]{1,0:T(8,128)} %copy-done.26) | copy-start | bytes 1572868
  291.9 30.9 %copy-start.19 = (bf16[256,1024]{1,0:T(8,128)(2,1)S(1)}, bf16[256,1024]{1,0:T(8,128)(2,1)}, u32[]{:S(2)}) copy-start(bf16[256,1024]{1,0:T(8,128)(2,1)} %copy-done.18) | copy-start | bytes 1572868
  309.3 14.5 %copy-start.39 = (f32[1,1024]{1,0:T(1,128)}, f32[1,1024]{1,0:T(1,128)S(1)}, u32[]{:S(2)}) copy-start(f32[1,1024]{1,0:T(1,128)S(1)} %get-tuple-element.149) | copy-start | bytes 12292
  309.3 14.5 %copy-start.40 = (f32[1,1024]{1,0:T(1,128)}, f32[1,1024]{1,0:T(1,128)S(1)}, u32[]{:S(2)}) copy-start(f32[1,1024]{1,0:T(1,128)S(1)} %get-tuple-element.150) | copy-start | bytes 12292
  311.8 8.7 %copy-start.31 = (bf16[128,1024]{1,0:T(8,128)(2,1)}, bf16[128,1024]{1,0:T(8,128)(2,1)S(1)}, u32[]{:S(2)}) copy-start(bf16[128,1024]{1,0:T(8,128)(2,1)S(1)} %get-tuple-element.121) | copy-start | bytes 786436
  311.8 12.0 %copy-start.47 = (f32[128]{0:T(128)S(1)}, f32[128]{0:T(128)}, u32[]{:S(2)}) copy-start(f32[128]{0:T(128)} %copy-done.46) | copy-start | bytes 1540
  312.1 11.8 %copy-start.49 = (f32[128]{0:T(128)S(1)}, f32[128]{0:T(128)}, u32[]{:S(2)}) copy-start(f32[128]{0:T(128)} %copy-done.48) | copy-start | bytes 1540
  312.1 11.8 %copy-start.51 = (f32[128]{0:T(128)S(1)}, f32[128]{0:T(128)}, u32[]{:S(2)}) copy-start(f32[128]{0:T(128)} %copy-done.50) | copy-start | bytes 1540
  312.1 11.8 %copy-start.53 = (f32[128]{0:T(128)S(1)}, f32[128]{0:T(128)}, u32[]{:S(2)}) copy-start(f32[128]{0:T(128)} %copy-done.52) | copy-start | bytes 1540
  312.7 11.1 %collective-permute-start.2 = (bf16[2,1024]{1,0:T(2,128)(2,1)}, bf16[2,1024]{1,0:T(2,128)(2,1)}, u32[]{:S(2)}, u32[]{:S(2)}) collective-permute-start(bf16[2,1024]{1,0:T(2,128)(2,1)} %get-tuple-element.142), channel_id=1, source_target_pairs={{1,0},{3,2},{5,4},{7,6},{9,8},{11,10},{13,12},{15,14},{17,16},{19,... | collective-permute-start | bytes 12296 | tf_op jit(solution)/shard_map/ppermute | solution.py:35
  314.0 9.8 %collective-permute-start.3 = (bf16[2,1024]{1,0:T(2,128)(2,1)}, bf16[2,1024]{1,0:T(2,128)(2,1)}, u32[]{:S(2)}, u32[]{:S(2)}) collective-permute-start(bf16[2,1024]{1,0:T(2,128)(2,1)} %get-tuple-element.143), channel_id=1, source_target_pairs={{0,1},{2,3},{4,5},{6,7},{8,9},{10,11},{12,13},{14,15},{16,17},{18,... | collective-permute-start | bytes 12296 | tf_op jit(solution)/shard_map/ppermute | solution.py:34
  320.6 3.3 copy-start.32
  322.8 2.7 copy-start.23
  325.7 4.7 copy-start.57
  325.7 4.7 copy-start.61
  325.7 5.0 copy-start.30
  329.5 1.8 copy-start.1
  329.5 2.0 copy-start.8
  329.5 2.2 copy-start.14
  331.0 16.9 %copy-start.2 = (bf16[128,1024]{1,0:T(8,128)(2,1)}, bf16[128,1024]{1,0:T(8,128)(2,1)S(1)}, u32[]{:S(2)}) copy-start(bf16[128,1024]{1,0:T(8,128)(2,1)S(1)} %get-tuple-element.124.refs_0_.refs_15_) | copy-start | bytes 786436
  331.8 16.2 %copy-start.43 = (f32[128]{0:T(128)S(1)}, f32[128]{0:T(128)}, u32[]{:S(2)}) copy-start(f32[128]{0:T(128)} %copy-done.42) | copy-start | bytes 1540
  331.8 16.2 %copy-start.55 = (f32[128]{0:T(128)S(1)}, f32[128]{0:T(128)}, u32[]{:S(2)}) copy-start(f32[128]{0:T(128)} %copy-done.54) | copy-start | bytes 1540
  348.0 1.9 copy-start.4
  349.8 16.4 %copy-start.25 = (bf16[128,1024]{1,0:T(8,128)(2,1)S(1)}, bf16[128,1024]{1,0:T(8,128)(2,1)}, u32[]{:S(2)}) copy-start(bf16[128,1024]{1,0:T(8,128)(2,1)} %param.19) | copy-start | bytes 786436
  349.8 16.4 %copy-start.45 = (f32[128]{0:T(128)S(1)}, f32[128]{0:T(128)}, u32[]{:S(2)}) copy-start(f32[128]{0:T(128)} %copy-done.44) | copy-start | bytes 1540
  349.8 16.4 %copy-start.59 = (f32[128]{0:T(128)S(1)}, f32[128]{0:T(128)}, u32[]{:S(2)}) copy-start(f32[128]{0:T(128)} %copy-done.58) | copy-start | bytes 1540
  349.8 16.7 %copy-start.41 = (f32[1024]{0:T(1024)S(1)}, f32[1024]{0:T(1024)}, u32[]{:S(2)}) copy-start(f32[1024]{0:T(1024)} %get-tuple-element.87) | copy-start | bytes 12292
  364.5 1.0 copy-start.10
  521.9 6.7 %copy-start.34 = (f32[32,1024]{1,0:T(8,128)S(1)}, f32[32,1024]{1,0:T(8,128)}, u32[]{:S(2)}) copy-start(f32[32,1024]{1,0:T(8,128)} %get-tuple-element.86) | copy-start | bytes 393220
  (5 other events, 4.1 us)

commit v6 on v5

--- a/solution.py
+++ b/solution.py
@@ -192,50 +192,6 @@
         name="gather_weights",
     )(*shards)
     return tuple(out.reshape(-1, shard.shape[-1]) for out, shard in zip(outs, shards))
-
-
-def sum_kernel(cube, value, out, held, sent, send, recv):
-    bits = range(cube.count)
-    greet(cube, bits)
-    sent[0] = value[...]
-    for k in bits:
-        copy = pltpu.make_async_remote_copy(
-            src_ref=sent.at[k],
-            dst_ref=held.at[k],
-            send_sem=send.at[k],
-            recv_sem=recv.at[k],
-            device_id=cube.partner(k),
-            device_id_type=MESH,
-        )
-        copy.start()
-        copy.wait()
-        if k + 1 < cube.count:
-            sent[k + 1] = sent[k] + held[k]
-        else:
-            out[...] = sent[k] + held[k]
-
-
-def sum_fast(value, cube, number):
-    return pl.pallas_call(
-        functools.partial(sum_kernel, cube),
-        out_shape=jax.ShapeDtypeStruct(value.shape, value.dtype),
-        in_specs=[pl.BlockSpec(memory_space=pltpu.VMEM)],
-        out_specs=pl.BlockSpec(memory_space=pltpu.VMEM),
-        scratch_shapes=[
-            pltpu.VMEM((cube.count,) + value.shape, value.dtype),
-            pltpu.VMEM((cube.count,) + value.shape, value.dtype),
-            pltpu.SemaphoreType.DMA((cube.count,)),
-            pltpu.SemaphoreType.DMA((cube.count,)),
-        ],
-        compiler_params=pltpu.CompilerParams(collective_id=number, has_side_effects=True),
-        name="sum_over_devices",
-    )(value)
-
-
-def sum_everywhere(values, cube, number):
-    if cube is None:
-        return lax.psum(values, AXES)
-    return flat_unpack(sum_fast(flat_pack(values), cube, number), values)
 
 
 def gradient_kernel(cube, shapes, kinds, tile, *refs):
@@ -971,11 +927,324 @@
     )(first, second, weight_in, weight_out)
 
 
-def cube_of(shards, rel_table):
+def rounds_of(cube):
+    bits = list(range(cube.count))
+    return [bits[i : i + 2] for i in range(0, cube.count, 2)]
+
+
+def flipped(cube, bits):
+    batch, seq = (lax.axis_index("batch"), lax.axis_index("seq"))
+    for k in bits:
+        step = 1 - 2 * cube.bit(k)
+        if k < cube.seq_bits:
+            seq = seq + step * (1 << k)
+        else:
+            batch = batch + step * (1 << (k - cube.seq_bits))
+    return (batch, seq)
+
+
+def masks_of(bits):
+    return [[bits[0]], [bits[1]], bits] if len(bits) == 2 else [bits]
+
+
+def greet_rounds(cube):
+    barrier, count = (pltpu.get_barrier_semaphore(), 0)
+    for bits in rounds_of(cube):
+        for mask in masks_of(bits):
+            pl.semaphore_signal(
+                barrier, inc=1, device_id=flipped(cube, mask), device_id_type=MESH
+            )
+            count += 1
+    pl.semaphore_wait(barrier, count)
+
+
+def sum_rounds(cube, value, slots, send, recv):
+    for r, bits in enumerate(rounds_of(cube)):
+        mine = sum(cube.bit(k) * (1 << i) for i, k in enumerate(bits))
+        slots[r, mine] = value
+        copies = []
+        for i, mask in enumerate(masks_of(bits)):
+            copies.append(
+                pltpu.make_async_remote_copy(
+                    src_ref=slots.at[r, mine],
+                    dst_ref=slots.at[r, mine],
+                    send_sem=send.at[r, i],
+                    recv_sem=recv.at[r, i],
+                    device_id=flipped(cube, mask),
+                    device_id_type=MESH,
+                )
+            )
+            copies[i].start()
+        for copy in copies:
+            copy.wait()
+        value = slots[r, 0] + slots[r, 1]
+        if len(bits) == 2:
+            value = value + (slots[r, 2] + slots[r, 3])
+    return value
+
+
+def conv_halo(cube, wide, halo_send, halo_recv, send, recv):
+    rows = wide.shape[0] - 16
+    mine = cube.bit(0)
+    halo_send[...] = wide[pl.ds(pl.multiple_of(8 + (1 - mine) * (rows - 8), 8), 8), :]
+    copy = to_partner(cube, 0, halo_send, halo_recv, send.at[0], recv.at[0])
+    copy.start()
+    edge = pl.ds(pl.multiple_of(mine * (rows + 8), 8), 8)
+    wide[edge, :] = jnp.zeros((8, wide.shape[1]), jnp.float32)
+    copy.wait()
+    wide[pl.ds(pl.multiple_of((1 - mine) * (rows + 8), 8), 8), :] = halo_recv[...]
+
+
+def row_sum(values):
+    return jnp.sum(values, axis=0, keepdims=True)
+
+
+def conv_kernel(cube, taps, *refs):
+    values, norms, marks, weight_in, weight_out = refs[:5]
+    after, unit_out, inverse_out, hidden, gate, sigma, wide, centred, swish, stats = refs[5:15]
+    into, outof, mixed, slots, halo_send, halo_recv, load, send, recv, h_send, h_recv = refs[15:]
+    rows, width = values.shape
+    block = width // 4
+    loads = [
+        pltpu.make_async_copy(weight_in, into, load.at[0]),
+        pltpu.make_async_copy(weight_out, outof, load.at[1]),
+    ]
+    for one in loads:
+        one.start()
+
+    def normalise(i, carry):
+        part = pl.ds(pl.multiple_of(i * 32, 32), 32)
+        here = values[part, :]
+        away = here - jnp.mean(here, axis=1, keepdims=True)
+        inverse = lax.rsqrt(jnp.mean(away * away, axis=1, keepdims=True) + epsilon)
+        unit = away * inverse
+        unit_out[part, :] = unit
+        inverse_out[part, :] = jnp.broadcast_to(inverse, (32, 128))
+        hidden[part, :] = (unit * norms[0:1, :] + norms[1:2, :]).astype(jnp.bfloat16)
+        return carry
+
+    lax.fori_loop(0, rows // 32, normalise, 0)
+    greet_rounds(cube)
+    loads[0].wait()
+
+    def point(i, carry):
+        part = pl.ds(pl.multiple_of(i * block, block), block)
+        other = pl.ds(pl.multiple_of(width + i * block, block), block)
+        level = matmul(hidden[...], into[:, part])
+        open_ = jax.nn.sigmoid(matmul(hidden[...], into[:, other]))
+        gate[:, part] = level
+        sigma[:, part] = open_
+        wide[pl.ds(8, rows), part] = (level * open_).astype(jnp.bfloat16).astype(jnp.float32)
+        return carry
+
+    lax.fori_loop(0, 4, point, 0)
+    conv_halo(cube, wide, halo_send, halo_recv, h_send, h_recv)
+    reach = taps // 2
+    mask = marks[:, taps : taps + 1]
+
+    def mix(i, carry):
+        part = pl.ds(pl.multiple_of(i * block, block), block)
+        total = jnp.zeros((rows, block), jnp.float32)
+        for o in range(taps):
+            total = total + norms[8 + o : 9 + o, part] * (
+                wide[8 + o - reach : 8 + o - reach + rows, part] * marks[:, o : o + 1]
+            )
+        mixed[:, part] = total
+        masked = total * mask
+        stats[0:1, part] = row_sum(masked)
+        stats[1:2, part] = row_sum(masked * total)
+        return carry
+
+    lax.fori_loop(0, 4, mix, 0)
+    stats[2:3, :] = jnp.broadcast_to(row_sum(mask), (1, width))
+    stats[3:8, :] = jnp.zeros((5, width), jnp.float32)
+    total = sum_rounds(cube, stats[...], slots, send, recv)
+    count = total[2:3, :]
+    mean = total[0:1, :] / count
+    var = total[1:2, :] / count - mean * mean
+    stats[0:1, :] = mean
+    stats[1:2, :] = var
+    stats[2:3, :] = count
+    stats[3:4, :] = lax.rsqrt(var + epsilon)
+
+    def finish(i, carry):
+        part = pl.ds(pl.multiple_of(i * block, block), block)
+        middle = (mixed[:, part] - stats[0:1, part]) * stats[3:4, part]
+        centred[:, part] = middle
+        swish[:, part] = jax.nn.silu(middle * norms[2:3, part] + norms[3:4, part]).astype(
+            jnp.bfloat16
+        )
+        return carry
+
+    lax.fori_loop(0, 4, finish, 0)
+    loads[1].wait()
+
+    def project(i, carry):
+        part = pl.ds(pl.multiple_of(i * block, block), block)
+        after[:, part] = values[:, part] + matmul(swish[...], outof[:, part])
+        return carry
+
+    lax.fori_loop(0, 4, project, 0)
+
+
+def conv_back_kernel(cube, taps, *refs):
+    d_values, norms, marks, stats, centred, wide, gate, sigma, unit, inverse = refs[:10]
+    weight_in, weight_out = refs[10:12]
+    d_after, attn_branch, branch, d_point, sums = refs[12:17]
+    into, outof, d_bn, d_wide, d_norm, pack, slots, halo_send, halo_recv, load, send, recv, h_send, h_recv = refs[17:]
+    rows, width = d_values.shape
+    block = width // 4
+    loads = [
+        pltpu.make_async_copy(weight_out, outof, load.at[0]),
+        pltpu.make_async_copy(weight_in, into, load.at[1]),
+    ]
+    for one in loads:
+        one.start()
+    branch[...] = d_values[...].astype(jnp.bfloat16)
+    greet_rounds(cube)
+    reach = taps // 2
+    mask = marks[:, taps : taps + 1]
+    loads[0].wait()
+
+    def enter(i, carry):
+        part = pl.ds(pl.multiple_of(i * block, block), block)
+        middle = centred[:, part]
+        slope = swish_slope(middle * norms[2:3, part] + norms[3:4, part])
+        value = transposed_right(branch[...], outof[part, :]) * slope
+        d_bn[:, part] = value
+        masked = value * mask
+        pack[0:1, part] = row_sum(masked * middle)
+        pack[1:2, part] = row_sum(masked)
+        return carry
+
+    lax.fori_loop(0, 4, enter, 0)
+    pack[2:8, :] = jnp.zeros((6, width), jnp.float32)
+    pack[...] = sum_rounds(cube, pack[...], slots, send, recv)
+
+    def spread(i, carry):
+        part = pl.ds(pl.multiple_of(i * block, block), block)
+        share = mask * (pack[1:2, part] + centred[:, part] * pack[0:1, part])
+        value = (
+            norms[2:3, part] * stats[3:4, part] * (d_bn[:, part] - share / stats[2:3, part])
+        )
+        d_wide[pl.ds(8, rows), part] = value.astype(jnp.bfloat16).astype(jnp.float32)
+        return carry
+
+    lax.fori_loop(0, 4, spread, 0)
+    conv_halo(cube, d_wide, halo_send, halo_recv, h_send, h_recv)
+    sums[...] = jnp.zeros_like(sums)
+
+    def unmix(i, carry):
+        part = pl.ds(pl.multiple_of(i * block, block), block)
+        own = d_wide[8 : 8 + rows, part]
+        total = jnp.zeros((rows, block), jnp.float32)
+        for o in range(taps):
+            back = taps - 1 - o
+            sums[o : o + 1, part] = row_sum(
+                own * (wide[8 + o - reach : 8 + o - reach + rows, part] * marks[:, o : o + 1])
+            )
+            total = total + norms[8 + o : 9 + o, part] * (
+                d_wide[8 + back - reach : 8 + back - reach + rows, part]
+                * marks[:, back : back + 1]
+            )
+        open_ = sigma[:, part]
+        other = pl.ds(pl.multiple_of(width + i * block, block), block)
+        d_point[:, part] = (total * open_).astype(jnp.bfloat16)
+        d_point[:, other] = (total * gate[:, part] * open_ * (1.0 - open_)).astype(jnp.bfloat16)
+        return carry
+
+    lax.fori_loop(0, 4, unmix, 0)
+    loads[1].wait()
+
+    def project(i, carry):
+        part = pl.ds(pl.multiple_of(i * block, block), block)
+        value = transposed_right(d_point[...], into[part, :])
+        d_norm[:, part] = value
+        sums[8:9, part] = row_sum(value * unit[:, part])
+        sums[9:10, part] = row_sum(value)
+        return carry
+
+    lax.fori_loop(0, 4, project, 0)
+    sums[10:12, :] = pack[0:2, :]
+
+    def leave(i, carry):
+        part = pl.ds(pl.multiple_of(i * 32, 32), 32)
+        here = unit[part, :]
+        d_unit = d_norm[part, :] * norms[0:1, :]
+        value = d_values[part, :] + inverse[part, 0:1] * (
+            d_unit
+            - jnp.mean(d_unit, axis=1, keepdims=True)
+            - here * jnp.mean(d_unit * here, axis=1, keepdims=True)
+        )
+        d_after[part, :] = value
+        attn_branch[part, :] = value.astype(jnp.bfloat16)
+        return carry
+
+    lax.fori_loop(0, rows // 32, leave, 0)
+
+
+def conv_fast(cube, taps, small, weights, forward):
+    rows, width = small[0].shape
+    vmem = pl.BlockSpec(memory_space=pltpu.VMEM)
+    wide, full, half = ((rows + 16, width), (rows, width), (rows, 2 * width))
+    single, double = (jnp.float32, jnp.bfloat16)
+    if forward:
+        shapes = [
+            (full, single),
+            (full, single),
+            ((rows, 128), single),
+            (full, double),
+            (full, single),
+            (full, single),
+            (wide, single),
+            (full, single),
+            (full, double),
+            ((8, width), single),
+        ]
+        own = [pltpu.VMEM(full, single)]
+    else:
+        shapes = [(full, single), (full, double), (full, double), (half, double), ((16, width), single)]
+        own = [
+            pltpu.VMEM(full, single),
+            pltpu.VMEM(wide, single),
+            pltpu.VMEM(full, single),
+            pltpu.VMEM((8, width), single),
+        ]
+    rounds = len(rounds_of(cube))
+    return pl.pallas_call(
+        functools.partial(conv_kernel if forward else conv_back_kernel, cube, taps),
+        out_shape=[jax.ShapeDtypeStruct(shape, dtype) for shape, dtype in shapes],
+        in_specs=[vmem] * len(small) + [pl.BlockSpec(memory_space=pl.ANY)] * 2,
+        out_specs=[vmem] * len(shapes),
+        scratch_shapes=[
+            pltpu.VMEM(weights[0].shape, double),
+            pltpu.VMEM(weights[1].shape, double),
+        ]
+        + own
+        + [
+            pltpu.VMEM((rounds, 4, 8, width), single),
+            pltpu.VMEM((8, width), single),
+            pltpu.VMEM((8, width), single),
+            pltpu.SemaphoreType.DMA((2,)),
+            pltpu.SemaphoreType.DMA((rounds, 3)),
+            pltpu.SemaphoreType.DMA((rounds, 3)),
+            pltpu.SemaphoreType.DMA((1,)),
+            pltpu.SemaphoreType.DMA((1,)),
+        ],
+        compiler_params=pltpu.CompilerParams(
+            collective_id=1 if forward else 2,
+            has_side_effects=True,
+            vmem_limit_bytes=48 * 1024 * 1024,
+        ),
+        name="conv" if forward else "conv_back",
+    )(*small, *weights)
+
+
+def cube_of(shards, rel_table, depth_w):
     batch, seq = (lax.axis_size("batch"), lax.axis_size("seq"))
     if seq != 2 or batch < 8 or batch & (batch - 1):
         return None
-    if rel_table.shape[0] > 128 or rel_table.shape[1] != 128:
+    if depth_w.shape[0] > 5 or rel_table.shape[0] > 128 or rel_table.shape[1] != 128:
         return None
     if any(shard.shape[0] % 32 or shard.shape[1] % 1024 for shard in shards):
         return None
@@ -1204,7 +1473,7 @@
         ffn2_in,
         ffn2_out,
     )
-    cube = cube_of(shards, rel_table)
+    cube = cube_of(shards, rel_table, depth_w)
     gathered = gather_all(shards, cube)
     start_values = frames.astype(jnp.float32)
     after_first, kept_first = ffn_forward(
@@ -1256,35 +1525,51 @@
         after_attn, context, heads_kept, probs_kept = attend_fast(
             cube, attn_hidden, after_first, same, table, gathered[2:6]
         )
-    conv_norm, conv_unit, conv_inverse = norm_forward(after_attn, norm_gains[2], norm_biases[2])
-    conv_hidden = conv_norm.astype(jnp.bfloat16)
-    pointwise = matmul(conv_hidden, gathered[6])
-    gate_half = pointwise[:, :width]
-    sigma_half = jax.nn.sigmoid(pointwise[:, width:])
-    gated = (gate_half * sigma_half).astype(jnp.bfloat16)
-    gated_wide = padded_2(gated, (("seq", 0),), reach)
     kernel = depth_w.astype(jnp.float32)
-    mixed = jnp.zeros((frames_here, width), jnp.float32)
-    for offset in range(kernel_size):
-        same = (wide_segment[offset : offset + frames_here] == own_segment).astype(jnp.float32)[
-            :, None
+    if cube is None:
+        conv_norm, conv_unit, conv_inverse = norm_forward(after_attn, norm_gains[2], norm_biases[2])
+        conv_hidden = conv_norm.astype(jnp.bfloat16)
+        pointwise = matmul(conv_hidden, gathered[6])
+        gate_half = pointwise[:, :width]
+        sigma_half = jax.nn.sigmoid(pointwise[:, width:])
+        gated = (gate_half * sigma_half).astype(jnp.bfloat16)
+        gated_wide = padded_2(gated, (("seq", 0),), reach)
+        mixed = jnp.zeros((frames_here, width), jnp.float32)
+        for offset in range(kernel_size):
+            same = (wide_segment[offset : offset + frames_here] == own_segment).astype(jnp.float32)[
+                :, None
+            ]
+            mixed = (
+                mixed
+                + kernel[offset] * gated_wide[offset : offset + frames_here].astype(jnp.float32) * same
+            )
+        total, squares, count = lax.psum(
+            (jnp.sum(mixed * mask, axis=0), jnp.sum(mixed * mixed * mask, axis=0), jnp.sum(mask)),
+            AXES,
+        )
+        mean = total / count
+        var = squares / count - mean * mean
+        bn_inverse = lax.rsqrt(var + epsilon)
+        centred = (mixed - mean) * bn_inverse
+        bn_out = centred * bn_gain + bn_shift
+        conv_swish = jax.nn.silu(bn_out).astype(jnp.bfloat16)
+        after_conv = after_attn + matmul(conv_swish, gathered[7])
+    else:
+        marks = [
+            wide_segment[offset : offset + frames_here] == own_segment
+            for offset in range(kernel_size)
         ]
-        mixed = (
-            mixed
-            + kernel[offset] * gated_wide[offset : offset + frames_here].astype(jnp.float32) * same
-        )
-    total, squares, count = sum_everywhere(
-        (jnp.sum(mixed * mask, axis=0), jnp.sum(mixed * mixed * mask, axis=0), jnp.sum(mask)),
-        cube,
-        1,
-    )
-    mean = total / count
-    var = squares / count - mean * mean
-    bn_inverse = lax.rsqrt(var + epsilon)
-    centred = (mixed - mean) * bn_inverse
-    bn_out = centred * bn_gain + bn_shift
-    conv_swish = jax.nn.silu(bn_out).astype(jnp.bfloat16)
-    after_conv = after_attn + matmul(conv_swish, gathered[7])
+        marks = jnp.stack(marks, axis=1).astype(jnp.float32)
+        marks = jnp.concatenate([marks, mask], axis=1)
+        marks = jnp.pad(marks, ((0, 0), (0, 8 - marks.shape[1])))
+        blank = jnp.zeros((4, width), jnp.float32)
+        norms = [norm_gains[2], norm_biases[2], bn_gain, bn_shift]
+        norms = jnp.concatenate([jnp.stack(norms), blank, kernel, blank[:3]])
+        after_conv, *conv_kept, conv_swish, stats = conv_fast(
+            cube, kernel_size, (after_attn, norms, marks), (gathered[6], gathered[7]), True
+        )
+        conv_unit, conv_inverse, conv_hidden, gate_half, sigma_half, gated_wide, centred = conv_kept
+        var, count = (stats[1], stats[2])
     after_second, kept_second = ffn_forward(
         after_conv, norm_gains[3], norm_biases[3], gathered[8], gathered[9], cube, 8
     )
@@ -1299,43 +1584,65 @@
     d_conv_res, grad_two_in, grad_two_out, gain_three, shift_three = ffn_backward(
         d_second, kept_second, norm_gains[3], gathered[8], gathered[9], cube, 9
     )
-    conv_branch = d_conv_res.astype(jnp.bfloat16)
-    d_bn_out = transposed_right(conv_branch, gathered[7]) * swish_slope(bn_out)
-    grad_bn_gain, grad_bn_shift = sum_everywhere(
-        (jnp.sum(d_bn_out * centred * mask, axis=0), jnp.sum(d_bn_out * mask, axis=0)), cube, 2
-    )
-    d_mixed = (
-        bn_gain * bn_inverse * (d_bn_out - mask * (grad_bn_shift + centred * grad_bn_gain) / count)
-    )
-    d_mixed = d_mixed.astype(jnp.bfloat16)
-    d_mixed_wide = padded_2(d_mixed, (("seq", 0),), reach)
-    d_mixed_value = d_mixed.astype(jnp.float32)
-    d_gated = jnp.zeros((frames_here, width), jnp.float32)
-    kernel_rows = []
-    for offset in range(kernel_size):
-        same = (wide_segment[offset : offset + frames_here] == own_segment).astype(jnp.float32)[
-            :, None
-        ]
-        shifted_in = gated_wide[offset : offset + frames_here].astype(jnp.float32)
-        kernel_rows.append(jnp.sum(d_mixed_value * shifted_in * same, axis=0))
-        back = 2 * reach - offset
-        same_back = (wide_segment[back : back + frames_here] == own_segment).astype(jnp.float32)[
-            :, None
-        ]
-        d_gated = (
-            d_gated
-            + kernel[offset]
-            * d_mixed_wide[back : back + frames_here].astype(jnp.float32)
-            * same_back
-        )
-    d_pointwise = jnp.concatenate(
-        [d_gated * sigma_half, d_gated * gate_half * sigma_half * (1.0 - sigma_half)], axis=1
-    ).astype(jnp.bfloat16)
-    d_conv_norm, gain_two, shift_two = norm_backward(
-        transposed_right(d_pointwise, gathered[6]), conv_unit, conv_inverse, norm_gains[2]
-    )
-    d_attn_res = d_conv_res + d_conv_norm
-    attn_branch = d_attn_res.astype(jnp.bfloat16)
+    if cube is None:
+        conv_branch = d_conv_res.astype(jnp.bfloat16)
+        d_bn_out = transposed_right(conv_branch, gathered[7]) * swish_slope(bn_out)
+        grad_bn_gain, grad_bn_shift = lax.psum(
+            (jnp.sum(d_bn_out * centred * mask, axis=0), jnp.sum(d_bn_out * mask, axis=0)), AXES
+        )
+        d_mixed = (
+            bn_gain * bn_inverse * (d_bn_out - mask * (grad_bn_shift + centred * grad_bn_gain) / count)
+        )
+        d_mixed = d_mixed.astype(jnp.bfloat16)
+        d_mixed_wide = padded_2(d_mixed, (("seq", 0),), reach)
+        d_mixed_value = d_mixed.astype(jnp.float32)
+        d_gated = jnp.zeros((frames_here, width), jnp.float32)
+        kernel_rows = []
+        for offset in range(kernel_size):
+            same = (wide_segment[offset : offset + frames_here] == own_segment).astype(jnp.float32)[
+                :, None
+            ]
+            shifted_in = gated_wide[offset : offset + frames_here].astype(jnp.float32)
+            kernel_rows.append(jnp.sum(d_mixed_value * shifted_in * same, axis=0))
+            back = 2 * reach - offset
+            same_back = (wide_segment[back : back + frames_here] == own_segment).astype(jnp.float32)[
+                :, None
+            ]
+            d_gated = (
+                d_gated
+                + kernel[offset]
+                * d_mixed_wide[back : back + frames_here].astype(jnp.float32)
+                * same_back
+            )
+        d_pointwise = jnp.concatenate(
+            [d_gated * sigma_half, d_gated * gate_half * sigma_half * (1.0 - sigma_half)], axis=1
+        ).astype(jnp.bfloat16)
+        d_conv_norm, gain_two, shift_two = norm_backward(
+            transposed_right(d_pointwise, gathered[6]), conv_unit, conv_inverse, norm_gains[2]
+        )
+        d_attn_res = d_conv_res + d_conv_norm
+        attn_branch = d_attn_res.astype(jnp.bfloat16)
+    else:
+        d_attn_res, attn_branch, conv_branch, d_pointwise, sums = conv_fast(
+            cube,
+            kernel_size,
+            (
+                d_conv_res,
+                norms,
+                marks,
+                stats,
+                centred,
+                gated_wide,
+                gate_half,
+                sigma_half,
+                conv_unit,
+                conv_inverse,
+            ),
+            (gathered[6], gathered[7]),
+            False,
+        )
+        kernel_rows = [sums[offset] for offset in range(kernel_size)]
+        gain_two, shift_two, grad_bn_gain, grad_bn_shift = sums[8], sums[9], sums[10], sums[11]
     if cube is None:
         d_context = (
             transposed_right(attn_branch, gathered[5])

time: 549 us -> 521 us (0.949)
  starting transfers between devices: 11.2 us -> 0 us
  matrix products: 10.7 us -> 0 us
  other arithmetic: 23 us -> 13.5 us
  Pallas kernels: 444 us -> 450 us
    ppermute x4 -> x0, starting transfers between devices: 11.2 us -> none  [the longest x2 8.61 us: padded_2(): before = lax.ppermute(last, axis, up)]
    dot_general x4 -> x0, matrix products: 10.7 us -> none  [the longest x2 5.53 us: transposed_right(): lax.dot_general(left, right, (((1,), (1,)), ((), ())), preferred_element_...]
    pallas_call x2, Pallas kernels: 33.4 us -> 41 us  [conv_fast(): pl.pallas_call(functools.partial(conv_kernel if forward else conv_back_ke...]
    unnamed x135 -> x144, local copies, waits for them, and re-layouts: 15.3 us -> 18.4 us
  transfers between devices with their start and end apart: 4 -> 0, of which waited for: 0 -> 0; matrix products, arithmetic and copies ran while one was open for 2% -> 0% of each run, Pallas kernels for 0% -> 0%
where the time goes in v6:
time: 521 us; the launch traced here: 512 us
  Pallas kernels  450 us (86%)
  local copies, waits for them, and re-layouts  46.7 us (9%)
  other arithmetic  13.5 us (3%)
    pallas_call x1, Pallas kernels, gather_fast(): pl.pallas_call(functools.partial(gather_kernel, cube, plans, items), out_...  162 us
    pallas_call x1, Pallas kernels, gradients_fast(): pl.pallas_call(functools.partial(gradient_kernel, cube, shapes, kinds, ti...  155 us
    pallas_call x4, Pallas kernels, ffn_fast(): pl.pallas_call(functools.partial(ffn_back_kernel if backward else ffn_ker...  58.7 us
    pallas_call x2, Pallas kernels, conv_fast(): pl.pallas_call(functools.partial(conv_kernel if forward else conv_back_ke...  41 us
    unnamed x144, local copies, waits for them, and re-layouts  18.4 us
    pallas_call x1, Pallas kernels, attend_fast(): pl.pallas_call(functools.partial(attend_kernel, cube, REL_LEFT, REL_RIGHT...  17.1 us
    pallas_call x1, Pallas kernels, attend_back_fast(): pl.pallas_call(functools.partial(attend_back_kernel, cube, REL_LEFT, REL_...  16.7 us

profile of v6, /device:TPU:0, one launch (start us, length us, event | category | flops | bytes accessed | tf_op | source)
XLA Modules:
  0.0 512.4 jit_solution(9092883304667950617)
XLA Ops:
  0.7 1.6 fusion.9
  2.3 1.1 convert_reduce_fusion
  3.4 1.2 multiply_reduce_fusion.11
  4.6 1.2 add_convert_fusion.4.refs_0_
  5.8 1.1 reshape.277
  7.0 0.8 reshape.278.refs_2_
  7.8 1.1 reshape.279
  8.9 0.8 reshape.280.refs_5_
  9.8 162.0 %gather_weights.1 = (bf16[2,2,2,2,2,32,1024]{6,5,4,3,2,1,0:T(8,128)(2,1)}, bf16[2,2,2,2,2,32,2048]{6,5,4,3,2,1,0:T(8,128)(2,1)}, bf16[2,2,2,2,2,32,2048]{6,5,4,3...) custom-call(bf16[32,1024]{1,0:T(8,128)(2,1)} %refs_0_.1, ...), custom_call_target="tpu_custom_call" | custom-call | tf_op jit(solution)/shard_map/gather_weights/pallas_call | solution.py:179
  171.8 17.2 %ffn.2 = (f32[128,1024]{1,0:T(8,128)S(1)}, f32[256,2048]{1,0:T(8,128)S(1)}, bf16[256,2048]{1,0:T(8,128)(2,1)S(1)}, bf16[256,1024]{1,0:T(8,128)(2,1)S(1)}) custom-call(bf16[128,1024]{1,0:T(8,128)(2,1)S(1)} %add_convert_fusion.4.refs_0_, f32[128,1024]{1,0:T(8,128)S(1)} %convert_element_type.51.refs_1_, bf16[1024,2048]{1,0:T(8,128)(2,1)} %bitcast.117, ...), custom_call_target="tpu_custom_call" | custom-call | tf_op jit(solution)/shard_map/ffn/pallas_call | solution.py:908
  189.1 1.3 copy-done.2
  190.4 1.0 copy-done.11
  191.4 0.8 copy-done.29
  193.8 17.1 %attend.1 = (f32[128,1024]{1,0:T(8,128)S(1)}, bf16[128,1024]{1,0:T(8,128)(2,1)S(1)}, bf16[3,256,512]{2,1,0:T(8,128)(2,1)S(1)}, f32[4,256,256]{2,1,0:T(8,128)S(1)}) custom-call(bf16[128,1024]{1,0:T(8,128)(2,1)S(1)} %add_convert_fusion.3.refs_0_, f32[128,1024]{1,0:T(8,128)S(1)} %get-tuple-element.70.refs_1_, f32[256,256]{1,0:T(8,128)S(1)} %compare_convert_fusion.refs_2_, ...), custom_call_target="tpu_custom_call" | custom-call | tf_op jit(solution)/shard_map/attend/pallas_call | solution.py:620
  210.9 1.0 copy-done.6
  211.9 0.9 copy-done.13
  212.8 0.7 copy-done.33
  214.5 19.2 %conv.1 = (f32[128,1024]{1,0:T(8,128)S(1)}, f32[128,1024]{1,0:T(8,128)S(1)}, f32[128,128]{1,0:T(8,128)S(1)}, bf16[128,1024]{1,0:T(8,128)(2,1)S(1)}, f32[128,1024...) custom-call(f32[128,1024]{1,0:T(8,128)S(1)} %get-tuple-element.75.re, ...), custom_call_target="tpu_custom_call" | custom-call | tf_op jit(solution)/shard_map/conv/pallas_call | solution.py:1214
  233.7 0.8 copy-done.16
  234.5 0.8 copy-done.20
  235.3 0.8 copy-done.22
  236.1 0.8 copy-done.24
  236.9 0.8 copy-done.26
  237.7 0.7 copy-done.35
  239.1 13.5 %ffn.3 = (f32[128,1024]{1,0:T(8,128)S(1)}, f32[256,2048]{1,0:T(8,128)S(1)}, bf16[256,2048]{1,0:T(8,128)(2,1)S(1)}, bf16[256,1024]{1,0:T(8,128)(2,1)S(1)}) custom-call(bf16[128,1024]{1,0:T(8,128)(2,1)S(1)} %add_convert_fusion.2.refs_0_, f32[128,1024]{1,0:T(8,128)S(1)} %get-tuple-element.78.refs_1_, bf16[1024,2048]{1,0:T(8,128)(2,1)} %bitcast.121, ...), custom_call_target="tpu_custom_call" | custom-call | tf_op jit(solution)/shard_map/ffn/pallas_call | solution.py:908
  252.7 1.3 copy-done.4
  254.0 0.8 copy-done.31
  255.2 0.9 multiply_reduce_fusion
  256.5 13.8 %ffn_back.2 = (f32[128,1024]{1,0:T(8,128)S(1)}, bf16[256,2048]{1,0:T(8,128)(2,1)S(1)}, bf16[256,1024]{1,0:T(8,128)(2,1)S(1)}) custom-call(bf16[128,1024]{1,0:T(8,128)(2,1)S(1)} %multiply_convert_fusion.1.refs_0_, f32[256,2048]{1,0:T(8,128)S(1)} %copy-done.5, bf16[1024,2048]{1,0:T(8,128)(2,1)} %bitcast.122, bf16[2048,1024]{1,0:T(8,128)(2,1)} %bitcast.124), custom_call_target="tpu_custom_call" | custom-call | tf_op jit(solution)/shard_map/ffn_back/pallas_call | solution.py:908
  270.4 0.8 multiply_reduce_fusion.1
  271.4 1.1 multiply_add_fusion.1
  272.6 21.7 %conv_back.1 = (f32[128,1024]{1,0:T(8,128)S(1)}, bf16[128,1024]{1,0:T(8,128)(2,1)S(1)}, bf16[128,1024]{1,0:T(8,128)(2,1)S(1)}, bf16[128,2048]{1,0:T(8,128)(2,1)S(1)}, f32[16,1024]{1,0:T(8,128)S(1)}) custom-call(f32[128,1024]{1,0:T(8,128)S(1)} %get-tuple-element.141.refs_0_, f32[16,1024]{1,0:T(8,128)S(1)} %concatenate.9.refs_1_, f32[128,8]{1,0:T(8,128)S(1)} %pad.13.refs_2_, ...), custom_call_target="tpu_custom_call" | custom-call | tf_op jit(solution)/shard_map/conv_back/pallas_call | solution.py:1214
  294.4 0.8 copy-done.19
  295.2 0.7 copy-done.32
  296.0 16.7 %attend_back.1 = (f32[128,1024]{1,0:T(8,128)S(1)}, bf16[128,3072]{1,0:T(8,128)(2,1)S(1)}, f32[128,128]{1,0:T(8,128)S(1)}) custom-call(bf16[128,1024]{1,0:T(8,128)(2,1)S(1)} %get-tuple-element.92.refs_0_.refs_15_, bf16[3,256,512]{2,1,0:T(8,128)(2,1)S(1)} %copy-done.14, f32[4,256,256]{2,1,0:T(8,128)S(1)} %copy-done.7, bf16[128,128]{1,0:T(8,128)(2,1)S(1)} %pad.12.refs_3_, ...), custom_call_target="tpu_custom_call" | custom-call | tf_op jit(solution)/shard_map/attend_back/pallas_call | solution.py:750
  313.0 1.1 multiply_convert_fusion
  314.1 0.7 copy-done.3
  314.8 14.2 %ffn_back.3 = (f32[128,1024]{1,0:T(8,128)S(1)}, bf16[256,2048]{1,0:T(8,128)(2,1)S(1)}, bf16[256,1024]{1,0:T(8,128)(2,1)S(1)}) custom-call(bf16[128,1024]{1,0:T(8,128)(2,1)S(1)} %get-tuple-element.133.refs_0_, f32[256,2048]{1,0:T(8,128)S(1)} %copy-done.3, bf16[1024,2048]{1,0:T(8,128)(2,1)} %bitcast.118, bf16[2048,1024]{1,0:T(8,128)(2,1)} %bitcast.120), custom_call_target="tpu_custom_call" | custom-call | tf_op jit(solution)/shard_map/ffn_back/pallas_call | solution.py:908
  329.0 1.0 copy-done.9
  330.0 0.9 multiply_reduce_fusion.3
  330.9 0.6 fusion.8
  331.7 0.7 reshape.305.refs_16_
  332.4 1.3 copy.92
  333.7 2.1 copy.93
  335.8 1.8 copy.96
  337.6 1.8 copy.98
  339.4 0.8 copy.99
  340.3 0.8 fusion.11
  341.1 0.8 copy.97
  341.9 1.3 copy.95
  343.2 1.0 copy.94
  344.2 154.7 %reduce_gradients.1 = (f32[23,32,1024]{2,1,0:T(8,128)}, f32[2,2,2,32,1024]{4,3,2,1,0:T(8,128)}, f32[32,1024]{1,0:T(8,128)}) custom-call(bf16[2,2,2,2,128,256]{5,4,3,2,1,0:T(8,128)(2,1)} %bitcast.133, bf16[2,2,2,2,64,256]{5,4,3,2,1,0:T(8,128)(2,1)} %bitcast.135, bf16[2,2,2,2,64,256]{5,4,3,2,1,0:T(8,128)(2,1)} %bitcast.136, ...), custom_call_target="tpu_custom_call" | custom-call | tf_op jit(solution)/shard_map/reduce_gradients/pallas_call | solution.py:435
  499.0 1.3 fusion.5
  500.8 1.2 reshape.306
  502.5 1.2 reshape.311
  503.7 1.2 slice_bitcast_fusion
  505.5 0.8 fusion.6
  506.2 1.1 fusion.4
  507.5 0.8 copy.106
  508.3 0.7 slice_bitcast_fusion.2
  509.1 0.6 slice.176
  509.7 0.6 fusion.7
  510.4 1.0 add_convert_fusion
  511.4 0.6 add_divide_fusion
  (186 shorter events, 6.8 us)
Async XLA Ops:
  0.7 171.1 %copy-start.37 = (bf16[128,1024]{1,0:T(8,128)(2,1)S(1)}, bf16[128,1024]{1,0:T(8,128)(2,1)}, u32[]{:S(2)}) copy-start(bf16[128,1024]{1,0:T(8,128)(2,1)} %param.19) | copy-start | bytes 786436
  2.3 190.2 %copy-start.44 = (f32[1,1024]{1,0:T(1,128)}, f32[1,1024]{1,0:T(1,128)S(1)}, u32[]{:S(2)}) copy-start(f32[1,1024]{1,0:T(1,128)S(1)} %get-tuple-element.171) | copy-start | bytes 12292
  3.4 168.4 %copy-start.56 = (f32[128]{0:T(128)}, f32[128]{0:T(128)S(1)}, u32[]{:S(2)}) copy-start(f32[128]{0:T(128)S(1)} %broadcast_multiply_fusion.11) | copy-start | bytes 1540
  4.6 184.5 %copy-start.62 = (f32[128]{0:T(128)}, f32[128]{0:T(128)S(1)}, u32[]{:S(2)}) copy-start(f32[128]{0:T(128)S(1)} %add_rsqrt_fusion.3) | copy-start | bytes 1540
  171.8 20.9 %copy-start.69 = (s32[1,4]{1,0:T(1,128)S(1)}, s32[1,4]{1,0:T(1,128)}, u32[]{:S(2)}) copy-start(s32[1,4]{1,0:T(1,128)} %param.20) | copy-start | bytes 52
  171.8 21.4 %copy-start.46 = (bf16[73,128]{1,0:T(8,128)(2,1)S(1)}, bf16[73,128]{1,0:T(8,128)(2,1)}, u32[]{:S(2)}) copy-start(bf16[73,128]{1,0:T(8,128)(2,1)} %param.33) | copy-start | bytes 56068
  189.1 1.3 copy-start.2
  190.4 1.0 copy-start.11
  192.1 1.6 copy-start
  192.3 18.6 %copy-start.54 = (f32[128]{0:T(128)}, f32[128]{0:T(128)S(1)}, u32[]{:S(2)}) copy-start(f32[128]{0:T(128)S(1)} %broadcast_multiply_fusion.10) | copy-start | bytes 1540
  193.7 20.6 %copy-start.53 = (bf16[5,1024]{1,0:T(8,128)(2,1)S(1)}, bf16[5,1024]{1,0:T(8,128)(2,1)}, u32[]{:S(2)}) copy-start(bf16[5,1024]{1,0:T(8,128)(2,1)} %param.32) | copy-start | bytes 30724
  193.7 20.6 %copy-start.65 = (f32[1024]{0:T(1024)S(1)}, f32[1024]{0:T(1024)}, u32[]{:S(2)}) copy-start(f32[1024]{0:T(1024)} %param.36) | copy-start | bytes 12292
  193.7 20.6 %copy-start.66 = (f32[1024]{0:T(1024)S(1)}, f32[1024]{0:T(1024)}, u32[]{:S(2)}) copy-start(f32[1024]{0:T(1024)} %param.37) | copy-start | bytes 12292
  210.9 1.0 copy-start.6
  211.9 0.9 copy-start.13
  214.5 24.3 %copy-start.48 = (f32[1,1024]{1,0:T(1,128)S(1)}, f32[1,1024]{1,0:T(1,128)}, u32[]{:S(2)}) copy-start(f32[1,1024]{1,0:T(1,128)} %get-tuple-element.169) | copy-start | bytes 12292
  233.7 0.8 copy-start.16
  234.5 0.8 copy-start.20
  235.3 0.8 copy-start.22
  236.1 0.8 copy-start.24
  236.9 0.8 copy-start.26
  239.1 16.0 %copy-start.40 = (bf16[128,1024]{1,0:T(8,128)(2,1)S(1)}, bf16[128,1024]{1,0:T(8,128)(2,1)}, u32[]{:S(2)}) copy-start(bf16[128,1024]{1,0:T(8,128)(2,1)} %param.21) | copy-start | bytes 786436
  239.1 16.1 %copy-start.61 = (f32[128]{0:T(128)S(1)}, f32[128]{0:T(128)}, u32[]{:S(2)}) copy-start(f32[128]{0:T(128)} %get-tuple-element.163) | copy-start | bytes 1540
  252.7 1.3 copy-start.4
  254.0 0.8 copy-start.31
  254.9 1.6 copy-start.5
  256.5 14.8 %copy-start.47 = (f32[1,1024]{1,0:T(1,128)S(1)}, f32[1,1024]{1,0:T(1,128)}, u32[]{:S(2)}) copy-start(f32[1,1024]{1,0:T(1,128)} %get-tuple-element.173) | copy-start | bytes 12292
  270.4 1.0 copy-start.8
  270.4 2.1 copy-start.18
  270.4 2.1 copy-start.17
  270.4 2.1 copy-start.21
  270.4 2.1 copy-start.23
  270.4 2.1 copy-start.25
  270.4 2.2 copy-start.27
  272.6 23.3 %copy-start.1 = (bf16[2,2,2,2,2,32,1024]{6,5,4,3,2,1,0:T(8,128)(2,1)S(1)}, bf16[2,2,2,2,2,32,1024]{6,5,4,3,2,1,0:T(8,128)(2,1)}, u32[]{:S(2)}) copy-start(bf16[2,2,2,2,2,32,1024]{6,5,4,3,2,1,0:T(8,128)(2,1)} %get-tuple-element.71) | copy-start | bytes 6291460
  272.6 23.3 %copy-start.7 = (f32[4,256,256]{2,1,0:T(8,128)S(1)}, f32[4,256,256]{2,1,0:T(8,128)}, u32[]{:S(2)}) copy-start(f32[4,256,256]{2,1,0:T(8,128)} %copy-done.6) | copy-start | bytes 3145732
  272.6 23.3 %copy-start.14 = (bf16[3,256,512]{2,1,0:T(8,128)(2,1)S(1)}, bf16[3,256,512]{2,1,0:T(8,128)(2,1)}, u32[]{:S(2)}) copy-start(bf16[3,256,512]{2,1,0:T(8,128)(2,1)} %copy-done.13) | copy-start | bytes 2359300
  294.4 0.8 copy-start.19
  295.9 16.8 %copy-start.10 = (bf16[128,1024]{1,0:T(8,128)(2,1)}, bf16[128,1024]{1,0:T(8,128)(2,1)S(1)}, u32[]{:S(2)}) copy-start(bf16[128,1024]{1,0:T(8,128)(2,1)S(1)} %get-tuple-element.92.refs_0_.refs_15_) | copy-start | bytes 786436
  295.9 16.8 %copy-start.55 = (f32[128]{0:T(128)S(1)}, f32[128]{0:T(128)}, u32[]{:S(2)}) copy-start(f32[128]{0:T(128)} %copy-done.54) | copy-start | bytes 1540
  295.9 16.8 %copy-start.60 = (f32[128]{0:T(128)S(1)}, f32[128]{0:T(128)}, u32[]{:S(2)}) copy-start(f32[128]{0:T(128)} %copy-done.59) | copy-start | bytes 1540
  312.7 16.3 %copy-start.15 = (bf16[128,3072]{1,0:T(8,128)(2,1)}, bf16[128,3072]{1,0:T(8,128)(2,1)S(1)}, u32[]{:S(2)}) copy-start(bf16[128,3072]{1,0:T(8,128)(2,1)S(1)} %get-tuple-element.110.refs_13_) | copy-start | bytes 2359300
  312.7 2.1 copy-start.3
  314.8 15.2 %copy-start.38 = (bf16[128,1024]{1,0:T(8,128)(2,1)S(1)}, bf16[128,1024]{1,0:T(8,128)(2,1)}, u32[]{:S(2)}) copy-start(bf16[128,1024]{1,0:T(8,128)(2,1)} %param.19) | copy-start | bytes 786436
  314.8 15.2 %copy-start.57 = (f32[128]{0:T(128)S(1)}, f32[128]{0:T(128)}, u32[]{:S(2)}) copy-start(f32[128]{0:T(128)} %copy-done.56) | copy-start | bytes 1540
  314.8 15.2 %copy-start.63 = (f32[128]{0:T(128)S(1)}, f32[128]{0:T(128)}, u32[]{:S(2)}) copy-start(f32[128]{0:T(128)} %copy-done.62) | copy-start | bytes 1540
  314.8 16.7 %copy-start.50 = (f32[1024]{0:T(1024)S(1)}, f32[1024]{0:T(1024)}, u32[]{:S(2)}) copy-start(f32[1024]{0:T(1024)} %get-tuple-element.121) | copy-start | bytes 12292
  314.8 16.7 %copy-start.52 = (f32[1024]{0:T(1024)S(1)}, f32[1024]{0:T(1024)}, u32[]{:S(2)}) copy-start(f32[1024]{0:T(1024)} %get-tuple-element.117) | copy-start | bytes 12292
  314.8 16.8 %copy-start.49 = (f32[1024]{0:T(1024)S(1)}, f32[1024]{0:T(1024)}, u32[]{:S(2)}) copy-start(f32[1024]{0:T(1024)} %get-tuple-element.132) | copy-start | bytes 12292
  314.8 16.8 %copy-start.51 = (f32[1024]{0:T(1024)S(1)}, f32[1024]{0:T(1024)}, u32[]{:S(2)}) copy-start(f32[1024]{0:T(1024)} %get-tuple-element.128) | copy-start | bytes 12292
  329.0 1.0 copy-start.9
  330.0 2.4 copy-start.28
  330.0 9.4 %copy-start.34 = (bf16[128,1024]{1,0:T(8,128)(2,1)S(1)}, bf16[128,1024]{1,0:T(8,128)(2,1)}, u32[]{:S(2)}) copy-start(bf16[128,1024]{1,0:T(8,128)(2,1)} %copy-done.33) | copy-start | bytes 786436
  330.9 9.3 %copy-start.45 = (f32[1,1024]{1,0:T(1,128)S(1)}, f32[1,1024]{1,0:T(1,128)}, u32[]{:S(2)}) copy-start(f32[1,1024]{1,0:T(1,128)} %copy-done.44) | copy-start | bytes 12292
  332.4 9.5 %copy-start.12 = (bf16[256,2048]{1,0:T(8,128)(2,1)S(1)}, bf16[256,2048]{1,0:T(8,128)(2,1)}, u32[]{:S(2)}) copy-start(bf16[256,2048]{1,0:T(8,128)(2,1)} %copy-done.11) | copy-start | bytes 3145732
  333.7 9.5 %copy-start.30 = (bf16[256,1024]{1,0:T(8,128)(2,1)S(1)}, bf16[256,1024]{1,0:T(8,128)(2,1)}, u32[]{:S(2)}) copy-start(bf16[256,1024]{1,0:T(8,128)(2,1)} %copy-done.29) | copy-start | bytes 1572868
  503.7 2.5 copy-start.42
  505.2 3.9 copy-start.43
  505.2 5.2 %copy-start.68 = (f32[128]{0:T(128)S(1)}, f32[128]{0:T(128)}, u32[]{:S(2)}) copy-start(f32[128]{0:T(128)} %get-tuple-element.124) | copy-start | bytes 1540
  505.2 5.2 %copy-start.67 = (f32[128]{0:T(128)S(1)}, f32[128]{0:T(128)}, u32[]{:S(2)}) copy-start(f32[128]{0:T(128)} %get-tuple-element.125) | copy-start | bytes 1540
  505.2 5.2 %copy-start.39 = (bf16[128,1024]{1,0:T(8,128)(2,1)S(1)}, bf16[128,1024]{1,0:T(8,128)(2,1)}, u32[]{:S(2)}) copy-start(bf16[128,1024]{1,0:T(8,128)(2,1)} %param.19) | copy-start | bytes 786436
  505.2 5.2 %copy-start.41 = (f32[128,1024]{1,0:T(8,128)S(1)}, f32[128,1024]{1,0:T(8,128)}, u32[]{:S(2)}) copy-start(f32[128,1024]{1,0:T(8,128)} %get-tuple-element.134) | copy-start | bytes 1572868
  505.2 5.2 %copy-start.58 = (f32[128]{0:T(128)S(1)}, f32[128]{0:T(128)}, u32[]{:S(2)}) copy-start(f32[128]{0:T(128)} %copy-done.56) | copy-start | bytes 1540
  505.2 5.2 %copy-start.64 = (f32[128]{0:T(128)S(1)}, f32[128]{0:T(128)}, u32[]{:S(2)}) copy-start(f32[128]{0:T(128)} %copy-done.62) | copy-start | bytes 1540
  (6 other events, 4.1 us)

commit v7 on v6

--- a/solution.py
+++ b/solution.py
@@ -12,6 +12,8 @@
 AXES = ("batch", "seq")
 ALL_SHARES = (3, 1, 0)
 ROWS = 64
+PACE = 1
+TURNS = (1, 0, 3, 4, 5, 8, 6, 2, 7, 9)
 HALF_SHARES = (5, 3)
 PAIR_SHARES = (2, 2)
 
@@ -83,10 +85,11 @@
     pl.semaphore_wait(barrier, len(bits))
 
 
-def gather_kernel(cube, plans, items, *refs):
+def gather_kernel(cube, plans, items, first_in, first_out, *refs):
     count = len(plans)
-    shards, outs = (refs[:count], refs[count : 2 * count])
-    send, recv, local = refs[2 * count :]
+    shards, (hidden, before), refs = (refs[:count], refs[count : count + 2], refs[count + 2 :])
+    outs, results, refs = (refs[:count], refs[count : count + 4], refs[count + 4 :])
+    (send, recv, local), scratch = (refs[:3], refs[3:])
     own = [cube.bit(k) for k in range(cube.count)]
     kept = []
     for m, (bits, paired) in enumerate(plans):
@@ -117,11 +120,17 @@
     for chunk in items:
         numbers.append(range(at, at + len(chunk)))
         at += len(chunk)
+    arrive, steps = ffn_steps(
+        cube, hidden, before, outs[first_in].at, outs[first_out].at, *results, *scratch
+    )
+    arrive[0]()
     for number in range(len(flat)):
         copy(number, 0).start()
     for one in kept:
         one.wait()
     most = max(len(order) for _, order, _ in flat)
+    waiting = {m: sum(item[0] == m for item in flat) for m in (first_in, first_out)}
+    pending = []
     for turn in range(len(items) + most):
         for stage in range(most):
             for late in (0, 1):
@@ -135,6 +144,21 @@
                     copy(number, stage).wait_recv()
                     if stage + 1 < stages:
                         copy(number, stage + 1).start()
+                    elif flat[number][0] in waiting:
+                        waiting[flat[number][0]] -= 1
+        if waiting[first_in] == 0:
+            waiting[first_in] = -1
+            arrive[1]()
+            pending += steps[0]
+        if waiting[first_out] == 0 and waiting[first_in] < 0:
+            waiting[first_out] = -1
+            arrive[2]()
+            pending += steps[1]
+        for _ in range(PACE):
+            if pending:
+                pending.pop(0)()
+    for step in pending:
+        step()
     for number, (_, order, _) in enumerate(flat):
         for stage in range(len(order)):
             copy(number, stage).wait_send()
@@ -150,7 +174,7 @@
     return parts
 
 
-def gather_fast(shards, kinds, cube):
+def gather_fast(shards, kinds, cube, hidden, values, first_in, first_out):
     core, x, y, z = ([cube.core], cube.x, cube.y, cube.z)
     every = list(range(cube.count))[::-1]
     plans, items, shapes = ([], [], [])
@@ -176,22 +200,42 @@
                     ]
                 )
     count, copies = (len(shards), sum(len(chunk) for chunk in items))
+    local, width = values.shape
+    wide = shards[first_in].shape[-1]
+    vmem = pl.BlockSpec(memory_space=pltpu.VMEM)
     outs = pl.pallas_call(
-        functools.partial(gather_kernel, cube, plans, items),
+        functools.partial(gather_kernel, cube, plans, items, first_in, first_out),
         out_shape=[
             jax.ShapeDtypeStruct(shape, shard.dtype) for shape, shard in zip(shapes, shards)
+        ]
+        + [
+            jax.ShapeDtypeStruct((local, width), jnp.float32),
+            jax.ShapeDtypeStruct((2 * local, wide), jnp.float32),
+            jax.ShapeDtypeStruct((2 * local, wide), jnp.bfloat16),
+            jax.ShapeDtypeStruct((2 * local, width), jnp.bfloat16),
         ],
-        in_specs=[pl.BlockSpec(memory_space=pl.ANY)] * count,
-        out_specs=[pl.BlockSpec(memory_space=pl.ANY)] * count,
+        in_specs=[pl.BlockSpec(memory_space=pl.ANY)] * count + [vmem] * 2,
+        out_specs=[pl.BlockSpec(memory_space=pl.ANY)] * count + [vmem] * 4,
         scratch_shapes=[
             pltpu.SemaphoreType.DMA((copies, cube.count)),
             pltpu.SemaphoreType.DMA((copies, cube.count)),
             pltpu.SemaphoreType.DMA((count,)),
+            pltpu.VMEM(shapes[first_in], jnp.bfloat16),
+            pltpu.VMEM(shapes[first_out], jnp.bfloat16),
+            pltpu.VMEM((2 * local, width), jnp.bfloat16),
+            pltpu.VMEM((local, width), jnp.bfloat16),
+            pltpu.VMEM((local, width), jnp.bfloat16),
+            pltpu.SemaphoreType.DMA((5,)),
+            pltpu.SemaphoreType.DMA((3,)),
+            pltpu.SemaphoreType.DMA((3,)),
         ],
-        compiler_params=pltpu.CompilerParams(collective_id=0, has_side_effects=True),
+        compiler_params=pltpu.CompilerParams(
+            collective_id=0, has_side_effects=True, vmem_limit_bytes=48 * 1024 * 1024
+        ),
         name="gather_weights",
-    )(*shards)
-    return tuple(out.reshape(-1, shard.shape[-1]) for out, shard in zip(outs, shards))
+    )(*shards, hidden, values)
+    whole = tuple(out.reshape(-1, shard.shape[-1]) for out, shard in zip(outs, shards))
+    return whole, outs[count:]
 
 
 def gradient_kernel(cube, shapes, kinds, tile, *refs):
@@ -503,14 +547,22 @@
     return shard.reshape(rows, columns // 256, 2, 128).transpose(2, 0, 1, 3).reshape(2, rows, -1)
 
 
-def gather_all(shards, cube):
+def gather_all(shards, cube, hidden, values):
     if cube is None:
-        return tuple(lax.all_gather(shard, AXES, axis=0, tiled=True) for shard in shards)
+        return tuple(lax.all_gather(shard, AXES, axis=0, tiled=True) for shard in shards), None
     kinds = ("pair", "half") + ("all",) * 6 + ("pair", "half")
     shards = [parities(shard) if kind == "pair" else shard for shard, kind in zip(shards, kinds)]
-    turns = (2, 6, 0, 3, 4, 8, 5, 7, 1, 9)
-    outs = gather_fast([shards[m] for m in turns], [kinds[m] for m in turns], cube)
-    return tuple(outs[turns.index(m)] for m in range(len(shards)))
+    turns = TURNS
+    outs, first = gather_fast(
+        [shards[m] for m in turns],
+        [kinds[m] for m in turns],
+        cube,
+        hidden,
+        values,
+        turns.index(0),
+        turns.index(1),
+    )
+    return tuple(outs[turns.index(m)] for m in range(len(shards))), first
 
 
 def distance_rows(group, left, right, backwards):
@@ -775,64 +827,110 @@
     )(branch, heads_in, probs, table, *matrices)
 
 
+def ffn_steps(
+    cube,
+    hidden,
+    before,
+    weight_in,
+    weight_out,
+    after,
+    act,
+    swish,
+    hidden_out,
+    into,
+    outof,
+    both,
+    away,
+    arrived,
+    load,
+    send,
+    recv,
+):
+    rows, width = hidden.shape
+    depth, wide = into.shape[-2:]
+    step, half = (wide // 4, width // 2)
+    _, _, own_rows, away_rows = halves(cube, rows, half)
+    exchange = to_partner(cube, 0, both.at[own_rows], both.at[own_rows], send.at[0], recv.at[0])
+    lead = (slice(None),) * (len(into.shape) - 2)
+
+    def load_in(q):
+        part = lead + (slice(None), pl.ds(q * step, step))
+        return pltpu.make_async_copy(weight_in[part], into.at[part], load.at[q])
+
+    def load_out():
+        whole = (slice(None),) * len(outof.shape)
+        return pltpu.make_async_copy(weight_out[whole], outof.at[whole], load.at[4])
+
+    def back(q):
+        part = pl.ds(q * half, half)
+        return to_partner(
+            cube, 0, away.at[:, part], arrived.at[:, part], send.at[1 + q], recv.at[1 + q]
+        )
+
+    def begin():
+        both[own_rows, :] = hidden[...]
+        exchange.start()
+
+    def first_there():
+        for q in range(4):
+            load_in(q).start()
+
+    def second_there():
+        load_out().start()
+
+    def activate(q, rows_here, wait):
+        wait()
+        part = pl.ds(q * step, step)
+        weights = into[lead + (slice(None), part)].reshape(width, step)
+        value = matmul(both[rows_here, :], weights)
+        act[rows_here, part] = value
+        swish[rows_here, part] = jax.nn.silu(value).astype(jnp.bfloat16)
+
+    def there(q):
+        if q == 0:
+            load_out().wait()
+        part = pl.ds(q * half, half)
+        weights = outof[(slice(None),) * (len(outof.shape) - 1) + (part,)].reshape(wide, half)
+        away[:, part] = matmul(swish[away_rows, :], weights).astype(jnp.bfloat16)
+        back(q).start()
+
+    def here(q):
+        part = pl.ds(q * half, half)
+        weights = outof[(slice(None),) * (len(outof.shape) - 1) + (part,)].reshape(wide, half)
+        after[:, part] = before[:, part] + 0.5 * matmul(swish[own_rows, :], weights)
+
+    def end():
+        hidden_out[...] = both[...]
+        for q in range(2):
+            part = pl.ds(q * half, half)
+            back(q).wait_recv()
+            after[:, part] += 0.5 * arrived[:, part].astype(jnp.float32)
+        exchange.wait_send()
+        for q in range(2):
+            back(q).wait_send()
+
+    def nothing():
+        pass
+
+    one = [functools.partial(activate, q, own_rows, load_in(q).wait) for q in range(4)]
+    one += [
+        functools.partial(activate, q, away_rows, nothing if q else exchange.wait_recv)
+        for q in range(4)
+    ]
+    two = [functools.partial(there, q) for q in range(2)]
+    two += [functools.partial(here, q) for q in range(2)] + [end]
+    return (begin, first_there, second_there), (one, two)
+
+
 def ffn_kernel(cube, *refs):
     hidden, before, weight_in, weight_out = refs[:4]
-    after, act, swish, hidden_out = refs[4:8]
-    into, outof, both, away, arrived, load, send, recv = refs[8:]
-    rows, width = hidden.shape
-    wide = into.shape[1]
-    step = wide // 4
-    own_columns, away_columns, own_rows, away_rows = halves(cube, rows, width // 2)
-    loads = []
-    for q in range(4):
-        part = pl.ds(q * step, step)
-        loads.append(
-            pltpu.make_async_copy(weight_in.at[:, part], into.at[:, part], load.at[q])
-        )
-    loads.append(pltpu.make_async_copy(weight_out, outof, load.at[4]))
-    for one in loads:
-        one.start()
-    both[own_rows, :] = hidden[...]
+    arrive, steps = ffn_steps(cube, hidden, before, weight_in.at, weight_out.at, *refs[4:])
+    arrive[1]()
+    arrive[2]()
     greet(cube, [0])
-    exchange = to_partner(
-        cube, 0, both.at[own_rows], both.at[own_rows], send.at[0], recv.at[0]
-    )
-    exchange.start()
-
-    def activate(q, rows_here):
-        part = pl.ds(q * step, step)
-        value = matmul(both[rows_here, :], into[:, part])
-        act[rows_here, part] = value
-        swish[rows_here, part] = jax.nn.silu(value).astype(jnp.bfloat16)
-
-    for q in range(4):
-        loads[q].wait()
-        activate(q, own_rows)
-    loads[4].wait()
-    exchange.wait_recv()
-    for q in range(4):
-        activate(q, away_rows)
-    half = width // 2
-    back = []
-    for q in range(2):
-        part = pl.ds(q * half, half)
-        away[:, part] = matmul(swish[away_rows, :], outof[:, part]).astype(jnp.bfloat16)
-        back.append(
-            to_partner(
-                cube, 0, away.at[:, part], arrived.at[:, part], send.at[1 + q], recv.at[1 + q]
-            )
-        )
-        back[q].start()
-    hidden_out[...] = both[...]
-    for q in range(2):
-        part = pl.ds(q * half, half)
-        after[:, part] = before[:, part] + 0.5 * matmul(swish[own_rows, :], outof[:, part])
-    for q in range(2):
-        part = pl.ds(q * half, half)
-        back[q].wait_recv()
-        after[:, part] += 0.5 * arrived[:, part].astype(jnp.float32)
-    for one in [exchange] + back:
-        one.wait_send()
+    arrive[0]()
+    for step in steps[0] + steps[1]:
+        step()
 
 
 def ffn_back_kernel(cube, *refs):
@@ -1474,11 +1572,20 @@
         ffn2_out,
     )
     cube = cube_of(shards, rel_table, depth_w)
-    gathered = gather_all(shards, cube)
     start_values = frames.astype(jnp.float32)
-    after_first, kept_first = ffn_forward(
-        start_values, norm_gains[0], norm_biases[0], gathered[0], gathered[1], cube, 7
-    )
+    first_norm, first_unit, first_inverse = norm_forward(
+        start_values, norm_gains[0], norm_biases[0]
+    )
+    gathered, kept_first = gather_all(
+        shards, cube, first_norm.astype(jnp.bfloat16), start_values
+    )
+    if cube is None:
+        after_first, kept_first = ffn_forward(
+            start_values, norm_gains[0], norm_biases[0], gathered[0], gathered[1], cube, 7
+        )
+    else:
+        after_first, act, swish, hidden = kept_first
+        kept_first = (hidden, act, swish, first_unit, first_inverse)
     attn_norm, attn_unit, attn_inverse = norm_forward(after_first, norm_gains[1], norm_biases[1])
     attn_hidden = attn_norm.astype(jnp.bfloat16)
     if cube is None:

time: 521 us -> 510 us (0.979)
  Pallas kernels: 450 us -> 442 us
    pallas_call x4 -> x3, Pallas kernels: 58.7 us -> 42.3 us  [ffn_fast(): pl.pallas_call(functools.partial(ffn_back_kernel if backward else ffn_ker...]
    pallas_call x1, Pallas kernels: 162 us -> 170 us  [gather_fast(): pl.pallas_call(functools.partial(gather_kernel, cube, plans, items, first...]
    unnamed x144 -> x158, local copies, waits for them, and re-layouts: 18.4 us -> 17.1 us
where the time goes in v7:
time: 510 us; the launch traced here: 502 us
  Pallas kernels  442 us (87%)
  local copies, waits for them, and re-layouts  43.9 us (9%)
  other arithmetic  13.5 us (3%)
    pallas_call x1, Pallas kernels, gather_fast(): pl.pallas_call(functools.partial(gather_kernel, cube, plans, items, first...  170 us
    pallas_call x1, Pallas kernels, gradients_fast(): pl.pallas_call(functools.partial(gradient_kernel, cube, shapes, kinds, ti...  154 us
    pallas_call x3, Pallas kernels, ffn_fast(): pl.pallas_call(functools.partial(ffn_back_kernel if backward else ffn_ker...  42.3 us
    pallas_call x2, Pallas kernels, conv_fast(): pl.pallas_call(functools.partial(conv_kernel if forward else conv_back_ke...  41 us
    pallas_call x1, Pallas kernels, attend_fast(): pl.pallas_call(functools.partial(attend_kernel, cube, REL_LEFT, REL_RIGHT...  17.8 us
    unnamed x158, local copies, waits for them, and re-layouts  17.1 us
    pallas_call x1, Pallas kernels, attend_back_fast(): pl.pallas_call(functools.partial(attend_back_kernel, cube, REL_LEFT, REL_...  16.6 us

profile of v7, /device:TPU:0, one launch (start us, length us, event | category | flops | bytes accessed | tf_op | source)
XLA Modules:
  0.0 502.0 jit_solution(6853052418629652322)
XLA Ops:
  0.8 1.6 fusion.9
  2.4 1.1 convert_reduce_fusion
  3.5 1.2 multiply_reduce_fusion.11
  4.7 1.2 add_convert_fusion.4.refs_10_
  5.9 1.1 reshape.277
  7.2 1.1 reshape.279
  8.6 170.4 %gather_weights.1 = (bf16[2,2,2,2,128,1024]{5,4,3,2,1,0:T(8,128)(2,1)}, bf16[2,2,2,2,2,32,2048]{6,5,4,3,2,1,0:T(8,128)(2,1)}, bf16[2,2,2,2,2,32,1024]{6,5,4,3,2,...) custom-call(bf16[128,1024]{1,0:T(8,128)(2,1)S(1)} %copy-done.31, ...), custom_call_target="tpu_custom_call" | custom-call | tf_op jit(solution)/shard_map/gather_weights/pallas_call | solution.py:206
  179.1 1.0 copy-done.10
  180.0 0.8 copy-done.28
  181.9 0.5 copy-done
  182.4 17.8 %attend.1 = (f32[128,1024]{1,0:T(8,128)S(1)}, bf16[128,1024]{1,0:T(8,128)(2,1)S(1)}, bf16[3,256,512]{2,1,0:T(8,128)(2,1)S(1)}, f32[4,256,256]{2,1,0:T(8,128)S(1)}) custom-call(bf16[128,1024]{1,0:T(8,128)(2,1)S(1)} %add_convert_fusion.3.refs_0_, f32[128,1024]{1,0:T(8,128)S(1)} %get-tuple-element.68.refs_1_, f32[256,256]{1,0:T(8,128)S(1)} %compare_convert_fusion.refs_2_, ...), custom_call_target="tpu_custom_call" | custom-call | tf_op jit(solution)/shard_map/attend/pallas_call | solution.py:672
  200.2 1.0 copy-done.5
  201.3 0.9 copy-done.12
  202.1 0.7 copy-done.34
  202.9 0.6 compare_convert_fusion.1
  203.8 19.4 %conv.1 = (f32[128,1024]{1,0:T(8,128)S(1)}, f32[128,1024]{1,0:T(8,128)S(1)}, f32[128,128]{1,0:T(8,128)S(1)}, bf16[128,1024]{1,0:T(8,128)(2,1)S(1)}, f32[128,1024...) custom-call(f32[128,1024]{1,0:T(8,128)S(1)} %get-tuple-element.73.re, ...), custom_call_target="tpu_custom_call" | custom-call | tf_op jit(solution)/shard_map/conv/pallas_call | solution.py:1312
  223.3 0.8 copy-done.15
  224.1 0.8 copy-done.19
  224.9 0.8 copy-done.21
  225.7 0.8 copy-done.23
  226.5 0.8 copy-done.25
  227.3 0.7 copy-done.36
  228.7 13.8 %ffn.1 = (f32[128,1024]{1,0:T(8,128)S(1)}, f32[256,2048]{1,0:T(8,128)S(1)}, bf16[256,2048]{1,0:T(8,128)(2,1)S(1)}, bf16[256,1024]{1,0:T(8,128)(2,1)S(1)}) custom-call(bf16[128,1024]{1,0:T(8,128)(2,1)S(1)} %add_convert_fusion.2.refs_0_, f32[128,1024]{1,0:T(8,128)S(1)} %get-tuple-element.76.refs_1_, bf16[1024,2048]{1,0:T(8,128)(2,1)} %bitcast.117, ...), custom_call_target="tpu_custom_call" | custom-call | tf_op jit(solution)/shard_map/ffn/pallas_call | solution.py:1006
  242.5 1.3 copy-done.3
  243.8 0.8 copy-done.30
  245.0 0.9 multiply_reduce_fusion
  246.3 13.8 %ffn_back.2 = (f32[128,1024]{1,0:T(8,128)S(1)}, bf16[256,2048]{1,0:T(8,128)(2,1)S(1)}, bf16[256,1024]{1,0:T(8,128)(2,1)S(1)}) custom-call(bf16[128,1024]{1,0:T(8,128)(2,1)S(1)} %multiply_convert_fusion.1.refs_0_, f32[256,2048]{1,0:T(8,128)S(1)} %copy-done.4, bf16[1024,2048]{1,0:T(8,128)(2,1)} %bitcast.118, bf16[2048,1024]{1,0:T(8,128)(2,1)} %bitcast.120), custom_call_target="tpu_custom_call" | custom-call | tf_op jit(solution)/shard_map/ffn_back/pallas_call | solution.py:1006
  260.2 0.8 multiply_reduce_fusion.1
  261.1 1.1 multiply_add_fusion.1
  262.4 21.6 %conv_back.1 = (f32[128,1024]{1,0:T(8,128)S(1)}, bf16[128,1024]{1,0:T(8,128)(2,1)S(1)}, bf16[128,1024]{1,0:T(8,128)(2,1)S(1)}, bf16[128,2048]{1,0:T(8,128)(2,1)S(1)}, f32[16,1024]{1,0:T(8,128)S(1)}) custom-call(f32[128,1024]{1,0:T(8,128)S(1)} %get-tuple-element.141.refs_0_, f32[16,1024]{1,0:T(8,128)S(1)} %concatenate.9.refs_1_, f32[128,8]{1,0:T(8,128)S(1)} %pad.13.refs_2_, ...), custom_call_target="tpu_custom_call" | custom-call | tf_op jit(solution)/shard_map/conv_back/pallas_call | solution.py:1312
  284.0 0.8 copy-done.18
  284.8 0.7 copy-done.33
  285.5 16.6 %attend_back.1 = (f32[128,1024]{1,0:T(8,128)S(1)}, bf16[128,3072]{1,0:T(8,128)(2,1)S(1)}, f32[128,128]{1,0:T(8,128)S(1)}) custom-call(bf16[128,1024]{1,0:T(8,128)(2,1)S(1)} %get-tuple-element.90.refs_0_.refs_15_, bf16[3,256,512]{2,1,0:T(8,128)(2,1)S(1)} %copy-done.13, f32[4,256,256]{2,1,0:T(8,128)S(1)} %copy-done.6, bf16[128,128]{1,0:T(8,128)(2,1)S(1)} %pad.12.refs_3_, ...), custom_call_target="tpu_custom_call" | custom-call | tf_op jit(solution)/shard_map/attend_back/pallas_call | solution.py:802
  302.4 1.1 multiply_convert_fusion
  303.5 0.7 copy-done.2
  304.3 14.8 %ffn_back.3 = (f32[128,1024]{1,0:T(8,128)S(1)}, bf16[256,2048]{1,0:T(8,128)(2,1)S(1)}, bf16[256,1024]{1,0:T(8,128)(2,1)S(1)}) custom-call(bf16[128,1024]{1,0:T(8,128)(2,1)S(1)} %get-tuple-element.133.refs_0_, f32[256,2048]{1,0:T(8,128)S(1)} %copy-done.2, bf16[1024,2048]{1,0:T(8,128)(2,1)} %bitcast.132, bf16[2048,1024]{1,0:T(8,128)(2,1)} %bitcast.131), custom_call_target="tpu_custom_call" | custom-call | tf_op jit(solution)/shard_map/ffn_back/pallas_call | solution.py:1006
  319.0 1.0 copy-done.8
  320.0 0.9 multiply_reduce_fusion.3
  320.9 0.6 fusion.8
  321.7 0.7 reshape.305.refs_16_
  322.4 1.3 copy.92
  323.7 2.1 copy.93
  325.8 1.8 copy.96
  327.6 1.8 copy.98
  329.4 0.8 copy.99
  330.2 0.8 fusion.11
  331.1 0.8 copy.97
  331.9 1.3 copy.95
  333.2 1.0 copy.94
  334.2 154.3 %reduce_gradients.1 = (f32[23,32,1024]{2,1,0:T(8,128)}, f32[2,2,2,32,1024]{4,3,2,1,0:T(8,128)}, f32[32,1024]{1,0:T(8,128)}) custom-call(bf16[2,2,2,2,128,256]{5,4,3,2,1,0:T(8,128)(2,1)} %bitcast.129, bf16[2,2,2,2,64,256]{5,4,3,2,1,0:T(8,128)(2,1)} %bitcast.133, bf16[2,2,2,2,64,256]{5,4,3,2,1,0:T(8,128)(2,1)} %bitcast.134, ...), custom_call_target="tpu_custom_call" | custom-call | tf_op jit(solution)/shard_map/reduce_gradients/pallas_call | solution.py:479
  488.6 1.3 fusion.5
  489.9 0.4 copy.100
  490.4 1.2 reshape.306
  491.7 0.4 copy.103
  492.1 1.2 reshape.311
  493.3 1.2 slice_bitcast_fusion
  495.1 0.8 fusion.6
  495.8 1.1 fusion.4
  497.1 0.8 copy.106
  497.9 0.7 slice_bitcast_fusion.2
  498.7 0.6 slice.176
  499.3 0.6 fusion.7
  500.0 1.0 add_convert_fusion
  501.0 0.6 add_divide_fusion
  (199 shorter events, 5.1 us)
Async XLA Ops:
  0.7 7.8 %copy-start.44 = (bf16[128,1024]{1,0:T(8,128)(2,1)S(1)}, bf16[128,1024]{1,0:T(8,128)(2,1)}, u32[]{:S(2)}) copy-start(bf16[128,1024]{1,0:T(8,128)(2,1)} %param.19) | copy-start | bytes 786436
  0.7 7.9 %copy-start.31 = (bf16[128,1024]{1,0:T(8,128)(2,1)S(1)}, bf16[128,1024]{1,0:T(8,128)(2,1)}, u32[]{:S(2)}) copy-start(bf16[128,1024]{1,0:T(8,128)(2,1)} %refs_0_.1) | copy-start | bytes 786436
  0.7 7.9 %copy-start.42 = (bf16[32,1024]{1,0:T(8,128)(2,1)S(1)}, bf16[32,1024]{1,0:T(8,128)(2,1)}, u32[]{:S(2)}) copy-start(bf16[32,1024]{1,0:T(8,128)(2,1)} %refs_7_.1) | copy-start | bytes 196612
  0.7 7.9 %copy-start.39 = (bf16[32,1024]{1,0:T(8,128)(2,1)S(1)}, bf16[32,1024]{1,0:T(8,128)(2,1)}, u32[]{:S(2)}) copy-start(bf16[32,1024]{1,0:T(8,128)(2,1)} %refs_2_.1) | copy-start | bytes 196612
  0.7 7.9 %copy-start.40 = (bf16[32,1024]{1,0:T(8,128)(2,1)S(1)}, bf16[32,1024]{1,0:T(8,128)(2,1)}, u32[]{:S(2)}) copy-start(bf16[32,1024]{1,0:T(8,128)(2,1)} %refs_3_.1) | copy-start | bytes 196612
  0.7 7.9 %copy-start.41 = (bf16[32,1024]{1,0:T(8,128)(2,1)S(1)}, bf16[32,1024]{1,0:T(8,128)(2,1)}, u32[]{:S(2)}) copy-start(bf16[32,1024]{1,0:T(8,128)(2,1)} %refs_4_.1) | copy-start | bytes 196612
  0.7 7.9 %copy-start.38 = (bf16[32,2048]{1,0:T(8,128)(2,1)S(1)}, bf16[32,2048]{1,0:T(8,128)(2,1)}, u32[]{:S(2)}) copy-start(bf16[32,2048]{1,0:T(8,128)(2,1)} %refs_6_.1) | copy-start | bytes 393220
  0.7 7.9 %copy-start.43 = (bf16[32,1024]{1,0:T(8,128)(2,1)S(1)}, bf16[32,1024]{1,0:T(8,128)(2,1)}, u32[]{:S(2)}) copy-start(bf16[32,1024]{1,0:T(8,128)(2,1)} %refs_8_.1) | copy-start | bytes 196612
  0.7 7.9 %copy-start.32 = (bf16[128,1024]{1,0:T(8,128)(2,1)S(1)}, bf16[128,1024]{1,0:T(8,128)(2,1)}, u32[]{:S(2)}) copy-start(bf16[128,1024]{1,0:T(8,128)(2,1)} %refs_9_.1) | copy-start | bytes 786436
  2.4 178.8 %copy-start.51 = (f32[1,1024]{1,0:T(1,128)}, f32[1,1024]{1,0:T(1,128)S(1)}, u32[]{:S(2)}) copy-start(f32[1,1024]{1,0:T(1,128)S(1)} %get-tuple-element.171) | copy-start | bytes 12292
  3.5 175.5 %copy-start.63 = (f32[128]{0:T(128)}, f32[128]{0:T(128)S(1)}, u32[]{:S(2)}) copy-start(f32[128]{0:T(128)S(1)} %broadcast_multiply_fusion.11) | copy-start | bytes 1540
  4.7 174.4 %copy-start.69 = (f32[128]{0:T(128)}, f32[128]{0:T(128)S(1)}, u32[]{:S(2)}) copy-start(f32[128]{0:T(128)S(1)} %add_rsqrt_fusion.3) | copy-start | bytes 1540
  8.3 173.0 %copy-start.76 = (s32[1,4]{1,0:T(1,128)S(1)}, s32[1,4]{1,0:T(1,128)}, u32[]{:S(2)}) copy-start(s32[1,4]{1,0:T(1,128)} %param.20) | copy-start | bytes 52
  8.3 173.6 %copy-start.53 = (bf16[73,128]{1,0:T(8,128)(2,1)S(1)}, bf16[73,128]{1,0:T(8,128)(2,1)}, u32[]{:S(2)}) copy-start(bf16[73,128]{1,0:T(8,128)(2,1)} %param.33) | copy-start | bytes 56068
  179.0 1.0 copy-start.10
  180.8 1.6 copy-start
  180.9 19.3 %copy-start.61 = (f32[128]{0:T(128)}, f32[128]{0:T(128)S(1)}, u32[]{:S(2)}) copy-start(f32[128]{0:T(128)S(1)} %broadcast_multiply_fusion.10) | copy-start | bytes 1540
  182.4 21.3 %copy-start.60 = (bf16[5,1024]{1,0:T(8,128)(2,1)S(1)}, bf16[5,1024]{1,0:T(8,128)(2,1)}, u32[]{:S(2)}) copy-start(bf16[5,1024]{1,0:T(8,128)(2,1)} %param.32) | copy-start | bytes 30724
  182.4 21.3 %copy-start.72 = (f32[1024]{0:T(1024)S(1)}, f32[1024]{0:T(1024)}, u32[]{:S(2)}) copy-start(f32[1024]{0:T(1024)} %param.36) | copy-start | bytes 12292
  182.4 21.4 %copy-start.73 = (f32[1024]{0:T(1024)S(1)}, f32[1024]{0:T(1024)}, u32[]{:S(2)}) copy-start(f32[1024]{0:T(1024)} %param.37) | copy-start | bytes 12292
  200.2 1.0 copy-start.5
  201.3 0.9 copy-start.12
  203.8 24.5 %copy-start.55 = (f32[1,1024]{1,0:T(1,128)S(1)}, f32[1,1024]{1,0:T(1,128)}, u32[]{:S(2)}) copy-start(f32[1,1024]{1,0:T(1,128)} %get-tuple-element.169) | copy-start | bytes 12292
  228.7 16.3 %copy-start.47 = (bf16[128,1024]{1,0:T(8,128)(2,1)S(1)}, bf16[128,1024]{1,0:T(8,128)(2,1)}, u32[]{:S(2)}) copy-start(bf16[128,1024]{1,0:T(8,128)(2,1)} %param.21) | copy-start | bytes 786436
  228.7 16.3 %copy-start.68 = (f32[128]{0:T(128)S(1)}, f32[128]{0:T(128)}, u32[]{:S(2)}) copy-start(f32[128]{0:T(128)} %get-tuple-element.163) | copy-start | bytes 1540
  242.5 1.3 copy-start.3
  244.7 1.6 copy-start.4
  246.3 14.8 %copy-start.54 = (f32[1,1024]{1,0:T(1,128)S(1)}, f32[1,1024]{1,0:T(1,128)}, u32[]{:S(2)}) copy-start(f32[1,1024]{1,0:T(1,128)} %get-tuple-element.173) | copy-start | bytes 12292
  260.1 1.0 copy-start.7
  260.1 2.1 copy-start.17
  260.1 2.1 copy-start.16
  260.1 2.1 copy-start.20
  260.1 2.1 copy-start.22
  260.1 2.1 copy-start.24
  260.2 2.2 copy-start.26
  262.4 23.1 %copy-start.1 = (bf16[2,2,2,2,2,32,1024]{6,5,4,3,2,1,0:T(8,128)(2,1)S(1)}, bf16[2,2,2,2,2,32,1024]{6,5,4,3,2,1,0:T(8,128)(2,1)}, u32[]{:S(2)}) copy-start(bf16[2,2,2,2,2,32,1024]{6,5,4,3,2,1,0:T(8,128)(2,1)} %get-tuple-element.69) | copy-start | bytes 6291460
  262.4 23.1 %copy-start.6 = (f32[4,256,256]{2,1,0:T(8,128)S(1)}, f32[4,256,256]{2,1,0:T(8,128)}, u32[]{:S(2)}) copy-start(f32[4,256,256]{2,1,0:T(8,128)} %copy-done.5) | copy-start | bytes 3145732
  262.4 23.1 %copy-start.13 = (bf16[3,256,512]{2,1,0:T(8,128)(2,1)S(1)}, bf16[3,256,512]{2,1,0:T(8,128)(2,1)}, u32[]{:S(2)}) copy-start(bf16[3,256,512]{2,1,0:T(8,128)(2,1)} %copy-done.12) | copy-start | bytes 2359300
  285.5 16.6 %copy-start.9 = (bf16[128,1024]{1,0:T(8,128)(2,1)}, bf16[128,1024]{1,0:T(8,128)(2,1)S(1)}, u32[]{:S(2)}) copy-start(bf16[128,1024]{1,0:T(8,128)(2,1)S(1)} %get-tuple-element.90.refs_0_.refs_15_) | copy-start | bytes 786436
  285.5 16.6 %copy-start.62 = (f32[128]{0:T(128)S(1)}, f32[128]{0:T(128)}, u32[]{:S(2)}) copy-start(f32[128]{0:T(128)} %copy-done.61) | copy-start | bytes 1540
  285.5 16.6 %copy-start.67 = (f32[128]{0:T(128)S(1)}, f32[128]{0:T(128)}, u32[]{:S(2)}) copy-start(f32[128]{0:T(128)} %copy-done.66) | copy-start | bytes 1540
  302.1 16.9 %copy-start.14 = (bf16[128,3072]{1,0:T(8,128)(2,1)}, bf16[128,3072]{1,0:T(8,128)(2,1)S(1)}, u32[]{:S(2)}) copy-start(bf16[128,3072]{1,0:T(8,128)(2,1)S(1)} %get-tuple-element.110.refs_13_) | copy-start | bytes 2359300
  302.1 2.1 copy-start.2
  304.2 15.8 %copy-start.45 = (bf16[128,1024]{1,0:T(8,128)(2,1)S(1)}, bf16[128,1024]{1,0:T(8,128)(2,1)}, u32[]{:S(2)}) copy-start(bf16[128,1024]{1,0:T(8,128)(2,1)} %param.19) | copy-start | bytes 786436
  304.2 15.8 %copy-start.64 = (f32[128]{0:T(128)S(1)}, f32[128]{0:T(128)}, u32[]{:S(2)}) copy-start(f32[128]{0:T(128)} %copy-done.63) | copy-start | bytes 1540
  304.2 15.8 %copy-start.70 = (f32[128]{0:T(128)S(1)}, f32[128]{0:T(128)}, u32[]{:S(2)}) copy-start(f32[128]{0:T(128)} %copy-done.69) | copy-start | bytes 1540
  304.2 17.3 %copy-start.57 = (f32[1024]{0:T(1024)S(1)}, f32[1024]{0:T(1024)}, u32[]{:S(2)}) copy-start(f32[1024]{0:T(1024)} %get-tuple-element.121) | copy-start | bytes 12292
  304.2 17.3 %copy-start.59 = (f32[1024]{0:T(1024)S(1)}, f32[1024]{0:T(1024)}, u32[]{:S(2)}) copy-start(f32[1024]{0:T(1024)} %get-tuple-element.117) | copy-start | bytes 12292
  304.2 17.4 %copy-start.56 = (f32[1024]{0:T(1024)S(1)}, f32[1024]{0:T(1024)}, u32[]{:S(2)}) copy-start(f32[1024]{0:T(1024)} %get-tuple-element.132) | copy-start | bytes 12292
  304.2 17.4 %copy-start.58 = (f32[1024]{0:T(1024)S(1)}, f32[1024]{0:T(1024)}, u32[]{:S(2)}) copy-start(f32[1024]{0:T(1024)} %get-tuple-element.128) | copy-start | bytes 12292
  319.0 1.0 copy-start.8
  320.0 2.4 copy-start.27
  320.0 9.4 %copy-start.35 = (bf16[128,1024]{1,0:T(8,128)(2,1)S(1)}, bf16[128,1024]{1,0:T(8,128)(2,1)}, u32[]{:S(2)}) copy-start(bf16[128,1024]{1,0:T(8,128)(2,1)} %copy-done.34) | copy-start | bytes 786436
  320.9 9.3 %copy-start.52 = (f32[1,1024]{1,0:T(1,128)S(1)}, f32[1,1024]{1,0:T(1,128)}, u32[]{:S(2)}) copy-start(f32[1,1024]{1,0:T(1,128)} %copy-done.51) | copy-start | bytes 12292
  322.4 9.5 %copy-start.11 = (bf16[256,2048]{1,0:T(8,128)(2,1)S(1)}, bf16[256,2048]{1,0:T(8,128)(2,1)}, u32[]{:S(2)}) copy-start(bf16[256,2048]{1,0:T(8,128)(2,1)} %copy-done.10) | copy-start | bytes 3145732
  323.7 9.5 %copy-start.29 = (bf16[256,1024]{1,0:T(8,128)(2,1)S(1)}, bf16[256,1024]{1,0:T(8,128)(2,1)}, u32[]{:S(2)}) copy-start(bf16[256,1024]{1,0:T(8,128)(2,1)} %copy-done.28) | copy-start | bytes 1572868
  493.3 2.5 copy-start.49
  494.8 3.9 copy-start.50
  494.8 5.2 %copy-start.75 = (f32[128]{0:T(128)S(1)}, f32[128]{0:T(128)}, u32[]{:S(2)}) copy-start(f32[128]{0:T(128)} %get-tuple-element.124) | copy-start | bytes 1540
  494.8 5.2 %copy-start.74 = (f32[128]{0:T(128)S(1)}, f32[128]{0:T(128)}, u32[]{:S(2)}) copy-start(f32[128]{0:T(128)} %get-tuple-element.125) | copy-start | bytes 1540
  494.8 5.2 %copy-start.46 = (bf16[128,1024]{1,0:T(8,128)(2,1)S(1)}, bf16[128,1024]{1,0:T(8,128)(2,1)}, u32[]{:S(2)}) copy-start(bf16[128,1024]{1,0:T(8,128)(2,1)} %param.19) | copy-start | bytes 786436
  494.8 5.2 %copy-start.48 = (f32[128,1024]{1,0:T(8,128)S(1)}, f32[128,1024]{1,0:T(8,128)}, u32[]{:S(2)}) copy-start(f32[128,1024]{1,0:T(8,128)} %get-tuple-element.134) | copy-start | bytes 1572868
  494.8 5.2 %copy-start.65 = (f32[128]{0:T(128)S(1)}, f32[128]{0:T(128)}, u32[]{:S(2)}) copy-start(f32[128]{0:T(128)} %copy-done.63) | copy-start | bytes 1540
  494.8 5.2 %copy-start.71 = (f32[128]{0:T(128)S(1)}, f32[128]{0:T(128)}, u32[]{:S(2)}) copy-start(f32[128]{0:T(128)} %copy-done.69) | copy-start | bytes 1540
  (13 other events, 9.7 us)

commit v8 on v7

--- a/solution.py
+++ b/solution.py
@@ -12,7 +12,7 @@
 AXES = ("batch", "seq")
 ALL_SHARES = (3, 1, 0)
 ROWS = 64
-PACE = 1
+PACE = 2
 TURNS = (1, 0, 3, 4, 5, 8, 6, 2, 7, 9)
 HALF_SHARES = (5, 3)
 PAIR_SHARES = (2, 2)
@@ -251,7 +251,7 @@
     x_send, x_recv, local, c_send, c_recv, send, recv, cross_send, cross_recv, v_send, v_recv = refs
     rows, columns = tile
     number, depth = (out.shape[0], total.shape[0])
-    lags = [3 + 2 * stage for stage in range(stages)]
+    lags = [3 + stage + stage // 2 for stage in range(stages)]
     x, c = (cube.bit(0), cube.bit(cube.core))
     dims = sorted(order, reverse=True)
     bits = [cube.bit(k) for k in order]
@@ -472,7 +472,7 @@
         pltpu.VMEM((number,) + (2,) * (stages - 1 - stage) + tile, jnp.bfloat16)
         for stage in range(stages)
     ]
-    depth = 3 + 2 * (stages - 1) + 1
+    depth = 3 + (stages - 1) + (stages - 1) // 2 + 1
     paired = kinds.count("pair")
     vmem = pl.BlockSpec(memory_space=pltpu.VMEM)
     values = pltpu.VMEM((cube.count,) + value.shape, value.dtype)

time: 510 us -> 503 us (0.986)
  Pallas kernels: 442 us -> 436 us
    pallas_call x1, Pallas kernels: 170 us -> 165 us  [gather_fast(): pl.pallas_call(functools.partial(gather_kernel, cube, plans, items, first...]
where the time goes in v8:
time: 503 us; the launch traced here: 496 us
  Pallas kernels  436 us (87%)
  local copies, waits for them, and re-layouts  43.9 us (9%)
  other arithmetic  13.5 us (3%)
    pallas_call x1, Pallas kernels, gather_fast(): pl.pallas_call(functools.partial(gather_kernel, cube, plans, items, first...  165 us
    pallas_call x1, Pallas kernels, gradients_fast(): pl.pallas_call(functools.partial(gradient_kernel, cube, shapes, kinds, ti...  153 us
    pallas_call x3, Pallas kernels, ffn_fast(): pl.pallas_call(functools.partial(ffn_back_kernel if backward else ffn_ker...  42.9 us
    pallas_call x2, Pallas kernels, conv_fast(): pl.pallas_call(functools.partial(conv_kernel if forward else conv_back_ke...  40.9 us
    pallas_call x1, Pallas kernels, attend_fast(): pl.pallas_call(functools.partial(attend_kernel, cube, REL_LEFT, REL_RIGHT...  18.9 us
    unnamed x158, local copies, waits for them, and re-layouts  17.1 us
    pallas_call x1, Pallas kernels, attend_back_fast(): pl.pallas_call(functools.partial(attend_back_kernel, cube, REL_LEFT, REL_...  15.9 us

profile of v8, /device:TPU:0, one launch (start us, length us, event | category | flops | bytes accessed | tf_op | source)
XLA Modules:
  0.0 495.5 jit_solution(15582754405974871490)
XLA Ops:
  0.8 1.6 fusion.9
  2.4 1.1 convert_reduce_fusion
  3.5 1.2 multiply_reduce_fusion.11
  4.7 1.2 add_convert_fusion.4.refs_10_
  5.9 1.1 reshape.277
  7.2 1.1 reshape.279
  8.6 164.7 %gather_weights.1 = (bf16[2,2,2,2,128,1024]{5,4,3,2,1,0:T(8,128)(2,1)}, bf16[2,2,2,2,2,32,2048]{6,5,4,3,2,1,0:T(8,128)(2,1)}, bf16[2,2,2,2,2,32,1024]{6,5,4,3,2,...) custom-call(bf16[128,1024]{1,0:T(8,128)(2,1)S(1)} %copy-done.31, ...), custom_call_target="tpu_custom_call" | custom-call | tf_op jit(solution)/shard_map/gather_weights/pallas_call | solution.py:206
  173.4 1.0 copy-done.10
  174.4 0.8 copy-done.28
  176.2 0.5 copy-done
  176.7 18.9 %attend.1 = (f32[128,1024]{1,0:T(8,128)S(1)}, bf16[128,1024]{1,0:T(8,128)(2,1)S(1)}, bf16[3,256,512]{2,1,0:T(8,128)(2,1)S(1)}, f32[4,256,256]{2,1,0:T(8,128)S(1)}) custom-call(bf16[128,1024]{1,0:T(8,128)(2,1)S(1)} %add_convert_fusion.3.refs_0_, f32[128,1024]{1,0:T(8,128)S(1)} %get-tuple-element.68.refs_1_, f32[256,256]{1,0:T(8,128)S(1)} %compare_convert_fusion.refs_2_, ...), custom_call_target="tpu_custom_call" | custom-call | tf_op jit(solution)/shard_map/attend/pallas_call | solution.py:672
  195.6 1.0 copy-done.5
  196.7 0.9 copy-done.12
  197.5 0.7 copy-done.34
  198.3 0.6 compare_convert_fusion.1
  199.2 19.4 %conv.1 = (f32[128,1024]{1,0:T(8,128)S(1)}, f32[128,1024]{1,0:T(8,128)S(1)}, f32[128,128]{1,0:T(8,128)S(1)}, bf16[128,1024]{1,0:T(8,128)(2,1)S(1)}, f32[128,1024...) custom-call(f32[128,1024]{1,0:T(8,128)S(1)} %get-tuple-element.73.re, ...), custom_call_target="tpu_custom_call" | custom-call | tf_op jit(solution)/shard_map/conv/pallas_call | solution.py:1312
  218.7 0.8 copy-done.15
  219.5 0.8 copy-done.19
  220.3 0.8 copy-done.21
  221.1 0.8 copy-done.23
  221.9 0.8 copy-done.25
  222.7 0.7 copy-done.36
  224.1 13.3 %ffn.1 = (f32[128,1024]{1,0:T(8,128)S(1)}, f32[256,2048]{1,0:T(8,128)S(1)}, bf16[256,2048]{1,0:T(8,128)(2,1)S(1)}, bf16[256,1024]{1,0:T(8,128)(2,1)S(1)}) custom-call(bf16[128,1024]{1,0:T(8,128)(2,1)S(1)} %add_convert_fusion.2.refs_0_, f32[128,1024]{1,0:T(8,128)S(1)} %get-tuple-element.76.refs_1_, bf16[1024,2048]{1,0:T(8,128)(2,1)} %bitcast.117, ...), custom_call_target="tpu_custom_call" | custom-call | tf_op jit(solution)/shard_map/ffn/pallas_call | solution.py:1006
  237.4 1.3 copy-done.3
  238.7 0.8 copy-done.30
  239.9 0.9 multiply_reduce_fusion
  241.2 14.6 %ffn_back.2 = (f32[128,1024]{1,0:T(8,128)S(1)}, bf16[256,2048]{1,0:T(8,128)(2,1)S(1)}, bf16[256,1024]{1,0:T(8,128)(2,1)S(1)}) custom-call(bf16[128,1024]{1,0:T(8,128)(2,1)S(1)} %multiply_convert_fusion.1.refs_0_, f32[256,2048]{1,0:T(8,128)S(1)} %copy-done.4, bf16[1024,2048]{1,0:T(8,128)(2,1)} %bitcast.118, bf16[2048,1024]{1,0:T(8,128)(2,1)} %bitcast.120), custom_call_target="tpu_custom_call" | custom-call | tf_op jit(solution)/shard_map/ffn_back/pallas_call | solution.py:1006
  255.9 0.8 multiply_reduce_fusion.1
  256.9 1.1 multiply_add_fusion.1
  258.2 21.5 %conv_back.1 = (f32[128,1024]{1,0:T(8,128)S(1)}, bf16[128,1024]{1,0:T(8,128)(2,1)S(1)}, bf16[128,1024]{1,0:T(8,128)(2,1)S(1)}, bf16[128,2048]{1,0:T(8,128)(2,1)S(1)}, f32[16,1024]{1,0:T(8,128)S(1)}) custom-call(f32[128,1024]{1,0:T(8,128)S(1)} %get-tuple-element.141.refs_0_, f32[16,1024]{1,0:T(8,128)S(1)} %concatenate.9.refs_1_, f32[128,8]{1,0:T(8,128)S(1)} %pad.13.refs_2_, ...), custom_call_target="tpu_custom_call" | custom-call | tf_op jit(solution)/shard_map/conv_back/pallas_call | solution.py:1312
  279.7 0.8 copy-done.18
  280.5 0.7 copy-done.33
  281.2 15.9 %attend_back.1 = (f32[128,1024]{1,0:T(8,128)S(1)}, bf16[128,3072]{1,0:T(8,128)(2,1)S(1)}, f32[128,128]{1,0:T(8,128)S(1)}) custom-call(bf16[128,1024]{1,0:T(8,128)(2,1)S(1)} %get-tuple-element.90.refs_0_.refs_15_, bf16[3,256,512]{2,1,0:T(8,128)(2,1)S(1)} %copy-done.13, f32[4,256,256]{2,1,0:T(8,128)S(1)} %copy-done.6, bf16[128,128]{1,0:T(8,128)(2,1)S(1)} %pad.12.refs_3_, ...), custom_call_target="tpu_custom_call" | custom-call | tf_op jit(solution)/shard_map/attend_back/pallas_call | solution.py:802
  297.5 1.1 multiply_convert_fusion
  298.6 0.7 copy-done.2
  299.3 15.0 %ffn_back.3 = (f32[128,1024]{1,0:T(8,128)S(1)}, bf16[256,2048]{1,0:T(8,128)(2,1)S(1)}, bf16[256,1024]{1,0:T(8,128)(2,1)S(1)}) custom-call(bf16[128,1024]{1,0:T(8,128)(2,1)S(1)} %get-tuple-element.133.refs_0_, f32[256,2048]{1,0:T(8,128)S(1)} %copy-done.2, bf16[1024,2048]{1,0:T(8,128)(2,1)} %bitcast.132, bf16[2048,1024]{1,0:T(8,128)(2,1)} %bitcast.131), custom_call_target="tpu_custom_call" | custom-call | tf_op jit(solution)/shard_map/ffn_back/pallas_call | solution.py:1006
  314.3 1.0 copy-done.8
  315.3 0.9 multiply_reduce_fusion.3
  316.2 0.6 fusion.8
  317.0 0.7 reshape.305.refs_16_
  317.7 1.3 copy.92
  319.0 2.1 copy.93
  321.1 1.8 copy.96
  322.9 1.8 copy.98
  324.7 0.8 copy.99
  325.5 0.8 fusion.11
  326.3 0.8 copy.97
  327.2 1.3 copy.95
  328.5 1.0 copy.94
  329.5 152.6 %reduce_gradients.1 = (f32[23,32,1024]{2,1,0:T(8,128)}, f32[2,2,2,32,1024]{4,3,2,1,0:T(8,128)}, f32[32,1024]{1,0:T(8,128)}) custom-call(bf16[2,2,2,2,128,256]{5,4,3,2,1,0:T(8,128)(2,1)} %bitcast.129, bf16[2,2,2,2,64,256]{5,4,3,2,1,0:T(8,128)(2,1)} %bitcast.133, bf16[2,2,2,2,64,256]{5,4,3,2,1,0:T(8,128)(2,1)} %bitcast.134, ...), custom_call_target="tpu_custom_call" | custom-call | tf_op jit(solution)/shard_map/reduce_gradients/pallas_call | solution.py:479
  482.1 1.3 fusion.5
  483.4 0.4 copy.100
  483.9 1.2 reshape.306
  485.2 0.4 copy.103
  485.6 1.2 reshape.311
  486.8 1.2 slice_bitcast_fusion
  488.6 0.8 fusion.6
  489.3 1.1 fusion.4
  490.6 0.8 copy.106
  491.4 0.7 slice_bitcast_fusion.2
  492.2 0.6 slice.176
  492.8 0.6 fusion.7
  493.5 1.0 add_convert_fusion
  494.5 0.6 add_divide_fusion
  (199 shorter events, 5.1 us)
Async XLA Ops:
  0.7 7.8 %copy-start.44 = (bf16[128,1024]{1,0:T(8,128)(2,1)S(1)}, bf16[128,1024]{1,0:T(8,128)(2,1)}, u32[]{:S(2)}) copy-start(bf16[128,1024]{1,0:T(8,128)(2,1)} %param.19) | copy-start | bytes 786436
  0.7 7.9 %copy-start.31 = (bf16[128,1024]{1,0:T(8,128)(2,1)S(1)}, bf16[128,1024]{1,0:T(8,128)(2,1)}, u32[]{:S(2)}) copy-start(bf16[128,1024]{1,0:T(8,128)(2,1)} %refs_0_.1) | copy-start | bytes 786436
  0.7 7.9 %copy-start.42 = (bf16[32,1024]{1,0:T(8,128)(2,1)S(1)}, bf16[32,1024]{1,0:T(8,128)(2,1)}, u32[]{:S(2)}) copy-start(bf16[32,1024]{1,0:T(8,128)(2,1)} %refs_7_.1) | copy-start | bytes 196612
  0.7 7.9 %copy-start.39 = (bf16[32,1024]{1,0:T(8,128)(2,1)S(1)}, bf16[32,1024]{1,0:T(8,128)(2,1)}, u32[]{:S(2)}) copy-start(bf16[32,1024]{1,0:T(8,128)(2,1)} %refs_2_.1) | copy-start | bytes 196612
  0.7 7.9 %copy-start.40 = (bf16[32,1024]{1,0:T(8,128)(2,1)S(1)}, bf16[32,1024]{1,0:T(8,128)(2,1)}, u32[]{:S(2)}) copy-start(bf16[32,1024]{1,0:T(8,128)(2,1)} %refs_3_.1) | copy-start | bytes 196612
  0.7 7.9 %copy-start.41 = (bf16[32,1024]{1,0:T(8,128)(2,1)S(1)}, bf16[32,1024]{1,0:T(8,128)(2,1)}, u32[]{:S(2)}) copy-start(bf16[32,1024]{1,0:T(8,128)(2,1)} %refs_4_.1) | copy-start | bytes 196612
  0.7 7.9 %copy-start.38 = (bf16[32,2048]{1,0:T(8,128)(2,1)S(1)}, bf16[32,2048]{1,0:T(8,128)(2,1)}, u32[]{:S(2)}) copy-start(bf16[32,2048]{1,0:T(8,128)(2,1)} %refs_6_.1) | copy-start | bytes 393220
  0.7 7.9 %copy-start.43 = (bf16[32,1024]{1,0:T(8,128)(2,1)S(1)}, bf16[32,1024]{1,0:T(8,128)(2,1)}, u32[]{:S(2)}) copy-start(bf16[32,1024]{1,0:T(8,128)(2,1)} %refs_8_.1) | copy-start | bytes 196612
  0.7 7.9 %copy-start.32 = (bf16[128,1024]{1,0:T(8,128)(2,1)S(1)}, bf16[128,1024]{1,0:T(8,128)(2,1)}, u32[]{:S(2)}) copy-start(bf16[128,1024]{1,0:T(8,128)(2,1)} %refs_9_.1) | copy-start | bytes 786436
  2.4 173.1 %copy-start.51 = (f32[1,1024]{1,0:T(1,128)}, f32[1,1024]{1,0:T(1,128)S(1)}, u32[]{:S(2)}) copy-start(f32[1,1024]{1,0:T(1,128)S(1)} %get-tuple-element.171) | copy-start | bytes 12292
  3.5 169.9 %copy-start.63 = (f32[128]{0:T(128)}, f32[128]{0:T(128)S(1)}, u32[]{:S(2)}) copy-start(f32[128]{0:T(128)S(1)} %broadcast_multiply_fusion.11) | copy-start | bytes 1540
  4.7 168.7 %copy-start.69 = (f32[128]{0:T(128)}, f32[128]{0:T(128)S(1)}, u32[]{:S(2)}) copy-start(f32[128]{0:T(128)S(1)} %add_rsqrt_fusion.3) | copy-start | bytes 1540
  8.3 167.4 %copy-start.76 = (s32[1,4]{1,0:T(1,128)S(1)}, s32[1,4]{1,0:T(1,128)}, u32[]{:S(2)}) copy-start(s32[1,4]{1,0:T(1,128)} %param.20) | copy-start | bytes 52
  8.3 167.9 %copy-start.53 = (bf16[73,128]{1,0:T(8,128)(2,1)S(1)}, bf16[73,128]{1,0:T(8,128)(2,1)}, u32[]{:S(2)}) copy-start(bf16[73,128]{1,0:T(8,128)(2,1)} %param.33) | copy-start | bytes 56068
  173.4 1.0 copy-start.10
  175.1 1.6 copy-start
  175.3 20.4 %copy-start.61 = (f32[128]{0:T(128)}, f32[128]{0:T(128)S(1)}, u32[]{:S(2)}) copy-start(f32[128]{0:T(128)S(1)} %broadcast_multiply_fusion.10) | copy-start | bytes 1540
  176.7 22.4 %copy-start.60 = (bf16[5,1024]{1,0:T(8,128)(2,1)S(1)}, bf16[5,1024]{1,0:T(8,128)(2,1)}, u32[]{:S(2)}) copy-start(bf16[5,1024]{1,0:T(8,128)(2,1)} %param.32) | copy-start | bytes 30724
  176.7 22.4 %copy-start.72 = (f32[1024]{0:T(1024)S(1)}, f32[1024]{0:T(1024)}, u32[]{:S(2)}) copy-start(f32[1024]{0:T(1024)} %param.36) | copy-start | bytes 12292
  176.7 22.4 %copy-start.73 = (f32[1024]{0:T(1024)S(1)}, f32[1024]{0:T(1024)}, u32[]{:S(2)}) copy-start(f32[1024]{0:T(1024)} %param.37) | copy-start | bytes 12292
  195.6 1.0 copy-start.5
  196.7 0.9 copy-start.12
  199.2 24.5 %copy-start.55 = (f32[1,1024]{1,0:T(1,128)S(1)}, f32[1,1024]{1,0:T(1,128)}, u32[]{:S(2)}) copy-start(f32[1,1024]{1,0:T(1,128)} %get-tuple-element.169) | copy-start | bytes 12292
  224.1 15.8 %copy-start.47 = (bf16[128,1024]{1,0:T(8,128)(2,1)S(1)}, bf16[128,1024]{1,0:T(8,128)(2,1)}, u32[]{:S(2)}) copy-start(bf16[128,1024]{1,0:T(8,128)(2,1)} %param.21) | copy-start | bytes 786436
  224.1 15.8 %copy-start.68 = (f32[128]{0:T(128)S(1)}, f32[128]{0:T(128)}, u32[]{:S(2)}) copy-start(f32[128]{0:T(128)} %get-tuple-element.163) | copy-start | bytes 1540
  237.4 1.3 copy-start.3
  239.6 1.6 copy-start.4
  241.2 15.7 %copy-start.54 = (f32[1,1024]{1,0:T(1,128)S(1)}, f32[1,1024]{1,0:T(1,128)}, u32[]{:S(2)}) copy-start(f32[1,1024]{1,0:T(1,128)} %get-tuple-element.173) | copy-start | bytes 12292
  255.9 1.0 copy-start.7
  255.9 2.1 copy-start.17
  255.9 2.1 copy-start.16
  255.9 2.1 copy-start.20
  255.9 2.1 copy-start.22
  255.9 2.1 copy-start.24
  255.9 2.2 copy-start.26
  258.1 23.0 %copy-start.1 = (bf16[2,2,2,2,2,32,1024]{6,5,4,3,2,1,0:T(8,128)(2,1)S(1)}, bf16[2,2,2,2,2,32,1024]{6,5,4,3,2,1,0:T(8,128)(2,1)}, u32[]{:S(2)}) copy-start(bf16[2,2,2,2,2,32,1024]{6,5,4,3,2,1,0:T(8,128)(2,1)} %get-tuple-element.69) | copy-start | bytes 6291460
  258.2 23.0 %copy-start.6 = (f32[4,256,256]{2,1,0:T(8,128)S(1)}, f32[4,256,256]{2,1,0:T(8,128)}, u32[]{:S(2)}) copy-start(f32[4,256,256]{2,1,0:T(8,128)} %copy-done.5) | copy-start | bytes 3145732
  258.2 23.1 %copy-start.13 = (bf16[3,256,512]{2,1,0:T(8,128)(2,1)S(1)}, bf16[3,256,512]{2,1,0:T(8,128)(2,1)}, u32[]{:S(2)}) copy-start(bf16[3,256,512]{2,1,0:T(8,128)(2,1)} %copy-done.12) | copy-start | bytes 2359300
  281.2 15.9 %copy-start.9 = (bf16[128,1024]{1,0:T(8,128)(2,1)}, bf16[128,1024]{1,0:T(8,128)(2,1)S(1)}, u32[]{:S(2)}) copy-start(bf16[128,1024]{1,0:T(8,128)(2,1)S(1)} %get-tuple-element.90.refs_0_.refs_15_) | copy-start | bytes 786436
  281.2 16.0 %copy-start.62 = (f32[128]{0:T(128)S(1)}, f32[128]{0:T(128)}, u32[]{:S(2)}) copy-start(f32[128]{0:T(128)} %copy-done.61) | copy-start | bytes 1540
  281.2 16.0 %copy-start.67 = (f32[128]{0:T(128)S(1)}, f32[128]{0:T(128)}, u32[]{:S(2)}) copy-start(f32[128]{0:T(128)} %copy-done.66) | copy-start | bytes 1540
  297.1 17.1 %copy-start.14 = (bf16[128,3072]{1,0:T(8,128)(2,1)}, bf16[128,3072]{1,0:T(8,128)(2,1)S(1)}, u32[]{:S(2)}) copy-start(bf16[128,3072]{1,0:T(8,128)(2,1)S(1)} %get-tuple-element.110.refs_13_) | copy-start | bytes 2359300
  297.2 2.1 copy-start.2
  299.2 16.1 %copy-start.45 = (bf16[128,1024]{1,0:T(8,128)(2,1)S(1)}, bf16[128,1024]{1,0:T(8,128)(2,1)}, u32[]{:S(2)}) copy-start(bf16[128,1024]{1,0:T(8,128)(2,1)} %param.19) | copy-start | bytes 786436
  299.2 16.1 %copy-start.64 = (f32[128]{0:T(128)S(1)}, f32[128]{0:T(128)}, u32[]{:S(2)}) copy-start(f32[128]{0:T(128)} %copy-done.63) | copy-start | bytes 1540
  299.2 16.1 %copy-start.70 = (f32[128]{0:T(128)S(1)}, f32[128]{0:T(128)}, u32[]{:S(2)}) copy-start(f32[128]{0:T(128)} %copy-done.69) | copy-start | bytes 1540
  299.2 17.6 %copy-start.57 = (f32[1024]{0:T(1024)S(1)}, f32[1024]{0:T(1024)}, u32[]{:S(2)}) copy-start(f32[1024]{0:T(1024)} %get-tuple-element.121) | copy-start | bytes 12292
  299.2 17.6 %copy-start.59 = (f32[1024]{0:T(1024)S(1)}, f32[1024]{0:T(1024)}, u32[]{:S(2)}) copy-start(f32[1024]{0:T(1024)} %get-tuple-element.117) | copy-start | bytes 12292
  299.2 17.6 %copy-start.56 = (f32[1024]{0:T(1024)S(1)}, f32[1024]{0:T(1024)}, u32[]{:S(2)}) copy-start(f32[1024]{0:T(1024)} %get-tuple-element.132) | copy-start | bytes 12292
  299.3 17.6 %copy-start.58 = (f32[1024]{0:T(1024)S(1)}, f32[1024]{0:T(1024)}, u32[]{:S(2)}) copy-start(f32[1024]{0:T(1024)} %get-tuple-element.128) | copy-start | bytes 12292
  314.3 1.0 copy-start.8
  315.3 2.4 copy-start.27
  315.3 9.4 %copy-start.35 = (bf16[128,1024]{1,0:T(8,128)(2,1)S(1)}, bf16[128,1024]{1,0:T(8,128)(2,1)}, u32[]{:S(2)}) copy-start(bf16[128,1024]{1,0:T(8,128)(2,1)} %copy-done.34) | copy-start | bytes 786436
  316.2 9.3 %copy-start.52 = (f32[1,1024]{1,0:T(1,128)S(1)}, f32[1,1024]{1,0:T(1,128)}, u32[]{:S(2)}) copy-start(f32[1,1024]{1,0:T(1,128)} %copy-done.51) | copy-start | bytes 12292
  317.7 9.5 %copy-start.11 = (bf16[256,2048]{1,0:T(8,128)(2,1)S(1)}, bf16[256,2048]{1,0:T(8,128)(2,1)}, u32[]{:S(2)}) copy-start(bf16[256,2048]{1,0:T(8,128)(2,1)} %copy-done.10) | copy-start | bytes 3145732
  319.0 9.5 %copy-start.29 = (bf16[256,1024]{1,0:T(8,128)(2,1)S(1)}, bf16[256,1024]{1,0:T(8,128)(2,1)}, u32[]{:S(2)}) copy-start(bf16[256,1024]{1,0:T(8,128)(2,1)} %copy-done.28) | copy-start | bytes 1572868
  486.8 2.5 copy-start.49
  488.3 3.9 copy-start.50
  488.3 5.2 %copy-start.75 = (f32[128]{0:T(128)S(1)}, f32[128]{0:T(128)}, u32[]{:S(2)}) copy-start(f32[128]{0:T(128)} %get-tuple-element.124) | copy-start | bytes 1540
  488.3 5.2 %copy-start.74 = (f32[128]{0:T(128)S(1)}, f32[128]{0:T(128)}, u32[]{:S(2)}) copy-start(f32[128]{0:T(128)} %get-tuple-element.125) | copy-start | bytes 1540
  488.3 5.2 %copy-start.46 = (bf16[128,1024]{1,0:T(8,128)(2,1)S(1)}, bf16[128,1024]{1,0:T(8,128)(2,1)}, u32[]{:S(2)}) copy-start(bf16[128,1024]{1,0:T(8,128)(2,1)} %param.19) | copy-start | bytes 786436
  488.3 5.2 %copy-start.48 = (f32[128,1024]{1,0:T(8,128)S(1)}, f32[128,1024]{1,0:T(8,128)}, u32[]{:S(2)}) copy-start(f32[128,1024]{1,0:T(8,128)} %get-tuple-element.134) | copy-start | bytes 1572868
  488.3 5.2 %copy-start.65 = (f32[128]{0:T(128)S(1)}, f32[128]{0:T(128)}, u32[]{:S(2)}) copy-start(f32[128]{0:T(128)} %copy-done.63) | copy-start | bytes 1540
  488.3 5.2 %copy-start.71 = (f32[128]{0:T(128)S(1)}, f32[128]{0:T(128)}, u32[]{:S(2)}) copy-start(f32[128]{0:T(128)} %copy-done.69) | copy-start | bytes 1540
  (13 other events, 9.7 us)
